TPU v7x, 256 devices: a whole 4x4x8 slice. The times are simulated.
256 devices in a mesh: rep: 128 (over z, y, x_hi, core), shard: 2 (over x_lo).
Axes of the slice: x: 4 (x_hi: 2, x_lo: 2; x = x_hi * 2 + x_lo), y: 4, z: 8, core: 2. Of those that a mesh axis runs over, the one named last changes fastest.
Arguments:
- grads: float32 [128, 4, 384, 1536], P('rep', None, 'shard'), may hold values from -6 to 6
- basis: float32 [4, 384, 128], P(None, 'shard'), may hold values from -0.3125 to 0.3125
- weights: float32 [4, 384, 1536], P(None, 'shard'), may hold values from -0.3125 to 0.3125
- first_moment: float32 [4, 128, 1536], P(None, 'shard'), may hold values from -6 to 6
- second_moment: float32 [4, 128, 1536], P(None, 'shard'), may hold values from 0.01 to 1
Outputs:
- new_weights: float32 [4, 384, 1536], P(None, 'shard')
- new_first: float32 [4, 128, 1536], P(None, 'shard')
- new_second: float32 [4, 128, 1536], P(None, 'shard')
- new_basis: float32 [4, 384, 128], P(None, 'shard')
All inputs are finite; a program needn't handle non-finite values.
Results may differ from a plain program's by a relative error of at most 0.000057.
Values sent between devices are 32-bit elements; how exact they have to be, the bound alone decides.
No kernel may reach another device: no remote copies, remote signals or barrier semaphores. Data moves between devices by JAX's collectives and lax.ppermute only.
A program may use at most 128 MiB of HBM per device.

v0:
```python
import jax
import jax.numpy as jnp
from jax import lax
from jax.sharding import PartitionSpec as P

ADAM_STEP = 100


HIGH = lax.Precision.HIGHEST


def on_device(grads, basis, weights, first_moment, second_moment):
    local_grad = grads[0]
    source = lax.psum(local_grad, "rep")
    partial_proj = jnp.einsum("ldr,ldf->lrf", basis, source, precision=HIGH)
    proj_mine = lax.psum_scatter(partial_proj, "shard", scatter_dimension=1, tiled=True)
    new_first = 0.9 * first_moment + 0.1 * proj_mine
    new_second = 0.999 * second_moment + 0.001 * proj_mine * proj_mine
    direction = (
        new_first
        / (1.0 - 0.9**ADAM_STEP)
        / (jnp.sqrt(new_second / (1.0 - 0.999**ADAM_STEP)) + 1e-08)
    )
    full_proj, full_dir = (
        lax.all_gather(proj_mine, "shard", axis=1, tiled=True),
        lax.all_gather(direction, "shard", axis=1, tiled=True),
    )
    update = jnp.einsum("ldr,lrf->ldf", basis, full_dir, precision=HIGH)
    new_weights = weights - 0.0125 * update
    refresh_local = jnp.einsum("ldf,lrf->ldr", source, full_proj, precision=HIGH)
    gram_part = jnp.einsum("ldr,lds->lrs", refresh_local, refresh_local, precision=HIGH)
    gram_whole = lax.psum(gram_part, "shard")
    sumsq = jnp.einsum("lrr->l", gram_whole)
    factor = jnp.sqrt(jnp.float32(basis.shape[2])) / (2.0 * jnp.sqrt(sumsq + 1e-06))
    scaled = refresh_local * factor[:, None, None]
    gram_scaled = gram_whole * (factor * factor)[:, None, None]
    new_basis = 1.5 * scaled - 0.5 * jnp.einsum("ldr,lrs->lds", scaled, gram_scaled, precision=HIGH)
    return (new_weights, new_first, new_second, new_basis)


def solution(mesh):
    placed = (
        P("rep", None, "shard", None),
        P(None, "shard", None),
        P(None, "shard", None),
        P(None, "shard", None),
        P(None, "shard", None),
    )
    return jax.shard_map(
        on_device,
        mesh=mesh,
        in_specs=placed,
        out_specs=(
            P(None, "shard", None),
            P(None, "shard", None),
            P(None, "shard", None),
            P(None, "shard", None),
        ),
        check_vma=False,
    )
```

profile of v0, /device:TPU:1, one launch (start us, length us, event | category | flops | bytes accessed | tf_op | source)
XLA Modules:
  0.0 1489.0 jit_solution(3544803541384285721)
XLA Ops:
  7.2 0.0 copy-start
  7.2 0.0 all-reduce.3.cloned.1.call-start
  7.2 0.7 all-reduce.3.cloned.1.call-update
  7.9 0.0 reduce-scatter.2.cloned.1.call-start
  8.0 1272.2 %all-reduce.3.cloned.1.call-done = f32[4,192,1536]{2,1,0:T(8,128)} async-done(((f32[4,192,1536]{2,1,0:T(8,128)}), f32[4,192,1536]{2,1,0:T(8,128)}) %all-reduce.3.cloned.1.call-update) | async-done | bytes 4718608 | tf_op jit(solution)/shard_map/psum | solution.py:14
  1280.1 0.0 copy-done
  1280.1 7.0 fusion.8
  1287.1 0.0 copy-start.2
  1287.1 0.0 reduce-scatter.2.cloned.1.call-update
  1287.2 0.0 all-gather.5.cloned.1.call-start
  1287.2 47.3 %reduce-scatter.2.cloned.1.call-done = f32[4,64,1536]{2,1,0:T(8,128)} async-done(((f32[4,128,1536]{2,1,0:T(8,128)}), f32[4,64,1536]{2,1,0:T(8,128)}) %reduce-scatter.2.cloned.1.call-update) | async-done | bytes 1572880 | tf_op jit(solution)/shard_map/reduce_scatter | solution.py:16
  1334.5 0.0 copy-start.1
  1334.5 0.0 all-gather.5.cloned.1.call-update
  1334.5 0.0 all-gather.3.cloned.1.call-start
  1334.6 0.0 copy-done.2
  1334.6 1.3 copy-done.1
  1335.9 4.2 add_divide_fusion
  1340.1 0.0 all-gather.3.cloned.1.call-update
  1340.2 0.2 all-reduce.5.cloned.1.call-start
  1340.4 46.9 %all-gather.5.cloned.1.call-done = f32[4,128,1536]{2,1,0:T(8,128)} async-done(((f32[4,64,1536]{2,1,0:T(8,128)}), f32[4,128,1536]{2,1,0:T(8,128)}) %all-gather.5.cloned.1.call-update) | async-done | bytes 3145744 | tf_op jit(solution)/shard_map/all_gather | solution.py:25
  1387.3 7.5 fusion.9
  1394.9 1.8 fusion.10
  1396.7 0.0 all-reduce.5.cloned.1.call-update
  1396.7 43.9 %all-gather.3.cloned.1.call-done = f32[4,128,1536]{2,1,0:T(8,128)} async-done(((f32[4,64,1536]{2,1,0:T(8,128)}), f32[4,128,1536]{2,1,0:T(8,128)}) %all-gather.3.cloned.1.call-update) | async-done | bytes 3145744 | tf_op jit(solution)/shard_map/all_gather | solution.py:26
  1440.6 9.7 bitcast_subtract_fusion
  1450.3 28.8 %all-reduce.5.cloned.1.call-done = f32[4,128,128]{2,1,0:T(8,128)} async-done(((f32[4,128,128]{2,1,0:T(8,128)}), f32[4,128,128]{2,1,0:T(8,128)}) %all-reduce.5.cloned.1.call-update) | async-done | bytes 262160 | tf_op jit(solution)/shard_map/psum | solution.py:32
  1479.1 1.1 select_reduce_fusion
  1480.2 2.3 fusion.1
  (2 shorter events, 0.0 us)
Async XLA Ops:
  7.2 1273.0 %copy-start = (f32[4,192,128]{2,1,0:T(8,128)S(1)}, f32[4,192,128]{2,1,0:T(8,128)}, u32[]{:S(2)}) copy-start(f32[4,192,128]{2,1,0:T(8,128)} %param.6) | copy-start | bytes 1179652
  7.2 1272.9 %all-reduce.3.cloned.1.call-start = ((), (), s32[]{:S(2)}) async-start(), calls=%async_computation.1 | async-start | bytes 9437184 | tf_op jit(solution)/shard_map/psum | solution.py:14
  7.9 1326.6 %reduce-scatter.2.cloned.1.call-start = ((), (), s32[]{:S(2)}) async-start(), calls=%async_computation.2 | async-start | bytes 4718592 | tf_op jit(solution)/shard_map/reduce_scatter | solution.py:16
  1287.1 47.4 %copy-start.2 = (f32[4,64,1536]{2,1,0:T(8,128)S(1)}, f32[4,64,1536]{2,1,0:T(8,128)}, u32[]{:S(2)}) copy-start(f32[4,64,1536]{2,1,0:T(8,128)} %param.8) | copy-start | bytes 4718596
  1287.2 100.2 %all-gather.5.cloned.1.call-start = ((), (), s32[]{:S(2)}) async-start(), calls=%async_computation.4 | async-start | bytes 4718592 | tf_op jit(solution)/shard_map/all_gather | solution.py:25
  1334.5 1.4 copy-start.1
  1334.5 106.1 %all-gather.3.cloned.1.call-start = ((), (), s32[]{:S(2)}) async-start(), calls=%async_computation.3 | async-start | bytes 4718592 | tf_op jit(solution)/shard_map/all_gather | solution.py:26
  1340.2 138.9 %all-reduce.5.cloned.1.call-start = ((), (), s32[]{:S(2)}) async-start(), calls=%async_computation.5 | async-start | bytes 524288 | tf_op jit(solution)/shard_map/psum | solution.py:32
Sparse Core Ops, SparseCore 0:
  10.6 1269.4 all-reduce.2
  1287.3 47.1 reduce-scatter.1
  1336.3 50.9 all-gather.4
  1389.6 50.9 all-gather.2
  1443.6 35.4 all-reduce.4
where the time goes:
time: 1490 us
  waiting for transfers between devices  1440 us (97%)
  matrix products  28.3 us (2%)
    psum x1, waiting for transfers between devices, on_device(): source = lax.psum(local_grad, 'rep')  1270 us
    reduce_scatter x1, waiting for transfers between devices, on_device(): lax.psum_scatter(partial_proj, 'shard', scatter_dimension=1, tiled=True)  47.3 us
    all_gather x1, waiting for transfers between devices, on_device(): lax.all_gather(proj_mine, 'shard', axis=1, tiled=True)  46.9 us
    all_gather x1, waiting for transfers between devices, on_device(): lax.all_gather(direction, 'shard', axis=1, tiled=True)  43.9 us
  transfers between devices with their start and end apart: 5, of which 5 were waited for; matrix products, arithmetic and copies ran while one was open for 2% of the time, Pallas kernels for 0%

commit v1 on v0

v1 whole, which is shorter than its diff:
```python
import jax
import jax.numpy as jnp
from jax import lax
from jax.sharding import Mesh, PartitionSpec as P

ADAM_STEP = 100
HIGH = lax.Precision.HIGHEST

SIZES = {"z": 8, "y": 4, "xh": 2, "core": 2, "xl": 2}
REP = ("z", "y", "xh", "core")


def shift(x, axis, k):
    n = SIZES[axis]
    return lax.ppermute(x, axis, [(i, (i + k) % n) for i in range(n)])


def flip(x, axis, bit=1):
    n = SIZES[axis]
    return lax.ppermute(x, axis, [(i, i ^ bit) for i in range(n)])


def rows(x, index, count):
    return lax.dynamic_slice_in_dim(x, index * count, count, 0)


def in_order(index, mine, other):
    first = index == 0
    return jnp.where(first, mine, other), jnp.where(first, other, mine)


def scatter_direct(x, axis):
    n, me = SIZES[axis], lax.axis_index(axis)
    count = x.shape[0] // n
    total = rows(x, me, count)
    for k in range(1, n):
        total = total + shift(rows(x, (me + k) % n, count), axis, k)
    return total


def gather_direct(x, axis):
    n, me = SIZES[axis], lax.axis_index(axis)
    count = x.shape[0]
    out = jnp.zeros((n * count,) + x.shape[1:], x.dtype)
    out = lax.dynamic_update_slice_in_dim(out, x, me * count, 0)
    for k in range(1, n):
        out = lax.dynamic_update_slice_in_dim(out, shift(x, axis, k), ((me - k) % n) * count, 0)
    return out


def scatter_exchange(x, axis):
    n = SIZES[axis]
    parts = x.reshape((n, x.shape[0] // n) + x.shape[1:])
    return jnp.sum(lax.all_to_all(parts, axis, split_axis=0, concat_axis=0), axis=0)


def on_device(grads, basis, weights, first_moment, second_moment):
    layers, depth, width = grads.shape[1:]
    rank = basis.shape[2]
    half = layers // 2
    piece = width // 64
    z, y, xh = lax.axis_index("z"), lax.axis_index("y"), lax.axis_index("xh")
    core, xl = lax.axis_index("core"), lax.axis_index("xl")
    place = (y * 2 + xh) * 8 + z

    given = flip(rows(grads[0], 1 - core, half), "core")
    pair = rows(grads[0], core, half) + given
    held = pair.reshape(half * depth, width).T
    held = scatter_direct(held, "y")
    held = scatter_direct(held, "xh")
    total = scatter_exchange(held, "z").reshape(piece, half, depth)

    basis_pair = rows(basis, core, half)
    cut = [
        jnp.swapaxes(lax.dynamic_slice(m, (core * half, 0, place * piece), (half, rank // 2, piece)), 1, 2)
        for m in (first_moment, second_moment)
    ]
    cut = jnp.concatenate(cut, axis=2)
    low, high = in_order(xl, cut, flip(cut, "xl"))
    first = jnp.concatenate([low[:, :, : rank // 2], high[:, :, : rank // 2]], axis=2)
    second = jnp.concatenate([low[:, :, rank // 2 :], high[:, :, rank // 2 :]], axis=2)

    proj = jnp.einsum("fld,ldr->lfr", total, basis_pair, precision=HIGH)
    proj = proj + flip(proj, "xl")
    new_first = 0.9 * first + 0.1 * proj
    new_second = 0.999 * second + 0.001 * proj * proj
    direction = (
        new_first
        / (1.0 - 0.9**ADAM_STEP)
        / (jnp.sqrt(new_second / (1.0 - 0.999**ADAM_STEP)) + 1e-08)
    )
    mine = jnp.where(xl == 0, proj[:, :, : rank // 2], proj[:, :, rank // 2 :])
    packed = jnp.concatenate([direction[0], direction[1], mine[0], mine[1]], axis=1)

    refresh = jnp.einsum("fld,lfr->ldr", total, proj, precision=HIGH)
    part = scatter_exchange(refresh.reshape(half * depth, rank), "z")
    part = part + flip(part, "y", 1)
    part = part + flip(part, "y", 2)
    part = part + flip(part, "xh")
    refresh = lax.all_gather(part, "z", axis=0, tiled=True).reshape(half, depth, rank)
    gram = jnp.einsum("ldr,lds->lrs", refresh, refresh, precision=HIGH)
    gram = gram + flip(gram, "xl")
    sumsq = jnp.einsum("lrr->l", gram)
    factor = jnp.sqrt(jnp.float32(rank)) / (2.0 * jnp.sqrt(sumsq + 1e-06))
    scaled = refresh * factor[:, None, None]
    gram_scaled = gram * (factor * factor)[:, None, None]
    basis_new = 1.5 * scaled - 0.5 * jnp.einsum("ldr,lrs->lds", scaled, gram_scaled, precision=HIGH)
    new_basis = jnp.concatenate(in_order(core, basis_new, flip(basis_new, "core")), axis=0)

    packed = lax.all_gather(packed, "z", axis=0, tiled=True)
    packed = gather_direct(packed, "xh")
    packed = gather_direct(packed, "y")
    packed = jnp.stack(in_order(core, packed, flip(packed, "core")))
    dirs = packed[:, :, : half * rank].reshape(2, width, half, rank)
    own = packed[:, :, half * rank :].reshape(2, width, half, rank // 2)
    own = jnp.transpose(own, (0, 2, 3, 1)).reshape(layers, rank // 2, width)
    new_first = 0.9 * first_moment + 0.1 * own
    new_second = 0.999 * second_moment + 0.001 * own * own
    dirs = jnp.transpose(dirs, (0, 2, 1, 3)).reshape(layers, width, rank)
    update = jnp.einsum("ldr,lfr->ldf", basis, dirs, precision=HIGH)
    new_weights = weights - 0.0125 * update
    return (new_weights, new_first, new_second, new_basis)


def solution(mesh):
    fine = Mesh(mesh.devices.reshape(8, 4, 2, 2, 2), ("z", "y", "xh", "core", "xl"))
    split = P(None, "xl", None)
    return jax.shard_map(
        on_device,
        mesh=fine,
        in_specs=(P(REP, None, "xl", None), split, split, split, split),
        out_specs=(split, split, split, split),
        check_vma=False,
    )
```

time: 1490 us -> 225 us (0.15)
  waiting for transfers between devices: 1440 us -> 76.2 us
  starting transfers between devices: 0.38 us -> 53.7 us
  blocking collectives: 0 us -> 51 us
  matrix products: 28.3 us -> 9.18 us
  local copies, waits for them, and re-layouts: 1.34 us -> 18.9 us
    psum x2 -> x0, waiting for transfers between devices: 1300 us -> none  [the longest x1 1270 us: on_device(): source = lax.psum(local_grad, 'rep')]
    all_gather x2 -> x0, waiting for transfers between devices: 90.8 us -> none  [the longest x1 46.9 us: on_device(): lax.all_gather(proj_mine, 'shard', axis=1, tiled=True)]
    ppermute x0 -> x17, waiting for transfers between devices: none -> 68.8 us  [the longest x8 49.8 us: shift(): return lax.ppermute(x, axis, [(i, (i + k) % n) for i in range(n)])]
    reduce_scatter x1 -> x0, waiting for transfers between devices: 47.3 us -> none  [on_device(): lax.psum_scatter(partial_proj, 'shard', scatter_dimension=1, tiled=True)]
    ppermute x0 -> x17, starting transfers between devices: none -> 45.5 us  [the longest x9 34.5 us: flip(): return lax.ppermute(x, axis, [(i, i ^ bit) for i in range(n)])]
    all_gather x0 -> x2, blocking collectives: none -> 37.4 us  [the longest x1 18.8 us: on_device(): packed = lax.all_gather(packed, 'z', axis=0, tiled=True)]
    dot_general x4, matrix products: 26 us -> 8.78 us  [the longest x1 7.35 us: on_device(): update = jnp.einsum('ldr,lfr->ldf', basis, dirs, precision=HIGH)]
  transfers between devices with their start and end apart: 5 -> 18, of which waited for: 5 -> 15; matrix products, arithmetic and copies ran while one was open for 2% -> 5% of each run, Pallas kernels for 0% -> 0%
where the time goes in v1:
time: 225 us
  waiting for transfers between devices  76.2 us (34%)
  starting transfers between devices  53.7 us (24%)
  blocking collectives  51 us (23%)
  local copies, waits for them, and re-layouts  18.9 us (8%)
  other arithmetic  14.8 us (7%)
  matrix products  9.18 us (4%)
    ppermute x8, waiting for transfers between devices, shift(): return lax.ppermute(x, axis, [(i, (i + k) % n) for i in range(n)])  49.8 us
    ppermute x9, starting transfers between devices, flip(): return lax.ppermute(x, axis, [(i, i ^ bit) for i in range(n)])  34.5 us
    ppermute x9, waiting for transfers between devices, flip(): return lax.ppermute(x, axis, [(i, i ^ bit) for i in range(n)])  19 us
    all_gather x1, blocking collectives, on_device(): packed = lax.all_gather(packed, 'z', axis=0, tiled=True)  18.8 us
    all_gather x1, blocking collectives, on_device(): lax.all_gather(part, 'z', axis=0, tiled=True).reshape(half, depth, rank)  18.6 us
    all_to_all x1, blocking collectives, scatter_exchange(): lax.all_to_all(parts, axis, split_axis=0, concat_axis=0)  13.6 us
    ppermute x8, starting transfers between devices, shift(): return lax.ppermute(x, axis, [(i, (i + k) % n) for i in range(n)])  11 us
    all_to_all x1, starting transfers between devices, scatter_exchange(): lax.all_to_all(parts, axis, split_axis=0, concat_axis=0)  8.19 us
  transfers between devices with their start and end apart: 18, of which 15 were waited for; matrix products, arithmetic and copies ran while one was open for 5% of the time, Pallas kernels for 0%

profile of v1, /device:TPU:1, one launch (start us, length us, event | category | flops | bytes accessed | tf_op | source)
XLA Modules:
  0.0 224.6 jit_solution(4249226077808333504)
XLA Ops:
  0.7 1.9 dynamic-slice_bitcast_fusion
  2.5 3.3 %collective-permute-start.1 = (f32[2,192,1536]{2,1,0:T(8,128)S(1)}, f32[2,192,1536]{2,1,0:T(8,128)}, u32[]{:S(2)}, u32[]{:S(2)}) collective-permute-start(f32[2,192,1536]{2,1,0:T(8,128)S(1)} %dynamic-slice_bitcast_fusion), channel_id=1, source_target_pairs={{0,2},{2,0},{1,3},{3,1},{4,6},{6,4},{5,7},{7,5},{8,10},{10,8},{9,1... | collective-permute-start | bytes 7077896 | tf_op jit(solution)/shard_map/ppermute | solution.py:20
  5.9 4.3 %collective-permute-done.1 = f32[2,192,1536]{2,1,0:T(8,128)} collective-permute-done((f32[2,192,1536]{2,1,0:T(8,128)S(1)}, f32[2,192,1536]{2,1,0:T(8,128)}, u32[]{:S(2)}, u32[]{:S(2)}) %collective-permute-start.1) | collective-permute-done | bytes 2359328 | tf_op jit(solution)/shard_map/ppermute | solution.py:20
  10.1 2.8 %bitcast_add_fusion = f32[2,192,1536]{2,1,0:T(8,128)S(1)} fusion(f32[2,192,1536]{2,1,0:T(8,128)} %collective-permute-done.1, f32[1,4,192,1536]{3,2,1,0:T(8,128)} %param.5, s32[]{:T(128)S(6)} %select_n.129), kind=kLoop, calls=%fused_computation.7 | loop fusion | flops 589824 | bytes 7077892 | tf_op jit(solution)/shard_map/add | solution.py:67
  12.9 1.2 dynamic-slice_bitcast_fusion.3
  14.1 1.0 collective-permute-start.4
  15.1 0.3 collective-permute-start.3
  15.4 0.7 collective-permute-start.2
  16.1 12.8 %collective-permute-done.4 = f32[384,384]{0,1:T(8,128)} collective-permute-done((f32[384,384]{0,1:T(8,128)}, f32[384,384]{0,1:T(8,128)}, u32[]{:S(2)}, u32[]{:S(2)}) %collective-permute-start.4) | collective-permute-done | bytes 589856 | tf_op jit(solution)/shard_map/ppermute | solution.py:15
  28.9 2.3 %collective-permute-done.3 = f32[384,384]{0,1:T(8,128)} collective-permute-done((f32[384,384]{0,1:T(8,128)}, f32[384,384]{0,1:T(8,128)}, u32[]{:S(2)}, u32[]{:S(2)}) %collective-permute-start.3) | collective-permute-done | bytes 589856 | tf_op jit(solution)/shard_map/ppermute | solution.py:15
  31.2 13.3 %collective-permute-done.2 = f32[384,384]{0,1:T(8,128)} collective-permute-done((f32[384,384]{0,1:T(8,128)S(1)}, f32[384,384]{0,1:T(8,128)}, u32[]{:S(2)}, u32[]{:S(2)}) %collective-permute-start.2) | collective-permute-done | bytes 589856 | tf_op jit(solution)/shard_map/ppermute | solution.py:15
  44.5 1.5 fusion.4
  46.0 0.2 constant_dynamic-slice_fusion
  46.2 2.8 %collective-permute-start.5 = (f32[192,384]{0,1:T(8,128)S(1)}, f32[192,384]{0,1:T(8,128)S(1)}, u32[]{:S(2)}, u32[]{:S(2)}) collective-permute-start(f32[192,384]{0,1:T(8,128)S(1)} %constant_dynamic-slice_fusion), channel_id=1, source_target_pairs={{0,4},{4,0},{1,5},{5,1},{2,6},{6,2},{3,7},{7,3},{8,12},{12,8},{9,1... | collective-permute-start | bytes 884744 | tf_op jit(solution)/shard_map/ppermute | solution.py:15
  49.0 1.1 constant_dynamic-slice_fusion.1
  50.3 7.6 %collective-permute-done.5 = f32[192,384]{0,1:T(8,128)S(1)} collective-permute-done((f32[192,384]{0,1:T(8,128)S(1)}, f32[192,384]{0,1:T(8,128)S(1)}, u32[]{:S(2)}, u32[]{:S(2)}) %collective-permute-start.5) | collective-permute-done | bytes 294944 | tf_op jit(solution)/shard_map/ppermute | solution.py:15
  57.8 0.2 dynamic-slice_add_fusion
  58.0 0.9 copy.21
  58.9 8.2 %all-to-all-start = ((f32[8,24,384]{2,1,0:T(8,128)}), f32[8,24,384]{2,1,0:T(8,128)S(1)}, u32[]{:S(2)}, u32[]{:S(2)}) async-start(f32[8,24,384]{2,1,0:T(8,128)} %bitcast.9), calls=%async_computation | async-start | bytes 589824 | tf_op jit(solution)/shard_map/all_to_all | solution.py:54
  67.1 1.2 collective-permute-start
  68.4 1.5 collective-permute-done
  70.0 7.4 %all-to-all-done = f32[8,24,384]{2,1,0:T(8,128)S(1)} async-done(((f32[8,24,384]{2,1,0:T(8,128)}), f32[8,24,384]{2,1,0:T(8,128)S(1)}, u32[]{:S(2)}, u32[]{:S(2)}) %all-to-all-start) | async-done | bytes 294944 | tf_op jit(solution)/shard_map/all_to_all | solution.py:54
  77.4 0.1 reshape.43
  77.5 0.3 fusion.5
  77.8 1.3 collective-permute-start.6
  79.1 1.4 collective-permute-done.6
  80.5 0.1 fusion.20
  80.8 18.8 %all_gather.6 = f32[192,384]{1,0:T(8,128)S(1)} all-gather(f32[24,384]{1,0:T(8,128)S(1)} %pad_maximum_fusion.3), channel_id=1, replica_groups=mesh['z'=8,'y'=4,'xh'=2,'core'=2,'xl'=2] {'z'}, dimensions={0}, use_global_device_ids=true | all-gather | bytes 331776 | tf_op jit(solution)/shard_map/all_gather | solution.py:110
  99.6 2.7 %collective-permute-start.7 = (f32[192,384]{1,0:T(8,128)S(1)}, f32[192,384]{1,0:T(8,128)S(1)}, u32[]{:S(2)}, u32[]{:S(2)}) collective-permute-start(f32[192,384]{1,0:T(8,128)S(1)} %all_gather.6), channel_id=1, source_target_pairs={{0,4},{4,0},{1,5},{5,1},{2,6},{6,2},{3,7},{7,3},{8,12},{12,8},{9,1... | collective-permute-start | bytes 884744 | tf_op jit(solution)/shard_map/ppermute | solution.py:15
  102.3 0.2 copy.23
  102.5 3.5 %dynamic_update_slice.18 = f32[384,384]{0,1:T(8,128)S(1)} dynamic-update-slice(f32[384,384]{0,1:T(8,128)S(1)} %broadcast_in_dim.15, f32[192,384]{0,1:T(8,128)S(1)} %copy.23, s32[]{:T(128)S(6)} %select_n.141, s32[]{:T(128)} %constant.94.clone.1) | dynamic-update-slice | bytes 589828 | tf_op jit(solution)/shard_map/dynamic_update_slice | solution.py:45
  106.0 0.6 collective-permute-done.7
  106.6 0.2 copy.24
  106.8 3.4 %dynamic_update_slice.19 = f32[384,384]{0,1:T(8,128)S(1)} dynamic-update-slice(f32[384,384]{0,1:T(8,128)S(1)} %dynamic_update_slice.18, f32[192,384]{0,1:T(8,128)S(1)} %copy.24, s32[]{:T(128)S(6)} %select_n.147, s32[]{:T(128)} %constant.94.clone.1) | dynamic-update-slice | bytes 589828 | tf_op jit(solution)/shard_map/dynamic_update_slice | solution.py:47
  110.3 1.3 collective-permute-start.9
  111.6 2.0 collective-permute-start.10
  113.6 0.3 broadcast_in_dim.14
  114.0 13.3 %collective-permute-done.8 = f32[384,384]{0,1:T(8,128)} collective-permute-done((f32[384,384]{0,1:T(8,128)S(1)}, f32[384,384]{0,1:T(8,128)}, u32[]{:S(2)}, u32[]{:S(2)}) %collective-permute-start.8) | collective-permute-done | bytes 589856 | tf_op jit(solution)/shard_map/ppermute | solution.py:15
  127.2 1.1 constant_dynamic-update-slice_fusion.2
  128.4 1.1 constant_dynamic-update-slice_fusion.1
  129.5 1.1 constant_dynamic-update-slice_fusion
  130.7 13.0 %collective-permute-start.11 = (f32[1536,384]{0,1:T(8,128)S(1)}, f32[1536,384]{0,1:T(8,128)}, u32[]{:S(2)}, u32[]{:S(2)}) collective-permute-start(f32[1536,384]{0,1:T(8,128)S(1)} %constant_dynamic-update-slice_fusion), channel_id=1, source_target_pairs={{0,2},{2,0},{1,3},{3,1},{4,6},{6,4},{5,7},{7,5},{8,10},{10,8},{9,1... | collective-permute-start | bytes 7077896 | tf_op jit(solution)/shard_map/ppermute | solution.py:20
  143.7 0.5 fusion.13
  144.2 13.6 %all_to_all.10 = f32[8,48,128]{2,1,0:T(8,128)S(1)} all-to-all(f32[8,48,128]{2,1,0:T(8,128)S(1)} %bitcast.53), channel_id=1, replica_groups=mesh['z'=8,'y'=4,'xh'=2,'core'=2,'xl'=2] {'z'}, dimensions={0} | all-to-all | bytes 393216 | tf_op jit(solution)/shard_map/all_to_all | solution.py:54
  157.9 2.7 %collective-permute-done.12 = f32[48,128]{1,0:T(8,128)S(1)} collective-permute-done((f32[48,128]{1,0:T(8,128)S(1)}, f32[48,128]{1,0:T(8,128)S(1)}, u32[]{:S(2)}, u32[]{:S(2)}) %collective-permute-start.12) | collective-permute-done | bytes 24608 | tf_op jit(solution)/shard_map/ppermute | solution.py:20
  160.6 0.3 collective-permute-start.13
  160.8 3.9 %collective-permute-done.13 = f32[48,128]{1,0:T(8,128)S(1)} collective-permute-done((f32[48,128]{1,0:T(8,128)S(1)}, f32[48,128]{1,0:T(8,128)S(1)}, u32[]{:S(2)}, u32[]{:S(2)}) %collective-permute-start.13) | collective-permute-done | bytes 24608 | tf_op jit(solution)/shard_map/ppermute | solution.py:20
  164.7 2.8 %collective-permute-start.14 = (f32[48,128]{1,0:T(8,128)S(1)}, f32[48,128]{1,0:T(8,128)S(1)}, u32[]{:S(2)}, u32[]{:S(2)}) collective-permute-start(f32[48,128]{1,0:T(8,128)S(1)} %add.190), channel_id=1, source_target_pairs={{0,4},{4,0},{1,5},{5,1},{2,6},{6,2},{3,7},{7,3},{8,12},{12,8},{9,1... | collective-permute-start | bytes 73736 | tf_op jit(solution)/shard_map/ppermute | solution.py:20
  167.6 1.4 collective-permute-done.14
  168.9 18.6 %all_gather.7 = f32[384,128]{1,0:T(8,128)S(1)} all-gather(f32[48,128]{1,0:T(8,128)S(1)} %add.191), channel_id=1, replica_groups=mesh['z'=8,'y'=4,'xh'=2,'core'=2,'xl'=2] {'z'}, dimensions={0}, use_global_device_ids=true | all-gather | bytes 221184 | tf_op jit(solution)/shard_map/all_gather | solution.py:100
  187.6 0.7 fusion.27
  188.2 1.3 collective-permute-start.15
  189.6 2.9 %collective-permute-done.15 = f32[2,128,128]{2,1,0:T(8,128)S(1)} collective-permute-done((f32[2,128,128]{2,1,0:T(8,128)S(1)}, f32[2,128,128]{2,1,0:T(8,128)S(1)}, u32[]{:S(2)}, u32[]{:S(2)}) %collective-permute-start.15) | collective-permute-done | bytes 131104 | tf_op jit(solution)/shard_map/ppermute | solution.py:20
  192.4 0.1 select_reduce_fusion
  192.6 0.4 multiply_subtract_fusion
  193.0 11.1 %collective-permute-start.16 = (f32[2,192,128]{2,1,0:T(8,128)S(1)}, f32[2,192,128]{2,1,0:T(8,128)S(1)}, u32[]{:S(2)}, u32[]{:S(2)}) collective-permute-start(f32[2,192,128]{2,1,0:T(8,128)S(1)} %multiply_subtract_fusion), channel_id=1, source_target_pairs={{0,2},{2,0},{1,3},{3,1},{4,6},{6,4},{5,7},{7,5},{8,10},{10,8},{9,1... | collective-permute-start | bytes 589832 | tf_op jit(solution)/shard_map/ppermute | solution.py:20
  204.1 1.1 collective-permute-done.16
  205.2 0.8 pad_maximum_fusion.2
  206.0 2.1 select_bitcast_fusion
  208.1 1.7 pad_maximum_fusion.1
  209.8 0.3 pad_maximum_fusion
  210.1 2.4 %copy.25 = f32[2,3072,128]{2,1,0:T(8,128)} copy(f32[2,3072,128]{1,2,0:T(8,128)S(1)} %pad_maximum_fusion) | data formatting | bytes 6291456 | tf_op jit(solution)/shard_map/concatenate
  212.4 4.9 %fusion = (f32[4,64,1536]{2,1,0:T(8,128)}, f32[4,64,1536]{2,1,0:T(8,128)}) fusion(f32[4,64,1536]{2,1,0:T(8,128)} %bitcast.50, f32[4,64,1536]{2,1,0:T(8,128)} %param.9, f32[4,64,1536]{2,1,0:T(8,128)} %param.8), kind=kLoop, calls=%fused_computation.11 | loop fusion | flops 2752512 | bytes 7864320 | tf_op jit(solution)/shard_map/add | solution.py:118
  217.3 7.3 %bitcast_subtract_fusion = f32[4,192,1536]{2,1,0:T(8,128)} fusion(f32[4,192,1536]{2,1,0:T(8,128)} %param.7, f32[4,1536,128]{2,1,0:T(8,128)S(1)} %bitcast.47, f32[4,192,128]{2,1,0:T(8,128)S(1)} %copy-done), kind=kOutput, calls=%fused_computation.4 | convolution fusion | flops 1814298624 | bytes 12976128 | tf_op jit(solution)/shard_map/ldr,lfr->ldf/dot_general | solution.py:120
  (29 shorter events, 1.0 us)
Async XLA Ops:
  0.6 76.8 %copy-start = (f32[4,192,128]{2,1,0:T(8,128)S(1)}, f32[4,192,128]{2,1,0:T(8,128)}, u32[]{:S(2)}) copy-start(f32[4,192,128]{2,1,0:T(8,128)} %param.6) | copy-start | bytes 1179652
  2.5 7.6 %collective-permute-start.1 = (f32[2,192,1536]{2,1,0:T(8,128)S(1)}, f32[2,192,1536]{2,1,0:T(8,128)}, u32[]{:S(2)}, u32[]{:S(2)}) collective-permute-start(f32[2,192,1536]{2,1,0:T(8,128)S(1)} %dynamic-slice_bitcast_fusion), channel_id=1, source_target_pairs={{0,2},{2,0},{1,3},{3,1},{4,6},{6,4},{5,7},{7,5},{8,10},{10,8},{9,1... | collective-permute-start | bytes 7077896 | tf_op jit(solution)/shard_map/ppermute | solution.py:20
  14.1 14.9 %collective-permute-start.4 = (f32[384,384]{0,1:T(8,128)}, f32[384,384]{0,1:T(8,128)}, u32[]{:S(2)}, u32[]{:S(2)}) collective-permute-start(f32[384,384]{0,1:T(8,128)} %get-tuple-element.16), channel_id=1, source_target_pairs={{0,24},{8,0},{16,8},{24,16},{1,25},{9,1},{17,9},{25,17},{2,26},{10... | collective-permute-start | bytes 1769480 | tf_op jit(solution)/shard_map/ppermute | solution.py:15
  15.1 16.1 %collective-permute-start.3 = (f32[384,384]{0,1:T(8,128)}, f32[384,384]{0,1:T(8,128)}, u32[]{:S(2)}, u32[]{:S(2)}) collective-permute-start(f32[384,384]{0,1:T(8,128)} %get-tuple-element.17), channel_id=1, source_target_pairs={{0,16},{8,24},{16,0},{24,8},{1,17},{9,25},{17,1},{25,9},{2,18},{10... | collective-permute-start | bytes 1769480 | tf_op jit(solution)/shard_map/ppermute | solution.py:15
  15.4 29.0 %collective-permute-start.2 = (f32[384,384]{0,1:T(8,128)S(1)}, f32[384,384]{0,1:T(8,128)}, u32[]{:S(2)}, u32[]{:S(2)}) collective-permute-start(f32[384,384]{0,1:T(8,128)S(1)} %get-tuple-element.15), channel_id=1, source_target_pairs={{0,8},{8,16},{16,24},{24,0},{1,9},{9,17},{17,25},{25,1},{2,10},{10... | collective-permute-start | bytes 1769480 | tf_op jit(solution)/shard_map/ppermute | solution.py:15
  46.2 11.6 %collective-permute-start.5 = (f32[192,384]{0,1:T(8,128)S(1)}, f32[192,384]{0,1:T(8,128)S(1)}, u32[]{:S(2)}, u32[]{:S(2)}) collective-permute-start(f32[192,384]{0,1:T(8,128)S(1)} %constant_dynamic-slice_fusion), channel_id=1, source_target_pairs={{0,4},{4,0},{1,5},{5,1},{2,6},{6,2},{3,7},{7,3},{8,12},{12,8},{9,1... | collective-permute-start | bytes 884744 | tf_op jit(solution)/shard_map/ppermute | solution.py:15
  58.9 18.5 %all-to-all-start = ((f32[8,24,384]{2,1,0:T(8,128)}), f32[8,24,384]{2,1,0:T(8,128)S(1)}, u32[]{:S(2)}, u32[]{:S(2)}) async-start(f32[8,24,384]{2,1,0:T(8,128)} %bitcast.9), calls=%async_computation | async-start | bytes 589824 | tf_op jit(solution)/shard_map/all_to_all | solution.py:54
  67.1 2.7 %collective-permute-start = (f32[2,24,128]{2,1,0:T(8,128)S(1)}, f32[2,24,128]{2,1,0:T(8,128)S(1)}, u32[]{:S(2)}, u32[]{:S(2)}) collective-permute-start(f32[2,24,128]{2,1,0:T(8,128)S(1)} %pad_maximum_fusion.4), channel_id=1, source_target_pairs={{0,1},{1,0},{2,3},{3,2},{4,5},{5,4},{6,7},{7,6},{8,9},{9,8},{10,11... | collective-permute-start | bytes 73736 | tf_op jit(solution)/shard_map/ppermute | solution.py:20
  77.8 2.8 %collective-permute-start.6 = (f32[2,24,128]{2,1,0:T(8,128)S(1)}, f32[2,24,128]{2,1,0:T(8,128)S(1)}, u32[]{:S(2)}, u32[]{:S(2)}) collective-permute-start(f32[2,24,128]{2,1,0:T(8,128)S(1)} %fusion.5), channel_id=1, source_target_pairs={{0,1},{1,0},{2,3},{3,2},{4,5},{5,4},{6,7},{7,6},{8,9},{9,8},{10,11... | collective-permute-start | bytes 73736 | tf_op jit(solution)/shard_map/ppermute | solution.py:20
  99.6 7.1 %collective-permute-start.7 = (f32[192,384]{1,0:T(8,128)S(1)}, f32[192,384]{1,0:T(8,128)S(1)}, u32[]{:S(2)}, u32[]{:S(2)}) collective-permute-start(f32[192,384]{1,0:T(8,128)S(1)} %all_gather.6), channel_id=1, source_target_pairs={{0,4},{4,0},{1,5},{5,1},{2,6},{6,2},{3,7},{7,3},{8,12},{12,8},{9,1... | collective-permute-start | bytes 884744 | tf_op jit(solution)/shard_map/ppermute | solution.py:15
  110.2 17.0 %collective-permute-start.8 = (f32[384,384]{0,1:T(8,128)S(1)}, f32[384,384]{0,1:T(8,128)}, u32[]{:S(2)}, u32[]{:S(2)}) collective-permute-start(f32[384,384]{0,1:T(8,128)S(1)} %dynamic_update_slice.19), channel_id=1, source_target_pairs={{0,8},{8,16},{16,24},{24,0},{1,9},{9,17},{17,25},{25,1},{2,10},{10... | collective-permute-start | bytes 1769480 | tf_op jit(solution)/shard_map/ppermute | solution.py:15
  110.3 18.1 %collective-permute-start.9 = (f32[384,384]{0,1:T(8,128)S(1)}, f32[384,384]{0,1:T(8,128)}, u32[]{:S(2)}, u32[]{:S(2)}) collective-permute-start(f32[384,384]{0,1:T(8,128)S(1)} %dynamic_update_slice.19), channel_id=1, source_target_pairs={{0,16},{8,24},{16,0},{24,8},{1,17},{9,25},{17,1},{25,9},{2,18},{10... | collective-permute-start | bytes 1769480 | tf_op jit(solution)/shard_map/ppermute | solution.py:15
  111.6 17.9 %collective-permute-start.10 = (f32[384,384]{0,1:T(8,128)S(1)}, f32[384,384]{0,1:T(8,128)}, u32[]{:S(2)}, u32[]{:S(2)}) collective-permute-start(f32[384,384]{0,1:T(8,128)S(1)} %dynamic_update_slice.19), channel_id=1, source_target_pairs={{0,24},{8,0},{16,8},{24,16},{1,25},{9,1},{17,9},{25,17},{2,26},{10... | collective-permute-start | bytes 1769480 | tf_op jit(solution)/shard_map/ppermute | solution.py:15
  130.7 75.3 %collective-permute-start.11 = (f32[1536,384]{0,1:T(8,128)S(1)}, f32[1536,384]{0,1:T(8,128)}, u32[]{:S(2)}, u32[]{:S(2)}) collective-permute-start(f32[1536,384]{0,1:T(8,128)S(1)} %constant_dynamic-update-slice_fusion), channel_id=1, source_target_pairs={{0,2},{2,0},{1,3},{3,1},{4,6},{6,4},{5,7},{7,5},{8,10},{10,8},{9,1... | collective-permute-start | bytes 7077896 | tf_op jit(solution)/shard_map/ppermute | solution.py:20
  157.8 2.8 %collective-permute-start.12 = (f32[48,128]{1,0:T(8,128)S(1)}, f32[48,128]{1,0:T(8,128)S(1)}, u32[]{:S(2)}, u32[]{:S(2)}) collective-permute-start(f32[48,128]{1,0:T(8,128)S(1)} %reduce_sum.28), channel_id=1, source_target_pairs={{0,8},{8,0},{16,24},{24,16},{1,9},{9,1},{17,25},{25,17},{2,10},{10... | collective-permute-start | bytes 73736 | tf_op jit(solution)/shard_map/ppermute | solution.py:20
  160.6 4.2 %collective-permute-start.13 = (f32[48,128]{1,0:T(8,128)S(1)}, f32[48,128]{1,0:T(8,128)S(1)}, u32[]{:S(2)}, u32[]{:S(2)}) collective-permute-start(f32[48,128]{1,0:T(8,128)S(1)} %add.189), channel_id=1, source_target_pairs={{0,16},{8,24},{16,0},{24,8},{1,17},{9,25},{17,1},{25,9},{2,18},{10... | collective-permute-start | bytes 73736 | tf_op jit(solution)/shard_map/ppermute | solution.py:20
  164.7 4.2 %collective-permute-start.14 = (f32[48,128]{1,0:T(8,128)S(1)}, f32[48,128]{1,0:T(8,128)S(1)}, u32[]{:S(2)}, u32[]{:S(2)}) collective-permute-start(f32[48,128]{1,0:T(8,128)S(1)} %add.190), channel_id=1, source_target_pairs={{0,4},{4,0},{1,5},{5,1},{2,6},{6,2},{3,7},{7,3},{8,12},{12,8},{9,1... | collective-permute-start | bytes 73736 | tf_op jit(solution)/shard_map/ppermute | solution.py:20
  188.2 4.2 %collective-permute-start.15 = (f32[2,128,128]{2,1,0:T(8,128)S(1)}, f32[2,128,128]{2,1,0:T(8,128)S(1)}, u32[]{:S(2)}, u32[]{:S(2)}) collective-permute-start(f32[2,128,128]{2,1,0:T(8,128)S(1)} %fusion.27), channel_id=1, source_target_pairs={{0,1},{1,0},{2,3},{3,2},{4,5},{5,4},{6,7},{7,6},{8,9},{9,8},{10,11... | collective-permute-start | bytes 393224 | tf_op jit(solution)/shard_map/ppermute | solution.py:20
  193.0 12.2 %collective-permute-start.16 = (f32[2,192,128]{2,1,0:T(8,128)S(1)}, f32[2,192,128]{2,1,0:T(8,128)S(1)}, u32[]{:S(2)}, u32[]{:S(2)}) collective-permute-start(f32[2,192,128]{2,1,0:T(8,128)S(1)} %multiply_subtract_fusion), channel_id=1, source_target_pairs={{0,2},{2,0},{1,3},{3,1},{4,6},{6,4},{5,7},{7,5},{8,10},{10,8},{9,1... | collective-permute-start | bytes 589832 | tf_op jit(solution)/shard_map/ppermute | solution.py:20
  212.4 4.9 %copy-start.1 = (f32[2,3072,128]{2,1,0:T(8,128)S(1)}, f32[2,3072,128]{2,1,0:T(8,128)}, u32[]{:S(2)}) copy-start(f32[2,3072,128]{2,1,0:T(8,128)} %copy.25) | copy-start | bytes 9437188

commit v2 on v1

v2 whole, which is shorter than its diff:
```python
import functools

import jax
import jax.numpy as jnp
from jax import lax
from jax.experimental import pallas as pl
from jax.experimental.pallas import tpu as pltpu
from jax.sharding import Mesh, PartitionSpec as P

ADAM_STEP = 100
HIGH = lax.Precision.HIGHEST

SIZES = {"z": 8, "y": 4, "xh": 2, "core": 2, "xl": 2}
REP = ("z", "y", "xh", "core")
ORDERS = (("y", "xh"), ("xh", "y"), ("y", "xh"))
CHUNKS = len(ORDERS)


def shift(x, axis, k):
    n = SIZES[axis]
    return lax.ppermute(x, axis, [(i, (i + k) % n) for i in range(n)])


def flip(x, axis, bit=1):
    n = SIZES[axis]
    return lax.ppermute(x, axis, [(i, i ^ bit) for i in range(n)])


def rows(x, index, count):
    return lax.dynamic_slice_in_dim(x, index * count, count, 0)


def in_order(index, mine, other):
    first = index == 0
    return jnp.where(first, mine, other), jnp.where(first, other, mine)


def after(x, *others):
    return lax.optimization_barrier((x, *others))[0]


def blocks(x, axis):
    n, me = SIZES[axis], lax.axis_index(axis)
    return [rows(x, (me + k) % n, x.shape[0] // n) for k in range(n)]


def scatter(own, sent, axis):
    for k, block in enumerate(sent, 1):
        own = own + shift(block, axis, k)
    return own


def gather(x, axis):
    n, me = SIZES[axis], lax.axis_index(axis)
    if n == 2:
        return jnp.concatenate(in_order(me, x, flip(x, axis)), axis=0)
    count = x.shape[0]
    out = jnp.zeros((n * count,) + x.shape[1:], x.dtype)
    out = lax.dynamic_update_slice_in_dim(out, x, me * count, 0)
    for k in range(1, n):
        out = lax.dynamic_update_slice_in_dim(out, shift(x, axis, k), ((me - k) % n) * count, 0)
    return out


def exchange(parts, axis):
    return lax.all_to_all(parts, axis, split_axis=0, concat_axis=0)


def copies(x, axis):
    return jnp.broadcast_to(x, (SIZES[axis],) + x.shape)


def finish_kernel(core, dir_own, dir_other, proj_own, proj_other, basis, weights, first, second, *rest):
    out_weights, out_first, out_second = rest[-3:]
    layer = pl.program_id(0)
    here = core[0] == layer // 2
    direction = jnp.where(here, dir_own[...], dir_other[...])
    update = lax.dot_general(
        basis[0], direction, (((1,), (1,)), ((), ())), precision=HIGH, preferred_element_type=jnp.float32
    )
    out_weights[0] = weights[0] - 0.0125 * update
    proj = jnp.where(here, proj_own[...], proj_other[...]).T
    half = proj.shape[0] // 2
    proj = jnp.where(layer % 2 == 0, proj[:half], proj[half:])
    out_first[0] = 0.9 * first[0] + 0.1 * proj
    out_second[0] = 0.999 * second[0] + 0.001 * proj * proj


def finish(chunk, core, own, other, basis, weights, first, second, before):
    layers, depth, width = weights.shape
    rank, some = basis.shape[2], own.shape[0]
    own_dir = pl.BlockSpec((some, rank), lambda l, c: (0, l % 2))
    own_proj = pl.BlockSpec((some, rank), lambda l, c: (0, 2))
    whole = pl.BlockSpec((1, depth, rank), lambda l, c: (l, 0, 0))
    tall = pl.BlockSpec((1, depth, some), lambda l, c: (l, 0, chunk))
    low = pl.BlockSpec((1, first.shape[1], some), lambda l, c: (l, 0, chunk))
    kept = [] if before is None else list(before)
    return pl.pallas_call(
        finish_kernel,
        grid_spec=pltpu.PrefetchScalarGridSpec(
            num_scalar_prefetch=1,
            grid=(layers,),
            in_specs=[own_dir, own_dir, own_proj, own_proj, whole, tall, low, low]
            + [pl.BlockSpec(memory_space=pl.ANY)] * len(kept),
            out_specs=[tall, low, low],
        ),
        out_shape=[jax.ShapeDtypeStruct(a.shape, a.dtype) for a in (weights, first, second)],
        input_output_aliases={9 + i: i for i in range(len(kept))},
        name="finish",
    )(core.reshape(1), own, other, own, other, basis, weights, first, second, *kept)


def on_device(grads, basis, weights, first_moment, second_moment):
    layers, depth, width = grads.shape[1:]
    rank = basis.shape[2]
    half = layers // 2
    some = width // CHUNKS
    small = some // 64
    z, y, xh = lax.axis_index("z"), lax.axis_index("y"), lax.axis_index("xh")
    core, xl = lax.axis_index("core"), lax.axis_index("xl")
    grad = grads[0]

    given = []
    for chunk in range(CHUNKS):
        if given:
            grad = after(grad, given[-1])
        given.append(lax.dynamic_slice(grad, ((1 - core) * half, 0, chunk * some), (half, depth, some)))
    grad = after(grad, given[-1])
    given = [flip(g, "core") for g in given]
    first_sent = []
    for chunk, order in enumerate(ORDERS):
        held = lax.dynamic_slice(grad, (core * half, 0, chunk * some), (half, depth, some)) + given[chunk]
        own, *sent = blocks(held.reshape(half * depth, some).T, order[0])
        grad = after(grad, *sent)
        first_sent.append((own, sent))
    last = first_sent[-1][1]
    second_sent = []
    for (own, sent), order in zip(first_sent, ORDERS):
        own, *sent = blocks(scatter(after(own, *last), sent, order[0]), order[1])
        second_sent.append((own, sent))
        last = sent
    pieces, places = [], []
    for chunk, ((own, sent), order) in enumerate(zip(second_sent, ORDERS)):
        held = scatter(after(own, *last), sent, order[1])
        pieces.append(held.reshape(SIZES["z"], small, half * depth))
        index = {"y": y, "xh": xh}
        place = (index[order[0]] * SIZES[order[1]] + index[order[1]]) * SIZES["z"] + z
        places.append(chunk * some + place * small)
    total = jnp.sum(exchange(jnp.concatenate(pieces, axis=1), "z"), axis=0)
    total = total.reshape(CHUNKS * small, half, depth)

    basis_pair = rows(basis, core, half)
    cut = []
    for moment in (first_moment, second_moment):
        mine = [lax.dynamic_slice(moment, (core * half, 0, at), (half, rank // 2, small)) for at in places]
        cut.append(jnp.swapaxes(jnp.concatenate(mine, axis=2), 1, 2))
    cut = jnp.concatenate(cut, axis=2)
    low, high = in_order(xl, cut, flip(cut, "xl"))
    first = jnp.concatenate([low[:, :, : rank // 2], high[:, :, : rank // 2]], axis=2)
    second = jnp.concatenate([low[:, :, rank // 2 :], high[:, :, rank // 2 :]], axis=2)

    proj = jnp.einsum("fld,ldr->lfr", total, basis_pair, precision=HIGH)
    proj = proj + flip(proj, "xl")
    new_first = 0.9 * first + 0.1 * proj
    new_second = 0.999 * second + 0.001 * proj * proj
    direction = (
        new_first
        / (1.0 - 0.9**ADAM_STEP)
        / (jnp.sqrt(new_second / (1.0 - 0.999**ADAM_STEP)) + 1e-08)
    )
    mine = jnp.where(xl == 0, proj[:, :, : rank // 2], proj[:, :, rank // 2 :])
    packed = jnp.stack([direction[0], direction[1], jnp.concatenate([mine[0], mine[1]], axis=1)])
    packed = packed.reshape(3 * CHUNKS * small, rank)

    refresh = jnp.einsum("fld,lfr->ldr", total, proj, precision=HIGH)
    refresh = refresh.reshape(SIZES["z"], half * depth // SIZES["z"], rank)
    both = exchange(jnp.concatenate([copies(packed, "z"), refresh], axis=1), "z")
    packed = both[:, : packed.shape[0]].reshape(SIZES["z"], 3, CHUNKS, small, rank)
    part = jnp.sum(both[:, 3 * CHUNKS * small :], axis=0)

    held = [
        jnp.concatenate([packed[:, i, chunk].reshape(SIZES["z"] * small, rank) for i in range(3)], axis=1)
        for chunk in range(CHUNKS)
    ]
    part = after(part, *held)
    wide = [gather(h, order[1]) for h, order in zip(held, ORDERS)]
    part = part + flip(part, "y", 1)
    part = after(part, wide[0], wide[2])
    part = part + flip(part, "y", 2)
    part = after(part, *wide)
    part = part + flip(part, "xh")
    ready = []
    for w, order in zip(wide, ORDERS):
        w = gather(w, order[0])
        ready.append((w, flip(w, "core")))
    done = None
    for chunk, (own, other) in enumerate(ready):
        done = finish(chunk, core, own, other, basis, weights, first_moment, second_moment, done)
    new_weights, new_first, new_second = done

    refresh = exchange(copies(part, "z"), "z").reshape(half, depth, rank)
    gram = jnp.einsum("ldr,lds->lrs", refresh, refresh, precision=HIGH)
    gram = gram + flip(gram, "xl")
    sumsq = jnp.einsum("lrr->l", gram)
    factor = jnp.sqrt(jnp.float32(rank)) / (2.0 * jnp.sqrt(sumsq + 1e-06))
    scaled = refresh * factor[:, None, None]
    gram_scaled = gram * (factor * factor)[:, None, None]
    basis_new = 1.5 * scaled - 0.5 * jnp.einsum("ldr,lrs->lds", scaled, gram_scaled, precision=HIGH)
    new_basis = jnp.concatenate(in_order(core, basis_new, flip(basis_new, "core")), axis=0)
    return (new_weights, new_first, new_second, new_basis)


def solution(mesh):
    fine = Mesh(mesh.devices.reshape(8, 4, 2, 2, 2), ("z", "y", "xh", "core", "xl"))
    split = P(None, "xl", None)
    return jax.shard_map(
        on_device,
        mesh=fine,
        in_specs=(P(REP, None, "xl", None), split, split, split, split),
        out_specs=(split, split, split, split),
        check_vma=False,
    )
```

time: 225 us -> 157 us (0.70)
  blocking collectives: 51 us -> 0 us
  waiting for transfers between devices: 76.2 us -> 41.1 us
  starting transfers between devices: 53.7 us -> 75.1 us
  Pallas kernels: 0 us -> 16.7 us
  local copies, waits for them, and re-layouts: 18.9 us -> 10.3 us
  matrix products: 9.18 us -> 1.84 us
  other arithmetic: 14.8 us -> 9.89 us
    ppermute x8 -> x21, waiting for transfers between devices: 49.8 us -> 9.73 us  [shift(): return lax.ppermute(x, axis, [(i, (i + k) % n) for i in range(n)])]
    all_gather x2 -> x0, blocking collectives: 37.4 us -> none  [the longest x1 18.8 us: on_device(): packed = lax.all_gather(packed, 'z', axis=0, tiled=True)]
    ppermute x8 -> x21, starting transfers between devices: 11 us -> 29.2 us  [shift(): return lax.ppermute(x, axis, [(i, (i + k) % n) for i in range(n)])]
    pallas_call x0 -> x3, Pallas kernels: none -> 16.7 us  [finish(): pl.pallas_call(finish_kernel, grid_spec=pltpu.PrefetchScalarGridSpec(num_...]
    all_to_all x1 -> x0, blocking collectives: 13.6 us -> none  [scatter_exchange(): lax.all_to_all(parts, axis, split_axis=0, concat_axis=0)]
    all_to_all x1 -> x3, waiting for transfers between devices: 7.36 us -> 18.4 us  [exchange(): return lax.all_to_all(parts, axis, split_axis=0, concat_axis=0)]
    dynamic_update_slice x6 -> x9, local copies, waits for them, and re-layouts: 10.4 us -> 0.16 us  [gather(): lax.dynamic_update_slice_in_dim(out, shift(x, axis, k), (me - k) % n * co...]
    dot_general x1 -> x0, matrix products: 7.35 us -> none  [on_device(): update = jnp.einsum('ldr,lfr->ldf', basis, dirs, precision=HIGH)]
  transfers between devices with their start and end apart: 18 -> 40, of which waited for: 15 -> 12; matrix products, arithmetic and copies ran while one was open for 5% -> 10% of each run, Pallas kernels for 0% -> 7%
where the time goes in v2:
time: 157 us; the launch traced here: 156 us
  starting transfers between devices  75.1 us (48%)
  waiting for transfers between devices  41.1 us (26%)
  Pallas kernels  16.7 us (11%)
  local copies, waits for them, and re-layouts  10.3 us (7%)
  other arithmetic  9.89 us (6%)
  matrix products  1.84 us (1%)
    ppermute x16, starting transfers between devices, flip(): return lax.ppermute(x, axis, [(i, i ^ bit) for i in range(n)])  32.4 us
    ppermute x21, starting transfers between devices, shift(): return lax.ppermute(x, axis, [(i, (i + k) % n) for i in range(n)])  29.2 us
    all_to_all x3, waiting for transfers between devices, exchange(): return lax.all_to_all(parts, axis, split_axis=0, concat_axis=0)  18.4 us
    pallas_call x3, Pallas kernels, finish(): pl.pallas_call(finish_kernel, grid_spec=pltpu.PrefetchScalarGridSpec(num_...  16.7 us
    all_to_all x3, starting transfers between devices, exchange(): return lax.all_to_all(parts, axis, split_axis=0, concat_axis=0)  13.4 us
    ppermute x16, waiting for transfers between devices, flip(): return lax.ppermute(x, axis, [(i, i ^ bit) for i in range(n)])  13 us
    ppermute x21, waiting for transfers between devices, shift(): return lax.ppermute(x, axis, [(i, (i + k) % n) for i in range(n)])  9.73 us
    dynamic_slice x3, local copies, waits for them, and re-layouts, on_device(): lax.dynamic_slice(grad, ((1 - core) * half, 0, chunk * some), (half, dept...  5.31 us
  transfers between devices with their start and end apart: 40, of which 12 were waited for; matrix products, arithmetic and copies ran while one was open for 10% of the time, Pallas kernels for 7%

profile of v2, /device:TPU:1, one launch (start us, length us, event | category | flops | bytes accessed | tf_op | source)
XLA Modules:
  0.0 156.4 jit_solution(5487121862634653062)
XLA Ops:
  0.6 2.1 %dynamic-slice_bitcast_fusion = f32[2,192,512]{2,1,0:T(8,128)} fusion(f32[1,4,192,1536]{3,2,1,0:T(8,128)} %param.5, s32[]{:T(128)S(6)} %select_n.249), kind=kLoop, calls=%fused_computation.6 | loop fusion | bytes 1572868 | tf_op jit(solution)/shard_map/dynamic_slice | solution.py:127
  2.7 3.2 %collective-permute-start.1 = (f32[2,192,512]{2,1,0:T(8,128)}, f32[2,192,512]{2,1,0:T(8,128)S(1)}, u32[]{:S(2)}, u32[]{:S(2)}) collective-permute-start(f32[2,192,512]{2,1,0:T(8,128)} %dynamic-slice_bitcast_fusion), channel_id=1, source_target_pairs={{0,2},{2,0},{1,3},{3,1},{4,6},{6,4},{5,7},{7,5},{8,10},{10,8},{9,1... | collective-permute-start | bytes 2359304 | tf_op jit(solution)/shard_map/ppermute | solution.py:26
  5.9 2.1 %constant_dynamic-slice_fusion.9 = f32[2,192,512]{2,1,0:T(8,128)} fusion(f32[4,192,1536]{2,1,0:T(8,128)} %bitcast.65, s32[]{:T(128)S(6)} %select_n.249), kind=kLoop, calls=%fused_computation.99 | loop fusion | bytes 1572868 | tf_op jit(solution)/shard_map/dynamic_slice | solution.py:127
  8.0 1.2 constant_dynamic-slice_fusion.8
  9.2 0.6 collective-permute-start.3
  9.8 1.2 constant_dynamic-slice_fusion.12
  11.4 1.3 dynamic-slice_add_fusion.2
  12.9 2.2 %collective-permute-start.5 = (f32[128,384]{0,1:T(8,128)S(1)}, f32[128,384]{0,1:T(8,128)S(1)}, u32[]{:S(2)}, u32[]{:S(2)}) collective-permute-start(f32[128,384]{0,1:T(8,128)S(1)} %get-tuple-element.70), channel_id=1, source_target_pairs={{0,16},{8,24},{16,0},{24,8},{1,17},{9,25},{17,1},{25,9},{2,18},{10... | collective-permute-start | bytes 589832 | tf_op jit(solution)/shard_map/ppermute | solution.py:21
  15.1 1.1 collective-permute-start.6
  16.2 1.3 dynamic-slice_add_fusion.1
  17.5 2.8 %collective-permute-start.7 = (f32[256,384]{0,1:T(8,128)S(1)}, f32[256,384]{0,1:T(8,128)S(1)}, u32[]{:S(2)}, u32[]{:S(2)}) collective-permute-start(f32[256,384]{0,1:T(8,128)S(1)} %get-tuple-element.73), channel_id=1, source_target_pairs={{0,4},{4,0},{1,5},{5,1},{2,6},{6,2},{3,7},{7,3},{8,12},{12,8},{9,1... | collective-permute-start | bytes 1179656 | tf_op jit(solution)/shard_map/ppermute | solution.py:21
  20.4 1.3 dynamic-slice_add_fusion
  21.9 1.4 collective-permute-start.8
  23.3 0.9 collective-permute-done.5
  24.3 1.0 collective-permute-start.9
  25.5 2.2 %collective-permute-start.11 = (f32[64,384]{0,1:T(8,128)S(1)}, f32[64,384]{0,1:T(8,128)S(1)}, u32[]{:S(2)}, u32[]{:S(2)}) collective-permute-start(f32[64,384]{0,1:T(8,128)S(1)} %get-tuple-element.98), channel_id=1, source_target_pairs={{0,4},{4,0},{1,5},{5,1},{2,6},{6,2},{3,7},{7,3},{8,12},{12,8},{9,1... | collective-permute-start | bytes 294920 | tf_op jit(solution)/shard_map/ppermute | solution.py:21
  27.7 1.1 collective-permute-done.7
  29.1 0.5 collective-permute-start.12
  29.6 1.6 %collective-permute-start.13 = (f32[64,384]{0,1:T(8,128)S(1)}, f32[64,384]{0,1:T(8,128)}, u32[]{:S(2)}, u32[]{:S(2)}) collective-permute-start(f32[64,384]{0,1:T(8,128)S(1)} %get-tuple-element.78), channel_id=1, source_target_pairs={{0,16},{8,24},{16,0},{24,8},{1,17},{9,25},{17,1},{25,9},{2,18},{10... | collective-permute-start | bytes 294920 | tf_op jit(solution)/shard_map/ppermute | solution.py:21
  31.2 2.0 %collective-permute-start.14 = (f32[64,384]{0,1:T(8,128)S(1)}, f32[64,384]{0,1:T(8,128)}, u32[]{:S(2)}, u32[]{:S(2)}) collective-permute-start(f32[64,384]{0,1:T(8,128)S(1)} %get-tuple-element.77), channel_id=1, source_target_pairs={{0,24},{8,0},{16,8},{24,16},{1,25},{9,1},{17,9},{25,17},{2,26},{10... | collective-permute-start | bytes 294920 | tf_op jit(solution)/shard_map/ppermute | solution.py:21
  33.4 1.7 %collective-permute-start.15 = (f32[64,384]{0,1:T(8,128)S(1)}, f32[64,384]{0,1:T(8,128)S(1)}, u32[]{:S(2)}, u32[]{:S(2)}) collective-permute-start(f32[64,384]{0,1:T(8,128)S(1)} %get-tuple-element.99), channel_id=1, source_target_pairs={{0,4},{4,0},{1,5},{5,1},{2,6},{6,2},{3,7},{7,3},{8,12},{12,8},{9,1... | collective-permute-start | bytes 294920 | tf_op jit(solution)/shard_map/ppermute | solution.py:21
  35.3 7.7 %collective-permute-done.12 = f32[64,384]{0,1:T(8,128)S(1)} collective-permute-done((f32[64,384]{0,1:T(8,128)S(1)}, f32[64,384]{0,1:T(8,128)S(1)}, u32[]{:S(2)}, u32[]{:S(2)}) %collective-permute-start.12) | collective-permute-done | bytes 98336 | tf_op jit(solution)/shard_map/ppermute | solution.py:21
  42.9 1.1 add_add_fusion
  44.2 0.7 pad_maximum_fusion.3
  45.0 6.4 %all-to-all-start = ((f32[8,24,384]{2,1,0:T(8,128)}), f32[8,24,384]{2,1,0:T(8,128)S(1)}, u32[]{:S(2)}, u32[]{:S(2)}) async-start(f32[8,24,384]{2,1,0:T(8,128)} %pad_maximum_fusion.3), calls=%async_computation | async-start | bytes 589824 | tf_op jit(solution)/shard_map/all_to_all | solution.py:66
  51.5 1.2 collective-permute-start
  52.7 1.7 %collective-permute-done = f32[2,24,128]{2,1,0:T(8,128)S(1)} collective-permute-done((f32[2,24,128]{2,1,0:T(8,128)S(1)}, f32[2,24,128]{2,1,0:T(8,128)S(1)}, u32[]{:S(2)}, u32[]{:S(2)}) %collective-permute-start) | collective-permute-done | bytes 24608 | tf_op jit(solution)/shard_map/ppermute | solution.py:26
  54.5 6.8 %all-to-all-done = f32[8,24,384]{2,1,0:T(8,128)S(1)} async-done(((f32[8,24,384]{2,1,0:T(8,128)}), f32[8,24,384]{2,1,0:T(8,128)S(1)}, u32[]{:S(2)}, u32[]{:S(2)}) %all-to-all-start) | async-done | bytes 294944 | tf_op jit(solution)/shard_map/all_to_all | solution.py:66
  61.8 0.9 collective-permute-start.16
  62.8 1.8 %collective-permute-done.16 = f32[2,24,128]{2,1,0:T(8,128)S(1)} collective-permute-done((f32[2,24,128]{2,1,0:T(8,128)S(1)}, f32[2,24,128]{2,1,0:T(8,128)S(1)}, u32[]{:S(2)}, u32[]{:S(2)}) %collective-permute-start.16) | collective-permute-done | bytes 24608 | tf_op jit(solution)/shard_map/ppermute | solution.py:26
  64.7 0.5 fusion.7
  65.4 0.8 pad_maximum_fusion.1
  66.2 3.5 %all-to-all-start.1 = ((f32[8,120,128]{2,1,0:T(8,128)}), f32[8,120,128]{2,1,0:T(8,128)S(1)}, u32[]{:S(2)}, u32[]{:S(2)}) async-start(f32[8,120,128]{2,1,0:T(8,128)} %pad_maximum_fusion.1), calls=%async_computation.1 | async-start | bytes 983040 | tf_op jit(solution)/shard_map/all_to_all | solution.py:66
  69.7 11.6 %all-to-all-done.1 = f32[8,120,128]{2,1,0:T(8,128)S(1)} async-done(((f32[8,120,128]{2,1,0:T(8,128)}), f32[8,120,128]{2,1,0:T(8,128)S(1)}, u32[]{:S(2)}, u32[]{:S(2)}) %all-to-all-start.1) | async-done | bytes 491552 | tf_op jit(solution)/shard_map/all_to_all | solution.py:66
  81.3 2.3 %collective-permute-start.27 = (f32[64,384]{1,0:T(8,128)S(1)}, f32[64,384]{1,0:T(8,128)S(1)}, u32[]{:S(2)}, u32[]{:S(2)}) collective-permute-start(f32[64,384]{1,0:T(8,128)S(1)} %pad_maximum_fusion.8), channel_id=1, source_target_pairs={{0,4},{4,0},{1,5},{5,1},{2,6},{6,2},{3,7},{7,3},{8,12},{12,8},{9,1... | collective-permute-start | bytes 294920 | tf_op jit(solution)/shard_map/ppermute | solution.py:26
  83.7 1.1 collective-permute-start.32
  84.9 0.6 collective-permute-start.17
  85.5 0.6 collective-permute-start.22
  86.0 1.7 %collective-permute-start.23 = (f32[64,384]{1,0:T(8,128)S(1)}, f32[64,384]{1,0:T(8,128)S(1)}, u32[]{:S(2)}, u32[]{:S(2)}) collective-permute-start(f32[64,384]{1,0:T(8,128)S(1)} %get-tuple-element.101), channel_id=1, source_target_pairs={{0,16},{8,24},{16,0},{24,8},{1,17},{9,25},{17,1},{25,9},{2,18},{10... | collective-permute-start | bytes 294920 | tf_op jit(solution)/shard_map/ppermute | solution.py:21
  87.7 1.8 %collective-permute-start.24 = (f32[64,384]{1,0:T(8,128)S(1)}, f32[64,384]{1,0:T(8,128)S(1)}, u32[]{:S(2)}, u32[]{:S(2)}) collective-permute-start(f32[64,384]{1,0:T(8,128)S(1)} %get-tuple-element.101), channel_id=1, source_target_pairs={{0,24},{8,0},{16,8},{24,16},{1,25},{9,1},{17,9},{25,17},{2,26},{10... | collective-permute-start | bytes 294920 | tf_op jit(solution)/shard_map/ppermute | solution.py:21
  89.9 2.6 %collective-permute-start.29 = (f32[128,384]{1,0:T(8,128)S(1)}, f32[128,384]{1,0:T(8,128)S(1)}, u32[]{:S(2)}, u32[]{:S(2)}) collective-permute-start(f32[128,384]{1,0:T(8,128)S(1)} %get-tuple-element.89), channel_id=1, source_target_pairs={{0,16},{8,24},{16,0},{24,8},{1,17},{9,25},{17,1},{25,9},{2,18},{10... | collective-permute-start | bytes 589832 | tf_op jit(solution)/shard_map/ppermute | solution.py:21
  92.5 0.7 pad_maximum_fusion.4
  93.2 0.4 collective-permute-start.33
  93.7 4.0 %collective-permute-done.33 = f32[48,128]{1,0:T(8,128)S(1)} collective-permute-done((f32[48,128]{1,0:T(8,128)S(1)}, f32[48,128]{1,0:T(8,128)S(1)}, u32[]{:S(2)}, u32[]{:S(2)}) %collective-permute-start.33) | collective-permute-done | bytes 24608 | tf_op jit(solution)/shard_map/ppermute | solution.py:26
  97.7 2.9 %collective-permute-start.34 = (f32[48,128]{1,0:T(8,128)S(1)}, f32[48,128]{1,0:T(8,128)S(1)}, u32[]{:S(2)}, u32[]{:S(2)}) collective-permute-start(f32[48,128]{1,0:T(8,128)S(1)} %add.339), channel_id=1, source_target_pairs={{0,4},{4,0},{1,5},{5,1},{2,6},{6,2},{3,7},{7,3},{8,12},{12,8},{9,1... | collective-permute-start | bytes 73736 | tf_op jit(solution)/shard_map/ppermute | solution.py:26
  100.6 1.1 collective-permute-start.30
  102.3 0.7 broadcast_in_dim.19
  103.0 3.5 %all-to-all-start.2 = ((f32[8,48,128]{2,1,0:T(8,128)}), f32[8,48,128]{2,1,0:T(8,128)S(1)}, u32[]{:S(2)}, u32[]{:S(2)}) async-start(f32[8,48,128]{2,1,0:T(8,128)} %broadcast_in_dim.19), calls=%async_computation.2 | async-start | bytes 393216 | tf_op jit(solution)/shard_map/all_to_all | solution.py:66
  106.5 2.6 %collective-permute-start.19 = (f32[128,384]{1,0:T(8,128)}, f32[128,384]{1,0:T(8,128)S(1)}, u32[]{:S(2)}, u32[]{:S(2)}) collective-permute-start(f32[128,384]{1,0:T(8,128)} %get-tuple-element.93), channel_id=1, source_target_pairs={{0,16},{8,24},{16,0},{24,8},{1,17},{9,25},{17,1},{25,9},{2,18},{10... | collective-permute-start | bytes 589832 | tf_op jit(solution)/shard_map/ppermute | solution.py:21
  109.1 1.8 %collective-permute-start.20 = (f32[128,384]{1,0:T(8,128)}, f32[128,384]{1,0:T(8,128)S(1)}, u32[]{:S(2)}, u32[]{:S(2)}) collective-permute-start(f32[128,384]{1,0:T(8,128)} %get-tuple-element.93), channel_id=1, source_target_pairs={{0,24},{8,0},{16,8},{24,16},{1,25},{9,1},{17,9},{25,17},{2,26},{10... | collective-permute-start | bytes 589832 | tf_op jit(solution)/shard_map/ppermute | solution.py:21
  110.9 10.8 %collective-permute-start.31 = (f32[512,384]{1,0:T(8,128)S(1)}, f32[512,384]{1,0:T(8,128)}, u32[]{:S(2)}, u32[]{:S(2)}) collective-permute-start(f32[512,384]{1,0:T(8,128)S(1)} %constant_dynamic-update-slice_fusion.dir_own.proj_own), channel_id=1, source_target_pairs={{0,2},{2,0},{1,3},{3,1},{4,6},{6,4},{5,7},{7,5},{8,10},{10,8},{9,1... | collective-permute-start | bytes 2359304 | tf_op jit(solution)/shard_map/ppermute | solution.py:26
  121.9 6.4 %collective-permute-start.21 = (f32[512,384]{1,0:T(8,128)S(1)}, f32[512,384]{1,0:T(8,128)S(1)}, u32[]{:S(2)}, u32[]{:S(2)}) collective-permute-start(f32[512,384]{1,0:T(8,128)S(1)} %constant_dynamic-update-slice_fusion.8.dir_own.proj_own), channel_id=1, source_target_pairs={{0,2},{2,0},{1,3},{3,1},{4,6},{6,4},{5,7},{7,5},{8,10},{10,8},{9,1... | collective-permute-start | bytes 2359304 | tf_op jit(solution)/shard_map/ppermute | solution.py:26
  128.3 0.7 fusion.21
  128.9 0.6 collective-permute-start.35
  130.0 4.1 %collective-permute-done.35 = f32[2,128,128]{2,1,0:T(8,128)S(1)} collective-permute-done((f32[2,128,128]{2,1,0:T(8,128)S(1)}, f32[2,128,128]{2,1,0:T(8,128)S(1)}, u32[]{:S(2)}, u32[]{:S(2)}) %collective-permute-start.35) | collective-permute-done | bytes 131104 | tf_op jit(solution)/shard_map/ppermute | solution.py:26
  134.3 0.4 fusion
  134.7 0.9 collective-permute-start.36
  135.6 1.2 collective-permute-done.36
  136.8 1.0 broadcast_select_fusion.3
  137.7 0.8 pad_maximum_fusion.2
  138.5 5.6 %finish.3 = (f32[4,192,1536]{2,1,0:T(8,128)}, f32[4,64,1536]{2,1,0:T(8,128)}, f32[4,64,1536]{2,1,0:T(8,128)}) custom-call(s32[1]{0:T(128)} %bitcast.core, f32[512,384]{1,0:T(8,128)} %copy-done.2, f32[512,384]{1,0:T(8,128)} %collective-permute-done.31.dir_other.proj_other, f32[512,384]{1,0:T(8,128)} %copy-done.2, ...), custom_call_target="tpu_custom_call" | custom-call | tf_op jit(solution)/shard_map/finish/pallas_call | solution.py:98
  144.1 5.6 %finish.4 = (f32[4,192,1536]{2,1,0:T(8,128)}, f32[4,64,1536]{2,1,0:T(8,128)}, f32[4,64,1536]{2,1,0:T(8,128)}) custom-call(s32[1]{0:T(128)} %bitcast.core, f32[512,384]{1,0:T(8,128)} %copy-done, f32[512,384]{1,0:T(8,128)} %collective-permute-done.26.dir_other.proj_other, ...), custom_call_target="tpu_custom_call", output_to_operand_aliasing={{0}: (9, {}), {1}: (10, {}), {2}: (11, {})} | custom-call | tf_op jit(solution)/shard_map/finish/pallas_call | solution.py:98
  149.7 0.9 copy-done.4
  150.6 5.6 %finish.5 = (f32[4,192,1536]{2,1,0:T(8,128)}, f32[4,64,1536]{2,1,0:T(8,128)}, f32[4,64,1536]{2,1,0:T(8,128)}) custom-call(s32[1]{0:T(128)} %bitcast.core, f32[512,384]{1,0:T(8,128)} %copy-done.1, f32[512,384]{1,0:T(8,128)} %copy-done.4, f32[512,384]{1,0:T(8,128)} %copy-done.1, ...), custom_call_target="tpu_custom_call", output_to_operand_aliasing={{0}: (9, {}), {1}: (10, {}), {2}: (11, {})} | custom-call | tf_op jit(solution)/shard_map/finish/pallas_call | solution.py:98
  (110 shorter events, 4.8 us)
Async XLA Ops:
  2.7 8.7 %collective-permute-start.1 = (f32[2,192,512]{2,1,0:T(8,128)}, f32[2,192,512]{2,1,0:T(8,128)S(1)}, u32[]{:S(2)}, u32[]{:S(2)}) collective-permute-start(f32[2,192,512]{2,1,0:T(8,128)} %dynamic-slice_bitcast_fusion), channel_id=1, source_target_pairs={{0,2},{2,0},{1,3},{3,1},{4,6},{6,4},{5,7},{7,5},{8,10},{10,8},{9,1... | collective-permute-start | bytes 2359304 | tf_op jit(solution)/shard_map/ppermute | solution.py:26
  8.0 8.2 %collective-permute-start.2 = (f32[2,192,512]{2,1,0:T(8,128)}, f32[2,192,512]{2,1,0:T(8,128)S(1)}, u32[]{:S(2)}, u32[]{:S(2)}) collective-permute-start(f32[2,192,512]{2,1,0:T(8,128)} %constant_dynamic-slice_fusion.9), channel_id=1, source_target_pairs={{0,2},{2,0},{1,3},{3,1},{4,6},{6,4},{5,7},{7,5},{8,10},{10,8},{9,1... | collective-permute-start | bytes 2359304 | tf_op jit(solution)/shard_map/ppermute | solution.py:26
  9.2 11.2 %collective-permute-start.3 = (f32[2,192,512]{2,1,0:T(8,128)S(1)}, f32[2,192,512]{2,1,0:T(8,128)S(1)}, u32[]{:S(2)}, u32[]{:S(2)}) collective-permute-start(f32[2,192,512]{2,1,0:T(8,128)S(1)} %constant_dynamic-slice_fusion.8), channel_id=1, source_target_pairs={{0,2},{2,0},{1,3},{3,1},{4,6},{6,4},{5,7},{7,5},{8,10},{10,8},{9,1... | collective-permute-start | bytes 2359304 | tf_op jit(solution)/shard_map/ppermute | solution.py:26
  12.8 9.0 %collective-permute-start.4 = (f32[128,384]{0,1:T(8,128)S(1)}, f32[128,384]{0,1:T(8,128)S(1)}, u32[]{:S(2)}, u32[]{:S(2)}) collective-permute-start(f32[128,384]{0,1:T(8,128)S(1)} %get-tuple-element.71), channel_id=1, source_target_pairs={{0,8},{8,16},{16,24},{24,0},{1,9},{9,17},{17,25},{25,1},{2,10},{10... | collective-permute-start | bytes 589832 | tf_op jit(solution)/shard_map/ppermute | solution.py:21
  12.9 11.3 %collective-permute-start.5 = (f32[128,384]{0,1:T(8,128)S(1)}, f32[128,384]{0,1:T(8,128)S(1)}, u32[]{:S(2)}, u32[]{:S(2)}) collective-permute-start(f32[128,384]{0,1:T(8,128)S(1)} %get-tuple-element.70), channel_id=1, source_target_pairs={{0,16},{8,24},{16,0},{24,8},{1,17},{9,25},{17,1},{25,9},{2,18},{10... | collective-permute-start | bytes 589832 | tf_op jit(solution)/shard_map/ppermute | solution.py:21
  15.1 10.1 %collective-permute-start.6 = (f32[128,384]{0,1:T(8,128)S(1)}, f32[128,384]{0,1:T(8,128)S(1)}, u32[]{:S(2)}, u32[]{:S(2)}) collective-permute-start(f32[128,384]{0,1:T(8,128)S(1)} %get-tuple-element.69), channel_id=1, source_target_pairs={{0,24},{8,0},{16,8},{24,16},{1,25},{9,1},{17,9},{25,17},{2,26},{10... | collective-permute-start | bytes 589832 | tf_op jit(solution)/shard_map/ppermute | solution.py:21
  17.5 11.2 %collective-permute-start.7 = (f32[256,384]{0,1:T(8,128)S(1)}, f32[256,384]{0,1:T(8,128)S(1)}, u32[]{:S(2)}, u32[]{:S(2)}) collective-permute-start(f32[256,384]{0,1:T(8,128)S(1)} %get-tuple-element.73), channel_id=1, source_target_pairs={{0,4},{4,0},{1,5},{5,1},{2,6},{6,2},{3,7},{7,3},{8,12},{12,8},{9,1... | collective-permute-start | bytes 1179656 | tf_op jit(solution)/shard_map/ppermute | solution.py:21
  21.8 7.8 %collective-permute-start.10 = (f32[128,384]{0,1:T(8,128)S(1)}, f32[128,384]{0,1:T(8,128)S(1)}, u32[]{:S(2)}, u32[]{:S(2)}) collective-permute-start(f32[128,384]{0,1:T(8,128)S(1)} %get-tuple-element.66), channel_id=1, source_target_pairs={{0,24},{8,0},{16,8},{24,16},{1,25},{9,1},{17,9},{25,17},{2,26},{10... | collective-permute-start | bytes 589832 | tf_op jit(solution)/shard_map/ppermute | solution.py:21
  21.9 9.3 %collective-permute-start.8 = (f32[128,384]{0,1:T(8,128)S(1)}, f32[128,384]{0,1:T(8,128)S(1)}, u32[]{:S(2)}, u32[]{:S(2)}) collective-permute-start(f32[128,384]{0,1:T(8,128)S(1)} %get-tuple-element.64), channel_id=1, source_target_pairs={{0,8},{8,16},{16,24},{24,0},{1,9},{9,17},{17,25},{25,1},{2,10},{10... | collective-permute-start | bytes 589832 | tf_op jit(solution)/shard_map/ppermute | solution.py:21
  24.3 8.9 %collective-permute-start.9 = (f32[128,384]{0,1:T(8,128)S(1)}, f32[128,384]{0,1:T(8,128)S(1)}, u32[]{:S(2)}, u32[]{:S(2)}) collective-permute-start(f32[128,384]{0,1:T(8,128)S(1)} %get-tuple-element.67), channel_id=1, source_target_pairs={{0,16},{8,24},{16,0},{24,8},{1,17},{9,25},{17,1},{25,9},{2,18},{10... | collective-permute-start | bytes 589832 | tf_op jit(solution)/shard_map/ppermute | solution.py:21
  25.5 9.7 %collective-permute-start.11 = (f32[64,384]{0,1:T(8,128)S(1)}, f32[64,384]{0,1:T(8,128)S(1)}, u32[]{:S(2)}, u32[]{:S(2)}) collective-permute-start(f32[64,384]{0,1:T(8,128)S(1)} %get-tuple-element.98), channel_id=1, source_target_pairs={{0,4},{4,0},{1,5},{5,1},{2,6},{6,2},{3,7},{7,3},{8,12},{12,8},{9,1... | collective-permute-start | bytes 294920 | tf_op jit(solution)/shard_map/ppermute | solution.py:21
  27.7 33.8 %copy-start.3 = (f32[4,192,128]{2,1,0:T(8,128)S(1)}, f32[4,192,128]{2,1,0:T(8,128)}, u32[]{:S(2)}) copy-start(f32[4,192,128]{2,1,0:T(8,128)} %basis.5) | copy-start | bytes 1179652
  29.1 13.8 %collective-permute-start.12 = (f32[64,384]{0,1:T(8,128)S(1)}, f32[64,384]{0,1:T(8,128)S(1)}, u32[]{:S(2)}, u32[]{:S(2)}) collective-permute-start(f32[64,384]{0,1:T(8,128)S(1)} %get-tuple-element.79), channel_id=1, source_target_pairs={{0,8},{8,16},{16,24},{24,0},{1,9},{9,17},{17,25},{25,1},{2,10},{10... | collective-permute-start | bytes 294920 | tf_op jit(solution)/shard_map/ppermute | solution.py:21
  29.6 13.3 %collective-permute-start.13 = (f32[64,384]{0,1:T(8,128)S(1)}, f32[64,384]{0,1:T(8,128)}, u32[]{:S(2)}, u32[]{:S(2)}) collective-permute-start(f32[64,384]{0,1:T(8,128)S(1)} %get-tuple-element.78), channel_id=1, source_target_pairs={{0,16},{8,24},{16,0},{24,8},{1,17},{9,25},{17,1},{25,9},{2,18},{10... | collective-permute-start | bytes 294920 | tf_op jit(solution)/shard_map/ppermute | solution.py:21
  31.2 11.7 %collective-permute-start.14 = (f32[64,384]{0,1:T(8,128)S(1)}, f32[64,384]{0,1:T(8,128)}, u32[]{:S(2)}, u32[]{:S(2)}) collective-permute-start(f32[64,384]{0,1:T(8,128)S(1)} %get-tuple-element.77), channel_id=1, source_target_pairs={{0,24},{8,0},{16,8},{24,16},{1,25},{9,1},{17,9},{25,17},{2,26},{10... | collective-permute-start | bytes 294920 | tf_op jit(solution)/shard_map/ppermute | solution.py:21
  33.4 10.7 %collective-permute-start.15 = (f32[64,384]{0,1:T(8,128)S(1)}, f32[64,384]{0,1:T(8,128)S(1)}, u32[]{:S(2)}, u32[]{:S(2)}) collective-permute-start(f32[64,384]{0,1:T(8,128)S(1)} %get-tuple-element.99), channel_id=1, source_target_pairs={{0,4},{4,0},{1,5},{5,1},{2,6},{6,2},{3,7},{7,3},{8,12},{12,8},{9,1... | collective-permute-start | bytes 294920 | tf_op jit(solution)/shard_map/ppermute | solution.py:21
  45.0 16.4 %all-to-all-start = ((f32[8,24,384]{2,1,0:T(8,128)}), f32[8,24,384]{2,1,0:T(8,128)S(1)}, u32[]{:S(2)}, u32[]{:S(2)}) async-start(f32[8,24,384]{2,1,0:T(8,128)} %pad_maximum_fusion.3), calls=%async_computation | async-start | bytes 589824 | tf_op jit(solution)/shard_map/all_to_all | solution.py:66
  51.5 2.9 %collective-permute-start = (f32[2,24,128]{2,1,0:T(8,128)S(1)}, f32[2,24,128]{2,1,0:T(8,128)S(1)}, u32[]{:S(2)}, u32[]{:S(2)}) collective-permute-start(f32[2,24,128]{2,1,0:T(8,128)S(1)} %pad_maximum_fusion.10), channel_id=1, source_target_pairs={{0,1},{1,0},{2,3},{3,2},{4,5},{5,4},{6,7},{7,6},{8,9},{9,8},{10,11... | collective-permute-start | bytes 73736 | tf_op jit(solution)/shard_map/ppermute | solution.py:26
  61.8 2.8 %collective-permute-start.16 = (f32[2,24,128]{2,1,0:T(8,128)S(1)}, f32[2,24,128]{2,1,0:T(8,128)S(1)}, u32[]{:S(2)}, u32[]{:S(2)}) collective-permute-start(f32[2,24,128]{2,1,0:T(8,128)S(1)} %fusion.2), channel_id=1, source_target_pairs={{0,1},{1,0},{2,3},{3,2},{4,5},{5,4},{6,7},{7,6},{8,9},{9,8},{10,11... | collective-permute-start | bytes 73736 | tf_op jit(solution)/shard_map/ppermute | solution.py:26
  66.2 15.1 %all-to-all-start.1 = ((f32[8,120,128]{2,1,0:T(8,128)}), f32[8,120,128]{2,1,0:T(8,128)S(1)}, u32[]{:S(2)}, u32[]{:S(2)}) async-start(f32[8,120,128]{2,1,0:T(8,128)} %pad_maximum_fusion.1), calls=%async_computation.1 | async-start | bytes 983040 | tf_op jit(solution)/shard_map/all_to_all | solution.py:66
  81.3 8.2 %collective-permute-start.27 = (f32[64,384]{1,0:T(8,128)S(1)}, f32[64,384]{1,0:T(8,128)S(1)}, u32[]{:S(2)}, u32[]{:S(2)}) collective-permute-start(f32[64,384]{1,0:T(8,128)S(1)} %pad_maximum_fusion.8), channel_id=1, source_target_pairs={{0,4},{4,0},{1,5},{5,1},{2,6},{6,2},{3,7},{7,3},{8,12},{12,8},{9,1... | collective-permute-start | bytes 294920 | tf_op jit(solution)/shard_map/ppermute | solution.py:26
  83.7 4.0 %collective-permute-start.32 = (f32[48,128]{1,0:T(8,128)S(1)}, f32[48,128]{1,0:T(8,128)S(1)}, u32[]{:S(2)}, u32[]{:S(2)}) collective-permute-start(f32[48,128]{1,0:T(8,128)S(1)} %slice_reduce_fusion), channel_id=1, source_target_pairs={{0,8},{8,0},{16,24},{24,16},{1,9},{9,1},{17,25},{25,17},{2,10},{10... | collective-permute-start | bytes 73736 | tf_op jit(solution)/shard_map/ppermute | solution.py:26
  84.9 5.0 %collective-permute-start.17 = (f32[64,384]{1,0:T(8,128)S(1)}, f32[64,384]{1,0:T(8,128)S(1)}, u32[]{:S(2)}, u32[]{:S(2)}) collective-permute-start(f32[64,384]{1,0:T(8,128)S(1)} %pad_maximum_fusion.6), channel_id=1, source_target_pairs={{0,4},{4,0},{1,5},{5,1},{2,6},{6,2},{3,7},{7,3},{8,12},{12,8},{9,1... | collective-permute-start | bytes 294920 | tf_op jit(solution)/shard_map/ppermute | solution.py:26
  85.5 7.7 %collective-permute-start.22 = (f32[64,384]{1,0:T(8,128)S(1)}, f32[64,384]{1,0:T(8,128)S(1)}, u32[]{:S(2)}, u32[]{:S(2)}) collective-permute-start(f32[64,384]{1,0:T(8,128)S(1)} %get-tuple-element.101), channel_id=1, source_target_pairs={{0,8},{8,16},{16,24},{24,0},{1,9},{9,17},{17,25},{25,1},{2,10},{10... | collective-permute-start | bytes 294920 | tf_op jit(solution)/shard_map/ppermute | solution.py:21
  86.0 7.6 %collective-permute-start.23 = (f32[64,384]{1,0:T(8,128)S(1)}, f32[64,384]{1,0:T(8,128)S(1)}, u32[]{:S(2)}, u32[]{:S(2)}) collective-permute-start(f32[64,384]{1,0:T(8,128)S(1)} %get-tuple-element.101), channel_id=1, source_target_pairs={{0,16},{8,24},{16,0},{24,8},{1,17},{9,25},{17,1},{25,9},{2,18},{10... | collective-permute-start | bytes 294920 | tf_op jit(solution)/shard_map/ppermute | solution.py:21
  87.7 6.0 %collective-permute-start.24 = (f32[64,384]{1,0:T(8,128)S(1)}, f32[64,384]{1,0:T(8,128)S(1)}, u32[]{:S(2)}, u32[]{:S(2)}) collective-permute-start(f32[64,384]{1,0:T(8,128)S(1)} %get-tuple-element.101), channel_id=1, source_target_pairs={{0,24},{8,0},{16,8},{24,16},{1,25},{9,1},{17,9},{25,17},{2,26},{10... | collective-permute-start | bytes 294920 | tf_op jit(solution)/shard_map/ppermute | solution.py:21
  89.7 16.8 %collective-permute-start.28 = (f32[128,384]{1,0:T(8,128)S(1)}, f32[128,384]{1,0:T(8,128)S(1)}, u32[]{:S(2)}, u32[]{:S(2)}) collective-permute-start(f32[128,384]{1,0:T(8,128)S(1)} %get-tuple-element.89), channel_id=1, source_target_pairs={{0,8},{8,16},{16,24},{24,0},{1,9},{9,17},{17,25},{25,1},{2,10},{10... | collective-permute-start | bytes 589832 | tf_op jit(solution)/shard_map/ppermute | solution.py:21
  89.9 19.2 %collective-permute-start.29 = (f32[128,384]{1,0:T(8,128)S(1)}, f32[128,384]{1,0:T(8,128)S(1)}, u32[]{:S(2)}, u32[]{:S(2)}) collective-permute-start(f32[128,384]{1,0:T(8,128)S(1)} %get-tuple-element.89), channel_id=1, source_target_pairs={{0,16},{8,24},{16,0},{24,8},{1,17},{9,25},{17,1},{25,9},{2,18},{10... | collective-permute-start | bytes 589832 | tf_op jit(solution)/shard_map/ppermute | solution.py:21
  93.2 4.5 %collective-permute-start.33 = (f32[48,128]{1,0:T(8,128)S(1)}, f32[48,128]{1,0:T(8,128)S(1)}, u32[]{:S(2)}, u32[]{:S(2)}) collective-permute-start(f32[48,128]{1,0:T(8,128)S(1)} %add.338), channel_id=1, source_target_pairs={{0,16},{8,24},{16,0},{24,8},{1,17},{9,25},{17,1},{25,9},{2,18},{10... | collective-permute-start | bytes 73736 | tf_op jit(solution)/shard_map/ppermute | solution.py:26
  97.7 4.2 %collective-permute-start.34 = (f32[48,128]{1,0:T(8,128)S(1)}, f32[48,128]{1,0:T(8,128)S(1)}, u32[]{:S(2)}, u32[]{:S(2)}) collective-permute-start(f32[48,128]{1,0:T(8,128)S(1)} %add.339), channel_id=1, source_target_pairs={{0,4},{4,0},{1,5},{5,1},{2,6},{6,2},{3,7},{7,3},{8,12},{12,8},{9,1... | collective-permute-start | bytes 73736 | tf_op jit(solution)/shard_map/ppermute | solution.py:26
  100.6 10.2 %collective-permute-start.30 = (f32[128,384]{1,0:T(8,128)S(1)}, f32[128,384]{1,0:T(8,128)S(1)}, u32[]{:S(2)}, u32[]{:S(2)}) collective-permute-start(f32[128,384]{1,0:T(8,128)S(1)} %get-tuple-element.89), channel_id=1, source_target_pairs={{0,24},{8,0},{16,8},{24,16},{1,25},{9,1},{17,9},{25,17},{2,26},{10... | collective-permute-start | bytes 589832 | tf_op jit(solution)/shard_map/ppermute | solution.py:21
  101.8 27.7 %collective-permute-start.25 = (f32[256,384]{1,0:T(8,128)S(1)}, f32[256,384]{1,0:T(8,128)S(1)}, u32[]{:S(2)}, u32[]{:S(2)}) collective-permute-start(f32[256,384]{1,0:T(8,128)S(1)} %constant_dynamic-update-slice_fusion.4), channel_id=1, source_target_pairs={{0,4},{4,0},{1,5},{5,1},{2,6},{6,2},{3,7},{7,3},{8,12},{12,8},{9,1... | collective-permute-start | bytes 1179656 | tf_op jit(solution)/shard_map/ppermute | solution.py:26
  101.9 19.9 %collective-permute-start.18 = (f32[128,384]{1,0:T(8,128)}, f32[128,384]{1,0:T(8,128)S(1)}, u32[]{:S(2)}, u32[]{:S(2)}) collective-permute-start(f32[128,384]{1,0:T(8,128)} %get-tuple-element.93), channel_id=1, source_target_pairs={{0,8},{8,16},{16,24},{24,0},{1,9},{9,17},{17,25},{25,1},{2,10},{10... | collective-permute-start | bytes 589832 | tf_op jit(solution)/shard_map/ppermute | solution.py:21
  103.0 25.3 %all-to-all-start.2 = ((f32[8,48,128]{2,1,0:T(8,128)}), f32[8,48,128]{2,1,0:T(8,128)S(1)}, u32[]{:S(2)}, u32[]{:S(2)}) async-start(f32[8,48,128]{2,1,0:T(8,128)} %broadcast_in_dim.19), calls=%async_computation.2 | async-start | bytes 393216 | tf_op jit(solution)/shard_map/all_to_all | solution.py:66
  106.5 15.3 %collective-permute-start.19 = (f32[128,384]{1,0:T(8,128)}, f32[128,384]{1,0:T(8,128)S(1)}, u32[]{:S(2)}, u32[]{:S(2)}) collective-permute-start(f32[128,384]{1,0:T(8,128)} %get-tuple-element.93), channel_id=1, source_target_pairs={{0,16},{8,24},{16,0},{24,8},{1,17},{9,25},{17,1},{25,9},{2,18},{10... | collective-permute-start | bytes 589832 | tf_op jit(solution)/shard_map/ppermute | solution.py:21
  109.1 12.7 %collective-permute-start.20 = (f32[128,384]{1,0:T(8,128)}, f32[128,384]{1,0:T(8,128)S(1)}, u32[]{:S(2)}, u32[]{:S(2)}) collective-permute-start(f32[128,384]{1,0:T(8,128)} %get-tuple-element.93), channel_id=1, source_target_pairs={{0,24},{8,0},{16,8},{24,16},{1,25},{9,1},{17,9},{25,17},{2,26},{10... | collective-permute-start | bytes 589832 | tf_op jit(solution)/shard_map/ppermute | solution.py:21
  110.9 27.6 %copy-start.2 = (f32[512,384]{1,0:T(8,128)}, f32[512,384]{1,0:T(8,128)S(1)}, u32[]{:S(2)}) copy-start(f32[512,384]{1,0:T(8,128)S(1)} %constant_dynamic-update-slice_fusion.dir_own.proj_own) | copy-start | bytes 2359300
  110.9 27.6 %collective-permute-start.31 = (f32[512,384]{1,0:T(8,128)S(1)}, f32[512,384]{1,0:T(8,128)}, u32[]{:S(2)}, u32[]{:S(2)}) collective-permute-start(f32[512,384]{1,0:T(8,128)S(1)} %constant_dynamic-update-slice_fusion.dir_own.proj_own), channel_id=1, source_target_pairs={{0,2},{2,0},{1,3},{3,1},{4,6},{6,4},{5,7},{7,5},{8,10},{10,8},{9,1... | collective-permute-start | bytes 2359304 | tf_op jit(solution)/shard_map/ppermute | solution.py:26
  121.9 22.2 %copy-start.1 = (f32[512,384]{1,0:T(8,128)}, f32[512,384]{1,0:T(8,128)S(1)}, u32[]{:S(2)}) copy-start(f32[512,384]{1,0:T(8,128)S(1)} %constant_dynamic-update-slice_fusion.8.dir_own.proj_own) | copy-start | bytes 2359300
  121.9 27.8 %collective-permute-start.21 = (f32[512,384]{1,0:T(8,128)S(1)}, f32[512,384]{1,0:T(8,128)S(1)}, u32[]{:S(2)}, u32[]{:S(2)}) collective-permute-start(f32[512,384]{1,0:T(8,128)S(1)} %constant_dynamic-update-slice_fusion.8.dir_own.proj_own), channel_id=1, source_target_pairs={{0,2},{2,0},{1,3},{3,1},{4,6},{6,4},{5,7},{7,5},{8,10},{10,8},{9,1... | collective-permute-start | bytes 2359304 | tf_op jit(solution)/shard_map/ppermute | solution.py:26
  128.9 5.2 %collective-permute-start.35 = (f32[2,128,128]{2,1,0:T(8,128)S(1)}, f32[2,128,128]{2,1,0:T(8,128)S(1)}, u32[]{:S(2)}, u32[]{:S(2)}) collective-permute-start(f32[2,128,128]{2,1,0:T(8,128)S(1)} %fusion.21), channel_id=1, source_target_pairs={{0,1},{1,0},{2,3},{3,2},{4,5},{5,4},{6,7},{7,6},{8,9},{9,8},{10,11... | collective-permute-start | bytes 393224 | tf_op jit(solution)/shard_map/ppermute | solution.py:26
  129.6 14.5 %copy-start = (f32[512,384]{1,0:T(8,128)}, f32[512,384]{1,0:T(8,128)S(1)}, u32[]{:S(2)}) copy-start(f32[512,384]{1,0:T(8,128)S(1)} %pad_maximum_fusion.dir_own.proj_own) | copy-start | bytes 2359300
  129.7 14.5 %collective-permute-start.26 = (f32[512,384]{1,0:T(8,128)S(1)}, f32[512,384]{1,0:T(8,128)}, u32[]{:S(2)}, u32[]{:S(2)}) collective-permute-start(f32[512,384]{1,0:T(8,128)S(1)} %pad_maximum_fusion.dir_own.proj_own), channel_id=1, source_target_pairs={{0,2},{2,0},{1,3},{3,1},{4,6},{6,4},{5,7},{7,5},{8,10},{10,8},{9,1... | collective-permute-start | bytes 2359304 | tf_op jit(solution)/shard_map/ppermute | solution.py:26
  134.7 2.1 %collective-permute-start.36 = (f32[2,192,128]{2,1,0:T(8,128)S(1)}, f32[2,192,128]{2,1,0:T(8,128)}, u32[]{:S(2)}, u32[]{:S(2)}) collective-permute-start(f32[2,192,128]{2,1,0:T(8,128)S(1)} %fusion), channel_id=1, source_target_pairs={{0,2},{2,0},{1,3},{3,1},{4,6},{6,4},{5,7},{7,5},{8,10},{10,8},{9,1... | collective-permute-start | bytes 589832 | tf_op jit(solution)/shard_map/ppermute | solution.py:26
  149.7 0.9 copy-start.4

commit v3 on v2

--- a/solution.py
+++ b/solution.py
@@ -16,11 +16,6 @@
 CHUNKS = len(ORDERS)
 
 
-def shift(x, axis, k):
-    n = SIZES[axis]
-    return lax.ppermute(x, axis, [(i, (i + k) % n) for i in range(n)])
-
-
 def flip(x, axis, bit=1):
     n = SIZES[axis]
     return lax.ppermute(x, axis, [(i, i ^ bit) for i in range(n)])
@@ -39,27 +34,25 @@
     return lax.optimization_barrier((x, *others))[0]
 
 
-def blocks(x, axis):
+def halves(x, axis):
     n, me = SIZES[axis], lax.axis_index(axis)
     return [rows(x, (me + k) % n, x.shape[0] // n) for k in range(n)]
 
 
-def scatter(own, sent, axis):
-    for k, block in enumerate(sent, 1):
-        own = own + shift(block, axis, k)
-    return own
-
-
 def gather(x, axis):
+    if SIZES[axis] == 2:
+        return jnp.concatenate(in_order(lax.axis_index(axis), x, flip(x, axis)), axis=0)
+    return exchange(copies(x, axis), axis).reshape((-1,) + x.shape[1:])
+
+
+def gather_shifts(x, axis, own):
     n, me = SIZES[axis], lax.axis_index(axis)
-    if n == 2:
-        return jnp.concatenate(in_order(me, x, flip(x, axis)), axis=0)
-    count = x.shape[0]
-    out = jnp.zeros((n * count,) + x.shape[1:], x.dtype)
-    out = lax.dynamic_update_slice_in_dim(out, x, me * count, 0)
+    out = jnp.zeros((n,) + x.shape, x.dtype)
+    out = lax.dynamic_update_slice_in_dim(out, own[None], me, 0)
     for k in range(1, n):
-        out = lax.dynamic_update_slice_in_dim(out, shift(x, axis, k), ((me - k) % n) * count, 0)
-    return out
+        moved = lax.ppermute(x, axis, [(i, (i + k) % n) for i in range(n)])
+        out = lax.dynamic_update_slice_in_dim(out, moved[None], (me - k) % n, 0)
+    return out.reshape((-1,) + x.shape[1:])
 
 
 def exchange(parts, axis):
@@ -68,6 +61,33 @@
 
 def copies(x, axis):
     return jnp.broadcast_to(x, (SIZES[axis],) + x.shape)
+
+
+def pair_kernel(core, grad, given, out):
+    both = grad[...] + given[...]
+    out[...] = both.reshape(-1, both.shape[2]).T
+
+
+def pair_sum(chunk, core, grad, given):
+    half, depth, some = given.shape
+    lanes = 256
+    steps = some // lanes
+    return pl.pallas_call(
+        pair_kernel,
+        grid_spec=pltpu.PrefetchScalarGridSpec(
+            num_scalar_prefetch=1,
+            grid=(steps,),
+            in_specs=[
+                pl.BlockSpec((half, depth, lanes), lambda i, c: (c[0], 0, chunk * steps + i)),
+                pl.BlockSpec((half, depth, lanes), lambda i, c: (0, 0, i)),
+            ],
+            out_specs=pl.BlockSpec((lanes, half * depth), lambda i, c: (i, 0)),
+        ),
+        out_shape=jax.ShapeDtypeStruct((some, half * depth), grad.dtype),
+        compiler_params=pltpu.CompilerParams(vmem_limit_bytes=12 << 20),
+        cost_estimate=pl.CostEstimate(flops=given.size, bytes_accessed=12 * given.size, transcendentals=0),
+        name="pair_sum",
+    )(core.reshape(1), grad, given)
 
 
 def finish_kernel(core, dir_own, dir_other, proj_own, proj_other, basis, weights, first, second, *rest):
@@ -106,6 +126,10 @@
         ),
         out_shape=[jax.ShapeDtypeStruct(a.shape, a.dtype) for a in (weights, first, second)],
         input_output_aliases={9 + i: i for i in range(len(kept))},
+        compiler_params=pltpu.CompilerParams(vmem_limit_bytes=12 << 20),
+        cost_estimate=pl.CostEstimate(
+            flops=12 * layers * depth * rank * some, bytes_accessed=8 * layers * (depth + rank) * some, transcendentals=0
+        ),
         name="finish",
     )(core.reshape(1), own, other, own, other, basis, weights, first, second, *kept)
 
@@ -119,30 +143,26 @@
     z, y, xh = lax.axis_index("z"), lax.axis_index("y"), lax.axis_index("xh")
     core, xl = lax.axis_index("core"), lax.axis_index("xl")
     grad = grads[0]
+    kept = [pltpu.with_memory_space_constraint(a, pltpu.HBM) for a in (grad, weights, first_moment, second_moment)]
 
     given = []
     for chunk in range(CHUNKS):
         if given:
             grad = after(grad, given[-1])
         given.append(lax.dynamic_slice(grad, ((1 - core) * half, 0, chunk * some), (half, depth, some)))
-    grad = after(grad, given[-1])
     given = [flip(g, "core") for g in given]
-    first_sent = []
+    held = [pair_sum(chunk, core, kept[0], given[chunk]) for chunk in range(CHUNKS)]
+    by_y = lambda x: jnp.sum(exchange(x.reshape((SIZES["y"], -1) + x.shape[1:]), "y"), axis=0)
+    own, sent = halves(held[1], "xh")
+    held[0] = by_y(held[0])
+    held[2] = by_y(held[2])
+    held[1] = by_y(own + flip(sent, "xh"))
+    for chunk in (0, 2):
+        own, sent = halves(held[chunk], "xh")
+        held[chunk] = own + flip(sent, "xh")
+    pieces, places = [], []
     for chunk, order in enumerate(ORDERS):
-        held = lax.dynamic_slice(grad, (core * half, 0, chunk * some), (half, depth, some)) + given[chunk]
-        own, *sent = blocks(held.reshape(half * depth, some).T, order[0])
-        grad = after(grad, *sent)
-        first_sent.append((own, sent))
-    last = first_sent[-1][1]
-    second_sent = []
-    for (own, sent), order in zip(first_sent, ORDERS):
-        own, *sent = blocks(scatter(after(own, *last), sent, order[0]), order[1])
-        second_sent.append((own, sent))
-        last = sent
-    pieces, places = [], []
-    for chunk, ((own, sent), order) in enumerate(zip(second_sent, ORDERS)):
-        held = scatter(after(own, *last), sent, order[1])
-        pieces.append(held.reshape(SIZES["z"], small, half * depth))
+        pieces.append(held[chunk].reshape(SIZES["z"], small, half * depth))
         index = {"y": y, "xh": xh}
         place = (index[order[0]] * SIZES[order[1]] + index[order[1]]) * SIZES["z"] + z
         places.append(chunk * some + place * small)
@@ -182,20 +202,21 @@
         jnp.concatenate([packed[:, i, chunk].reshape(SIZES["z"] * small, rank) for i in range(3)], axis=1)
         for chunk in range(CHUNKS)
     ]
-    part = after(part, *held)
-    wide = [gather(h, order[1]) for h, order in zip(held, ORDERS)]
-    part = part + flip(part, "y", 1)
-    part = after(part, wide[0], wide[2])
-    part = part + flip(part, "y", 2)
-    part = after(part, *wide)
+    count = held[1].shape[0]
+    extra = part.reshape(-1, half * depth)
+    both = exchange(copies(jnp.concatenate([held[1], extra]), "y"), "y")
+    middle = both[:, :count].reshape(SIZES["y"] * count, half * depth)
+    part = jnp.sum(both[:, count:], axis=0).reshape(part.shape)
     part = part + flip(part, "xh")
-    ready = []
-    for w, order in zip(wide, ORDERS):
-        w = gather(w, order[0])
-        ready.append((w, flip(w, "core")))
+    sides = [gather(held[chunk], "xh") for chunk in (0, 2)]
+    wide = [gather(sides[0], "y"), gather(middle, "xh")]
     done = None
-    for chunk, (own, other) in enumerate(ready):
-        done = finish(chunk, core, own, other, basis, weights, first_moment, second_moment, done)
+    for chunk in range(CHUNKS):
+        if chunk == 2:
+            moved = after(sides[1], wide[0])
+            wide.append(gather_shifts(moved, "y", after(moved, *done)))
+        other = flip(wide[chunk], "core")
+        done = finish(chunk, core, wide[chunk], other, basis, *kept[1:], done)
     new_weights, new_first, new_second = done
 
     refresh = exchange(copies(part, "z"), "z").reshape(half, depth, rank)

time: 157 us -> 163 us (1.038)
  blocking collectives: 0 us -> 14.3 us
  starting transfers between devices: 75.1 us -> 66.5 us
  other arithmetic: 9.89 us -> 4.54 us
  waiting for transfers between devices: 41.1 us -> 44.7 us
  Pallas kernels: 16.7 us -> 20 us
    ppermute x21 -> x3, starting transfers between devices: 29.2 us -> 2.86 us  [gather_shifts(): moved = lax.ppermute(x, axis, [(i, (i + k) % n) for i in range(n)])]
    all_to_all x3 -> x7, waiting for transfers between devices: 18.4 us -> 35.9 us  [exchange(): return lax.all_to_all(parts, axis, split_axis=0, concat_axis=0)]
    all_to_all x0 -> x1, blocking collectives: none -> 14.3 us  [exchange(): return lax.all_to_all(parts, axis, split_axis=0, concat_axis=0)]
    all_to_all x3 -> x7, starting transfers between devices: 13.4 us -> 27.3 us  [exchange(): return lax.all_to_all(parts, axis, split_axis=0, concat_axis=0)]
    ppermute x21 -> x3, waiting for transfers between devices: 9.73 us -> 0.01 us  [gather_shifts(): moved = lax.ppermute(x, axis, [(i, (i + k) % n) for i in range(n)])]
    pallas_call x0 -> x3, Pallas kernels: none -> 5.58 us  [pair_sum(): pl.pallas_call(pair_kernel, grid_spec=pltpu.PrefetchScalarGridSpec(num_sc...]
    add x11 -> x1, other arithmetic: 5.07 us -> 0.79 us  [on_device(): held[1] = by_y(own + flip(sent, 'xh'))]
    ppermute x16 -> x17, waiting for transfers between devices: 13 us -> 8.83 us  [flip(): return lax.ppermute(x, axis, [(i, i ^ bit) for i in range(n)])]
  transfers between devices with their start and end apart: 40 -> 27, of which waited for: 12 -> 10; matrix products, arithmetic and copies ran while one was open for 10% -> 6% of each run, Pallas kernels for 7% -> 9%
where the time goes in v3:
time: 163 us; the launch traced here: 162 us
  starting transfers between devices  66.5 us (41%)
  waiting for transfers between devices  44.7 us (27%)
  Pallas kernels  20 us (12%)
  blocking collectives  14.3 us (9%)
  local copies, waits for them, and re-layouts  9.03 us (6%)
  other arithmetic  4.54 us (3%)
  matrix products  1.83 us (1%)
    ppermute x17, starting transfers between devices, flip(): return lax.ppermute(x, axis, [(i, i ^ bit) for i in range(n)])  36.3 us
    all_to_all x7, waiting for transfers between devices, exchange(): return lax.all_to_all(parts, axis, split_axis=0, concat_axis=0)  35.9 us
    all_to_all x7, starting transfers between devices, exchange(): return lax.all_to_all(parts, axis, split_axis=0, concat_axis=0)  27.3 us
    pallas_call x3, Pallas kernels, finish(): pl.pallas_call(finish_kernel, grid_spec=pltpu.PrefetchScalarGridSpec(num_...  14.5 us
    all_to_all x1, blocking collectives, exchange(): return lax.all_to_all(parts, axis, split_axis=0, concat_axis=0)  14.3 us
    ppermute x17, waiting for transfers between devices, flip(): return lax.ppermute(x, axis, [(i, i ^ bit) for i in range(n)])  8.83 us
    pallas_call x3, Pallas kernels, pair_sum(): pl.pallas_call(pair_kernel, grid_spec=pltpu.PrefetchScalarGridSpec(num_sc...  5.58 us
    dynamic_slice x3, local copies, waits for them, and re-layouts, on_device(): lax.dynamic_slice(grad, ((1 - core) * half, 0, chunk * some), (half, dept...  4.43 us
  transfers between devices with their start and end apart: 27, of which 10 were waited for; matrix products, arithmetic and copies ran while one was open for 6% of the time, Pallas kernels for 9%

profile of v3, /device:TPU:1, one launch (start us, length us, event | category | flops | bytes accessed | tf_op | source)
XLA Modules:
  0.0 162.1 jit_solution(4560358965990052665)
XLA Ops:
  0.6 1.2 dynamic-slice_bitcast_fusion
  1.8 3.3 %collective-permute-start.1 = (f32[2,192,512]{2,1,0:T(8,128)S(1)}, f32[2,192,512]{2,1,0:T(8,128)S(1)}, u32[]{:S(2)}, u32[]{:S(2)}) collective-permute-start(f32[2,192,512]{2,1,0:T(8,128)S(1)} %dynamic-slice_bitcast_fusion), channel_id=1, source_target_pairs={{0,2},{2,0},{1,3},{3,1},{4,6},{6,4},{5,7},{7,5},{8,10},{10,8},{9,1... | collective-permute-start | bytes 2359304 | tf_op jit(solution)/shard_map/ppermute | solution.py:21
  5.2 1.2 constant_dynamic-slice_fusion.3
  6.3 0.1 collective-permute-start.3
  6.5 2.1 %constant_dynamic-slice_fusion.1 = f32[2,192,512]{2,1,0:T(8,128)} fusion(f32[4,192,1536]{2,1,0:T(8,128)} %bitcast.67, s32[]{:T(128)S(6)} %select_n.158), kind=kLoop, calls=%fused_computation.71 | loop fusion | bytes 1572868 | tf_op jit(solution)/shard_map/dynamic_slice | solution.py:152
  8.5 0.5 collective-permute-start.5
  9.0 2.1 %pair_sum.3 = f32[512,384]{1,0:T(8,128)} custom-call(s32[1]{0:T(128)} %bitcast.core, f32[4,192,1536]{2,1,0:T(8,128)} %bitcast.68, f32[2,192,512]{2,1,0:T(8,128)S(1)} %collective-permute-done.1.given), custom_call_target="tpu_custom_call" | custom-call | flops 196608 | bytes 2359296 | tf_op jit(solution)/shard_map/pair_sum/pallas_call | solution.py:75
  11.1 3.5 %all-to-all-start = ((f32[4,128,384]{2,1,0:T(8,128)}), f32[4,128,384]{2,1,0:T(8,128)S(1)}, u32[]{:S(2)}, u32[]{:S(2)}) async-start(f32[4,128,384]{2,1,0:T(8,128)} %bitcast.5), calls=%async_computation | async-start | bytes 1572864 | tf_op jit(solution)/shard_map/all_to_all | solution.py:59
  14.6 1.4 pair_sum.4
  16.1 1.7 %collective-permute-start.4 = (f32[256,384]{1,0:T(8,128)S(1)}, f32[256,384]{1,0:T(8,128)S(1)}, u32[]{:S(2)}, u32[]{:S(2)}) collective-permute-start(f32[256,384]{1,0:T(8,128)S(1)} %constant_dynamic-slice_fusion.2), channel_id=1, source_target_pairs={{0,4},{4,0},{1,5},{5,1},{2,6},{6,2},{3,7},{7,3},{8,12},{12,8},{9,1... | collective-permute-start | bytes 1179656 | tf_op jit(solution)/shard_map/ppermute | solution.py:21
  17.8 2.1 %pair_sum.5 = f32[512,384]{1,0:T(8,128)} custom-call(s32[1]{0:T(128)} %bitcast.core, f32[4,192,1536]{2,1,0:T(8,128)} %bitcast.70, f32[2,192,512]{2,1,0:T(8,128)S(1)} %collective-permute-done.5.given), custom_call_target="tpu_custom_call" | custom-call | flops 196608 | bytes 2359296 | tf_op jit(solution)/shard_map/pair_sum/pallas_call | solution.py:75
  19.9 7.1 %all-to-all-done = f32[4,128,384]{2,1,0:T(8,128)S(1)} async-done(((f32[4,128,384]{2,1,0:T(8,128)}), f32[4,128,384]{2,1,0:T(8,128)S(1)}, u32[]{:S(2)}, u32[]{:S(2)}) %all-to-all-start) | async-done | bytes 786464 | tf_op jit(solution)/shard_map/all_to_all | solution.py:59
  27.0 3.5 %all-to-all-start.2 = ((f32[4,128,384]{2,1,0:T(8,128)}), f32[4,128,384]{2,1,0:T(8,128)S(1)}, u32[]{:S(2)}, u32[]{:S(2)}) async-start(f32[4,128,384]{2,1,0:T(8,128)} %bitcast.9), calls=%async_computation.2 | async-start | bytes 1572864 | tf_op jit(solution)/shard_map/all_to_all | solution.py:59
  30.5 1.2 constant_dynamic-slice_fusion.7
  32.1 0.6 maximum_bitcast_fusion
  32.8 0.6 maximum_bitcast_fusion.1
  33.4 0.8 dynamic-slice_add_fusion
  34.2 1.5 collective-permute-start.2
  35.7 6.3 %all-to-all-done.2 = f32[4,128,384]{2,1,0:T(8,128)S(1)} async-done(((f32[4,128,384]{2,1,0:T(8,128)}), f32[4,128,384]{2,1,0:T(8,128)S(1)}, u32[]{:S(2)}, u32[]{:S(2)}) %all-to-all-start.2) | async-done | bytes 786464 | tf_op jit(solution)/shard_map/all_to_all | solution.py:59
  42.0 3.5 %all-to-all-start.1 = ((f32[4,64,384]{2,1,0:T(8,128)}), f32[4,64,384]{2,1,0:T(8,128)S(1)}, u32[]{:S(2)}, u32[]{:S(2)}) async-start(f32[4,64,384]{2,1,0:T(8,128)} %bitcast.7), calls=%async_computation.1 | async-start | bytes 786432 | tf_op jit(solution)/shard_map/all_to_all | solution.py:59
  45.6 1.1 collective-permute-start.6
  46.8 4.9 %all-to-all-done.1 = f32[4,64,384]{2,1,0:T(8,128)S(1)} async-done(((f32[4,64,384]{2,1,0:T(8,128)}), f32[4,64,384]{2,1,0:T(8,128)S(1)}, u32[]{:S(2)}, u32[]{:S(2)}) %all-to-all-start.1) | async-done | bytes 393248 | tf_op jit(solution)/shard_map/all_to_all | solution.py:59
  51.8 0.7 pad_maximum_fusion.3
  52.5 6.5 %all-to-all-start.3 = ((f32[8,24,384]{2,1,0:T(8,128)}), f32[8,24,384]{2,1,0:T(8,128)S(1)}, u32[]{:S(2)}, u32[]{:S(2)}) async-start(f32[8,24,384]{2,1,0:T(8,128)} %pad_maximum_fusion.3), calls=%async_computation.3 | async-start | bytes 589824 | tf_op jit(solution)/shard_map/all_to_all | solution.py:59
  59.0 0.1 pad_maximum_fusion.10
  59.1 1.2 collective-permute-start
  60.3 1.5 collective-permute-done
  62.0 6.8 %all-to-all-done.3 = f32[8,24,384]{2,1,0:T(8,128)S(1)} async-done(((f32[8,24,384]{2,1,0:T(8,128)}), f32[8,24,384]{2,1,0:T(8,128)S(1)}, u32[]{:S(2)}, u32[]{:S(2)}) %all-to-all-start.3) | async-done | bytes 294944 | tf_op jit(solution)/shard_map/all_to_all | solution.py:59
  68.8 0.1 reshape.81
  68.9 0.3 fusion.2
  69.2 1.3 collective-permute-start.7
  70.6 1.7 %collective-permute-done.7 = f32[2,24,128]{2,1,0:T(8,128)S(1)} collective-permute-done((f32[2,24,128]{2,1,0:T(8,128)S(1)}, f32[2,24,128]{2,1,0:T(8,128)S(1)}, u32[]{:S(2)}, u32[]{:S(2)}) %collective-permute-start.7) | collective-permute-done | bytes 24608 | tf_op jit(solution)/shard_map/ppermute | solution.py:21
  72.3 0.1 fusion.14
  72.4 0.5 fusion.7
  73.1 14.3 %all_to_all.40 = f32[8,120,128]{2,1,0:T(8,128)S(1)} all-to-all(f32[8,120,128]{2,1,0:T(8,128)S(1)} %pad_maximum_fusion.1), channel_id=1, replica_groups=mesh['z'=8,'y'=4,'xh'=2,'core'=2,'xl'=2] {'z'}, dimensions={0} | all-to-all | bytes 983040 | tf_op jit(solution)/shard_map/all_to_all | solution.py:59
  87.5 2.8 %collective-permute-start.9 = (f32[64,384]{1,0:T(8,128)S(1)}, f32[64,384]{1,0:T(8,128)S(1)}, u32[]{:S(2)}, u32[]{:S(2)}) collective-permute-start(f32[64,384]{1,0:T(8,128)S(1)} %pad_maximum_fusion.8), channel_id=1, source_target_pairs={{0,4},{4,0},{1,5},{5,1},{2,6},{6,2},{3,7},{7,3},{8,12},{12,8},{9,1... | collective-permute-start | bytes 294920 | tf_op jit(solution)/shard_map/ppermute | solution.py:21
  90.3 0.8 broadcast_in_dim.38
  91.1 3.5 %all-to-all-start.6 = ((f32[4,80,384]{2,1,0:T(8,128)}), f32[4,80,384]{2,1,0:T(8,128)S(1)}, u32[]{:S(2)}, u32[]{:S(2)}) async-start(f32[4,80,384]{2,1,0:T(8,128)} %broadcast_in_dim.38), calls=%async_computation.6 | async-start | bytes 983040 | tf_op jit(solution)/shard_map/all_to_all | solution.py:59
  94.7 6.7 %all-to-all-done.6 = f32[4,80,384]{2,1,0:T(8,128)S(1)} async-done(((f32[4,80,384]{2,1,0:T(8,128)}), f32[4,80,384]{2,1,0:T(8,128)S(1)}, u32[]{:S(2)}, u32[]{:S(2)}) %all-to-all-start.6) | async-done | bytes 491552 | tf_op jit(solution)/shard_map/all_to_all | solution.py:59
  101.3 0.9 broadcast_in_dim.37
  102.3 3.5 %all-to-all-start.5 = ((f32[4,128,384]{2,1,0:T(8,128)}), f32[4,128,384]{2,1,0:T(8,128)S(1)}, u32[]{:S(2)}, u32[]{:S(2)}) async-start(f32[4,128,384]{2,1,0:T(8,128)} %broadcast_in_dim.37), calls=%async_computation.5 | async-start | bytes 1572864 | tf_op jit(solution)/shard_map/all_to_all | solution.py:59
  105.8 0.3 collective-permute-start.17
  106.1 4.0 %collective-permute-done.17 = f32[48,128]{1,0:T(8,128)S(1)} collective-permute-done((f32[48,128]{1,0:T(8,128)S(1)}, f32[48,128]{1,0:T(8,128)S(1)}, u32[]{:S(2)}, u32[]{:S(2)}) %collective-permute-start.17) | collective-permute-done | bytes 24608 | tf_op jit(solution)/shard_map/ppermute | solution.py:21
  110.1 4.0 %all-to-all-done.5 = f32[4,128,384]{2,1,0:T(8,128)S(1)} async-done(((f32[4,128,384]{2,1,0:T(8,128)}), f32[4,128,384]{2,1,0:T(8,128)S(1)}, u32[]{:S(2)}, u32[]{:S(2)}) %all-to-all-start.5) | async-done | bytes 786464 | tf_op jit(solution)/shard_map/all_to_all | solution.py:59
  114.1 0.7 broadcast_in_dim.43
  114.8 3.4 %all-to-all-start.7 = ((f32[8,48,128]{2,1,0:T(8,128)}), f32[8,48,128]{2,1,0:T(8,128)S(1)}, u32[]{:S(2)}, u32[]{:S(2)}) async-start(f32[8,48,128]{2,1,0:T(8,128)} %broadcast_in_dim.43), calls=%async_computation.7 | async-start | bytes 393216 | tf_op jit(solution)/shard_map/all_to_all | solution.py:59
  118.2 0.3 collective-permute-start.10
  118.6 2.8 %collective-permute-start.8 = (f32[64,384]{1,0:T(8,128)S(1)}, f32[64,384]{1,0:T(8,128)S(1)}, u32[]{:S(2)}, u32[]{:S(2)}) collective-permute-start(f32[64,384]{1,0:T(8,128)S(1)} %pad_maximum_fusion.7), channel_id=1, source_target_pairs={{0,4},{4,0},{1,5},{5,1},{2,6},{6,2},{3,7},{7,3},{8,12},{12,8},{9,1... | collective-permute-start | bytes 294920 | tf_op jit(solution)/shard_map/ppermute | solution.py:21
  121.4 9.8 %collective-permute-start.12 = (f32[512,384]{1,0:T(8,128)S(1)}, f32[512,384]{1,0:T(8,128)S(1)}, u32[]{:S(2)}, u32[]{:S(2)}) collective-permute-start(f32[512,384]{1,0:T(8,128)S(1)} %bitcast.63), channel_id=1, source_target_pairs={{0,2},{2,0},{1,3},{3,1},{4,6},{6,4},{5,7},{7,5},{8,10},{10,8},{9,1... | collective-permute-start | bytes 2359304 | tf_op jit(solution)/shard_map/ppermute | solution.py:21
  131.2 0.7 fusion.21
  131.9 0.6 collective-permute-start.18
  132.6 6.2 %collective-permute-start.11 = (f32[512,384]{1,0:T(8,128)S(1)}, f32[512,384]{1,0:T(8,128)S(1)}, u32[]{:S(2)}, u32[]{:S(2)}) collective-permute-start(f32[512,384]{1,0:T(8,128)S(1)} %pad_maximum_fusion.dir_own.proj_own), channel_id=1, source_target_pairs={{0,2},{2,0},{1,3},{3,1},{4,6},{6,4},{5,7},{7,5},{8,10},{10,8},{9,1... | collective-permute-start | bytes 2359304 | tf_op jit(solution)/shard_map/ppermute | solution.py:21
  138.9 0.4 collective-permute-start.13
  139.2 1.8 %collective-permute-start.14 = (f32[128,384]{1,0:T(8,128)S(1)}, f32[128,384]{1,0:T(8,128)S(1)}, u32[]{:S(2)}, u32[]{:S(2)}) collective-permute-start(f32[128,384]{1,0:T(8,128)S(1)} %pad_maximum_fusion.4), channel_id=1, source_target_pairs={{0,16},{8,24},{16,0},{24,8},{1,17},{9,25},{17,1},{25,9},{2,18},{10... | collective-permute-start | bytes 589832 | tf_op jit(solution)/shard_map/ppermute | solution.py:53
  141.0 0.7 collective-permute-start.15
  141.7 0.1 select_reduce_fusion
  141.9 4.8 %finish.3 = (f32[4,192,1536]{2,1,0:T(8,128)}, f32[4,64,1536]{2,1,0:T(8,128)}, f32[4,64,1536]{2,1,0:T(8,128)}) custom-call(s32[1]{0:T(128)} %bitcast.core, f32[512,384]{1,0:T(8,128)S(1)} %bitcast.64, f32[512,384]{1,0:T(8,128)S(1)} %collective-permute-done.12.dir_other.proj_other, f32[512,384]{1,0:T(8,128)S(1)} %bitcast.65, ...), custom_call_target="tpu_custom_call" | custom-call | flops 603979776 | bytes 5242880 | tf_op jit(solution)/shard_map/finish/pallas_call | solution.py:118
  146.7 4.8 %finish.4 = (f32[4,192,1536]{2,1,0:T(8,128)}, f32[4,64,1536]{2,1,0:T(8,128)}, f32[4,64,1536]{2,1,0:T(8,128)}) custom-call(s32[1]{0:T(128)} %bitcast.core, f32[512,384]{1,0:T(8,128)S(1)} %pad_maximum_fusion.dir_own.proj_own, f32[512,384]{1,0:T(8,128)S(1)} %collective-permute-done.11.dir_other.proj_other, ...), custom_call_target="tpu_custom_call", output_to_operand_aliasing={{0}: (9, {}), {1}: (10, {}), {2}: (11, {})} | custom-call | flops 603979776 | bytes 5242880 | tf_op jit(solution)/shard_map/finish/pallas_call | solution.py:118
  151.7 2.5 %collective-permute-start.16 = (f32[512,384]{1,0:T(8,128)S(1)}, f32[512,384]{1,0:T(8,128)S(1)}, u32[]{:S(2)}, u32[]{:S(2)}) collective-permute-start(f32[512,384]{1,0:T(8,128)S(1)} %bitcast.60), channel_id=1, source_target_pairs={{0,2},{2,0},{1,3},{3,1},{4,6},{6,4},{5,7},{7,5},{8,10},{10,8},{9,1... | collective-permute-start | bytes 2359304 | tf_op jit(solution)/shard_map/ppermute | solution.py:21
  154.3 0.4 fusion
  154.7 0.1 collective-permute-start.19
  154.8 1.7 %collective-permute-done.19 = f32[2,192,128]{2,1,0:T(8,128)S(1)} collective-permute-done((f32[2,192,128]{2,1,0:T(8,128)S(1)}, f32[2,192,128]{2,1,0:T(8,128)S(1)}, u32[]{:S(2)}, u32[]{:S(2)}) %collective-permute-start.19) | collective-permute-done | bytes 196640 | tf_op jit(solution)/shard_map/ppermute | solution.py:21
  156.5 0.8 pad_maximum_fusion.2
  157.3 4.8 %finish.5 = (f32[4,192,1536]{2,1,0:T(8,128)}, f32[4,64,1536]{2,1,0:T(8,128)}, f32[4,64,1536]{2,1,0:T(8,128)}) custom-call(s32[1]{0:T(128)} %bitcast.core, f32[512,384]{1,0:T(8,128)S(1)} %bitcast.61, f32[512,384]{1,0:T(8,128)S(1)} %collective-permute-done.16.dir_other.proj_other, ...), custom_call_target="tpu_custom_call", output_to_operand_aliasing={{0}: (9, {}), {1}: (10, {}), {2}: (11, {})} | custom-call | flops 603979776 | bytes 5242880 | tf_op jit(solution)/shard_map/finish/pallas_call | solution.py:118
  (72 shorter events, 1.6 us)
Async XLA Ops:
  1.8 7.2 %collective-permute-start.1 = (f32[2,192,512]{2,1,0:T(8,128)S(1)}, f32[2,192,512]{2,1,0:T(8,128)S(1)}, u32[]{:S(2)}, u32[]{:S(2)}) collective-permute-start(f32[2,192,512]{2,1,0:T(8,128)S(1)} %dynamic-slice_bitcast_fusion), channel_id=1, source_target_pairs={{0,2},{2,0},{1,3},{3,1},{4,6},{6,4},{5,7},{7,5},{8,10},{10,8},{9,1... | collective-permute-start | bytes 2359304 | tf_op jit(solution)/shard_map/ppermute | solution.py:21
  6.3 8.3 %collective-permute-start.3 = (f32[2,192,512]{2,1,0:T(8,128)S(1)}, f32[2,192,512]{2,1,0:T(8,128)S(1)}, u32[]{:S(2)}, u32[]{:S(2)}) collective-permute-start(f32[2,192,512]{2,1,0:T(8,128)S(1)} %constant_dynamic-slice_fusion.3), channel_id=1, source_target_pairs={{0,2},{2,0},{1,3},{3,1},{4,6},{6,4},{5,7},{7,5},{8,10},{10,8},{9,1... | collective-permute-start | bytes 2359304 | tf_op jit(solution)/shard_map/ppermute | solution.py:21
  8.5 9.3 %collective-permute-start.5 = (f32[2,192,512]{2,1,0:T(8,128)}, f32[2,192,512]{2,1,0:T(8,128)S(1)}, u32[]{:S(2)}, u32[]{:S(2)}) collective-permute-start(f32[2,192,512]{2,1,0:T(8,128)} %constant_dynamic-slice_fusion.1), channel_id=1, source_target_pairs={{0,2},{2,0},{1,3},{3,1},{4,6},{6,4},{5,7},{7,5},{8,10},{10,8},{9,1... | collective-permute-start | bytes 2359304 | tf_op jit(solution)/shard_map/ppermute | solution.py:21
  11.1 15.9 %all-to-all-start = ((f32[4,128,384]{2,1,0:T(8,128)}), f32[4,128,384]{2,1,0:T(8,128)S(1)}, u32[]{:S(2)}, u32[]{:S(2)}) async-start(f32[4,128,384]{2,1,0:T(8,128)} %bitcast.5), calls=%async_computation | async-start | bytes 1572864 | tf_op jit(solution)/shard_map/all_to_all | solution.py:59
  16.1 17.3 %collective-permute-start.4 = (f32[256,384]{1,0:T(8,128)S(1)}, f32[256,384]{1,0:T(8,128)S(1)}, u32[]{:S(2)}, u32[]{:S(2)}) collective-permute-start(f32[256,384]{1,0:T(8,128)S(1)} %constant_dynamic-slice_fusion.2), channel_id=1, source_target_pairs={{0,4},{4,0},{1,5},{5,1},{2,6},{6,2},{3,7},{7,3},{8,12},{12,8},{9,1... | collective-permute-start | bytes 1179656 | tf_op jit(solution)/shard_map/ppermute | solution.py:21
  27.0 15.0 %all-to-all-start.2 = ((f32[4,128,384]{2,1,0:T(8,128)}), f32[4,128,384]{2,1,0:T(8,128)S(1)}, u32[]{:S(2)}, u32[]{:S(2)}) async-start(f32[4,128,384]{2,1,0:T(8,128)} %bitcast.9), calls=%async_computation.2 | async-start | bytes 1572864 | tf_op jit(solution)/shard_map/all_to_all | solution.py:59
  34.2 12.5 %collective-permute-start.2 = (f32[64,384]{1,0:T(8,128)S(1)}, f32[64,384]{1,0:T(8,128)S(1)}, u32[]{:S(2)}, u32[]{:S(2)}) collective-permute-start(f32[64,384]{1,0:T(8,128)S(1)} %constant_dynamic-slice_fusion.4), channel_id=1, source_target_pairs={{0,4},{4,0},{1,5},{5,1},{2,6},{6,2},{3,7},{7,3},{8,12},{12,8},{9,1... | collective-permute-start | bytes 294920 | tf_op jit(solution)/shard_map/ppermute | solution.py:21
  42.0 9.7 %all-to-all-start.1 = ((f32[4,64,384]{2,1,0:T(8,128)}), f32[4,64,384]{2,1,0:T(8,128)S(1)}, u32[]{:S(2)}, u32[]{:S(2)}) async-start(f32[4,64,384]{2,1,0:T(8,128)} %bitcast.7), calls=%async_computation.1 | async-start | bytes 786432 | tf_op jit(solution)/shard_map/all_to_all | solution.py:59
  45.5 13.5 %copy-start.1 = (f32[2,24,64]{2,1,0:T(8,128)S(1)}, f32[2,24,64]{2,1,0:T(8,128)}, u32[]{:S(2)}) copy-start(f32[2,24,64]{2,1,0:T(8,128)} %maximum_bitcast_fusion) | copy-start | bytes 36868
  45.5 13.5 %copy-start.2 = (f32[2,24,64]{2,1,0:T(8,128)S(1)}, f32[2,24,64]{2,1,0:T(8,128)}, u32[]{:S(2)}) copy-start(f32[2,24,64]{2,1,0:T(8,128)} %maximum_bitcast_fusion.1) | copy-start | bytes 36868
  45.6 23.4 %copy-start = (f32[4,192,128]{2,1,0:T(8,128)S(1)}, f32[4,192,128]{2,1,0:T(8,128)}, u32[]{:S(2)}) copy-start(f32[4,192,128]{2,1,0:T(8,128)} %basis.5) | copy-start | bytes 1179652
  45.6 6.1 %collective-permute-start.6 = (f32[64,384]{1,0:T(8,128)S(1)}, f32[64,384]{1,0:T(8,128)S(1)}, u32[]{:S(2)}, u32[]{:S(2)}) collective-permute-start(f32[64,384]{1,0:T(8,128)S(1)} %constant_dynamic-slice_fusion), channel_id=1, source_target_pairs={{0,4},{4,0},{1,5},{5,1},{2,6},{6,2},{3,7},{7,3},{8,12},{12,8},{9,1... | collective-permute-start | bytes 294920 | tf_op jit(solution)/shard_map/ppermute | solution.py:21
  52.5 16.3 %all-to-all-start.3 = ((f32[8,24,384]{2,1,0:T(8,128)}), f32[8,24,384]{2,1,0:T(8,128)S(1)}, u32[]{:S(2)}, u32[]{:S(2)}) async-start(f32[8,24,384]{2,1,0:T(8,128)} %pad_maximum_fusion.3), calls=%async_computation.3 | async-start | bytes 589824 | tf_op jit(solution)/shard_map/all_to_all | solution.py:59
  59.1 2.7 %collective-permute-start = (f32[2,24,128]{2,1,0:T(8,128)S(1)}, f32[2,24,128]{2,1,0:T(8,128)S(1)}, u32[]{:S(2)}, u32[]{:S(2)}) collective-permute-start(f32[2,24,128]{2,1,0:T(8,128)S(1)} %pad_maximum_fusion.10), channel_id=1, source_target_pairs={{0,1},{1,0},{2,3},{3,2},{4,5},{5,4},{6,7},{7,6},{8,9},{9,8},{10,11... | collective-permute-start | bytes 73736 | tf_op jit(solution)/shard_map/ppermute | solution.py:21
  69.2 3.0 %collective-permute-start.7 = (f32[2,24,128]{2,1,0:T(8,128)S(1)}, f32[2,24,128]{2,1,0:T(8,128)S(1)}, u32[]{:S(2)}, u32[]{:S(2)}) collective-permute-start(f32[2,24,128]{2,1,0:T(8,128)S(1)} %fusion.2), channel_id=1, source_target_pairs={{0,1},{1,0},{2,3},{3,2},{4,5},{5,4},{6,7},{7,6},{8,9},{9,8},{10,11... | collective-permute-start | bytes 73736 | tf_op jit(solution)/shard_map/ppermute | solution.py:21
  87.5 7.1 %collective-permute-start.9 = (f32[64,384]{1,0:T(8,128)S(1)}, f32[64,384]{1,0:T(8,128)S(1)}, u32[]{:S(2)}, u32[]{:S(2)}) collective-permute-start(f32[64,384]{1,0:T(8,128)S(1)} %pad_maximum_fusion.8), channel_id=1, source_target_pairs={{0,4},{4,0},{1,5},{5,1},{2,6},{6,2},{3,7},{7,3},{8,12},{12,8},{9,1... | collective-permute-start | bytes 294920 | tf_op jit(solution)/shard_map/ppermute | solution.py:21
  91.1 10.2 %all-to-all-start.6 = ((f32[4,80,384]{2,1,0:T(8,128)}), f32[4,80,384]{2,1,0:T(8,128)S(1)}, u32[]{:S(2)}, u32[]{:S(2)}) async-start(f32[4,80,384]{2,1,0:T(8,128)} %broadcast_in_dim.38), calls=%async_computation.6 | async-start | bytes 983040 | tf_op jit(solution)/shard_map/all_to_all | solution.py:59
  102.3 11.8 %all-to-all-start.5 = ((f32[4,128,384]{2,1,0:T(8,128)}), f32[4,128,384]{2,1,0:T(8,128)S(1)}, u32[]{:S(2)}, u32[]{:S(2)}) async-start(f32[4,128,384]{2,1,0:T(8,128)} %broadcast_in_dim.37), calls=%async_computation.5 | async-start | bytes 1572864 | tf_op jit(solution)/shard_map/all_to_all | solution.py:59
  105.8 4.3 %collective-permute-start.17 = (f32[48,128]{1,0:T(8,128)S(1)}, f32[48,128]{1,0:T(8,128)S(1)}, u32[]{:S(2)}, u32[]{:S(2)}) collective-permute-start(f32[48,128]{1,0:T(8,128)S(1)} %reshape.89), channel_id=1, source_target_pairs={{0,4},{4,0},{1,5},{5,1},{2,6},{6,2},{3,7},{7,3},{8,12},{12,8},{9,1... | collective-permute-start | bytes 73736 | tf_op jit(solution)/shard_map/ppermute | solution.py:21
  114.8 16.5 %all-to-all-start.7 = ((f32[8,48,128]{2,1,0:T(8,128)}), f32[8,48,128]{2,1,0:T(8,128)S(1)}, u32[]{:S(2)}, u32[]{:S(2)}) async-start(f32[8,48,128]{2,1,0:T(8,128)} %broadcast_in_dim.43), calls=%async_computation.7 | async-start | bytes 393216 | tf_op jit(solution)/shard_map/all_to_all | solution.py:59
  118.2 14.3 %collective-permute-start.10 = (f32[256,384]{1,0:T(8,128)S(1)}, f32[256,384]{1,0:T(8,128)S(1)}, u32[]{:S(2)}, u32[]{:S(2)}) collective-permute-start(f32[256,384]{1,0:T(8,128)S(1)} %bitcast.73), channel_id=1, source_target_pairs={{0,4},{4,0},{1,5},{5,1},{2,6},{6,2},{3,7},{7,3},{8,12},{12,8},{9,1... | collective-permute-start | bytes 1179656 | tf_op jit(solution)/shard_map/ppermute | solution.py:21
  118.6 20.2 %collective-permute-start.8 = (f32[64,384]{1,0:T(8,128)S(1)}, f32[64,384]{1,0:T(8,128)S(1)}, u32[]{:S(2)}, u32[]{:S(2)}) collective-permute-start(f32[64,384]{1,0:T(8,128)S(1)} %pad_maximum_fusion.7), channel_id=1, source_target_pairs={{0,4},{4,0},{1,5},{5,1},{2,6},{6,2},{3,7},{7,3},{8,12},{12,8},{9,1... | collective-permute-start | bytes 294920 | tf_op jit(solution)/shard_map/ppermute | solution.py:21
  121.4 20.4 %collective-permute-start.12 = (f32[512,384]{1,0:T(8,128)S(1)}, f32[512,384]{1,0:T(8,128)S(1)}, u32[]{:S(2)}, u32[]{:S(2)}) collective-permute-start(f32[512,384]{1,0:T(8,128)S(1)} %bitcast.63), channel_id=1, source_target_pairs={{0,2},{2,0},{1,3},{3,1},{4,6},{6,4},{5,7},{7,5},{8,10},{10,8},{9,1... | collective-permute-start | bytes 2359304 | tf_op jit(solution)/shard_map/ppermute | solution.py:21
  131.9 9.1 %collective-permute-start.18 = (f32[2,128,128]{2,1,0:T(8,128)S(1)}, f32[2,128,128]{2,1,0:T(8,128)S(1)}, u32[]{:S(2)}, u32[]{:S(2)}) collective-permute-start(f32[2,128,128]{2,1,0:T(8,128)S(1)} %fusion.21), channel_id=1, source_target_pairs={{0,1},{1,0},{2,3},{3,2},{4,5},{5,4},{6,7},{7,6},{8,9},{9,8},{10,11... | collective-permute-start | bytes 393224 | tf_op jit(solution)/shard_map/ppermute | solution.py:21
  132.6 14.1 %collective-permute-start.11 = (f32[512,384]{1,0:T(8,128)S(1)}, f32[512,384]{1,0:T(8,128)S(1)}, u32[]{:S(2)}, u32[]{:S(2)}) collective-permute-start(f32[512,384]{1,0:T(8,128)S(1)} %pad_maximum_fusion.dir_own.proj_own), channel_id=1, source_target_pairs={{0,2},{2,0},{1,3},{3,1},{4,6},{6,4},{5,7},{7,5},{8,10},{10,8},{9,1... | collective-permute-start | bytes 2359304 | tf_op jit(solution)/shard_map/ppermute | solution.py:21
  138.9 12.8 %collective-permute-start.13 = (f32[128,384]{1,0:T(8,128)S(1)}, f32[128,384]{1,0:T(8,128)S(1)}, u32[]{:S(2)}, u32[]{:S(2)}) collective-permute-start(f32[128,384]{1,0:T(8,128)S(1)} %pad_maximum_fusion.4), channel_id=1, source_target_pairs={{0,8},{8,16},{16,24},{24,0},{1,9},{9,17},{17,25},{25,1},{2,10},{10... | collective-permute-start | bytes 589832 | tf_op jit(solution)/shard_map/ppermute | solution.py:53
  139.2 12.4 %collective-permute-start.14 = (f32[128,384]{1,0:T(8,128)S(1)}, f32[128,384]{1,0:T(8,128)S(1)}, u32[]{:S(2)}, u32[]{:S(2)}) collective-permute-start(f32[128,384]{1,0:T(8,128)S(1)} %pad_maximum_fusion.4), channel_id=1, source_target_pairs={{0,16},{8,24},{16,0},{24,8},{1,17},{9,25},{17,1},{25,9},{2,18},{10... | collective-permute-start | bytes 589832 | tf_op jit(solution)/shard_map/ppermute | solution.py:53
  141.0 10.7 %collective-permute-start.15 = (f32[128,384]{1,0:T(8,128)S(1)}, f32[128,384]{1,0:T(8,128)S(1)}, u32[]{:S(2)}, u32[]{:S(2)}) collective-permute-start(f32[128,384]{1,0:T(8,128)S(1)} %pad_maximum_fusion.4), channel_id=1, source_target_pairs={{0,24},{8,0},{16,8},{24,16},{1,25},{9,1},{17,9},{25,17},{2,26},{10... | collective-permute-start | bytes 589832 | tf_op jit(solution)/shard_map/ppermute | solution.py:53
  151.7 5.5 %collective-permute-start.16 = (f32[512,384]{1,0:T(8,128)S(1)}, f32[512,384]{1,0:T(8,128)S(1)}, u32[]{:S(2)}, u32[]{:S(2)}) collective-permute-start(f32[512,384]{1,0:T(8,128)S(1)} %bitcast.60), channel_id=1, source_target_pairs={{0,2},{2,0},{1,3},{3,1},{4,6},{6,4},{5,7},{7,5},{8,10},{10,8},{9,1... | collective-permute-start | bytes 2359304 | tf_op jit(solution)/shard_map/ppermute | solution.py:21
  154.7 1.8 %collective-permute-start.19 = (f32[2,192,128]{2,1,0:T(8,128)S(1)}, f32[2,192,128]{2,1,0:T(8,128)S(1)}, u32[]{:S(2)}, u32[]{:S(2)}) collective-permute-start(f32[2,192,128]{2,1,0:T(8,128)S(1)} %fusion), channel_id=1, source_target_pairs={{0,2},{2,0},{1,3},{3,1},{4,6},{6,4},{5,7},{7,5},{8,10},{10,8},{9,1... | collective-permute-start | bytes 589832 | tf_op jit(solution)/shard_map/ppermute | solution.py:21

commit v4 on v3

v4 whole, which is shorter than its diff:
```python
import jax
import jax.numpy as jnp
from jax import lax
from jax.experimental import pallas as pl
from jax.experimental.pallas import tpu as pltpu
from jax.sharding import Mesh, PartitionSpec as P

ADAM_STEP = 100
HIGH = lax.Precision.HIGHEST

SIZES = {"z": 8, "y": 4, "xh": 2, "core": 2, "xl": 2}
REP = ("z", "y", "xh", "core")
ORDERS = (("y", "xh"), ("xh", "y"), ("y", "xh"))
CHUNKS = len(ORDERS)
TOGETHER = (0, 2, 1)


def flip(x, axis, bit=1):
    n = SIZES[axis]
    return lax.ppermute(x, axis, [(i, i ^ bit) for i in range(n)])


def rows(x, index, count):
    return lax.dynamic_slice_in_dim(x, index * count, count, 0)


def in_order(index, mine, other):
    first = index == 0
    return jnp.where(first, mine, other), jnp.where(first, other, mine)


def after(x, *others):
    return lax.optimization_barrier((x, *others))[0]


def scatter(parts, axis):
    n = SIZES[axis]
    total = parts[0]
    for k in range(1, n):
        total = total + lax.ppermute(parts[k], axis, [(i, (i + k) % n) for i in range(n)])
    return total


def blocks(x, axis):
    n, me = SIZES[axis], lax.axis_index(axis)
    return [rows(x, (me + k) % n, x.shape[0] // n) for k in range(n)]


def gather(x, axis, own=None):
    n, me = SIZES[axis], lax.axis_index(axis)
    own = x if own is None else own
    if n == 2:
        return jnp.stack(in_order(me, own, flip(x, axis)))
    return settle(own, around(x, axis), axis)


def around(x, axis):
    n = SIZES[axis]
    return [lax.ppermute(x, axis, [(i, (i + k) % n) for i in range(n)]) for k in range(1, n)]


def settle(own, moved, axis):
    n, me = SIZES[axis], lax.axis_index(axis)
    out = jnp.zeros((n,) + own.shape, own.dtype)
    for k, block in enumerate([own] + moved):
        out = lax.dynamic_update_slice_in_dim(out, block[None], (me - k) % n, 0)
    return out


def exchange(parts, axis):
    return lax.all_to_all(parts, axis, split_axis=0, concat_axis=0)


def copies(x, axis):
    return jnp.broadcast_to(x, (SIZES[axis],) + x.shape)


def pair_kernel(where, grad, given, *outs):
    step = pl.program_id(0)
    both = grad[...] + given[...]
    both = both.reshape(-1, both.shape[2]).T
    for k, out in enumerate(outs):

        @pl.when(step == k)
        def _():
            out[...] = both


def pair_sum(chunk, core, axis, grad, given):
    half, depth, some = given.shape
    n = SIZES[axis]
    lanes = some // n
    out = jax.ShapeDtypeStruct((lanes, half * depth), grad.dtype)
    return pl.pallas_call(
        pair_kernel,
        grid_spec=pltpu.PrefetchScalarGridSpec(
            num_scalar_prefetch=1,
            grid=(n,),
            in_specs=[
                pl.BlockSpec((half, depth, lanes), lambda k, w: (w[0], 0, chunk * n + (w[1] + k) % n)),
                pl.BlockSpec((half, depth, lanes), lambda k, w: (0, 0, (w[1] + k) % n)),
            ],
            out_specs=[pl.BlockSpec(out.shape, lambda k, w: (0, 0))] * n,
        ),
        out_shape=[out] * n,
        compiler_params=pltpu.CompilerParams(vmem_limit_bytes=12 << 20),
        cost_estimate=pl.CostEstimate(flops=given.size, bytes_accessed=12 * given.size, transcendentals=0),
        name="pair_sum",
    )(jnp.stack([core, lax.axis_index(axis)]), grad, given)


def finish_kernel(core, own, other, basis, weights, first, second, *rest):
    out_weights, out_first, out_second = rest[-3:]
    layer = pl.program_id(1)
    rank = basis.shape[2]
    here = core[0] == layer // 2
    some = out_weights.shape[2]
    x = jnp.where(here, own[...].reshape(some, -1), other[...].reshape(some, -1))
    direction = jnp.where(layer % 2 == 0, x[:, :rank], x[:, rank : 2 * rank])
    update = lax.dot_general(
        basis[0], direction, (((1,), (1,)), ((), ())), precision=HIGH, preferred_element_type=jnp.float32
    )
    out_weights[0] = weights[0] - 0.0125 * update
    proj = x[:, 2 * rank :].T
    proj = jnp.where(layer % 2 == 0, proj[: rank // 2], proj[rank // 2 :])
    out_first[0] = 0.9 * first[0] + 0.1 * proj
    out_second[0] = 0.999 * second[0] + 0.001 * proj * proj


def finish(chunks, core, own, other, basis, weights, first, second, before):
    layers, depth, width = weights.shape
    rank, some = basis.shape[2], width // CHUNKS
    gap = chunks[-1] - chunks[0]
    small = own.shape[2]
    packed = pl.BlockSpec((own.shape[0], 1, small, own.shape[3]), lambda h, l, c: (0, h, 0, 0))
    whole = pl.BlockSpec((1, depth, rank), lambda h, l, c: (l, 0, 0))
    tall = pl.BlockSpec((1, depth, some), lambda h, l, c: (l, 0, chunks[0] + gap * h))
    low = pl.BlockSpec((1, first.shape[1], some), lambda h, l, c: (l, 0, chunks[0] + gap * h))
    kept = [] if before is None else list(before)
    return pl.pallas_call(
        finish_kernel,
        grid_spec=pltpu.PrefetchScalarGridSpec(
            num_scalar_prefetch=1,
            grid=(len(chunks), layers),
            in_specs=[packed, packed, whole, tall, low, low] + [pl.BlockSpec(memory_space=pl.ANY)] * len(kept),
            out_specs=[tall, low, low],
        ),
        out_shape=[jax.ShapeDtypeStruct(a.shape, a.dtype) for a in (weights, first, second)],
        input_output_aliases={7 + i: i for i in range(len(kept))},
        compiler_params=pltpu.CompilerParams(vmem_limit_bytes=20 << 20),
        cost_estimate=pl.CostEstimate(
            flops=12 * layers * depth * rank * some * len(chunks),
            bytes_accessed=8 * layers * (depth + rank) * some * len(chunks),
            transcendentals=0,
        ),
        name="finish",
    )(core.reshape(1), own, other, basis, weights, first, second, *kept)


def on_device(grads, basis, weights, first_moment, second_moment):
    layers, depth, width = grads.shape[1:]
    rank = basis.shape[2]
    half = layers // 2
    some = width // CHUNKS
    small = some // 64
    z, y, xh = lax.axis_index("z"), lax.axis_index("y"), lax.axis_index("xh")
    core, xl = lax.axis_index("core"), lax.axis_index("xl")
    grad = grads[0]
    kept = pltpu.with_memory_space_constraint(grad, pltpu.HBM)

    given = []
    for chunk in range(CHUNKS):
        if given:
            grad = after(grad, given[-1])
        given.append(lax.dynamic_slice(grad, ((1 - core) * half, 0, chunk * some), (half, depth, some)))
    given = [flip(g, "core") for g in given]
    sent = [list(pair_sum(chunk, core, order[0], kept, given[chunk])) for chunk, order in enumerate(ORDERS)]
    last = sent[-1]
    nearby = [pltpu.with_memory_space_constraint(a, pltpu.HBM) for a in (weights, first_moment, second_moment)]
    for stage in (0, 1):
        sums = []
        for parts, order in zip(sent, ORDERS):
            summed = scatter([after(parts[0], *last)] + parts[1:], order[stage])
            if stage == 0:
                summed = blocks(summed, order[1])
                last = summed
            sums.append(summed)
        sent = sums
    pieces, places = [], []
    for chunk in TOGETHER:
        order = ORDERS[chunk]
        pieces.append(sent[chunk].reshape(SIZES["z"], small, half * depth))
        index = {"y": y, "xh": xh}
        place = (index[order[0]] * SIZES[order[1]] + index[order[1]]) * SIZES["z"] + z
        places.append(chunk * some + place * small)
    total = jnp.sum(exchange(jnp.concatenate(pieces, axis=1), "z"), axis=0)
    total = total.reshape(CHUNKS * small, half, depth)

    basis_pair = rows(basis, core, half)
    cut = []
    for moment in (first_moment, second_moment):
        mine = [lax.dynamic_slice(moment, (core * half, 0, at), (half, rank // 2, small)) for at in places]
        cut.append(jnp.swapaxes(jnp.concatenate(mine, axis=2), 1, 2))
    cut = jnp.concatenate(cut, axis=2)
    low, high = in_order(xl, cut, flip(cut, "xl"))
    first = jnp.concatenate([low[:, :, : rank // 2], high[:, :, : rank // 2]], axis=2)
    second = jnp.concatenate([low[:, :, rank // 2 :], high[:, :, rank // 2 :]], axis=2)

    proj = jnp.einsum("fld,ldr->lfr", total, basis_pair, precision=HIGH)
    proj = proj + flip(proj, "xl")
    new_first = 0.9 * first + 0.1 * proj
    new_second = 0.999 * second + 0.001 * proj * proj
    direction = (
        new_first
        / (1.0 - 0.9**ADAM_STEP)
        / (jnp.sqrt(new_second / (1.0 - 0.999**ADAM_STEP)) + 1e-08)
    )
    mine = jnp.where(xl == 0, proj[:, :, : rank // 2], proj[:, :, rank // 2 :])
    packed = jnp.concatenate([direction[0], direction[1], mine[0], mine[1]], axis=1)

    refresh = jnp.einsum("fld,lfr->ldr", total, proj, precision=HIGH)
    refresh = refresh.reshape(SIZES["z"], 3, -1, rank)
    refresh = jnp.concatenate([refresh[:, i] for i in range(3)], axis=2)
    both = exchange(jnp.concatenate([copies(packed, "z"), refresh], axis=1), "z")
    large = both[:, : 2 * small].reshape(-1, 3 * rank)
    little = both[:, 2 * small : 3 * small].reshape(-1, 3 * rank)
    part = jnp.sum(both[:, 3 * small :], axis=0)

    little = jnp.concatenate([little, part])
    large = gather(large, "xh").reshape(-1, 3 * rank)
    moved = around(large, "y")
    little = settle(after(little, large), around(little, "y"), "y")
    part = jnp.sum(little[:, -part.shape[0] :], axis=0)
    little = little[:, : -part.shape[0]].reshape(-1, 3 * rank)
    part = part + flip(part, "xh")
    large = settle(large, moved, "y").reshape(-1, 2, small, 3 * rank)
    little = gather(little, "xh", after(little, large)).reshape(-1, 1, small, 3 * rank)
    done = finish((0, 2), core, large, flip(large, "core"), basis, *nearby, None)
    done = finish((1,), core, little, flip(little, "core"), basis, *nearby, done)
    new_weights, new_first, new_second = done

    refresh = after(exchange(copies(part, "z"), "z"), large)
    refresh = jnp.stack([refresh[:, :, i * rank : (i + 1) * rank] for i in range(3)], axis=1)
    refresh = refresh.reshape(half, depth, rank)
    gram = jnp.einsum("ldr,lds->lrs", refresh, refresh, precision=HIGH)
    gram = gram + flip(gram, "xl")
    sumsq = jnp.einsum("lrr->l", gram)
    factor = jnp.sqrt(jnp.float32(rank)) / (2.0 * jnp.sqrt(sumsq + 1e-06))
    scaled = refresh * factor[:, None, None]
    gram_scaled = gram * (factor * factor)[:, None, None]
    basis_new = 1.5 * scaled - 0.5 * jnp.einsum("ldr,lrs->lds", scaled, gram_scaled, precision=HIGH)
    new_basis = jnp.concatenate(in_order(core, basis_new, flip(basis_new, "core")), axis=0)
    return (new_weights, new_first, new_second, new_basis)


def solution(mesh):
    fine = Mesh(mesh.devices.reshape(8, 4, 2, 2, 2), ("z", "y", "xh", "core", "xl"))
    split = P(None, "xl", None)
    return jax.shard_map(
        on_device,
        mesh=fine,
        in_specs=(P(REP, None, "xl", None), split, split, split, split),
        out_specs=(split, split, split, split),
        check_vma=False,
    )
```

time: 163 us -> 154 us (0.945)
  blocking collectives: 14.3 us -> 0 us
  local copies, waits for them, and re-layouts: 9.03 us -> 13.1 us
  waiting for transfers between devices: 44.7 us -> 40.7 us
  other arithmetic: 4.54 us -> 8.53 us
    ppermute x3 -> x18, starting transfers between devices: 2.86 us -> 24 us  [the longest x12 14 us: scatter(): lax.ppermute(parts[k], axis, [(i, (i + k) % n) for i in range(n)])]
    all_to_all x7 -> x3, waiting for transfers between devices: 35.9 us -> 18.4 us  [exchange(): return lax.all_to_all(parts, axis, split_axis=0, concat_axis=0)]
    ppermute x3 -> x18, waiting for transfers between devices: 0.01 us -> 14.4 us  [the longest x6 7.72 us: around(): lax.ppermute(x, axis, [(i, (i + k) % n) for i in range(n)])]
    all_to_all x1 -> x0, blocking collectives: 14.3 us -> none  [exchange(): return lax.all_to_all(parts, axis, split_axis=0, concat_axis=0)]
    all_to_all x7 -> x3, starting transfers between devices: 27.3 us -> 15.1 us  [exchange(): return lax.all_to_all(parts, axis, split_axis=0, concat_axis=0)]
    ppermute x17 -> x12, starting transfers between devices: 36.3 us -> 25.9 us  [flip(): return lax.ppermute(x, axis, [(i, i ^ bit) for i in range(n)])]
    dynamic_update_slice x4 -> x8, local copies, waits for them, and re-layouts: 0.08 us -> 3.17 us  [settle(): out = lax.dynamic_update_slice_in_dim(out, block[None], (me - k) % n, 0)]
    pallas_call x3, Pallas kernels: 5.58 us -> 8 us  [pair_sum(): pl.pallas_call(pair_kernel, grid_spec=pltpu.PrefetchScalarGridSpec(num_sc...]
  transfers between devices with their start and end apart: 27 -> 33, of which waited for: 10 -> 12; matrix products, arithmetic and copies ran while one was open for 6% -> 13% of each run, Pallas kernels for 9% -> 11%
where the time goes in v4:
time: 154 us; the launch traced here: 153 us
  starting transfers between devices  64.9 us (42%)
  waiting for transfers between devices  40.7 us (26%)
  Pallas kernels  21.6 us (14%)
  local copies, waits for them, and re-layouts  13.1 us (9%)
  other arithmetic  8.53 us (6%)
  matrix products  2.52 us (2%)
    ppermute x12, starting transfers between devices, flip(): return lax.ppermute(x, axis, [(i, i ^ bit) for i in range(n)])  25.9 us
    all_to_all x3, waiting for transfers between devices, exchange(): return lax.all_to_all(parts, axis, split_axis=0, concat_axis=0)  18.4 us
    all_to_all x3, starting transfers between devices, exchange(): return lax.all_to_all(parts, axis, split_axis=0, concat_axis=0)  15.1 us
    ppermute x12, starting transfers between devices, scatter(): lax.ppermute(parts[k], axis, [(i, (i + k) % n) for i in range(n)])  14 us
    pallas_call x2, Pallas kernels, finish(): pl.pallas_call(finish_kernel, grid_spec=pltpu.PrefetchScalarGridSpec(num_...  13.6 us
    ppermute x6, starting transfers between devices, around(): lax.ppermute(x, axis, [(i, (i + k) % n) for i in range(n)])  9.98 us
    pallas_call x3, Pallas kernels, pair_sum(): pl.pallas_call(pair_kernel, grid_spec=pltpu.PrefetchScalarGridSpec(num_sc...  8 us
    ppermute x12, waiting for transfers between devices, flip(): return lax.ppermute(x, axis, [(i, i ^ bit) for i in range(n)])  7.98 us
  transfers between devices with their start and end apart: 33, of which 12 were waited for; matrix products, arithmetic and copies ran while one was open for 13% of the time, Pallas kernels for 11%

profile of v4, /device:TPU:1, one launch (start us, length us, event | category | flops | bytes accessed | tf_op | source)
XLA Modules:
  0.0 152.6 jit_solution(17240932875939667154)
XLA Ops:
  0.6 1.2 dynamic-slice_bitcast_fusion
  1.8 3.3 %collective-permute-start.1 = (f32[2,192,512]{2,1,0:T(8,128)S(1)}, f32[2,192,512]{2,1,0:T(8,128)S(1)}, u32[]{:S(2)}, u32[]{:S(2)}) collective-permute-start(f32[2,192,512]{2,1,0:T(8,128)S(1)} %dynamic-slice_bitcast_fusion), channel_id=1, source_target_pairs={{0,2},{2,0},{1,3},{3,1},{4,6},{6,4},{5,7},{7,5},{8,10},{10,8},{9,1... | collective-permute-start | bytes 2359304 | tf_op jit(solution)/shard_map/ppermute | solution.py:20
  5.2 2.1 %constant_dynamic-slice_fusion.9 = f32[2,192,512]{2,1,0:T(8,128)} fusion(f32[4,192,1536]{2,1,0:T(8,128)} %bitcast.87, s32[]{:T(128)S(6)} %select_n.182), kind=kLoop, calls=%fused_computation.80 | loop fusion | bytes 1572868 | tf_op jit(solution)/shard_map/dynamic_slice | solution.py:175
  7.2 2.1 %constant_dynamic-slice_fusion.8 = f32[2,192,512]{2,1,0:T(8,128)} fusion(f32[4,192,1536]{2,1,0:T(8,128)} %bitcast.88, s32[]{:T(128)S(6)} %select_n.182), kind=kLoop, calls=%fused_computation.79 | loop fusion | bytes 1572868 | tf_op jit(solution)/shard_map/dynamic_slice | solution.py:175
  9.3 0.5 collective-permute-start.2
  9.8 1.2 constant_dynamic-slice_fusion.12
  11.0 0.7 copy.37
  11.8 0.7 copy.35
  12.5 0.7 copy.34
  13.2 1.3 maximum_bitcast_fusion.1
  14.6 3.0 %pair_sum.3 = (f32[128,384]{1,0:T(8,128)S(1)}, f32[128,384]{1,0:T(8,128)S(1)}, f32[128,384]{1,0:T(8,128)S(1)}, f32[128,384]{1,0:T(8,128)S(1)}) custom-call(s32[2]{0:T(128)S(1)} %pad_add_fusion.where, f32[4,192,1536]{2,1,0:T(8,128)} %bitcast.89, f32[2,192,512]{2,1,0:T(8,128)S(1)} %collective-permute-done.1.given), custom_call_target="tpu_custom_call" | custom-call | flops 196608 | bytes 2359296 | tf_op jit(solution)/shard_map/pair_sum/pallas_call | solution.py:94
  17.7 2.2 %collective-permute-start.4 = (f32[128,384]{1,0:T(8,128)S(1)}, f32[128,384]{1,0:T(8,128)}, u32[]{:S(2)}, u32[]{:S(2)}) collective-permute-start(f32[128,384]{1,0:T(8,128)S(1)} %get-tuple-element.40), channel_id=1, source_target_pairs={{0,16},{8,24},{16,0},{24,8},{1,17},{9,25},{17,1},{25,9},{2,18},{10... | collective-permute-start | bytes 589832 | tf_op jit(solution)/shard_map/ppermute | solution.py:40
  19.8 1.1 collective-permute-start.5
  21.0 2.0 %pair_sum.5 = (f32[256,384]{1,0:T(8,128)S(1)}, f32[256,384]{1,0:T(8,128)S(1)}) custom-call(s32[2]{0:T(128)S(1)} %pad_add_fusion.1.where, f32[4,192,1536]{2,1,0:T(8,128)} %bitcast.90, f32[2,192,512]{2,1,0:T(8,128)S(1)} %collective-permute-done.6.given), custom_call_target="tpu_custom_call" | custom-call | flops 196608 | bytes 2359296 | tf_op jit(solution)/shard_map/pair_sum/pallas_call | solution.py:94
  23.0 2.8 %collective-permute-start.7 = (f32[256,384]{1,0:T(8,128)S(1)}, f32[256,384]{1,0:T(8,128)}, u32[]{:S(2)}, u32[]{:S(2)}) collective-permute-start(f32[256,384]{1,0:T(8,128)S(1)} %get-tuple-element.44), channel_id=1, source_target_pairs={{0,4},{4,0},{1,5},{5,1},{2,6},{6,2},{3,7},{7,3},{8,12},{12,8},{9,1... | collective-permute-start | bytes 1179656 | tf_op jit(solution)/shard_map/ppermute | solution.py:40
  25.8 0.6 maximum_bitcast_fusion
  26.4 3.0 %pair_sum.4 = (f32[128,384]{1,0:T(8,128)S(1)}, f32[128,384]{1,0:T(8,128)S(1)}, f32[128,384]{1,0:T(8,128)S(1)}, f32[128,384]{1,0:T(8,128)S(1)}) custom-call(s32[2]{0:T(128)S(1)} %pad_add_fusion.where, f32[4,192,1536]{2,1,0:T(8,128)} %bitcast.91, f32[2,192,512]{2,1,0:T(8,128)S(1)} %collective-permute-done.2.given), custom_call_target="tpu_custom_call" | custom-call | flops 196608 | bytes 2359296 | tf_op jit(solution)/shard_map/pair_sum/pallas_call | solution.py:94
  29.4 0.5 collective-permute-start.8
  29.9 0.8 collective-permute-start.9
  30.7 1.7 %collective-permute-start.10 = (f32[128,384]{1,0:T(8,128)S(1)}, f32[128,384]{1,0:T(8,128)S(1)}, u32[]{:S(2)}, u32[]{:S(2)}) collective-permute-start(f32[128,384]{1,0:T(8,128)S(1)} %get-tuple-element.37), channel_id=1, source_target_pairs={{0,24},{8,0},{16,8},{24,16},{1,25},{9,1},{17,9},{25,17},{2,26},{10... | collective-permute-start | bytes 589832 | tf_op jit(solution)/shard_map/ppermute | solution.py:40
  32.4 1.2 add_add_fusion.1
  33.6 1.3 collective-permute-start.11
  34.9 1.0 add.223
  36.1 1.3 collective-permute-done.8
  37.4 1.3 collective-permute-start.15
  39.1 1.8 %collective-permute-start.14 = (f32[64,384]{1,0:T(8,128)S(1)}, f32[64,384]{1,0:T(8,128)S(1)}, u32[]{:S(2)}, u32[]{:S(2)}) collective-permute-start(f32[64,384]{1,0:T(8,128)S(1)} %get-tuple-element.80), channel_id=1, source_target_pairs={{0,16},{8,24},{16,0},{24,8},{1,17},{9,25},{17,1},{25,9},{2,18},{10... | collective-permute-start | bytes 294920 | tf_op jit(solution)/shard_map/ppermute | solution.py:40
  41.7 4.7 %collective-permute-done.12 = f32[64,384]{1,0:T(8,128)S(1)} collective-permute-done((f32[64,384]{1,0:T(8,128)S(1)}, f32[64,384]{1,0:T(8,128)S(1)}, u32[]{:S(2)}, u32[]{:S(2)}) %collective-permute-start.12) | collective-permute-done | bytes 98336 | tf_op jit(solution)/shard_map/ppermute | solution.py:40
  46.4 0.7 pad_maximum_fusion.3
  47.2 8.2 %all-to-all-start = ((f32[8,24,384]{2,1,0:T(8,128)}), f32[8,24,384]{2,1,0:T(8,128)S(1)}, u32[]{:S(2)}, u32[]{:S(2)}) async-start(f32[8,24,384]{2,1,0:T(8,128)} %pad_maximum_fusion.3), calls=%async_computation | async-start | bytes 589824 | tf_op jit(solution)/shard_map/all_to_all | solution.py:71
  55.5 0.5 collective-permute-start
  56.0 2.4 %collective-permute-done = f32[2,24,128]{2,1,0:T(8,128)S(1)} collective-permute-done((f32[2,24,128]{2,1,0:T(8,128)S(1)}, f32[2,24,128]{2,1,0:T(8,128)S(1)}, u32[]{:S(2)}, u32[]{:S(2)}) %collective-permute-start) | collective-permute-done | bytes 24608 | tf_op jit(solution)/shard_map/ppermute | solution.py:20
  58.5 6.7 %all-to-all-done = f32[8,24,384]{2,1,0:T(8,128)S(1)} async-done(((f32[8,24,384]{2,1,0:T(8,128)}), f32[8,24,384]{2,1,0:T(8,128)S(1)}, u32[]{:S(2)}, u32[]{:S(2)}) %all-to-all-start) | async-done | bytes 294944 | tf_op jit(solution)/shard_map/all_to_all | solution.py:71
  66.0 2.3 %collective-permute-done.16 = f32[2,24,128]{2,1,0:T(8,128)S(1)} collective-permute-done((f32[2,24,128]{2,1,0:T(8,128)S(1)}, f32[2,24,128]{2,1,0:T(8,128)S(1)}, u32[]{:S(2)}, u32[]{:S(2)}) %collective-permute-start.16) | collective-permute-done | bytes 24608 | tf_op jit(solution)/shard_map/ppermute | solution.py:20
  68.5 0.5 fusion.7
  69.2 0.8 maximum_maximum_fusion
  70.0 3.5 %all-to-all-start.1 = ((f32[8,40,384]{2,1,0:T(8,128)}), f32[8,40,384]{2,1,0:T(8,128)S(1)}, u32[]{:S(2)}, u32[]{:S(2)}) async-start(f32[8,40,384]{2,1,0:T(8,128)} %maximum_maximum_fusion), calls=%async_computation.1 | async-start | bytes 983040 | tf_op jit(solution)/shard_map/all_to_all | solution.py:71
  73.6 11.7 %all-to-all-done.1 = f32[8,40,384]{2,1,0:T(8,128)S(1)} async-done(((f32[8,40,384]{2,1,0:T(8,128)}), f32[8,40,384]{2,1,0:T(8,128)S(1)}, u32[]{:S(2)}, u32[]{:S(2)}) %all-to-all-start.1) | async-done | bytes 491552 | tf_op jit(solution)/shard_map/all_to_all | solution.py:71
  85.3 0.9 collective-permute-start.17
  86.2 4.0 %collective-permute-start.20 = (f32[80,384]{1,0:T(8,128)S(1)}, f32[80,384]{1,0:T(8,128)S(1)}, u32[]{:S(2)}, u32[]{:S(2)}) collective-permute-start(f32[80,384]{1,0:T(8,128)S(1)} %pad_maximum_fusion.5), channel_id=1, source_target_pairs={{0,24},{8,0},{16,8},{24,16},{1,25},{9,1},{17,9},{25,17},{2,26},{10... | collective-permute-start | bytes 368648 | tf_op jit(solution)/shard_map/ppermute | solution.py:59
  90.2 0.7 collective-permute-start.18
  90.9 0.8 collective-permute-done.17
  91.8 1.6 %collective-permute-start.22 = (f32[256,384]{1,0:T(8,128)S(1)}, f32[256,384]{1,0:T(8,128)}, u32[]{:S(2)}, u32[]{:S(2)}) collective-permute-start(f32[256,384]{1,0:T(8,128)S(1)} %bitcast.96), channel_id=1, source_target_pairs={{0,16},{8,24},{16,0},{24,8},{1,17},{9,25},{17,1},{25,9},{2,18},{10... | collective-permute-start | bytes 1179656 | tf_op jit(solution)/shard_map/ppermute | solution.py:59
  93.3 3.0 %collective-permute-start.21 = (f32[256,384]{1,0:T(8,128)S(1)}, f32[256,384]{1,0:T(8,128)}, u32[]{:S(2)}, u32[]{:S(2)}) collective-permute-start(f32[256,384]{1,0:T(8,128)S(1)} %bitcast.97), channel_id=1, source_target_pairs={{0,8},{8,16},{16,24},{24,0},{1,9},{9,17},{17,25},{25,1},{2,10},{10... | collective-permute-start | bytes 1179656 | tf_op jit(solution)/shard_map/ppermute | solution.py:59
  96.6 0.7 collective-permute-start.23
  97.3 2.2 %collective-permute-start.27 = (f32[16,384]{1,0:T(8,128)S(1)}, f32[16,384]{1,0:T(8,128)S(1)}, u32[]{:S(2)}, u32[]{:S(2)}) collective-permute-start(f32[16,384]{1,0:T(8,128)S(1)} %slice_reduce_fusion.1), channel_id=1, source_target_pairs={{0,4},{4,0},{1,5},{5,1},{2,6},{6,2},{3,7},{7,3},{8,12},{12,8},{9,1... | collective-permute-start | bytes 73736 | tf_op jit(solution)/shard_map/ppermute | solution.py:20
  99.5 0.8 collective-permute-start.24
  100.4 1.1 collective-permute-done.27
  101.5 0.7 broadcast_in_dim.51
  102.2 3.4 %all-to-all-start.2 = ((f32[8,16,384]{2,1,0:T(8,128)}), f32[8,16,384]{2,1,0:T(8,128)S(1)}, u32[]{:S(2)}, u32[]{:S(2)}) async-start(f32[8,16,384]{2,1,0:T(8,128)} %broadcast_in_dim.51), calls=%async_computation.2 | async-start | bytes 393216 | tf_op jit(solution)/shard_map/all_to_all | solution.py:71
  105.6 7.7 %collective-permute-done.21 = f32[256,384]{1,0:T(8,128)} collective-permute-done((f32[256,384]{1,0:T(8,128)S(1)}, f32[256,384]{1,0:T(8,128)}, u32[]{:S(2)}, u32[]{:S(2)}) %collective-permute-start.21) | collective-permute-done | bytes 393248 | tf_op jit(solution)/shard_map/ppermute | solution.py:59
  113.3 1.0 bitcast_dynamic-update-slice_fusion.2
  114.3 1.0 bitcast_dynamic-update-slice_fusion.1
  115.3 1.0 bitcast_dynamic-update-slice_fusion
  116.4 5.9 %collective-permute-start.26 = (f32[64,2,8,384]{3,2,1,0:T(8,128)S(1)}, f32[64,2,8,384]{3,2,1,0:T(8,128)}, u32[]{:S(2)}, u32[]{:S(2)}) collective-permute-start(f32[64,2,8,384]{3,2,1,0:T(8,128)S(1)} %bitcast.83), channel_id=1, source_target_pairs={{0,2},{2,0},{1,3},{3,1},{4,6},{6,4},{5,7},{7,5},{8,10},{10,8},{9,1... | collective-permute-start | bytes 4718600 | tf_op jit(solution)/shard_map/ppermute | solution.py:20
  122.3 0.7 fusion.22
  123.0 1.3 collective-permute-start.28
  124.4 6.8 %collective-permute-start.25 = (f32[64,1,8,384]{3,2,1,0:T(8,128)S(1)}, f32[64,1,8,384]{3,2,1,0:T(8,128)S(1)}, u32[]{:S(2)}, u32[]{:S(2)}) collective-permute-start(f32[64,1,8,384]{3,2,1,0:T(8,128)S(1)} %bitcast.85), channel_id=1, source_target_pairs={{0,2},{2,0},{1,3},{3,1},{4,6},{6,4},{5,7},{7,5},{8,10},{10,8},{9,1... | collective-permute-start | bytes 2359304 | tf_op jit(solution)/shard_map/ppermute | solution.py:20
  131.4 1.1 fusion
  132.5 3.3 %collective-permute-start.29 = (f32[2,192,128]{2,1,0:T(8,128)}, f32[2,192,128]{2,1,0:T(8,128)}, u32[]{:S(2)}, u32[]{:S(2)}) collective-permute-start(f32[2,192,128]{2,1,0:T(8,128)} %fusion), channel_id=1, source_target_pairs={{0,2},{2,0},{1,3},{3,1},{4,6},{6,4},{5,7},{7,5},{8,10},{10,8},{9,1... | collective-permute-start | bytes 589832 | tf_op jit(solution)/shard_map/ppermute | solution.py:20
  135.7 1.4 collective-permute-done.29
  137.1 1.0 broadcast_select_fusion.1
  138.2 0.8 pad_maximum_fusion.2
  139.0 8.9 %finish.2 = (f32[4,192,1536]{2,1,0:T(8,128)}, f32[4,64,1536]{2,1,0:T(8,128)}, f32[4,64,1536]{2,1,0:T(8,128)}) custom-call(s32[1]{0:T(128)} %bitcast.core, f32[64,2,8,384]{3,2,1,0:T(8,128)S(1)} %bitcast.84, f32[64,2,8,384]{3,2,1,0:T(8,128)} %collective-permute-done.26.other, f32[4,192,128]{2,1,0:T(8,128)S(1)} %copy-done, f32[4,192,1536]{2,1,0:T(8,128)} %weights.3, ...), custom_call_target="tpu_custom_call" | custom-call | flops 1207959552 | bytes 10485760 | tf_op jit(solution)/shard_map/finish/pallas_call | solution.py:140
  147.8 4.8 %finish.3 = (f32[4,192,1536]{2,1,0:T(8,128)}, f32[4,64,1536]{2,1,0:T(8,128)}, f32[4,64,1536]{2,1,0:T(8,128)}) custom-call(s32[1]{0:T(128)} %bitcast.core, f32[64,1,8,384]{3,2,1,0:T(8,128)S(1)} %bitcast.86, f32[64,1,8,384]{3,2,1,0:T(8,128)S(1)} %collective-permute-done.25.other, ...), custom_call_target="tpu_custom_call", output_to_operand_aliasing={{0}: (7, {}), {1}: (8, {}), {2}: (9, {})} | custom-call | flops 603979776 | bytes 5242880 | tf_op jit(solution)/shard_map/finish/pallas_call | solution.py:140
  (87 shorter events, 3.8 us)
Async XLA Ops:
  1.8 12.7 %collective-permute-start.1 = (f32[2,192,512]{2,1,0:T(8,128)S(1)}, f32[2,192,512]{2,1,0:T(8,128)S(1)}, u32[]{:S(2)}, u32[]{:S(2)}) collective-permute-start(f32[2,192,512]{2,1,0:T(8,128)S(1)} %dynamic-slice_bitcast_fusion), channel_id=1, source_target_pairs={{0,2},{2,0},{1,3},{3,1},{4,6},{6,4},{5,7},{7,5},{8,10},{10,8},{9,1... | collective-permute-start | bytes 2359304 | tf_op jit(solution)/shard_map/ppermute | solution.py:20
  7.2 13.8 %collective-permute-start.6 = (f32[2,192,512]{2,1,0:T(8,128)}, f32[2,192,512]{2,1,0:T(8,128)S(1)}, u32[]{:S(2)}, u32[]{:S(2)}) collective-permute-start(f32[2,192,512]{2,1,0:T(8,128)} %constant_dynamic-slice_fusion.9), channel_id=1, source_target_pairs={{0,2},{2,0},{1,3},{3,1},{4,6},{6,4},{5,7},{7,5},{8,10},{10,8},{9,1... | collective-permute-start | bytes 2359304 | tf_op jit(solution)/shard_map/ppermute | solution.py:20
  9.3 17.1 %collective-permute-start.2 = (f32[2,192,512]{2,1,0:T(8,128)}, f32[2,192,512]{2,1,0:T(8,128)S(1)}, u32[]{:S(2)}, u32[]{:S(2)}) collective-permute-start(f32[2,192,512]{2,1,0:T(8,128)} %constant_dynamic-slice_fusion.8), channel_id=1, source_target_pairs={{0,2},{2,0},{1,3},{3,1},{4,6},{6,4},{5,7},{7,5},{8,10},{10,8},{9,1... | collective-permute-start | bytes 2359304 | tf_op jit(solution)/shard_map/ppermute | solution.py:20
  17.6 12.4 %collective-permute-start.3 = (f32[128,384]{1,0:T(8,128)S(1)}, f32[128,384]{1,0:T(8,128)}, u32[]{:S(2)}, u32[]{:S(2)}) collective-permute-start(f32[128,384]{1,0:T(8,128)S(1)} %get-tuple-element.39), channel_id=1, source_target_pairs={{0,8},{8,16},{16,24},{24,0},{1,9},{9,17},{17,25},{25,1},{2,10},{10... | collective-permute-start | bytes 589832 | tf_op jit(solution)/shard_map/ppermute | solution.py:40
  17.7 13.1 %collective-permute-start.4 = (f32[128,384]{1,0:T(8,128)S(1)}, f32[128,384]{1,0:T(8,128)}, u32[]{:S(2)}, u32[]{:S(2)}) collective-permute-start(f32[128,384]{1,0:T(8,128)S(1)} %get-tuple-element.40), channel_id=1, source_target_pairs={{0,16},{8,24},{16,0},{24,8},{1,17},{9,25},{17,1},{25,9},{2,18},{10... | collective-permute-start | bytes 589832 | tf_op jit(solution)/shard_map/ppermute | solution.py:40
  19.8 12.6 %collective-permute-start.5 = (f32[128,384]{1,0:T(8,128)S(1)}, f32[128,384]{1,0:T(8,128)}, u32[]{:S(2)}, u32[]{:S(2)}) collective-permute-start(f32[128,384]{1,0:T(8,128)S(1)} %get-tuple-element.41), channel_id=1, source_target_pairs={{0,24},{8,0},{16,8},{24,16},{1,25},{9,1},{17,9},{25,17},{2,26},{10... | collective-permute-start | bytes 589832 | tf_op jit(solution)/shard_map/ppermute | solution.py:40
  21.0 4.8 %copy-start.3 = (f32[2,64,8]{1,2,0:T(8,128)S(1)}, f32[2,64,8]{1,2,0:T(8,128)}, u32[]{:S(2)}) copy-start(f32[2,64,8]{1,2,0:T(8,128)} %copy.35) | copy-start | bytes 12292
  21.0 4.8 %copy-start.4 = (f32[2,64,8]{1,2,0:T(8,128)S(1)}, f32[2,64,8]{1,2,0:T(8,128)}, u32[]{:S(2)}) copy-start(f32[2,64,8]{1,2,0:T(8,128)} %copy.34) | copy-start | bytes 12292
  23.0 11.9 %collective-permute-start.7 = (f32[256,384]{1,0:T(8,128)S(1)}, f32[256,384]{1,0:T(8,128)}, u32[]{:S(2)}, u32[]{:S(2)}) collective-permute-start(f32[256,384]{1,0:T(8,128)S(1)} %get-tuple-element.44), channel_id=1, source_target_pairs={{0,4},{4,0},{1,5},{5,1},{2,6},{6,2},{3,7},{7,3},{8,12},{12,8},{9,1... | collective-permute-start | bytes 1179656 | tf_op jit(solution)/shard_map/ppermute | solution.py:40
  29.4 8.0 %collective-permute-start.8 = (f32[128,384]{1,0:T(8,128)S(1)}, f32[128,384]{1,0:T(8,128)S(1)}, u32[]{:S(2)}, u32[]{:S(2)}) collective-permute-start(f32[128,384]{1,0:T(8,128)S(1)} %get-tuple-element.35), channel_id=1, source_target_pairs={{0,8},{8,16},{16,24},{24,0},{1,9},{9,17},{17,25},{25,1},{2,10},{10... | collective-permute-start | bytes 589832 | tf_op jit(solution)/shard_map/ppermute | solution.py:40
  29.9 9.1 %collective-permute-start.9 = (f32[128,384]{1,0:T(8,128)S(1)}, f32[128,384]{1,0:T(8,128)S(1)}, u32[]{:S(2)}, u32[]{:S(2)}) collective-permute-start(f32[128,384]{1,0:T(8,128)S(1)} %get-tuple-element.36), channel_id=1, source_target_pairs={{0,16},{8,24},{16,0},{24,8},{1,17},{9,25},{17,1},{25,9},{2,18},{10... | collective-permute-start | bytes 589832 | tf_op jit(solution)/shard_map/ppermute | solution.py:40
  30.7 10.5 %collective-permute-start.10 = (f32[128,384]{1,0:T(8,128)S(1)}, f32[128,384]{1,0:T(8,128)S(1)}, u32[]{:S(2)}, u32[]{:S(2)}) collective-permute-start(f32[128,384]{1,0:T(8,128)S(1)} %get-tuple-element.37), channel_id=1, source_target_pairs={{0,24},{8,0},{16,8},{24,16},{1,25},{9,1},{17,9},{25,17},{2,26},{10... | collective-permute-start | bytes 589832 | tf_op jit(solution)/shard_map/ppermute | solution.py:40
  33.6 8.1 %collective-permute-start.11 = (f32[64,384]{1,0:T(8,128)S(1)}, f32[64,384]{1,0:T(8,128)S(1)}, u32[]{:S(2)}, u32[]{:S(2)}) collective-permute-start(f32[64,384]{1,0:T(8,128)S(1)} %get-tuple-element.90), channel_id=1, source_target_pairs={{0,4},{4,0},{1,5},{5,1},{2,6},{6,2},{3,7},{7,3},{8,12},{12,8},{9,1... | collective-permute-start | bytes 294920 | tf_op jit(solution)/shard_map/ppermute | solution.py:40
  36.0 10.4 %collective-permute-start.13 = (f32[64,384]{1,0:T(8,128)S(1)}, f32[64,384]{1,0:T(8,128)S(1)}, u32[]{:S(2)}, u32[]{:S(2)}) collective-permute-start(f32[64,384]{1,0:T(8,128)S(1)} %get-tuple-element.78), channel_id=1, source_target_pairs={{0,8},{8,16},{16,24},{24,0},{1,9},{9,17},{17,25},{25,1},{2,10},{10... | collective-permute-start | bytes 294920 | tf_op jit(solution)/shard_map/ppermute | solution.py:40
  37.4 9.0 %collective-permute-start.15 = (f32[64,384]{1,0:T(8,128)S(1)}, f32[64,384]{1,0:T(8,128)S(1)}, u32[]{:S(2)}, u32[]{:S(2)}) collective-permute-start(f32[64,384]{1,0:T(8,128)S(1)} %get-tuple-element.79), channel_id=1, source_target_pairs={{0,24},{8,0},{16,8},{24,16},{1,25},{9,1},{17,9},{25,17},{2,26},{10... | collective-permute-start | bytes 294920 | tf_op jit(solution)/shard_map/ppermute | solution.py:40
  39.1 7.3 %collective-permute-start.14 = (f32[64,384]{1,0:T(8,128)S(1)}, f32[64,384]{1,0:T(8,128)S(1)}, u32[]{:S(2)}, u32[]{:S(2)}) collective-permute-start(f32[64,384]{1,0:T(8,128)S(1)} %get-tuple-element.80), channel_id=1, source_target_pairs={{0,16},{8,24},{16,0},{24,8},{1,17},{9,25},{17,1},{25,9},{2,18},{10... | collective-permute-start | bytes 294920 | tf_op jit(solution)/shard_map/ppermute | solution.py:40
  41.2 14.1 %copy-start.1 = (f32[2,24,64]{2,1,0:T(8,128)S(1)}, f32[2,24,64]{2,1,0:T(8,128)}, u32[]{:S(2)}) copy-start(f32[2,24,64]{2,1,0:T(8,128)} %maximum_bitcast_fusion.1) | copy-start | bytes 36868
  41.2 14.1 %copy-start.2 = (f32[2,24,64]{2,1,0:T(8,128)S(1)}, f32[2,24,64]{2,1,0:T(8,128)}, u32[]{:S(2)}) copy-start(f32[2,24,64]{2,1,0:T(8,128)} %maximum_bitcast_fusion) | copy-start | bytes 36868
  41.3 24.0 %copy-start = (f32[4,192,128]{2,1,0:T(8,128)S(1)}, f32[4,192,128]{2,1,0:T(8,128)}, u32[]{:S(2)}) copy-start(f32[4,192,128]{2,1,0:T(8,128)} %basis.3) | copy-start | bytes 1179652
  41.3 5.1 %collective-permute-start.12 = (f32[64,384]{1,0:T(8,128)S(1)}, f32[64,384]{1,0:T(8,128)S(1)}, u32[]{:S(2)}, u32[]{:S(2)}) collective-permute-start(f32[64,384]{1,0:T(8,128)S(1)} %get-tuple-element.88), channel_id=1, source_target_pairs={{0,4},{4,0},{1,5},{5,1},{2,6},{6,2},{3,7},{7,3},{8,12},{12,8},{9,1... | collective-permute-start | bytes 294920 | tf_op jit(solution)/shard_map/ppermute | solution.py:40
  47.2 18.0 %all-to-all-start = ((f32[8,24,384]{2,1,0:T(8,128)}), f32[8,24,384]{2,1,0:T(8,128)S(1)}, u32[]{:S(2)}, u32[]{:S(2)}) async-start(f32[8,24,384]{2,1,0:T(8,128)} %pad_maximum_fusion.3), calls=%async_computation | async-start | bytes 589824 | tf_op jit(solution)/shard_map/all_to_all | solution.py:71
  55.5 2.9 %collective-permute-start = (f32[2,24,128]{2,1,0:T(8,128)S(1)}, f32[2,24,128]{2,1,0:T(8,128)S(1)}, u32[]{:S(2)}, u32[]{:S(2)}) collective-permute-start(f32[2,24,128]{2,1,0:T(8,128)S(1)} %pad_maximum_fusion.7), channel_id=1, source_target_pairs={{0,1},{1,0},{2,3},{3,2},{4,5},{5,4},{6,7},{7,6},{8,9},{9,8},{10,11... | collective-permute-start | bytes 73736 | tf_op jit(solution)/shard_map/ppermute | solution.py:20
  65.6 2.8 %collective-permute-start.16 = (f32[2,24,128]{2,1,0:T(8,128)S(1)}, f32[2,24,128]{2,1,0:T(8,128)S(1)}, u32[]{:S(2)}, u32[]{:S(2)}) collective-permute-start(f32[2,24,128]{2,1,0:T(8,128)S(1)} %fusion.2), channel_id=1, source_target_pairs={{0,1},{1,0},{2,3},{3,2},{4,5},{5,4},{6,7},{7,6},{8,9},{9,8},{10,11... | collective-permute-start | bytes 73736 | tf_op jit(solution)/shard_map/ppermute | solution.py:20
  70.0 15.3 %all-to-all-start.1 = ((f32[8,40,384]{2,1,0:T(8,128)}), f32[8,40,384]{2,1,0:T(8,128)S(1)}, u32[]{:S(2)}, u32[]{:S(2)}) async-start(f32[8,40,384]{2,1,0:T(8,128)} %maximum_maximum_fusion), calls=%async_computation.1 | async-start | bytes 983040 | tf_op jit(solution)/shard_map/all_to_all | solution.py:71
  85.3 6.4 %collective-permute-start.17 = (f32[128,384]{1,0:T(8,128)S(1)}, f32[128,384]{1,0:T(8,128)S(1)}, u32[]{:S(2)}, u32[]{:S(2)}) collective-permute-start(f32[128,384]{1,0:T(8,128)S(1)} %bitcast.101), channel_id=1, source_target_pairs={{0,4},{4,0},{1,5},{5,1},{2,6},{6,2},{3,7},{7,3},{8,12},{12,8},{9,1... | collective-permute-start | bytes 589832 | tf_op jit(solution)/shard_map/ppermute | solution.py:20
  86.2 10.3 %collective-permute-start.20 = (f32[80,384]{1,0:T(8,128)S(1)}, f32[80,384]{1,0:T(8,128)S(1)}, u32[]{:S(2)}, u32[]{:S(2)}) collective-permute-start(f32[80,384]{1,0:T(8,128)S(1)} %pad_maximum_fusion.5), channel_id=1, source_target_pairs={{0,24},{8,0},{16,8},{24,16},{1,25},{9,1},{17,9},{25,17},{2,26},{10... | collective-permute-start | bytes 368648 | tf_op jit(solution)/shard_map/ppermute | solution.py:59
  90.2 6.3 %collective-permute-start.19 = (f32[80,384]{1,0:T(8,128)S(1)}, f32[80,384]{1,0:T(8,128)S(1)}, u32[]{:S(2)}, u32[]{:S(2)}) collective-permute-start(f32[80,384]{1,0:T(8,128)S(1)} %pad_maximum_fusion.5), channel_id=1, source_target_pairs={{0,16},{8,24},{16,0},{24,8},{1,17},{9,25},{17,1},{25,9},{2,18},{10... | collective-permute-start | bytes 368648 | tf_op jit(solution)/shard_map/ppermute | solution.py:59
  90.2 6.3 %collective-permute-start.18 = (f32[80,384]{1,0:T(8,128)S(1)}, f32[80,384]{1,0:T(8,128)S(1)}, u32[]{:S(2)}, u32[]{:S(2)}) collective-permute-start(f32[80,384]{1,0:T(8,128)S(1)} %pad_maximum_fusion.5), channel_id=1, source_target_pairs={{0,8},{8,16},{16,24},{24,0},{1,9},{9,17},{17,25},{25,1},{2,10},{10... | collective-permute-start | bytes 368648 | tf_op jit(solution)/shard_map/ppermute | solution.py:59
  91.8 22.5 %collective-permute-start.22 = (f32[256,384]{1,0:T(8,128)S(1)}, f32[256,384]{1,0:T(8,128)}, u32[]{:S(2)}, u32[]{:S(2)}) collective-permute-start(f32[256,384]{1,0:T(8,128)S(1)} %bitcast.96), channel_id=1, source_target_pairs={{0,16},{8,24},{16,0},{24,8},{1,17},{9,25},{17,1},{25,9},{2,18},{10... | collective-permute-start | bytes 1179656 | tf_op jit(solution)/shard_map/ppermute | solution.py:59
  93.3 19.9 %collective-permute-start.21 = (f32[256,384]{1,0:T(8,128)S(1)}, f32[256,384]{1,0:T(8,128)}, u32[]{:S(2)}, u32[]{:S(2)}) collective-permute-start(f32[256,384]{1,0:T(8,128)S(1)} %bitcast.97), channel_id=1, source_target_pairs={{0,8},{8,16},{16,24},{24,0},{1,9},{9,17},{17,25},{25,1},{2,10},{10... | collective-permute-start | bytes 1179656 | tf_op jit(solution)/shard_map/ppermute | solution.py:59
  96.6 18.7 %collective-permute-start.23 = (f32[256,384]{1,0:T(8,128)S(1)}, f32[256,384]{1,0:T(8,128)}, u32[]{:S(2)}, u32[]{:S(2)}) collective-permute-start(f32[256,384]{1,0:T(8,128)S(1)} %bitcast.98), channel_id=1, source_target_pairs={{0,24},{8,0},{16,8},{24,16},{1,25},{9,1},{17,9},{25,17},{2,26},{10... | collective-permute-start | bytes 1179656 | tf_op jit(solution)/shard_map/ppermute | solution.py:59
  97.3 4.2 %collective-permute-start.27 = (f32[16,384]{1,0:T(8,128)S(1)}, f32[16,384]{1,0:T(8,128)S(1)}, u32[]{:S(2)}, u32[]{:S(2)}) collective-permute-start(f32[16,384]{1,0:T(8,128)S(1)} %slice_reduce_fusion.1), channel_id=1, source_target_pairs={{0,4},{4,0},{1,5},{5,1},{2,6},{6,2},{3,7},{7,3},{8,12},{12,8},{9,1... | collective-permute-start | bytes 73736 | tf_op jit(solution)/shard_map/ppermute | solution.py:20
  99.5 24.8 %collective-permute-start.24 = (f32[256,384]{1,0:T(8,128)S(1)}, f32[256,384]{1,0:T(8,128)S(1)}, u32[]{:S(2)}, u32[]{:S(2)}) collective-permute-start(f32[256,384]{1,0:T(8,128)S(1)} %bitcast.94), channel_id=1, source_target_pairs={{0,4},{4,0},{1,5},{5,1},{2,6},{6,2},{3,7},{7,3},{8,12},{12,8},{9,1... | collective-permute-start | bytes 1179656 | tf_op jit(solution)/shard_map/ppermute | solution.py:20
  102.2 20.1 %all-to-all-start.2 = ((f32[8,16,384]{2,1,0:T(8,128)}), f32[8,16,384]{2,1,0:T(8,128)S(1)}, u32[]{:S(2)}, u32[]{:S(2)}) async-start(f32[8,16,384]{2,1,0:T(8,128)} %broadcast_in_dim.51), calls=%async_computation.2 | async-start | bytes 393216 | tf_op jit(solution)/shard_map/all_to_all | solution.py:71
  116.4 22.6 %collective-permute-start.26 = (f32[64,2,8,384]{3,2,1,0:T(8,128)S(1)}, f32[64,2,8,384]{3,2,1,0:T(8,128)}, u32[]{:S(2)}, u32[]{:S(2)}) collective-permute-start(f32[64,2,8,384]{3,2,1,0:T(8,128)S(1)} %bitcast.83), channel_id=1, source_target_pairs={{0,2},{2,0},{1,3},{3,1},{4,6},{6,4},{5,7},{7,5},{8,10},{10,8},{9,1... | collective-permute-start | bytes 4718600 | tf_op jit(solution)/shard_map/ppermute | solution.py:20
  123.0 8.3 %collective-permute-start.28 = (f32[2,128,128]{2,1,0:T(8,128)S(1)}, f32[2,128,128]{2,1,0:T(8,128)S(1)}, u32[]{:S(2)}, u32[]{:S(2)}) collective-permute-start(f32[2,128,128]{2,1,0:T(8,128)S(1)} %fusion.22), channel_id=1, source_target_pairs={{0,1},{1,0},{2,3},{3,2},{4,5},{5,4},{6,7},{7,6},{8,9},{9,8},{10,11... | collective-permute-start | bytes 393224 | tf_op jit(solution)/shard_map/ppermute | solution.py:20
  124.4 23.4 %collective-permute-start.25 = (f32[64,1,8,384]{3,2,1,0:T(8,128)S(1)}, f32[64,1,8,384]{3,2,1,0:T(8,128)S(1)}, u32[]{:S(2)}, u32[]{:S(2)}) collective-permute-start(f32[64,1,8,384]{3,2,1,0:T(8,128)S(1)} %bitcast.85), channel_id=1, source_target_pairs={{0,2},{2,0},{1,3},{3,1},{4,6},{6,4},{5,7},{7,5},{8,10},{10,8},{9,1... | collective-permute-start | bytes 2359304 | tf_op jit(solution)/shard_map/ppermute | solution.py:20
  132.5 4.7 %collective-permute-start.29 = (f32[2,192,128]{2,1,0:T(8,128)}, f32[2,192,128]{2,1,0:T(8,128)}, u32[]{:S(2)}, u32[]{:S(2)}) collective-permute-start(f32[2,192,128]{2,1,0:T(8,128)} %fusion), channel_id=1, source_target_pairs={{0,2},{2,0},{1,3},{3,1},{4,6},{6,4},{5,7},{7,5},{8,10},{10,8},{9,1... | collective-permute-start | bytes 589832 | tf_op jit(solution)/shard_map/ppermute | solution.py:20

commit v5 on v4

--- a/solution.py
+++ b/solution.py
@@ -73,40 +73,6 @@
 
 def copies(x, axis):
     return jnp.broadcast_to(x, (SIZES[axis],) + x.shape)
-
-
-def pair_kernel(where, grad, given, *outs):
-    step = pl.program_id(0)
-    both = grad[...] + given[...]
-    both = both.reshape(-1, both.shape[2]).T
-    for k, out in enumerate(outs):
-
-        @pl.when(step == k)
-        def _():
-            out[...] = both
-
-
-def pair_sum(chunk, core, axis, grad, given):
-    half, depth, some = given.shape
-    n = SIZES[axis]
-    lanes = some // n
-    out = jax.ShapeDtypeStruct((lanes, half * depth), grad.dtype)
-    return pl.pallas_call(
-        pair_kernel,
-        grid_spec=pltpu.PrefetchScalarGridSpec(
-            num_scalar_prefetch=1,
-            grid=(n,),
-            in_specs=[
-                pl.BlockSpec((half, depth, lanes), lambda k, w: (w[0], 0, chunk * n + (w[1] + k) % n)),
-                pl.BlockSpec((half, depth, lanes), lambda k, w: (0, 0, (w[1] + k) % n)),
-            ],
-            out_specs=[pl.BlockSpec(out.shape, lambda k, w: (0, 0))] * n,
-        ),
-        out_shape=[out] * n,
-        compiler_params=pltpu.CompilerParams(vmem_limit_bytes=12 << 20),
-        cost_estimate=pl.CostEstimate(flops=given.size, bytes_accessed=12 * given.size, transcendentals=0),
-        name="pair_sum",
-    )(jnp.stack([core, lax.axis_index(axis)]), grad, given)
 
 
 def finish_kernel(core, own, other, basis, weights, first, second, *rest):
@@ -166,17 +132,20 @@
     z, y, xh = lax.axis_index("z"), lax.axis_index("y"), lax.axis_index("xh")
     core, xl = lax.axis_index("core"), lax.axis_index("xl")
     grad = grads[0]
-    kept = pltpu.with_memory_space_constraint(grad, pltpu.HBM)
-
-    given = []
-    for chunk in range(CHUNKS):
-        if given:
-            grad = after(grad, given[-1])
-        given.append(lax.dynamic_slice(grad, ((1 - core) * half, 0, chunk * some), (half, depth, some)))
-    given = [flip(g, "core") for g in given]
-    sent = [list(pair_sum(chunk, core, order[0], kept, given[chunk])) for chunk, order in enumerate(ORDERS)]
+
+    given, sent = [], []
+    for step, chunk in (("give", 0), ("give", 1), ("add", 0), ("give", 2), ("add", 1), ("add", 2)):
+        if step == "give":
+            part = lax.dynamic_slice(grad, ((1 - core) * half, 0, chunk * some), (half, depth, some))
+            grad = after(grad, part)
+            given.append(flip(part, "core"))
+        else:
+            pair = lax.dynamic_slice(grad, (core * half, 0, chunk * some), (half, depth, some)) + given[chunk]
+            sent.append(blocks(pair.reshape(half * depth, some).T, ORDERS[chunk][0]))
+            grad = after(grad, *sent[-1])
     last = sent[-1]
     nearby = [pltpu.with_memory_space_constraint(a, pltpu.HBM) for a in (weights, first_moment, second_moment)]
+    early = last
     for stage in (0, 1):
         sums = []
         for parts, order in zip(sent, ORDERS):
@@ -192,7 +161,7 @@
         pieces.append(sent[chunk].reshape(SIZES["z"], small, half * depth))
         index = {"y": y, "xh": xh}
         place = (index[order[0]] * SIZES[order[1]] + index[order[1]]) * SIZES["z"] + z
-        places.append(chunk * some + place * small)
+        places.append(after(chunk * some + place * small, *early))
     total = jnp.sum(exchange(jnp.concatenate(pieces, axis=1), "z"), axis=0)
     total = total.reshape(CHUNKS * small, half, depth)
 
@@ -228,28 +197,35 @@
 
     little = jnp.concatenate([little, part])
     large = gather(large, "xh").reshape(-1, 3 * rank)
-    moved = around(large, "y")
-    little = settle(after(little, large), around(little, "y"), "y")
+    small_y = around(little, "y")
+    across = exchange(copies(large, "y"), "y").reshape(-1, 2, small, 3 * rank)
+    little = settle(after(little, large), small_y, "y")
     part = jnp.sum(little[:, -part.shape[0] :], axis=0)
     little = little[:, : -part.shape[0]].reshape(-1, 3 * rank)
     part = part + flip(part, "xh")
-    large = settle(large, moved, "y").reshape(-1, 2, small, 3 * rank)
-    little = gather(little, "xh", after(little, large)).reshape(-1, 1, small, 3 * rank)
-    done = finish((0, 2), core, large, flip(large, "core"), basis, *nearby, None)
-    done = finish((1,), core, little, flip(little, "core"), basis, *nearby, done)
-    new_weights, new_first, new_second = done
-
-    refresh = after(exchange(copies(part, "z"), "z"), large)
+    little = gather(little, "xh", after(little, across)).reshape(-1, 1, small, 3 * rank)
+
+    refresh = part
+    for bit in range(3):
+        if bit == 2:
+            refresh = after(refresh, across)
+        refresh = jnp.concatenate(in_order((z >> bit) & 1, refresh, flip(refresh, "z", 1 << bit)))
+    refresh = refresh.reshape(SIZES["z"], -1, 3 * rank)
     refresh = jnp.stack([refresh[:, :, i * rank : (i + 1) * rank] for i in range(3)], axis=1)
     refresh = refresh.reshape(half, depth, rank)
     gram = jnp.einsum("ldr,lds->lrs", refresh, refresh, precision=HIGH)
-    gram = gram + flip(gram, "xl")
+
+    other = flip(across, "core")
+    first_done = finish((0, 2), core, after(across, gram), other, basis, *nearby, None)
+    done = finish((1,), core, little, flip(little, "core"), basis, *nearby, first_done)
+    new_weights, new_first, new_second = done
+    gram = after(gram, *first_done) + flip(gram, "xl")
     sumsq = jnp.einsum("lrr->l", gram)
     factor = jnp.sqrt(jnp.float32(rank)) / (2.0 * jnp.sqrt(sumsq + 1e-06))
     scaled = refresh * factor[:, None, None]
     gram_scaled = gram * (factor * factor)[:, None, None]
     basis_new = 1.5 * scaled - 0.5 * jnp.einsum("ldr,lrs->lds", scaled, gram_scaled, precision=HIGH)
-    new_basis = jnp.concatenate(in_order(core, basis_new, flip(basis_new, "core")), axis=0)
+    new_basis = jnp.concatenate(in_order(core, after(basis_new, *done), flip(basis_new, "core")), axis=0)
     return (new_weights, new_first, new_second, new_basis)
 
 

time: 154 us -> 144 us (0.935)
  waiting for transfers between devices: 40.7 us -> 51.3 us
  Pallas kernels: 21.6 us -> 13.3 us
  starting transfers between devices: 64.9 us -> 57.9 us
  local copies, waits for them, and re-layouts: 13.1 us -> 9.01 us
    ppermute x12 -> x15, waiting for transfers between devices: 7.98 us -> 17.1 us  [flip(): return lax.ppermute(x, axis, [(i, i ^ bit) for i in range(n)])]
    pallas_call x3 -> x0, Pallas kernels: 8 us -> none  [pair_sum(): pl.pallas_call(pair_kernel, grid_spec=pltpu.PrefetchScalarGridSpec(num_sc...]
    ppermute x6 -> x3, waiting for transfers between devices: 7.72 us -> 0.01 us  [around(): lax.ppermute(x, axis, [(i, (i + k) % n) for i in range(n)])]
    all_to_all x3, waiting for transfers between devices: 18.4 us -> 24 us  [exchange(): return lax.all_to_all(parts, axis, split_axis=0, concat_axis=0)]
    ppermute x6 -> x3, starting transfers between devices: 9.98 us -> 4.36 us  [around(): lax.ppermute(x, axis, [(i, (i + k) % n) for i in range(n)])]
    add x0 -> x3, other arithmetic: none -> 3.82 us  [on_device(): lax.dynamic_slice(grad, (core * half, 0, chunk * some), (half, depth, some))]
    ppermute x12, waiting for transfers between devices: 6.63 us -> 10.2 us  [scatter(): lax.ppermute(parts[k], axis, [(i, (i + k) % n) for i in range(n)])]
    dynamic_update_slice x8 -> x4, local copies, waits for them, and re-layouts: 3.17 us -> 0.06 us  [settle(): out = lax.dynamic_update_slice_in_dim(out, block[None], (me - k) % n, 0)]
  transfers between devices with their start and end apart: 33 -> 33, of which waited for: 12 -> 14; matrix products, arithmetic and copies ran while one was open for 13% -> 10% of each run, Pallas kernels for 11% -> 9%
where the time goes in v5:
time: 144 us; the launch traced here: 143 us
  starting transfers between devices  57.9 us (40%)
  waiting for transfers between devices  51.3 us (36%)
  Pallas kernels  13.3 us (9%)
  local copies, waits for them, and re-layouts  9.01 us (6%)
  other arithmetic  8.45 us (6%)
  matrix products  1.84 us (1%)
    all_to_all x3, waiting for transfers between devices, exchange(): return lax.all_to_all(parts, axis, split_axis=0, concat_axis=0)  24 us
    ppermute x15, starting transfers between devices, flip(): return lax.ppermute(x, axis, [(i, i ^ bit) for i in range(n)])  23.1 us
    ppermute x15, waiting for transfers between devices, flip(): return lax.ppermute(x, axis, [(i, i ^ bit) for i in range(n)])  17.1 us
    ppermute x12, starting transfers between devices, scatter(): lax.ppermute(parts[k], axis, [(i, (i + k) % n) for i in range(n)])  15.2 us
    all_to_all x3, starting transfers between devices, exchange(): return lax.all_to_all(parts, axis, split_axis=0, concat_axis=0)  15.2 us
    pallas_call x2, Pallas kernels, finish(): pl.pallas_call(finish_kernel, grid_spec=pltpu.PrefetchScalarGridSpec(num_...  13.3 us
    ppermute x12, waiting for transfers between devices, scatter(): lax.ppermute(parts[k], axis, [(i, (i + k) % n) for i in range(n)])  10.2 us
    ppermute x3, starting transfers between devices, around(): lax.ppermute(x, axis, [(i, (i + k) % n) for i in range(n)])  4.36 us
  transfers between devices with their start and end apart: 33, of which 14 were waited for; matrix products, arithmetic and copies ran while one was open for 10% of the time, Pallas kernels for 9%

profile of v5, /device:TPU:1, one launch (start us, length us, event | category | flops | bytes accessed | tf_op | source)
XLA Modules:
  0.0 142.9 jit_solution(7558717866179956189)
XLA Ops:
  0.6 1.2 dynamic-slice_bitcast_fusion
  1.8 3.3 %collective-permute-start = (f32[2,192,512]{2,1,0:T(8,128)S(1)}, f32[2,192,512]{2,1,0:T(8,128)S(1)}, u32[]{:S(2)}, u32[]{:S(2)}) collective-permute-start(f32[2,192,512]{2,1,0:T(8,128)S(1)} %dynamic-slice_bitcast_fusion), channel_id=1, source_target_pairs={{0,2},{2,0},{1,3},{3,1},{4,6},{6,4},{5,7},{7,5},{8,10},{10,8},{9,1... | collective-permute-start | bytes 2359304 | tf_op jit(solution)/shard_map/ppermute | solution.py:20
  5.2 1.2 constant_dynamic-slice_fusion.15
  6.5 0.6 collective-permute-done
  7.1 1.3 dynamic-slice_add_fusion.2
  8.3 0.9 dynamic-slice_bitcast_fusion.7
  9.2 1.2 constant_dynamic-slice_fusion.14
  10.4 0.5 collective-permute-start.2
  10.9 1.0 collective-permute-start.6
  11.8 0.3 collective-permute-start.5
  12.2 0.7 collective-permute-start.4
  12.9 1.3 dynamic-slice_add_fusion.1
  14.3 2.8 %collective-permute-start.7 = (f32[256,384]{0,1:T(8,128)S(1)}, f32[256,384]{0,1:T(8,128)S(1)}, u32[]{:S(2)}, u32[]{:S(2)}) collective-permute-start(f32[256,384]{0,1:T(8,128)S(1)} %get-tuple-element.74), channel_id=1, source_target_pairs={{0,4},{4,0},{1,5},{5,1},{2,6},{6,2},{3,7},{7,3},{8,12},{12,8},{9,1... | collective-permute-start | bytes 1179656 | tf_op jit(solution)/shard_map/ppermute | solution.py:40
  17.1 1.3 dynamic-slice_add_fusion
  18.5 2.1 %collective-permute-start.10 = (f32[128,384]{0,1:T(8,128)S(1)}, f32[128,384]{0,1:T(8,128)S(1)}, u32[]{:S(2)}, u32[]{:S(2)}) collective-permute-start(f32[128,384]{0,1:T(8,128)S(1)} %get-tuple-element.70), channel_id=1, source_target_pairs={{0,24},{8,0},{16,8},{24,16},{1,25},{9,1},{17,9},{25,17},{2,26},{10... | collective-permute-start | bytes 589832 | tf_op jit(solution)/shard_map/ppermute | solution.py:40
  20.6 1.4 constant_dynamic-slice_fusion.10
  22.3 1.5 %collective-permute-start.9 = (f32[128,384]{0,1:T(8,128)S(1)}, f32[128,384]{0,1:T(8,128)S(1)}, u32[]{:S(2)}, u32[]{:S(2)}) collective-permute-start(f32[128,384]{0,1:T(8,128)S(1)} %get-tuple-element.71), channel_id=1, source_target_pairs={{0,16},{8,24},{16,0},{24,8},{1,17},{9,25},{17,1},{25,9},{2,18},{10... | collective-permute-start | bytes 589832 | tf_op jit(solution)/shard_map/ppermute | solution.py:40
  23.8 0.6 collective-permute-done.4
  24.4 1.2 add_add_fusion.2
  25.5 0.2 constant_dynamic-slice_fusion.6
  25.8 0.3 constant_dynamic-slice_fusion.4
  26.1 2.2 %collective-permute-start.15 = (f32[64,384]{0,1:T(8,128)S(1)}, f32[64,384]{0,1:T(8,128)S(1)}, u32[]{:S(2)}, u32[]{:S(2)}) collective-permute-start(f32[64,384]{0,1:T(8,128)S(1)} %get-tuple-element.87), channel_id=1, source_target_pairs={{0,24},{8,0},{16,8},{24,16},{1,25},{9,1},{17,9},{25,17},{2,26},{10... | collective-permute-start | bytes 294920 | tf_op jit(solution)/shard_map/ppermute | solution.py:40
  28.2 1.0 collective-permute-start.14
  29.3 0.5 collective-permute-start.13
  29.8 2.4 %collective-permute-start.11 = (f32[64,384]{0,1:T(8,128)S(1)}, f32[64,384]{0,1:T(8,128)S(1)}, u32[]{:S(2)}, u32[]{:S(2)}) collective-permute-start(f32[64,384]{0,1:T(8,128)S(1)} %get-tuple-element.100), channel_id=1, source_target_pairs={{0,4},{4,0},{1,5},{5,1},{2,6},{6,2},{3,7},{7,3},{8,12},{12,8},{9,1... | collective-permute-start | bytes 294920 | tf_op jit(solution)/shard_map/ppermute | solution.py:40
  32.2 3.5 %collective-permute-done.8 = f32[128,384]{0,1:T(8,128)S(1)} collective-permute-done((f32[128,384]{0,1:T(8,128)S(1)}, f32[128,384]{0,1:T(8,128)S(1)}, u32[]{:S(2)}, u32[]{:S(2)}) %collective-permute-start.8) | collective-permute-done | bytes 196640 | tf_op jit(solution)/shard_map/ppermute | solution.py:40
  35.9 0.7 collective-permute-start.12
  36.6 0.5 collective-permute-done.14
  37.1 5.6 %collective-permute-done.13 = f32[64,384]{0,1:T(8,128)S(1)} collective-permute-done((f32[64,384]{0,1:T(8,128)S(1)}, f32[64,384]{0,1:T(8,128)S(1)}, u32[]{:S(2)}, u32[]{:S(2)}) %collective-permute-start.13) | collective-permute-done | bytes 98336 | tf_op jit(solution)/shard_map/ppermute | solution.py:40
  43.2 0.7 pad_maximum_fusion.3
  44.0 8.2 %all-to-all-start = ((f32[8,24,384]{2,1,0:T(8,128)}), f32[8,24,384]{2,1,0:T(8,128)S(1)}, u32[]{:S(2)}, u32[]{:S(2)}) async-start(f32[8,24,384]{2,1,0:T(8,128)} %pad_maximum_fusion.3), calls=%async_computation | async-start | bytes 589824 | tf_op jit(solution)/shard_map/all_to_all | solution.py:71
  52.2 0.5 collective-permute-start.3
  52.8 2.4 %collective-permute-done.3 = f32[2,24,128]{2,1,0:T(8,128)S(1)} collective-permute-done((f32[2,24,128]{2,1,0:T(8,128)S(1)}, f32[2,24,128]{2,1,0:T(8,128)S(1)}, u32[]{:S(2)}, u32[]{:S(2)}) %collective-permute-start.3) | collective-permute-done | bytes 24608 | tf_op jit(solution)/shard_map/ppermute | solution.py:20
  55.3 6.7 %all-to-all-done = f32[8,24,384]{2,1,0:T(8,128)S(1)} async-done(((f32[8,24,384]{2,1,0:T(8,128)}), f32[8,24,384]{2,1,0:T(8,128)S(1)}, u32[]{:S(2)}, u32[]{:S(2)}) %all-to-all-start) | async-done | bytes 294944 | tf_op jit(solution)/shard_map/all_to_all | solution.py:71
  62.1 0.3 fusion.2
  62.4 0.4 collective-permute-start.16
  62.8 2.6 %collective-permute-done.16 = f32[2,24,128]{2,1,0:T(8,128)S(1)} collective-permute-done((f32[2,24,128]{2,1,0:T(8,128)S(1)}, f32[2,24,128]{2,1,0:T(8,128)S(1)}, u32[]{:S(2)}, u32[]{:S(2)}) %collective-permute-start.16) | collective-permute-done | bytes 24608 | tf_op jit(solution)/shard_map/ppermute | solution.py:20
  65.5 0.5 fusion.7
  66.2 0.8 maximum_maximum_fusion
  67.0 3.5 %all-to-all-start.1 = ((f32[8,40,384]{2,1,0:T(8,128)}), f32[8,40,384]{2,1,0:T(8,128)S(1)}, u32[]{:S(2)}, u32[]{:S(2)}) async-start(f32[8,40,384]{2,1,0:T(8,128)} %maximum_maximum_fusion), calls=%async_computation.1 | async-start | bytes 983040 | tf_op jit(solution)/shard_map/all_to_all | solution.py:71
  70.6 11.8 %all-to-all-done.1 = f32[8,40,384]{2,1,0:T(8,128)S(1)} async-done(((f32[8,40,384]{2,1,0:T(8,128)}), f32[8,40,384]{2,1,0:T(8,128)S(1)}, u32[]{:S(2)}, u32[]{:S(2)}) %all-to-all-start.1) | async-done | bytes 491552 | tf_op jit(solution)/shard_map/all_to_all | solution.py:71
  82.4 1.3 collective-permute-start.17
  83.8 2.3 %collective-permute-start.19 = (f32[80,384]{1,0:T(8,128)S(1)}, f32[80,384]{1,0:T(8,128)S(1)}, u32[]{:S(2)}, u32[]{:S(2)}) collective-permute-start(f32[80,384]{1,0:T(8,128)S(1)} %pad_maximum_fusion.6), channel_id=1, source_target_pairs={{0,16},{8,24},{16,0},{24,8},{1,17},{9,25},{17,1},{25,9},{2,18},{10... | collective-permute-start | bytes 368648 | tf_op jit(solution)/shard_map/ppermute | solution.py:59
  86.1 2.0 %collective-permute-start.20 = (f32[80,384]{1,0:T(8,128)S(1)}, f32[80,384]{1,0:T(8,128)S(1)}, u32[]{:S(2)}, u32[]{:S(2)}) collective-permute-start(f32[80,384]{1,0:T(8,128)S(1)} %pad_maximum_fusion.6), channel_id=1, source_target_pairs={{0,24},{8,0},{16,8},{24,16},{1,25},{9,1},{17,9},{25,17},{2,26},{10... | collective-permute-start | bytes 368648 | tf_op jit(solution)/shard_map/ppermute | solution.py:59
  88.1 0.5 collective-permute-done.17
  88.6 1.2 broadcast_in_dim.35
  89.9 3.6 %all-to-all-start.2 = ((f32[4,256,384]{2,1,0:T(8,128)}), f32[4,256,384]{2,1,0:T(8,128)S(1)}, u32[]{:S(2)}, u32[]{:S(2)}) async-start(f32[4,256,384]{2,1,0:T(8,128)} %broadcast_in_dim.35), calls=%async_computation.2 | async-start | bytes 3145728 | tf_op jit(solution)/shard_map/all_to_all | solution.py:71
  93.6 1.3 collective-permute-start.23
  94.9 3.0 %collective-permute-done.23 = f32[16,384]{1,0:T(8,128)S(1)} collective-permute-done((f32[16,384]{1,0:T(8,128)S(1)}, f32[16,384]{1,0:T(8,128)S(1)}, u32[]{:S(2)}, u32[]{:S(2)}) %collective-permute-start.23) | collective-permute-done | bytes 24608 | tf_op jit(solution)/shard_map/ppermute | solution.py:20
  97.9 0.3 collective-permute-start.24
  98.3 1.4 collective-permute-start.21
  99.7 0.9 collective-permute-done.24
  100.6 0.3 collective-permute-start.25
  100.9 5.6 %all-to-all-done.2 = f32[4,256,384]{2,1,0:T(8,128)S(1)} async-done(((f32[4,256,384]{2,1,0:T(8,128)}), f32[4,256,384]{2,1,0:T(8,128)S(1)}, u32[]{:S(2)}, u32[]{:S(2)}) %all-to-all-start.2) | async-done | bytes 1572896 | tf_op jit(solution)/shard_map/all_to_all | solution.py:71
  106.5 8.6 %collective-permute-start.27 = (f32[64,2,8,384]{3,2,1,0:T(8,128)S(1)}, f32[64,2,8,384]{3,2,1,0:T(8,128)S(1)}, u32[]{:S(2)}, u32[]{:S(2)}) collective-permute-start(f32[64,2,8,384]{3,2,1,0:T(8,128)S(1)} %bitcast.93), channel_id=1, source_target_pairs={{0,2},{2,0},{1,3},{3,1},{4,6},{6,4},{5,7},{7,5},{8,10},{10,8},{9,1... | collective-permute-start | bytes 4718600 | tf_op jit(solution)/shard_map/ppermute | solution.py:20
  115.1 0.3 collective-permute-start.26
  115.5 7.2 %collective-permute-done.26 = f32[64,384]{1,0:T(8,128)S(1)} collective-permute-done((f32[64,384]{1,0:T(8,128)S(1)}, f32[64,384]{1,0:T(8,128)S(1)}, u32[]{:S(2)}, u32[]{:S(2)}) %collective-permute-start.26) | collective-permute-done | bytes 98336 | tf_op jit(solution)/shard_map/ppermute | solution.py:20
  122.8 0.7 fusion.22
  123.4 0.8 collective-permute-start.28
  124.3 3.9 %collective-permute-start.22 = (f32[64,1,8,384]{3,2,1,0:T(8,128)S(1)}, f32[64,1,8,384]{3,2,1,0:T(8,128)S(1)}, u32[]{:S(2)}, u32[]{:S(2)}) collective-permute-start(f32[64,1,8,384]{3,2,1,0:T(8,128)S(1)} %bitcast.95), channel_id=1, source_target_pairs={{0,2},{2,0},{1,3},{3,1},{4,6},{6,4},{5,7},{7,5},{8,10},{10,8},{9,1... | collective-permute-start | bytes 2359304 | tf_op jit(solution)/shard_map/ppermute | solution.py:20
  128.2 8.5 %finish.2 = (f32[4,192,1536]{2,1,0:T(8,128)}, f32[4,64,1536]{2,1,0:T(8,128)}, f32[4,64,1536]{2,1,0:T(8,128)}) custom-call(s32[1]{0:T(128)} %bitcast.core, f32[64,2,8,384]{3,2,1,0:T(8,128)S(1)} %bitcast.94, f32[64,2,8,384]{3,2,1,0:T(8,128)S(1)} %collective-permute-done.27.other, f32[4,192,128]{2,1,0:T(8,128)S(1)} %copy-done, f32[4,192,1536]{2,1,0:T(8,128)} %weights.3, ...), custom_call_target="tpu_custom_call" | custom-call | flops 1207959552 | bytes 10485760 | tf_op jit(solution)/shard_map/finish/pallas_call | solution.py:106
  136.8 0.4 fusion
  137.4 4.8 %finish.3 = (f32[4,192,1536]{2,1,0:T(8,128)}, f32[4,64,1536]{2,1,0:T(8,128)}, f32[4,64,1536]{2,1,0:T(8,128)}) custom-call(s32[1]{0:T(128)} %bitcast.core, f32[64,1,8,384]{3,2,1,0:T(8,128)S(1)} %bitcast.96, f32[64,1,8,384]{3,2,1,0:T(8,128)S(1)} %collective-permute-done.22.other, ...), custom_call_target="tpu_custom_call", output_to_operand_aliasing={{0}: (7, {}), {1}: (8, {}), {2}: (9, {})} | custom-call | flops 603979776 | bytes 5242880 | tf_op jit(solution)/shard_map/finish/pallas_call | solution.py:106
  142.2 0.8 pad_maximum_fusion.2
  (84 shorter events, 3.1 us)
Async XLA Ops:
  1.8 5.2 %collective-permute-start = (f32[2,192,512]{2,1,0:T(8,128)S(1)}, f32[2,192,512]{2,1,0:T(8,128)S(1)}, u32[]{:S(2)}, u32[]{:S(2)}) collective-permute-start(f32[2,192,512]{2,1,0:T(8,128)S(1)} %dynamic-slice_bitcast_fusion), channel_id=1, source_target_pairs={{0,2},{2,0},{1,3},{3,1},{4,6},{6,4},{5,7},{7,5},{8,10},{10,8},{9,1... | collective-permute-start | bytes 2359304 | tf_op jit(solution)/shard_map/ppermute | solution.py:20
  6.3 6.5 %collective-permute-start.1 = (f32[2,192,512]{2,1,0:T(8,128)S(1)}, f32[2,192,512]{2,1,0:T(8,128)S(1)}, u32[]{:S(2)}, u32[]{:S(2)}) collective-permute-start(f32[2,192,512]{2,1,0:T(8,128)S(1)} %constant_dynamic-slice_fusion.15), channel_id=1, source_target_pairs={{0,2},{2,0},{1,3},{3,1},{4,6},{6,4},{5,7},{7,5},{8,10},{10,8},{9,1... | collective-permute-start | bytes 2359304 | tf_op jit(solution)/shard_map/ppermute | solution.py:20
  10.4 6.7 %collective-permute-start.2 = (f32[2,192,512]{2,1,0:T(8,128)S(1)}, f32[2,192,512]{2,1,0:T(8,128)S(1)}, u32[]{:S(2)}, u32[]{:S(2)}) collective-permute-start(f32[2,192,512]{2,1,0:T(8,128)S(1)} %constant_dynamic-slice_fusion.14), channel_id=1, source_target_pairs={{0,2},{2,0},{1,3},{3,1},{4,6},{6,4},{5,7},{7,5},{8,10},{10,8},{9,1... | collective-permute-start | bytes 2359304 | tf_op jit(solution)/shard_map/ppermute | solution.py:20
  10.9 11.5 %collective-permute-start.6 = (f32[128,384]{0,1:T(8,128)}, f32[128,384]{0,1:T(8,128)}, u32[]{:S(2)}, u32[]{:S(2)}) collective-permute-start(f32[128,384]{0,1:T(8,128)} %get-tuple-element.76), channel_id=1, source_target_pairs={{0,24},{8,0},{16,8},{24,16},{1,25},{9,1},{17,9},{25,17},{2,26},{10... | collective-permute-start | bytes 589832 | tf_op jit(solution)/shard_map/ppermute | solution.py:40
  11.8 12.0 %collective-permute-start.5 = (f32[128,384]{0,1:T(8,128)}, f32[128,384]{0,1:T(8,128)}, u32[]{:S(2)}, u32[]{:S(2)}) collective-permute-start(f32[128,384]{0,1:T(8,128)} %get-tuple-element.77), channel_id=1, source_target_pairs={{0,16},{8,24},{16,0},{24,8},{1,17},{9,25},{17,1},{25,9},{2,18},{10... | collective-permute-start | bytes 589832 | tf_op jit(solution)/shard_map/ppermute | solution.py:40
  12.2 12.2 %collective-permute-start.4 = (f32[128,384]{0,1:T(8,128)S(1)}, f32[128,384]{0,1:T(8,128)}, u32[]{:S(2)}, u32[]{:S(2)}) collective-permute-start(f32[128,384]{0,1:T(8,128)S(1)} %get-tuple-element.78), channel_id=1, source_target_pairs={{0,8},{8,16},{16,24},{24,0},{1,9},{9,17},{17,25},{25,1},{2,10},{10... | collective-permute-start | bytes 589832 | tf_op jit(solution)/shard_map/ppermute | solution.py:40
  14.3 11.5 %collective-permute-start.7 = (f32[256,384]{0,1:T(8,128)S(1)}, f32[256,384]{0,1:T(8,128)S(1)}, u32[]{:S(2)}, u32[]{:S(2)}) collective-permute-start(f32[256,384]{0,1:T(8,128)S(1)} %get-tuple-element.74), channel_id=1, source_target_pairs={{0,4},{4,0},{1,5},{5,1},{2,6},{6,2},{3,7},{7,3},{8,12},{12,8},{9,1... | collective-permute-start | bytes 1179656 | tf_op jit(solution)/shard_map/ppermute | solution.py:40
  18.5 10.8 %collective-permute-start.10 = (f32[128,384]{0,1:T(8,128)S(1)}, f32[128,384]{0,1:T(8,128)S(1)}, u32[]{:S(2)}, u32[]{:S(2)}) collective-permute-start(f32[128,384]{0,1:T(8,128)S(1)} %get-tuple-element.70), channel_id=1, source_target_pairs={{0,24},{8,0},{16,8},{24,16},{1,25},{9,1},{17,9},{25,17},{2,26},{10... | collective-permute-start | bytes 589832 | tf_op jit(solution)/shard_map/ppermute | solution.py:40
  22.3 7.5 %collective-permute-start.9 = (f32[128,384]{0,1:T(8,128)S(1)}, f32[128,384]{0,1:T(8,128)S(1)}, u32[]{:S(2)}, u32[]{:S(2)}) collective-permute-start(f32[128,384]{0,1:T(8,128)S(1)} %get-tuple-element.71), channel_id=1, source_target_pairs={{0,16},{8,24},{16,0},{24,8},{1,17},{9,25},{17,1},{25,9},{2,18},{10... | collective-permute-start | bytes 589832 | tf_op jit(solution)/shard_map/ppermute | solution.py:40
  23.8 11.9 %collective-permute-start.8 = (f32[128,384]{0,1:T(8,128)S(1)}, f32[128,384]{0,1:T(8,128)S(1)}, u32[]{:S(2)}, u32[]{:S(2)}) collective-permute-start(f32[128,384]{0,1:T(8,128)S(1)} %get-tuple-element.72), channel_id=1, source_target_pairs={{0,8},{8,16},{16,24},{24,0},{1,9},{9,17},{17,25},{25,1},{2,10},{10... | collective-permute-start | bytes 589832 | tf_op jit(solution)/shard_map/ppermute | solution.py:40
  26.1 10.6 %collective-permute-start.15 = (f32[64,384]{0,1:T(8,128)S(1)}, f32[64,384]{0,1:T(8,128)S(1)}, u32[]{:S(2)}, u32[]{:S(2)}) collective-permute-start(f32[64,384]{0,1:T(8,128)S(1)} %get-tuple-element.87), channel_id=1, source_target_pairs={{0,24},{8,0},{16,8},{24,16},{1,25},{9,1},{17,9},{25,17},{2,26},{10... | collective-permute-start | bytes 294920 | tf_op jit(solution)/shard_map/ppermute | solution.py:40
  28.2 8.9 %collective-permute-start.14 = (f32[64,384]{0,1:T(8,128)S(1)}, f32[64,384]{0,1:T(8,128)S(1)}, u32[]{:S(2)}, u32[]{:S(2)}) collective-permute-start(f32[64,384]{0,1:T(8,128)S(1)} %get-tuple-element.88), channel_id=1, source_target_pairs={{0,16},{8,24},{16,0},{24,8},{1,17},{9,25},{17,1},{25,9},{2,18},{10... | collective-permute-start | bytes 294920 | tf_op jit(solution)/shard_map/ppermute | solution.py:40
  29.3 13.5 %collective-permute-start.13 = (f32[64,384]{0,1:T(8,128)S(1)}, f32[64,384]{0,1:T(8,128)S(1)}, u32[]{:S(2)}, u32[]{:S(2)}) collective-permute-start(f32[64,384]{0,1:T(8,128)S(1)} %get-tuple-element.86), channel_id=1, source_target_pairs={{0,8},{8,16},{16,24},{24,0},{1,9},{9,17},{17,25},{25,1},{2,10},{10... | collective-permute-start | bytes 294920 | tf_op jit(solution)/shard_map/ppermute | solution.py:40
  29.8 13.1 %collective-permute-start.11 = (f32[64,384]{0,1:T(8,128)S(1)}, f32[64,384]{0,1:T(8,128)S(1)}, u32[]{:S(2)}, u32[]{:S(2)}) collective-permute-start(f32[64,384]{0,1:T(8,128)S(1)} %get-tuple-element.100), channel_id=1, source_target_pairs={{0,4},{4,0},{1,5},{5,1},{2,6},{6,2},{3,7},{7,3},{8,12},{12,8},{9,1... | collective-permute-start | bytes 294920 | tf_op jit(solution)/shard_map/ppermute | solution.py:40
  35.9 7.2 %collective-permute-start.12 = (f32[64,384]{0,1:T(8,128)S(1)}, f32[64,384]{0,1:T(8,128)S(1)}, u32[]{:S(2)}, u32[]{:S(2)}) collective-permute-start(f32[64,384]{0,1:T(8,128)S(1)} %get-tuple-element.98), channel_id=1, source_target_pairs={{0,4},{4,0},{1,5},{5,1},{2,6},{6,2},{3,7},{7,3},{8,12},{12,8},{9,1... | collective-permute-start | bytes 294920 | tf_op jit(solution)/shard_map/ppermute | solution.py:40
  43.0 19.1 %copy-start = (f32[4,192,128]{2,1,0:T(8,128)S(1)}, f32[4,192,128]{2,1,0:T(8,128)}, u32[]{:S(2)}) copy-start(f32[4,192,128]{2,1,0:T(8,128)} %basis.3) | copy-start | bytes 1179652
  44.0 18.0 %all-to-all-start = ((f32[8,24,384]{2,1,0:T(8,128)}), f32[8,24,384]{2,1,0:T(8,128)S(1)}, u32[]{:S(2)}, u32[]{:S(2)}) async-start(f32[8,24,384]{2,1,0:T(8,128)} %pad_maximum_fusion.3), calls=%async_computation | async-start | bytes 589824 | tf_op jit(solution)/shard_map/all_to_all | solution.py:71
  52.2 2.9 %collective-permute-start.3 = (f32[2,24,128]{2,1,0:T(8,128)S(1)}, f32[2,24,128]{2,1,0:T(8,128)S(1)}, u32[]{:S(2)}, u32[]{:S(2)}) collective-permute-start(f32[2,24,128]{2,1,0:T(8,128)S(1)} %pad_maximum_fusion.10), channel_id=1, source_target_pairs={{0,1},{1,0},{2,3},{3,2},{4,5},{5,4},{6,7},{7,6},{8,9},{9,8},{10,11... | collective-permute-start | bytes 73736 | tf_op jit(solution)/shard_map/ppermute | solution.py:20
  62.4 3.0 %collective-permute-start.16 = (f32[2,24,128]{2,1,0:T(8,128)S(1)}, f32[2,24,128]{2,1,0:T(8,128)S(1)}, u32[]{:S(2)}, u32[]{:S(2)}) collective-permute-start(f32[2,24,128]{2,1,0:T(8,128)S(1)} %fusion.2), channel_id=1, source_target_pairs={{0,1},{1,0},{2,3},{3,2},{4,5},{5,4},{6,7},{7,6},{8,9},{9,8},{10,11... | collective-permute-start | bytes 73736 | tf_op jit(solution)/shard_map/ppermute | solution.py:20
  67.0 15.4 %all-to-all-start.1 = ((f32[8,40,384]{2,1,0:T(8,128)}), f32[8,40,384]{2,1,0:T(8,128)S(1)}, u32[]{:S(2)}, u32[]{:S(2)}) async-start(f32[8,40,384]{2,1,0:T(8,128)} %maximum_maximum_fusion), calls=%async_computation.1 | async-start | bytes 983040 | tf_op jit(solution)/shard_map/all_to_all | solution.py:71
  82.4 6.1 %collective-permute-start.17 = (f32[128,384]{1,0:T(8,128)S(1)}, f32[128,384]{1,0:T(8,128)S(1)}, u32[]{:S(2)}, u32[]{:S(2)}) collective-permute-start(f32[128,384]{1,0:T(8,128)S(1)} %bitcast.112), channel_id=1, source_target_pairs={{0,4},{4,0},{1,5},{5,1},{2,6},{6,2},{3,7},{7,3},{8,12},{12,8},{9,1... | collective-permute-start | bytes 589832 | tf_op jit(solution)/shard_map/ppermute | solution.py:20
  83.7 9.8 %collective-permute-start.18 = (f32[80,384]{1,0:T(8,128)S(1)}, f32[80,384]{1,0:T(8,128)S(1)}, u32[]{:S(2)}, u32[]{:S(2)}) collective-permute-start(f32[80,384]{1,0:T(8,128)S(1)} %pad_maximum_fusion.6), channel_id=1, source_target_pairs={{0,8},{8,16},{16,24},{24,0},{1,9},{9,17},{17,25},{25,1},{2,10},{10... | collective-permute-start | bytes 368648 | tf_op jit(solution)/shard_map/ppermute | solution.py:59
  83.8 9.7 %collective-permute-start.19 = (f32[80,384]{1,0:T(8,128)S(1)}, f32[80,384]{1,0:T(8,128)S(1)}, u32[]{:S(2)}, u32[]{:S(2)}) collective-permute-start(f32[80,384]{1,0:T(8,128)S(1)} %pad_maximum_fusion.6), channel_id=1, source_target_pairs={{0,16},{8,24},{16,0},{24,8},{1,17},{9,25},{17,1},{25,9},{2,18},{10... | collective-permute-start | bytes 368648 | tf_op jit(solution)/shard_map/ppermute | solution.py:59
  86.1 7.5 %collective-permute-start.20 = (f32[80,384]{1,0:T(8,128)S(1)}, f32[80,384]{1,0:T(8,128)S(1)}, u32[]{:S(2)}, u32[]{:S(2)}) collective-permute-start(f32[80,384]{1,0:T(8,128)S(1)} %pad_maximum_fusion.6), channel_id=1, source_target_pairs={{0,24},{8,0},{16,8},{24,16},{1,25},{9,1},{17,9},{25,17},{2,26},{10... | collective-permute-start | bytes 368648 | tf_op jit(solution)/shard_map/ppermute | solution.py:59
  89.9 16.6 %all-to-all-start.2 = ((f32[4,256,384]{2,1,0:T(8,128)}), f32[4,256,384]{2,1,0:T(8,128)S(1)}, u32[]{:S(2)}, u32[]{:S(2)}) async-start(f32[4,256,384]{2,1,0:T(8,128)} %broadcast_in_dim.35), calls=%async_computation.2 | async-start | bytes 3145728 | tf_op jit(solution)/shard_map/all_to_all | solution.py:71
  93.6 4.3 %collective-permute-start.23 = (f32[16,384]{1,0:T(8,128)S(1)}, f32[16,384]{1,0:T(8,128)S(1)}, u32[]{:S(2)}, u32[]{:S(2)}) collective-permute-start(f32[16,384]{1,0:T(8,128)S(1)} %slice_reduce_fusion.1), channel_id=1, source_target_pairs={{0,4},{4,0},{1,5},{5,1},{2,6},{6,2},{3,7},{7,3},{8,12},{12,8},{9,1... | collective-permute-start | bytes 73736 | tf_op jit(solution)/shard_map/ppermute | solution.py:20
  97.9 2.7 %collective-permute-start.24 = (f32[16,384]{1,0:T(8,128)S(1)}, f32[16,384]{1,0:T(8,128)S(1)}, u32[]{:S(2)}, u32[]{:S(2)}) collective-permute-start(f32[16,384]{1,0:T(8,128)S(1)} %add.303), channel_id=1, source_target_pairs={{0,32},{32,0},{64,96},{96,64},{128,160},{160,128},{192,224},{224,1... | collective-permute-start | bytes 73736 | tf_op jit(solution)/shard_map/ppermute | solution.py:20
  98.3 17.2 %collective-permute-start.21 = (f32[256,384]{1,0:T(8,128)S(1)}, f32[256,384]{1,0:T(8,128)S(1)}, u32[]{:S(2)}, u32[]{:S(2)}) collective-permute-start(f32[256,384]{1,0:T(8,128)S(1)} %bitcast.107), channel_id=1, source_target_pairs={{0,4},{4,0},{1,5},{5,1},{2,6},{6,2},{3,7},{7,3},{8,12},{12,8},{9,1... | collective-permute-start | bytes 1179656 | tf_op jit(solution)/shard_map/ppermute | solution.py:20
  100.6 14.5 %collective-permute-start.25 = (f32[32,384]{1,0:T(8,128)S(1)}, f32[32,384]{1,0:T(8,128)S(1)}, u32[]{:S(2)}, u32[]{:S(2)}) collective-permute-start(f32[32,384]{1,0:T(8,128)S(1)} %pad_maximum_fusion.8), channel_id=1, source_target_pairs={{0,64},{32,96},{64,0},{96,32},{128,192},{160,224},{192,128},{224,1... | collective-permute-start | bytes 147464 | tf_op jit(solution)/shard_map/ppermute | solution.py:20
  106.5 21.7 %collective-permute-start.27 = (f32[64,2,8,384]{3,2,1,0:T(8,128)S(1)}, f32[64,2,8,384]{3,2,1,0:T(8,128)S(1)}, u32[]{:S(2)}, u32[]{:S(2)}) collective-permute-start(f32[64,2,8,384]{3,2,1,0:T(8,128)S(1)} %bitcast.93), channel_id=1, source_target_pairs={{0,2},{2,0},{1,3},{3,1},{4,6},{6,4},{5,7},{7,5},{8,10},{10,8},{9,1... | collective-permute-start | bytes 4718600 | tf_op jit(solution)/shard_map/ppermute | solution.py:20
  115.1 7.6 %collective-permute-start.26 = (f32[64,384]{1,0:T(8,128)S(1)}, f32[64,384]{1,0:T(8,128)S(1)}, u32[]{:S(2)}, u32[]{:S(2)}) collective-permute-start(f32[64,384]{1,0:T(8,128)S(1)} %pad_maximum_fusion.7), channel_id=1, source_target_pairs={{0,128},{32,160},{64,192},{96,224},{128,0},{160,32},{192,64},{224,... | collective-permute-start | bytes 294920 | tf_op jit(solution)/shard_map/ppermute | solution.py:20
  123.4 13.2 %collective-permute-start.28 = (f32[2,128,128]{2,1,0:T(8,128)S(1)}, f32[2,128,128]{2,1,0:T(8,128)S(1)}, u32[]{:S(2)}, u32[]{:S(2)}) collective-permute-start(f32[2,128,128]{2,1,0:T(8,128)S(1)} %fusion.22), channel_id=1, source_target_pairs={{0,1},{1,0},{2,3},{3,2},{4,5},{5,4},{6,7},{7,6},{8,9},{9,8},{10,11... | collective-permute-start | bytes 393224 | tf_op jit(solution)/shard_map/ppermute | solution.py:20
  124.3 13.1 %collective-permute-start.22 = (f32[64,1,8,384]{3,2,1,0:T(8,128)S(1)}, f32[64,1,8,384]{3,2,1,0:T(8,128)S(1)}, u32[]{:S(2)}, u32[]{:S(2)}) collective-permute-start(f32[64,1,8,384]{3,2,1,0:T(8,128)S(1)} %bitcast.95), channel_id=1, source_target_pairs={{0,2},{2,0},{1,3},{3,1},{4,6},{6,4},{5,7},{7,5},{8,10},{10,8},{9,1... | collective-permute-start | bytes 2359304 | tf_op jit(solution)/shard_map/ppermute | solution.py:20
  137.2 4.9 %collective-permute-start.29 = (f32[2,192,128]{2,1,0:T(8,128)S(1)}, f32[2,192,128]{2,1,0:T(8,128)S(1)}, u32[]{:S(2)}, u32[]{:S(2)}) collective-permute-start(f32[2,192,128]{2,1,0:T(8,128)S(1)} %fusion), channel_id=1, source_target_pairs={{0,2},{2,0},{1,3},{3,1},{4,6},{6,4},{5,7},{7,5},{8,10},{10,8},{9,1... | collective-permute-start | bytes 589832 | tf_op jit(solution)/shard_map/ppermute | solution.py:20

commit v6 on v5

--- a/solution.py
+++ b/solution.py
@@ -1,3 +1,5 @@
+import functools
+
 import jax
 import jax.numpy as jnp
 from jax import lax
@@ -75,52 +77,57 @@
     return jnp.broadcast_to(x, (SIZES[axis],) + x.shape)
 
 
-def finish_kernel(core, own, other, basis, weights, first, second, *rest):
-    out_weights, out_first, out_second = rest[-3:]
-    layer = pl.program_id(1)
+def finish_kernel(count, *refs):
+    sources = refs[1 : 1 + count]
+    basis, weights, first, second = refs[1 + count : 5 + count]
+    out_weights, out_first, out_second = refs[-3:]
     rank = basis.shape[2]
-    here = core[0] == layer // 2
     some = out_weights.shape[2]
-    x = jnp.where(here, own[...].reshape(some, -1), other[...].reshape(some, -1))
-    direction = jnp.where(layer % 2 == 0, x[:, :rank], x[:, rank : 2 * rank])
+    step = pl.program_id(1)
+    sources = [source[...].reshape(some, -1) for source in sources]
+    x = sources[0] if count == 1 else jnp.where(step < 2, *sources)
+    direction = jnp.where(step % 2 == 0, x[:, :rank], x[:, rank : 2 * rank])
     update = lax.dot_general(
         basis[0], direction, (((1,), (1,)), ((), ())), precision=HIGH, preferred_element_type=jnp.float32
     )
     out_weights[0] = weights[0] - 0.0125 * update
     proj = x[:, 2 * rank :].T
-    proj = jnp.where(layer % 2 == 0, proj[: rank // 2], proj[rank // 2 :])
+    proj = jnp.where(step % 2 == 0, proj[: rank // 2], proj[rank // 2 :])
     out_first[0] = 0.9 * first[0] + 0.1 * proj
     out_second[0] = 0.999 * second[0] + 0.001 * proj * proj
 
 
-def finish(chunks, core, own, other, basis, weights, first, second, before):
+def finish(chunks, pairs, sources, basis, weights, first, second, before):
     layers, depth, width = weights.shape
     rank, some = basis.shape[2], width // CHUNKS
     gap = chunks[-1] - chunks[0]
-    small = own.shape[2]
-    packed = pl.BlockSpec((own.shape[0], 1, small, own.shape[3]), lambda h, l, c: (0, h, 0, 0))
-    whole = pl.BlockSpec((1, depth, rank), lambda h, l, c: (l, 0, 0))
-    tall = pl.BlockSpec((1, depth, some), lambda h, l, c: (l, 0, chunks[0] + gap * h))
-    low = pl.BlockSpec((1, first.shape[1], some), lambda h, l, c: (l, 0, chunks[0] + gap * h))
+    shape = sources[0].shape
+    layer = lambda j, p: p[j // 2] * 2 + j % 2
+    packed = pl.BlockSpec((shape[0], 1) + shape[2:], lambda h, j, p: (0, h, 0, 0))
+    whole = pl.BlockSpec((1, depth, rank), lambda h, j, p: (layer(j, p), 0, 0))
+    tall = pl.BlockSpec((1, depth, some), lambda h, j, p: (layer(j, p), 0, chunks[0] + gap * h))
+    low = pl.BlockSpec((1, first.shape[1], some), lambda h, j, p: (layer(j, p), 0, chunks[0] + gap * h))
     kept = [] if before is None else list(before)
+    count = len(sources)
+    steps = 2 * count
     return pl.pallas_call(
-        finish_kernel,
+        functools.partial(finish_kernel, count),
         grid_spec=pltpu.PrefetchScalarGridSpec(
             num_scalar_prefetch=1,
-            grid=(len(chunks), layers),
-            in_specs=[packed, packed, whole, tall, low, low] + [pl.BlockSpec(memory_space=pl.ANY)] * len(kept),
+            grid=(len(chunks), steps),
+            in_specs=[packed] * count + [whole, tall, low, low] + [pl.BlockSpec(memory_space=pl.ANY)] * len(kept),
             out_specs=[tall, low, low],
         ),
         out_shape=[jax.ShapeDtypeStruct(a.shape, a.dtype) for a in (weights, first, second)],
-        input_output_aliases={7 + i: i for i in range(len(kept))},
+        input_output_aliases={5 + count + i: i for i in range(len(kept))},
         compiler_params=pltpu.CompilerParams(vmem_limit_bytes=20 << 20),
         cost_estimate=pl.CostEstimate(
-            flops=12 * layers * depth * rank * some * len(chunks),
-            bytes_accessed=8 * layers * (depth + rank) * some * len(chunks),
+            flops=12 * steps * depth * rank * some * len(chunks),
+            bytes_accessed=8 * steps * (depth + rank) * some * len(chunks),
             transcendentals=0,
         ),
         name="finish",
-    )(core.reshape(1), own, other, basis, weights, first, second, *kept)
+    )(jnp.stack(pairs), *sources, basis, weights, first, second, *kept)
 
 
 def on_device(grads, basis, weights, first_moment, second_moment):
@@ -188,7 +195,8 @@
     packed = jnp.concatenate([direction[0], direction[1], mine[0], mine[1]], axis=1)
 
     refresh = jnp.einsum("fld,lfr->ldr", total, proj, precision=HIGH)
-    refresh = refresh.reshape(SIZES["z"], 3, -1, rank)
+    refresh = refresh.reshape(2, 2, 2, 3, -1, rank)
+    refresh = jnp.transpose(refresh, (2, 1, 0, 3, 4, 5)).reshape(SIZES["z"], 3, -1, rank)
     refresh = jnp.concatenate([refresh[:, i] for i in range(3)], axis=2)
     both = exchange(jnp.concatenate([copies(packed, "z"), refresh], axis=1), "z")
     large = both[:, : 2 * small].reshape(-1, 3 * rank)
@@ -203,23 +211,26 @@
     part = jnp.sum(little[:, -part.shape[0] :], axis=0)
     little = little[:, : -part.shape[0]].reshape(-1, 3 * rank)
     part = part + flip(part, "xh")
-    little = gather(little, "xh", after(little, across)).reshape(-1, 1, small, 3 * rank)
+    little = gather(little, "xh").reshape(-1, 1, small, 3 * rank)
+
+    done = finish((0, 2), [core], [across], basis, *nearby, None)
 
     refresh = part
-    for bit in range(3):
-        if bit == 2:
-            refresh = after(refresh, across)
-        refresh = jnp.concatenate(in_order((z >> bit) & 1, refresh, flip(refresh, "z", 1 << bit)))
+    for bit in (2, 1, 0):
+        mine, moved = refresh, flip(refresh if bit else after(refresh, little), "z", 1 << bit)
+        if bit == 0:
+            mine = after(mine, *done)
+        refresh = jnp.concatenate(in_order((z >> bit) & 1, mine, moved))
     refresh = refresh.reshape(SIZES["z"], -1, 3 * rank)
     refresh = jnp.stack([refresh[:, :, i * rank : (i + 1) * rank] for i in range(3)], axis=1)
     refresh = refresh.reshape(half, depth, rank)
     gram = jnp.einsum("ldr,lds->lrs", refresh, refresh, precision=HIGH)
 
     other = flip(across, "core")
-    first_done = finish((0, 2), core, after(across, gram), other, basis, *nearby, None)
-    done = finish((1,), core, little, flip(little, "core"), basis, *nearby, first_done)
+    done = finish((0, 2), [1 - core], [after(other, gram)], basis, *nearby, done)
+    gram = after(gram, *done) + flip(gram, "xl")
+    done = finish((1,), [core, 1 - core], [little, flip(little, "core")], basis, *nearby, done)
     new_weights, new_first, new_second = done
-    gram = after(gram, *first_done) + flip(gram, "xl")
     sumsq = jnp.einsum("lrr->l", gram)
     factor = jnp.sqrt(jnp.float32(rank)) / (2.0 * jnp.sqrt(sumsq + 1e-06))
     scaled = refresh * factor[:, None, None]

time: 144 us -> 139 us (0.965)
  waiting for transfers between devices: 51.3 us -> 40.7 us
  starting transfers between devices: 57.9 us -> 61.4 us
  Pallas kernels: 13.3 us -> 15.6 us
    all_to_all x3, waiting for transfers between devices: 24 us -> 19.6 us  [exchange(): return lax.all_to_all(parts, axis, split_axis=0, concat_axis=0)]
    ppermute x15, waiting for transfers between devices: 17.1 us -> 13.6 us  [flip(): return lax.ppermute(x, axis, [(i, i ^ bit) for i in range(n)])]
    ppermute x15, starting transfers between devices: 23.1 us -> 26.1 us  [flip(): return lax.ppermute(x, axis, [(i, i ^ bit) for i in range(n)])]
    ppermute x12, waiting for transfers between devices: 10.2 us -> 7.41 us  [scatter(): lax.ppermute(parts[k], axis, [(i, (i + k) % n) for i in range(n)])]
    pallas_call x2 -> x3, Pallas kernels: 13.3 us -> 15.6 us  [finish(): pl.pallas_call(functools.partial(finish_kernel, count), grid_spec=pltpu.P...]
  transfers between devices with their start and end apart: 33 -> 33, of which waited for: 14 -> 11; matrix products, arithmetic and copies ran while one was open for 10% -> 10% of each run, Pallas kernels for 9% -> 11%
where the time goes in v6:
time: 139 us; the launch traced here: 138 us
  starting transfers between devices  61.4 us (44%)
  waiting for transfers between devices  40.7 us (29%)
  Pallas kernels  15.6 us (11%)
  local copies, waits for them, and re-layouts  9.03 us (6%)
  other arithmetic  8.51 us (6%)
  matrix products  1.84 us (1%)
    ppermute x15, starting transfers between devices, flip(): return lax.ppermute(x, axis, [(i, i ^ bit) for i in range(n)])  26.1 us
    all_to_all x3, waiting for transfers between devices, exchange(): return lax.all_to_all(parts, axis, split_axis=0, concat_axis=0)  19.6 us
    ppermute x12, starting transfers between devices, scatter(): lax.ppermute(parts[k], axis, [(i, (i + k) % n) for i in range(n)])  16.3 us
    pallas_call x3, Pallas kernels, finish(): pl.pallas_call(functools.partial(finish_kernel, count), grid_spec=pltpu.P...  15.6 us
    all_to_all x3, starting transfers between devices, exchange(): return lax.all_to_all(parts, axis, split_axis=0, concat_axis=0)  14.2 us
    ppermute x15, waiting for transfers between devices, flip(): return lax.ppermute(x, axis, [(i, i ^ bit) for i in range(n)])  13.6 us
    ppermute x12, waiting for transfers between devices, scatter(): lax.ppermute(parts[k], axis, [(i, (i + k) % n) for i in range(n)])  7.41 us
    ppermute x3, starting transfers between devices, around(): lax.ppermute(x, axis, [(i, (i + k) % n) for i in range(n)])  4.88 us
  transfers between devices with their start and end apart: 33, of which 11 were waited for; matrix products, arithmetic and copies ran while one was open for 10% of the time, Pallas kernels for 11%

profile of v6, /device:TPU:1, one launch (start us, length us, event | category | flops | bytes accessed | tf_op | source)
XLA Modules:
  0.0 138.3 jit_solution(10613788825650986827)
XLA Ops:
  0.6 1.2 dynamic-slice_bitcast_fusion
  1.8 3.3 %collective-permute-start = (f32[2,192,512]{2,1,0:T(8,128)S(1)}, f32[2,192,512]{2,1,0:T(8,128)S(1)}, u32[]{:S(2)}, u32[]{:S(2)}) collective-permute-start(f32[2,192,512]{2,1,0:T(8,128)S(1)} %dynamic-slice_bitcast_fusion), channel_id=1, source_target_pairs={{0,2},{2,0},{1,3},{3,1},{4,6},{6,4},{5,7},{7,5},{8,10},{10,8},{9,1... | collective-permute-start | bytes 2359304 | tf_op jit(solution)/shard_map/ppermute | solution.py:22
  5.2 1.2 constant_dynamic-slice_fusion.15
  6.5 0.6 collective-permute-done
  7.1 1.3 dynamic-slice_add_fusion.2
  8.3 0.9 dynamic-slice_bitcast_fusion.7
  9.2 1.2 constant_dynamic-slice_fusion.14
  10.4 0.5 collective-permute-start.2
  10.9 2.2 %collective-permute-start.5 = (f32[128,384]{0,1:T(8,128)}, f32[128,384]{0,1:T(8,128)}, u32[]{:S(2)}, u32[]{:S(2)}) collective-permute-start(f32[128,384]{0,1:T(8,128)} %get-tuple-element.83), channel_id=1, source_target_pairs={{0,16},{8,24},{16,0},{24,8},{1,17},{9,25},{17,1},{25,9},{2,18},{10... | collective-permute-start | bytes 589832 | tf_op jit(solution)/shard_map/ppermute | solution.py:42
  13.0 1.1 collective-permute-start.6
  14.1 1.3 dynamic-slice_add_fusion.1
  15.5 2.8 %collective-permute-start.7 = (f32[256,384]{0,1:T(8,128)S(1)}, f32[256,384]{0,1:T(8,128)S(1)}, u32[]{:S(2)}, u32[]{:S(2)}) collective-permute-start(f32[256,384]{0,1:T(8,128)S(1)} %get-tuple-element.80), channel_id=1, source_target_pairs={{0,4},{4,0},{1,5},{5,1},{2,6},{6,2},{3,7},{7,3},{8,12},{12,8},{9,1... | collective-permute-start | bytes 1179656 | tf_op jit(solution)/shard_map/ppermute | solution.py:42
  18.3 1.3 dynamic-slice_add_fusion
  19.6 0.1 dynamic-slice_bitcast_fusion.3
  19.8 1.4 %collective-permute-start.8 = (f32[128,384]{0,1:T(8,128)S(1)}, f32[128,384]{0,1:T(8,128)S(1)}, u32[]{:S(2)}, u32[]{:S(2)}) collective-permute-start(f32[128,384]{0,1:T(8,128)S(1)} %get-tuple-element.78), channel_id=1, source_target_pairs={{0,8},{8,16},{16,24},{24,0},{1,9},{9,17},{17,25},{25,1},{2,10},{10... | collective-permute-start | bytes 589832 | tf_op jit(solution)/shard_map/ppermute | solution.py:42
  21.3 1.2 collective-permute-done.5
  22.5 1.1 collective-permute-start.9
  23.5 1.2 add_add_fusion.2
  24.7 0.2 constant_dynamic-slice_fusion.6
  24.9 2.1 %collective-permute-start.11 = (f32[64,384]{0,1:T(8,128)S(1)}, f32[64,384]{0,1:T(8,128)S(1)}, u32[]{:S(2)}, u32[]{:S(2)}) collective-permute-start(f32[64,384]{0,1:T(8,128)S(1)} %get-tuple-element.106), channel_id=1, source_target_pairs={{0,4},{4,0},{1,5},{5,1},{2,6},{6,2},{3,7},{7,3},{8,12},{12,8},{9,1... | collective-permute-start | bytes 294920 | tf_op jit(solution)/shard_map/ppermute | solution.py:42
  27.1 0.3 constant_dynamic-slice_fusion.4
  27.3 0.1 collective-permute-start.13
  27.5 1.4 constant_dynamic-slice_fusion.10
  29.3 3.1 %collective-permute-start.14 = (f32[64,384]{0,1:T(8,128)S(1)}, f32[64,384]{0,1:T(8,128)S(1)}, u32[]{:S(2)}, u32[]{:S(2)}) collective-permute-start(f32[64,384]{0,1:T(8,128)S(1)} %get-tuple-element.94), channel_id=1, source_target_pairs={{0,16},{8,24},{16,0},{24,8},{1,17},{9,25},{17,1},{25,9},{2,18},{10... | collective-permute-start | bytes 294920 | tf_op jit(solution)/shard_map/ppermute | solution.py:42
  32.4 1.6 %collective-permute-start.15 = (f32[64,384]{0,1:T(8,128)S(1)}, f32[64,384]{0,1:T(8,128)S(1)}, u32[]{:S(2)}, u32[]{:S(2)}) collective-permute-start(f32[64,384]{0,1:T(8,128)S(1)} %get-tuple-element.93), channel_id=1, source_target_pairs={{0,24},{8,0},{16,8},{24,16},{1,25},{9,1},{17,9},{25,17},{2,26},{10... | collective-permute-start | bytes 294920 | tf_op jit(solution)/shard_map/ppermute | solution.py:42
  34.0 0.2 constant_dynamic-slice_fusion
  34.2 0.7 collective-permute-start.12
  34.9 6.1 %collective-permute-done.13 = f32[64,384]{0,1:T(8,128)S(1)} collective-permute-done((f32[64,384]{0,1:T(8,128)S(1)}, f32[64,384]{0,1:T(8,128)S(1)}, u32[]{:S(2)}, u32[]{:S(2)}) %collective-permute-start.13) | collective-permute-done | bytes 98336 | tf_op jit(solution)/shard_map/ppermute | solution.py:42
  41.2 0.1 copy.47
  41.5 0.7 pad_maximum_fusion.3
  42.2 7.1 %all-to-all-start = ((f32[8,24,384]{2,1,0:T(8,128)}), f32[8,24,384]{2,1,0:T(8,128)S(1)}, u32[]{:S(2)}, u32[]{:S(2)}) async-start(f32[8,24,384]{2,1,0:T(8,128)} %pad_maximum_fusion.3), calls=%async_computation | async-start | bytes 589824 | tf_op jit(solution)/shard_map/all_to_all | solution.py:73
  49.4 0.8 collective-permute-start.3
  50.3 2.1 %collective-permute-done.3 = f32[2,24,128]{2,1,0:T(8,128)S(1)} collective-permute-done((f32[2,24,128]{2,1,0:T(8,128)S(1)}, f32[2,24,128]{2,1,0:T(8,128)S(1)}, u32[]{:S(2)}, u32[]{:S(2)}) %collective-permute-start.3) | collective-permute-done | bytes 24608 | tf_op jit(solution)/shard_map/ppermute | solution.py:22
  52.5 6.6 %all-to-all-done = f32[8,24,384]{2,1,0:T(8,128)S(1)} async-done(((f32[8,24,384]{2,1,0:T(8,128)}), f32[8,24,384]{2,1,0:T(8,128)S(1)}, u32[]{:S(2)}, u32[]{:S(2)}) %all-to-all-start) | async-done | bytes 294944 | tf_op jit(solution)/shard_map/all_to_all | solution.py:73
  59.2 0.3 fusion.2
  59.5 0.8 collective-permute-start.16
  60.3 2.2 %collective-permute-done.16 = f32[2,24,128]{2,1,0:T(8,128)S(1)} collective-permute-done((f32[2,24,128]{2,1,0:T(8,128)S(1)}, f32[2,24,128]{2,1,0:T(8,128)S(1)}, u32[]{:S(2)}, u32[]{:S(2)}) %collective-permute-start.16) | collective-permute-done | bytes 24608 | tf_op jit(solution)/shard_map/ppermute | solution.py:22
  62.7 0.5 fusion.7
  63.4 0.8 maximum_maximum_fusion
  64.2 3.5 %all-to-all-start.1 = ((f32[8,40,384]{2,1,0:T(8,128)}), f32[8,40,384]{2,1,0:T(8,128)S(1)}, u32[]{:S(2)}, u32[]{:S(2)}) async-start(f32[8,40,384]{2,1,0:T(8,128)} %maximum_maximum_fusion), calls=%async_computation.1 | async-start | bytes 983040 | tf_op jit(solution)/shard_map/all_to_all | solution.py:73
  67.8 11.7 %all-to-all-done.1 = f32[8,40,384]{2,1,0:T(8,128)S(1)} async-done(((f32[8,40,384]{2,1,0:T(8,128)}), f32[8,40,384]{2,1,0:T(8,128)S(1)}, u32[]{:S(2)}, u32[]{:S(2)}) %all-to-all-start.1) | async-done | bytes 491552 | tf_op jit(solution)/shard_map/all_to_all | solution.py:73
  79.5 2.7 %collective-permute-start.17 = (f32[128,384]{1,0:T(8,128)S(1)}, f32[128,384]{1,0:T(8,128)S(1)}, u32[]{:S(2)}, u32[]{:S(2)}) collective-permute-start(f32[128,384]{1,0:T(8,128)S(1)} %bitcast.118), channel_id=1, source_target_pairs={{0,4},{4,0},{1,5},{5,1},{2,6},{6,2},{3,7},{7,3},{8,12},{12,8},{9,1... | collective-permute-start | bytes 589832 | tf_op jit(solution)/shard_map/ppermute | solution.py:22
  82.2 0.6 collective-permute-start.18
  82.8 4.3 %collective-permute-start.19 = (f32[80,384]{1,0:T(8,128)S(1)}, f32[80,384]{1,0:T(8,128)S(1)}, u32[]{:S(2)}, u32[]{:S(2)}) collective-permute-start(f32[80,384]{1,0:T(8,128)S(1)} %pad_maximum_fusion.6), channel_id=1, source_target_pairs={{0,16},{8,24},{16,0},{24,8},{1,17},{9,25},{17,1},{25,9},{2,18},{10... | collective-permute-start | bytes 368648 | tf_op jit(solution)/shard_map/ppermute | solution.py:61
  87.1 1.2 broadcast_in_dim.35
  88.4 3.6 %all-to-all-start.2 = ((f32[4,256,384]{2,1,0:T(8,128)}), f32[4,256,384]{2,1,0:T(8,128)S(1)}, u32[]{:S(2)}, u32[]{:S(2)}) async-start(f32[4,256,384]{2,1,0:T(8,128)} %broadcast_in_dim.35), calls=%async_computation.2 | async-start | bytes 3145728 | tf_op jit(solution)/shard_map/all_to_all | solution.py:73
  92.1 2.5 %collective-permute-start.24 = (f32[16,384]{1,0:T(8,128)S(1)}, f32[16,384]{1,0:T(8,128)S(1)}, u32[]{:S(2)}, u32[]{:S(2)}) collective-permute-start(f32[16,384]{1,0:T(8,128)S(1)} %slice_reduce_fusion.1), channel_id=1, source_target_pairs={{0,4},{4,0},{1,5},{5,1},{2,6},{6,2},{3,7},{7,3},{8,12},{12,8},{9,1... | collective-permute-start | bytes 73736 | tf_op jit(solution)/shard_map/ppermute | solution.py:22
  94.7 1.8 %collective-permute-done.24 = f32[16,384]{1,0:T(8,128)S(1)} collective-permute-done((f32[16,384]{1,0:T(8,128)S(1)}, f32[16,384]{1,0:T(8,128)S(1)}, u32[]{:S(2)}, u32[]{:S(2)}) %collective-permute-start.24) | collective-permute-done | bytes 24608 | tf_op jit(solution)/shard_map/ppermute | solution.py:22
  96.5 2.6 %collective-permute-start.21 = (f32[256,384]{1,0:T(8,128)S(1)}, f32[256,384]{1,0:T(8,128)S(1)}, u32[]{:S(2)}, u32[]{:S(2)}) collective-permute-start(f32[256,384]{1,0:T(8,128)S(1)} %bitcast.113), channel_id=1, source_target_pairs={{0,4},{4,0},{1,5},{5,1},{2,6},{6,2},{3,7},{7,3},{8,12},{12,8},{9,1... | collective-permute-start | bytes 1179656 | tf_op jit(solution)/shard_map/ppermute | solution.py:22
  99.1 3.9 %collective-permute-done.25 = f32[16,384]{1,0:T(8,128)S(1)} collective-permute-done((f32[16,384]{1,0:T(8,128)S(1)}, f32[16,384]{1,0:T(8,128)S(1)}, u32[]{:S(2)}, u32[]{:S(2)}) %collective-permute-start.25) | collective-permute-done | bytes 24608 | tf_op jit(solution)/shard_map/ppermute | solution.py:22
  103.0 1.1 collective-permute-start.26
  104.2 3.1 %collective-permute-done.26 = f32[32,384]{1,0:T(8,128)S(1)} collective-permute-done((f32[32,384]{1,0:T(8,128)S(1)}, f32[32,384]{1,0:T(8,128)S(1)}, u32[]{:S(2)}, u32[]{:S(2)}) %collective-permute-start.26) | collective-permute-done | bytes 49184 | tf_op jit(solution)/shard_map/ppermute | solution.py:22
  107.3 1.3 all-to-all-done.2
  108.6 10.5 %collective-permute-start.23 = (f32[64,2,8,384]{3,2,1,0:T(8,128)S(1)}, f32[64,2,8,384]{3,2,1,0:T(8,128)}, u32[]{:S(2)}, u32[]{:S(2)}) collective-permute-start(f32[64,2,8,384]{3,2,1,0:T(8,128)S(1)} %bitcast.99), channel_id=1, source_target_pairs={{0,2},{2,0},{1,3},{3,1},{4,6},{6,4},{5,7},{7,5},{8,10},{10,8},{9,1... | collective-permute-start | bytes 4718600 | tf_op jit(solution)/shard_map/ppermute | solution.py:22
  119.3 4.9 %finish.3 = (f32[4,192,1536]{2,1,0:T(8,128)}, f32[4,64,1536]{2,1,0:T(8,128)}, f32[4,64,1536]{2,1,0:T(8,128)}) custom-call(s32[1]{0:T(128)} %bitcast.refs_0_, f32[64,2,8,384]{3,2,1,0:T(8,128)S(1)} %bitcast.100, f32[4,192,128]{2,1,0:T(8,128)S(1)} %copy-done, f32[4,192,1536]{2,1,0:T(8,128)} %refs_4_.5, f32[4,64,1536]{2,1,0:T(8,128)} %refs_5_.5, ...), custom_call_target="tpu_custom_call" | custom-call | flops 603979776 | bytes 5242880 | tf_op jit(solution)/shard_map/finish/pallas_call | solution.py:113
  124.4 0.7 fusion.22
  125.0 0.3 collective-permute-start.28
  125.4 0.6 collective-permute-start.22
  126.0 5.3 %finish.4 = (f32[4,192,1536]{2,1,0:T(8,128)}, f32[4,64,1536]{2,1,0:T(8,128)}, f32[4,64,1536]{2,1,0:T(8,128)}) custom-call(s32[1]{0:T(128)} %bitcast.1.refs_0_, f32[64,2,8,384]{3,2,1,0:T(8,128)} %collective-permute-done.23.refs_1_, f32[4,192,128]{2,1,0:T(8,128)S(1)} %copy-done, ...), custom_call_target="tpu_custom_call", output_to_operand_aliasing={{0}: (6, {}), {1}: (7, {}), {2}: (8, {})} | custom-call | flops 603979776 | bytes 5242880 | tf_op jit(solution)/shard_map/finish/pallas_call | solution.py:113
  131.3 0.1 select_reduce_fusion
  131.4 0.4 fusion
  131.9 0.1 collective-permute-start.29
  132.1 5.4 %finish.5 = (f32[4,192,1536]{2,1,0:T(8,128)}, f32[4,64,1536]{2,1,0:T(8,128)}, f32[4,64,1536]{2,1,0:T(8,128)}) custom-call(s32[2]{0:T(128)S(1)} %pad_add_fusion.refs_0_, f32[64,1,8,384]{3,2,1,0:T(8,128)S(1)} %bitcast.102, f32[64,1,8,384]{3,2,1,0:T(8,128)S(1)} %collective-permute-done.22.refs_2_, ...), custom_call_target="tpu_custom_call", output_to_operand_aliasing={{0}: (7, {}), {1}: (8, {}), {2}: (9, {})} | custom-call | flops 603979776 | bytes 5242880 | tf_op jit(solution)/shard_map/finish/pallas_call | solution.py:113
  137.5 0.8 pad_maximum_fusion.2
  (87 shorter events, 2.6 us)
Async XLA Ops:
  1.8 5.2 %collective-permute-start = (f32[2,192,512]{2,1,0:T(8,128)S(1)}, f32[2,192,512]{2,1,0:T(8,128)S(1)}, u32[]{:S(2)}, u32[]{:S(2)}) collective-permute-start(f32[2,192,512]{2,1,0:T(8,128)S(1)} %dynamic-slice_bitcast_fusion), channel_id=1, source_target_pairs={{0,2},{2,0},{1,3},{3,1},{4,6},{6,4},{5,7},{7,5},{8,10},{10,8},{9,1... | collective-permute-start | bytes 2359304 | tf_op jit(solution)/shard_map/ppermute | solution.py:22
  6.3 7.8 %collective-permute-start.1 = (f32[2,192,512]{2,1,0:T(8,128)S(1)}, f32[2,192,512]{2,1,0:T(8,128)S(1)}, u32[]{:S(2)}, u32[]{:S(2)}) collective-permute-start(f32[2,192,512]{2,1,0:T(8,128)S(1)} %constant_dynamic-slice_fusion.15), channel_id=1, source_target_pairs={{0,2},{2,0},{1,3},{3,1},{4,6},{6,4},{5,7},{7,5},{8,10},{10,8},{9,1... | collective-permute-start | bytes 2359304 | tf_op jit(solution)/shard_map/ppermute | solution.py:22
  10.4 7.9 %collective-permute-start.2 = (f32[2,192,512]{2,1,0:T(8,128)S(1)}, f32[2,192,512]{2,1,0:T(8,128)S(1)}, u32[]{:S(2)}, u32[]{:S(2)}) collective-permute-start(f32[2,192,512]{2,1,0:T(8,128)S(1)} %constant_dynamic-slice_fusion.14), channel_id=1, source_target_pairs={{0,2},{2,0},{1,3},{3,1},{4,6},{6,4},{5,7},{7,5},{8,10},{10,8},{9,1... | collective-permute-start | bytes 2359304 | tf_op jit(solution)/shard_map/ppermute | solution.py:22
  10.9 8.9 %collective-permute-start.4 = (f32[128,384]{0,1:T(8,128)}, f32[128,384]{0,1:T(8,128)}, u32[]{:S(2)}, u32[]{:S(2)}) collective-permute-start(f32[128,384]{0,1:T(8,128)} %get-tuple-element.84), channel_id=1, source_target_pairs={{0,8},{8,16},{16,24},{24,0},{1,9},{9,17},{17,25},{25,1},{2,10},{10... | collective-permute-start | bytes 589832 | tf_op jit(solution)/shard_map/ppermute | solution.py:42
  10.9 11.6 %collective-permute-start.5 = (f32[128,384]{0,1:T(8,128)}, f32[128,384]{0,1:T(8,128)}, u32[]{:S(2)}, u32[]{:S(2)}) collective-permute-start(f32[128,384]{0,1:T(8,128)} %get-tuple-element.83), channel_id=1, source_target_pairs={{0,16},{8,24},{16,0},{24,8},{1,17},{9,25},{17,1},{25,9},{2,18},{10... | collective-permute-start | bytes 589832 | tf_op jit(solution)/shard_map/ppermute | solution.py:42
  13.0 10.5 %collective-permute-start.6 = (f32[128,384]{0,1:T(8,128)S(1)}, f32[128,384]{0,1:T(8,128)}, u32[]{:S(2)}, u32[]{:S(2)}) collective-permute-start(f32[128,384]{0,1:T(8,128)S(1)} %get-tuple-element.82), channel_id=1, source_target_pairs={{0,24},{8,0},{16,8},{24,16},{1,25},{9,1},{17,9},{25,17},{2,26},{10... | collective-permute-start | bytes 589832 | tf_op jit(solution)/shard_map/ppermute | solution.py:42
  15.5 11.5 %collective-permute-start.7 = (f32[256,384]{0,1:T(8,128)S(1)}, f32[256,384]{0,1:T(8,128)S(1)}, u32[]{:S(2)}, u32[]{:S(2)}) collective-permute-start(f32[256,384]{0,1:T(8,128)S(1)} %get-tuple-element.80), channel_id=1, source_target_pairs={{0,4},{4,0},{1,5},{5,1},{2,6},{6,2},{3,7},{7,3},{8,12},{12,8},{9,1... | collective-permute-start | bytes 1179656 | tf_op jit(solution)/shard_map/ppermute | solution.py:42
  19.7 9.6 %collective-permute-start.10 = (f32[128,384]{0,1:T(8,128)S(1)}, f32[128,384]{0,1:T(8,128)S(1)}, u32[]{:S(2)}, u32[]{:S(2)}) collective-permute-start(f32[128,384]{0,1:T(8,128)S(1)} %get-tuple-element.76), channel_id=1, source_target_pairs={{0,24},{8,0},{16,8},{24,16},{1,25},{9,1},{17,9},{25,17},{2,26},{10... | collective-permute-start | bytes 589832 | tf_op jit(solution)/shard_map/ppermute | solution.py:42
  19.8 12.6 %collective-permute-start.8 = (f32[128,384]{0,1:T(8,128)S(1)}, f32[128,384]{0,1:T(8,128)S(1)}, u32[]{:S(2)}, u32[]{:S(2)}) collective-permute-start(f32[128,384]{0,1:T(8,128)S(1)} %get-tuple-element.78), channel_id=1, source_target_pairs={{0,8},{8,16},{16,24},{24,0},{1,9},{9,17},{17,25},{25,1},{2,10},{10... | collective-permute-start | bytes 589832 | tf_op jit(solution)/shard_map/ppermute | solution.py:42
  22.5 11.5 %collective-permute-start.9 = (f32[128,384]{0,1:T(8,128)S(1)}, f32[128,384]{0,1:T(8,128)S(1)}, u32[]{:S(2)}, u32[]{:S(2)}) collective-permute-start(f32[128,384]{0,1:T(8,128)S(1)} %get-tuple-element.77), channel_id=1, source_target_pairs={{0,16},{8,24},{16,0},{24,8},{1,17},{9,25},{17,1},{25,9},{2,18},{10... | collective-permute-start | bytes 589832 | tf_op jit(solution)/shard_map/ppermute | solution.py:42
  24.9 16.2 %collective-permute-start.11 = (f32[64,384]{0,1:T(8,128)S(1)}, f32[64,384]{0,1:T(8,128)S(1)}, u32[]{:S(2)}, u32[]{:S(2)}) collective-permute-start(f32[64,384]{0,1:T(8,128)S(1)} %get-tuple-element.106), channel_id=1, source_target_pairs={{0,4},{4,0},{1,5},{5,1},{2,6},{6,2},{3,7},{7,3},{8,12},{12,8},{9,1... | collective-permute-start | bytes 294920 | tf_op jit(solution)/shard_map/ppermute | solution.py:42
  27.3 13.7 %collective-permute-start.13 = (f32[64,384]{0,1:T(8,128)S(1)}, f32[64,384]{0,1:T(8,128)S(1)}, u32[]{:S(2)}, u32[]{:S(2)}) collective-permute-start(f32[64,384]{0,1:T(8,128)S(1)} %get-tuple-element.92), channel_id=1, source_target_pairs={{0,8},{8,16},{16,24},{24,0},{1,9},{9,17},{17,25},{25,1},{2,10},{10... | collective-permute-start | bytes 294920 | tf_op jit(solution)/shard_map/ppermute | solution.py:42
  29.3 11.7 %collective-permute-start.14 = (f32[64,384]{0,1:T(8,128)S(1)}, f32[64,384]{0,1:T(8,128)S(1)}, u32[]{:S(2)}, u32[]{:S(2)}) collective-permute-start(f32[64,384]{0,1:T(8,128)S(1)} %get-tuple-element.94), channel_id=1, source_target_pairs={{0,16},{8,24},{16,0},{24,8},{1,17},{9,25},{17,1},{25,9},{2,18},{10... | collective-permute-start | bytes 294920 | tf_op jit(solution)/shard_map/ppermute | solution.py:42
  32.4 8.6 %collective-permute-start.15 = (f32[64,384]{0,1:T(8,128)S(1)}, f32[64,384]{0,1:T(8,128)S(1)}, u32[]{:S(2)}, u32[]{:S(2)}) collective-permute-start(f32[64,384]{0,1:T(8,128)S(1)} %get-tuple-element.93), channel_id=1, source_target_pairs={{0,24},{8,0},{16,8},{24,16},{1,25},{9,1},{17,9},{25,17},{2,26},{10... | collective-permute-start | bytes 294920 | tf_op jit(solution)/shard_map/ppermute | solution.py:42
  34.2 7.2 %collective-permute-start.12 = (f32[64,384]{0,1:T(8,128)S(1)}, f32[64,384]{0,1:T(8,128)S(1)}, u32[]{:S(2)}, u32[]{:S(2)}) collective-permute-start(f32[64,384]{0,1:T(8,128)S(1)} %get-tuple-element.104), channel_id=1, source_target_pairs={{0,4},{4,0},{1,5},{5,1},{2,6},{6,2},{3,7},{7,3},{8,12},{12,8},{9,1... | collective-permute-start | bytes 294920 | tf_op jit(solution)/shard_map/ppermute | solution.py:42
  41.2 18.0 %copy-start = (f32[4,192,128]{2,1,0:T(8,128)S(1)}, f32[4,192,128]{2,1,0:T(8,128)}, u32[]{:S(2)}) copy-start(f32[4,192,128]{2,1,0:T(8,128)} %refs_3_.5) | copy-start | bytes 1179652
  42.2 16.8 %all-to-all-start = ((f32[8,24,384]{2,1,0:T(8,128)}), f32[8,24,384]{2,1,0:T(8,128)S(1)}, u32[]{:S(2)}, u32[]{:S(2)}) async-start(f32[8,24,384]{2,1,0:T(8,128)} %pad_maximum_fusion.3), calls=%async_computation | async-start | bytes 589824 | tf_op jit(solution)/shard_map/all_to_all | solution.py:73
  49.4 2.9 %collective-permute-start.3 = (f32[2,24,128]{2,1,0:T(8,128)S(1)}, f32[2,24,128]{2,1,0:T(8,128)S(1)}, u32[]{:S(2)}, u32[]{:S(2)}) collective-permute-start(f32[2,24,128]{2,1,0:T(8,128)S(1)} %pad_maximum_fusion.10), channel_id=1, source_target_pairs={{0,1},{1,0},{2,3},{3,2},{4,5},{5,4},{6,7},{7,6},{8,9},{9,8},{10,11... | collective-permute-start | bytes 73736 | tf_op jit(solution)/shard_map/ppermute | solution.py:22
  59.5 3.0 %collective-permute-start.16 = (f32[2,24,128]{2,1,0:T(8,128)S(1)}, f32[2,24,128]{2,1,0:T(8,128)S(1)}, u32[]{:S(2)}, u32[]{:S(2)}) collective-permute-start(f32[2,24,128]{2,1,0:T(8,128)S(1)} %fusion.2), channel_id=1, source_target_pairs={{0,1},{1,0},{2,3},{3,2},{4,5},{5,4},{6,7},{7,6},{8,9},{9,8},{10,11... | collective-permute-start | bytes 73736 | tf_op jit(solution)/shard_map/ppermute | solution.py:22
  64.2 15.3 %all-to-all-start.1 = ((f32[8,40,384]{2,1,0:T(8,128)}), f32[8,40,384]{2,1,0:T(8,128)S(1)}, u32[]{:S(2)}, u32[]{:S(2)}) async-start(f32[8,40,384]{2,1,0:T(8,128)} %maximum_maximum_fusion), calls=%async_computation.1 | async-start | bytes 983040 | tf_op jit(solution)/shard_map/all_to_all | solution.py:73
  79.5 7.6 %collective-permute-start.17 = (f32[128,384]{1,0:T(8,128)S(1)}, f32[128,384]{1,0:T(8,128)S(1)}, u32[]{:S(2)}, u32[]{:S(2)}) collective-permute-start(f32[128,384]{1,0:T(8,128)S(1)} %bitcast.118), channel_id=1, source_target_pairs={{0,4},{4,0},{1,5},{5,1},{2,6},{6,2},{3,7},{7,3},{8,12},{12,8},{9,1... | collective-permute-start | bytes 589832 | tf_op jit(solution)/shard_map/ppermute | solution.py:22
  82.2 9.8 %collective-permute-start.18 = (f32[80,384]{1,0:T(8,128)S(1)}, f32[80,384]{1,0:T(8,128)S(1)}, u32[]{:S(2)}, u32[]{:S(2)}) collective-permute-start(f32[80,384]{1,0:T(8,128)S(1)} %pad_maximum_fusion.6), channel_id=1, source_target_pairs={{0,8},{8,16},{16,24},{24,0},{1,9},{9,17},{17,25},{25,1},{2,10},{10... | collective-permute-start | bytes 368648 | tf_op jit(solution)/shard_map/ppermute | solution.py:61
  82.8 9.3 %collective-permute-start.19 = (f32[80,384]{1,0:T(8,128)S(1)}, f32[80,384]{1,0:T(8,128)S(1)}, u32[]{:S(2)}, u32[]{:S(2)}) collective-permute-start(f32[80,384]{1,0:T(8,128)S(1)} %pad_maximum_fusion.6), channel_id=1, source_target_pairs={{0,16},{8,24},{16,0},{24,8},{1,17},{9,25},{17,1},{25,9},{2,18},{10... | collective-permute-start | bytes 368648 | tf_op jit(solution)/shard_map/ppermute | solution.py:61
  87.1 5.0 %collective-permute-start.20 = (f32[80,384]{1,0:T(8,128)S(1)}, f32[80,384]{1,0:T(8,128)S(1)}, u32[]{:S(2)}, u32[]{:S(2)}) collective-permute-start(f32[80,384]{1,0:T(8,128)S(1)} %pad_maximum_fusion.6), channel_id=1, source_target_pairs={{0,24},{8,0},{16,8},{24,16},{1,25},{9,1},{17,9},{25,17},{2,26},{10... | collective-permute-start | bytes 368648 | tf_op jit(solution)/shard_map/ppermute | solution.py:61
  88.4 20.2 %all-to-all-start.2 = ((f32[4,256,384]{2,1,0:T(8,128)}), f32[4,256,384]{2,1,0:T(8,128)S(1)}, u32[]{:S(2)}, u32[]{:S(2)}) async-start(f32[4,256,384]{2,1,0:T(8,128)} %broadcast_in_dim.35), calls=%async_computation.2 | async-start | bytes 3145728 | tf_op jit(solution)/shard_map/all_to_all | solution.py:73
  92.1 4.3 %collective-permute-start.24 = (f32[16,384]{1,0:T(8,128)S(1)}, f32[16,384]{1,0:T(8,128)S(1)}, u32[]{:S(2)}, u32[]{:S(2)}) collective-permute-start(f32[16,384]{1,0:T(8,128)S(1)} %slice_reduce_fusion.1), channel_id=1, source_target_pairs={{0,4},{4,0},{1,5},{5,1},{2,6},{6,2},{3,7},{7,3},{8,12},{12,8},{9,1... | collective-permute-start | bytes 73736 | tf_op jit(solution)/shard_map/ppermute | solution.py:22
  96.4 6.6 %collective-permute-start.25 = (f32[16,384]{1,0:T(8,128)S(1)}, f32[16,384]{1,0:T(8,128)S(1)}, u32[]{:S(2)}, u32[]{:S(2)}) collective-permute-start(f32[16,384]{1,0:T(8,128)S(1)} %add.303), channel_id=1, source_target_pairs={{0,128},{32,160},{64,192},{96,224},{128,0},{160,32},{192,64},{224,... | collective-permute-start | bytes 73736 | tf_op jit(solution)/shard_map/ppermute | solution.py:22
  96.5 22.6 %collective-permute-start.21 = (f32[256,384]{1,0:T(8,128)S(1)}, f32[256,384]{1,0:T(8,128)S(1)}, u32[]{:S(2)}, u32[]{:S(2)}) collective-permute-start(f32[256,384]{1,0:T(8,128)S(1)} %bitcast.113), channel_id=1, source_target_pairs={{0,4},{4,0},{1,5},{5,1},{2,6},{6,2},{3,7},{7,3},{8,12},{12,8},{9,1... | collective-permute-start | bytes 1179656 | tf_op jit(solution)/shard_map/ppermute | solution.py:22
  103.0 4.2 %collective-permute-start.26 = (f32[32,384]{1,0:T(8,128)S(1)}, f32[32,384]{1,0:T(8,128)S(1)}, u32[]{:S(2)}, u32[]{:S(2)}) collective-permute-start(f32[32,384]{1,0:T(8,128)S(1)} %pad_maximum_fusion.8), channel_id=1, source_target_pairs={{0,64},{32,96},{64,0},{96,32},{128,192},{160,224},{192,128},{224,1... | collective-permute-start | bytes 147464 | tf_op jit(solution)/shard_map/ppermute | solution.py:22
  108.6 17.4 %collective-permute-start.23 = (f32[64,2,8,384]{3,2,1,0:T(8,128)S(1)}, f32[64,2,8,384]{3,2,1,0:T(8,128)}, u32[]{:S(2)}, u32[]{:S(2)}) collective-permute-start(f32[64,2,8,384]{3,2,1,0:T(8,128)S(1)} %bitcast.99), channel_id=1, source_target_pairs={{0,2},{2,0},{1,3},{3,1},{4,6},{6,4},{5,7},{7,5},{8,10},{10,8},{9,1... | collective-permute-start | bytes 4718600 | tf_op jit(solution)/shard_map/ppermute | solution.py:22
  119.2 5.0 %collective-permute-start.27 = (f32[64,384]{1,0:T(8,128)S(1)}, f32[64,384]{1,0:T(8,128)S(1)}, u32[]{:S(2)}, u32[]{:S(2)}) collective-permute-start(f32[64,384]{1,0:T(8,128)S(1)} %pad_maximum_fusion.7), channel_id=1, source_target_pairs={{0,32},{32,0},{64,96},{96,64},{128,160},{160,128},{192,224},{224,1... | collective-permute-start | bytes 294920 | tf_op jit(solution)/shard_map/ppermute | solution.py:22
  125.0 6.3 %collective-permute-start.28 = (f32[2,128,128]{2,1,0:T(8,128)S(1)}, f32[2,128,128]{2,1,0:T(8,128)S(1)}, u32[]{:S(2)}, u32[]{:S(2)}) collective-permute-start(f32[2,128,128]{2,1,0:T(8,128)S(1)} %fusion.22), channel_id=1, source_target_pairs={{0,1},{1,0},{2,3},{3,2},{4,5},{5,4},{6,7},{7,6},{8,9},{9,8},{10,11... | collective-permute-start | bytes 393224 | tf_op jit(solution)/shard_map/ppermute | solution.py:22
  125.4 6.7 %collective-permute-start.22 = (f32[64,1,8,384]{3,2,1,0:T(8,128)S(1)}, f32[64,1,8,384]{3,2,1,0:T(8,128)S(1)}, u32[]{:S(2)}, u32[]{:S(2)}) collective-permute-start(f32[64,1,8,384]{3,2,1,0:T(8,128)S(1)} %bitcast.101), channel_id=1, source_target_pairs={{0,2},{2,0},{1,3},{3,1},{4,6},{6,4},{5,7},{7,5},{8,10},{10,8},{9,1... | collective-permute-start | bytes 2359304 | tf_op jit(solution)/shard_map/ppermute | solution.py:22
  131.9 5.6 %collective-permute-start.29 = (f32[2,192,128]{2,1,0:T(8,128)S(1)}, f32[2,192,128]{2,1,0:T(8,128)S(1)}, u32[]{:S(2)}, u32[]{:S(2)}) collective-permute-start(f32[2,192,128]{2,1,0:T(8,128)S(1)} %fusion), channel_id=1, source_target_pairs={{0,2},{2,0},{1,3},{3,1},{4,6},{6,4},{5,7},{7,5},{8,10},{10,8},{9,1... | collective-permute-start | bytes 589832 | tf_op jit(solution)/shard_map/ppermute | solution.py:22

commit v7 on v6

--- a/solution.py
+++ b/solution.py
@@ -77,54 +77,78 @@
     return jnp.broadcast_to(x, (SIZES[axis],) + x.shape)
 
 
-def finish_kernel(count, *refs):
-    sources = refs[1 : 1 + count]
+def finish_kernel(chunks, count, *refs):
+    pairs, *sources = refs[: 1 + count]
     basis, weights, first, second = refs[1 + count : 5 + count]
-    out_weights, out_first, out_second = refs[-3:]
-    rank = basis.shape[2]
-    some = out_weights.shape[2]
-    step = pl.program_id(1)
-    sources = [source[...].reshape(some, -1) for source in sources]
-    x = sources[0] if count == 1 else jnp.where(step < 2, *sources)
-    direction = jnp.where(step % 2 == 0, x[:, :rank], x[:, rank : 2 * rank])
-    update = lax.dot_general(
-        basis[0], direction, (((1,), (1,)), ((), ())), precision=HIGH, preferred_element_type=jnp.float32
-    )
-    out_weights[0] = weights[0] - 0.0125 * update
-    proj = x[:, 2 * rank :].T
-    proj = jnp.where(step % 2 == 0, proj[: rank // 2], proj[rank // 2 :])
-    out_first[0] = 0.9 * first[0] + 0.1 * proj
-    out_second[0] = 0.999 * second[0] + 0.001 * proj * proj
+    outs, (x, w, f, s, x_sem, in_sem, out_sem) = refs[-10:-7], refs[-7:]
+    rank, some = basis.shape[2], w.shape[2]
+    steps = [(h, k, j) for h in range(len(chunks)) for k in range(count) for j in range(2)]
+    loads, reads, writes = [], [], []
+    for i, (h, k, j) in enumerate(steps):
+        if j == 0:
+            loads.append(pltpu.make_async_copy(sources[k].at[:, h], x.at[i // 2], x_sem.at[i // 2]))
+            loads[-1].start()
+        layer, columns = pairs[k] * 2 + j, pl.ds(chunks[h] * some, some)
+        far = [a.at[layer, :, columns] for a in (weights, first, second, *outs)]
+        near = [a.at[i] for a in (w, f, s)]
+        reads.append([pltpu.make_async_copy(far[n], near[n], in_sem.at[i, n]) for n in range(3)])
+        writes.append([pltpu.make_async_copy(near[n], far[3 + n], out_sem.at[i, n]) for n in range(3)])
+        for copy in reads[-1]:
+            copy.start()
+    for i, (h, k, j) in enumerate(steps):
+        if j == 0:
+            loads[i // 2].wait()
+            both = x[i // 2, :, :, 2 * rank :].reshape(some, rank).T
+        for copy in reads[i]:
+            copy.wait()
+        direction = x[i // 2, :, :, j * rank : (j + 1) * rank].reshape(some, rank)
+        update = lax.dot_general(
+            basis[pairs[k] * 2 + j],
+            direction,
+            (((1,), (1,)), ((), ())),
+            precision=HIGH,
+            preferred_element_type=jnp.float32,
+        )
+        w[i] = w[i] - 0.0125 * update
+        proj = both[j * rank // 2 : (j + 1) * rank // 2]
+        f[i] = 0.9 * f[i] + 0.1 * proj
+        s[i] = 0.999 * s[i] + 0.001 * proj * proj
+        for copy in writes[i]:
+            copy.start()
+    for copies_out in writes:
+        for copy in copies_out:
+            copy.wait()
 
 
 def finish(chunks, pairs, sources, basis, weights, first, second, before):
     layers, depth, width = weights.shape
     rank, some = basis.shape[2], width // CHUNKS
-    gap = chunks[-1] - chunks[0]
-    shape = sources[0].shape
-    layer = lambda j, p: p[j // 2] * 2 + j % 2
-    packed = pl.BlockSpec((shape[0], 1) + shape[2:], lambda h, j, p: (0, h, 0, 0))
-    whole = pl.BlockSpec((1, depth, rank), lambda h, j, p: (layer(j, p), 0, 0))
-    tall = pl.BlockSpec((1, depth, some), lambda h, j, p: (layer(j, p), 0, chunks[0] + gap * h))
-    low = pl.BlockSpec((1, first.shape[1], some), lambda h, j, p: (layer(j, p), 0, chunks[0] + gap * h))
+    count = len(sources)
+    steps = 2 * count * len(chunks)
+    far = pl.BlockSpec(memory_space=pl.ANY)
     kept = [] if before is None else list(before)
-    count = len(sources)
-    steps = 2 * count
+    low = pltpu.VMEM((steps, first.shape[1], some), first.dtype)
     return pl.pallas_call(
-        functools.partial(finish_kernel, count),
-        grid_spec=pltpu.PrefetchScalarGridSpec(
-            num_scalar_prefetch=1,
-            grid=(len(chunks), steps),
-            in_specs=[packed] * count + [whole, tall, low, low] + [pl.BlockSpec(memory_space=pl.ANY)] * len(kept),
-            out_specs=[tall, low, low],
-        ),
+        functools.partial(finish_kernel, chunks, count),
+        in_specs=[pl.BlockSpec(memory_space=pltpu.SMEM)]
+        + [far] * count
+        + [pl.BlockSpec(memory_space=pltpu.VMEM)]
+        + [far] * (3 + len(kept)),
+        out_specs=[far] * 3,
         out_shape=[jax.ShapeDtypeStruct(a.shape, a.dtype) for a in (weights, first, second)],
         input_output_aliases={5 + count + i: i for i in range(len(kept))},
+        scratch_shapes=[
+            pltpu.VMEM((steps // 2,) + sources[0].shape[:1] + sources[0].shape[2:], weights.dtype),
+            pltpu.VMEM((steps, depth, some), weights.dtype),
+            low,
+            low,
+            pltpu.SemaphoreType.DMA((steps // 2,)),
+            pltpu.SemaphoreType.DMA((steps, 3)),
+            pltpu.SemaphoreType.DMA((steps, 3)),
+        ],
         compiler_params=pltpu.CompilerParams(vmem_limit_bytes=20 << 20),
         cost_estimate=pl.CostEstimate(
-            flops=12 * steps * depth * rank * some * len(chunks),
-            bytes_accessed=8 * steps * (depth + rank) * some * len(chunks),
-            transcendentals=0,
+            flops=12 * steps * depth * rank * some, bytes_accessed=8 * steps * (depth + rank) * some, transcendentals=0
         ),
         name="finish",
     )(jnp.stack(pairs), *sources, basis, weights, first, second, *kept)

time: 139 us -> 139 us (level)
  transfers between devices with their start and end apart: 33 -> 33, of which waited for: 11 -> 12; matrix products, arithmetic and copies ran while one was open for 10% -> 10% of each run, Pallas kernels for 11% -> 10%
where the time goes in v7:
time: 139 us; the launch traced here: 138 us
  starting transfers between devices  62.2 us (45%)
  waiting for transfers between devices  40.7 us (29%)
  Pallas kernels  14.4 us (10%)
  local copies, waits for them, and re-layouts  9.03 us (6%)
  other arithmetic  8.5 us (6%)
  matrix products  1.84 us (1%)
    ppermute x15, starting transfers between devices, flip(): return lax.ppermute(x, axis, [(i, i ^ bit) for i in range(n)])  26.9 us
    all_to_all x3, waiting for transfers between devices, exchange(): return lax.all_to_all(parts, axis, split_axis=0, concat_axis=0)  19.6 us
    ppermute x12, starting transfers between devices, scatter(): lax.ppermute(parts[k], axis, [(i, (i + k) % n) for i in range(n)])  16.3 us
    pallas_call x3, Pallas kernels, finish(): pl.pallas_call(functools.partial(finish_kernel, chunks, count), in_specs=...  14.4 us
    all_to_all x3, starting transfers between devices, exchange(): return lax.all_to_all(parts, axis, split_axis=0, concat_axis=0)  14.2 us
    ppermute x15, waiting for transfers between devices, flip(): return lax.ppermute(x, axis, [(i, i ^ bit) for i in range(n)])  13.7 us
    ppermute x12, waiting for transfers between devices, scatter(): lax.ppermute(parts[k], axis, [(i, (i + k) % n) for i in range(n)])  7.41 us
    ppermute x3, starting transfers between devices, around(): lax.ppermute(x, axis, [(i, (i + k) % n) for i in range(n)])  4.88 us
  transfers between devices with their start and end apart: 33, of which 12 were waited for; matrix products, arithmetic and copies ran while one was open for 10% of the time, Pallas kernels for 10%

profile of v7, /device:TPU:1, one launch (start us, length us, event | category | flops | bytes accessed | tf_op | source)
XLA Modules:
  0.0 137.9 jit_solution(743193582704337141)
XLA Ops:
  0.6 1.2 dynamic-slice_bitcast_fusion
  1.8 3.3 %collective-permute-start = (f32[2,192,512]{2,1,0:T(8,128)S(1)}, f32[2,192,512]{2,1,0:T(8,128)S(1)}, u32[]{:S(2)}, u32[]{:S(2)}) collective-permute-start(f32[2,192,512]{2,1,0:T(8,128)S(1)} %dynamic-slice_bitcast_fusion), channel_id=1, source_target_pairs={{0,2},{2,0},{1,3},{3,1},{4,6},{6,4},{5,7},{7,5},{8,10},{10,8},{9,1... | collective-permute-start | bytes 2359304 | tf_op jit(solution)/shard_map/ppermute | solution.py:22
  5.2 1.2 constant_dynamic-slice_fusion.15
  6.5 0.6 collective-permute-done
  7.1 1.3 dynamic-slice_add_fusion.2
  8.3 0.9 dynamic-slice_bitcast_fusion.7
  9.2 1.2 constant_dynamic-slice_fusion.14
  10.4 0.5 collective-permute-start.2
  10.9 2.2 %collective-permute-start.5 = (f32[128,384]{0,1:T(8,128)}, f32[128,384]{0,1:T(8,128)}, u32[]{:S(2)}, u32[]{:S(2)}) collective-permute-start(f32[128,384]{0,1:T(8,128)} %get-tuple-element.83), channel_id=1, source_target_pairs={{0,16},{8,24},{16,0},{24,8},{1,17},{9,25},{17,1},{25,9},{2,18},{10... | collective-permute-start | bytes 589832 | tf_op jit(solution)/shard_map/ppermute | solution.py:42
  13.0 1.1 collective-permute-start.6
  14.1 1.3 dynamic-slice_add_fusion.1
  15.5 2.8 %collective-permute-start.7 = (f32[256,384]{0,1:T(8,128)S(1)}, f32[256,384]{0,1:T(8,128)S(1)}, u32[]{:S(2)}, u32[]{:S(2)}) collective-permute-start(f32[256,384]{0,1:T(8,128)S(1)} %get-tuple-element.80), channel_id=1, source_target_pairs={{0,4},{4,0},{1,5},{5,1},{2,6},{6,2},{3,7},{7,3},{8,12},{12,8},{9,1... | collective-permute-start | bytes 1179656 | tf_op jit(solution)/shard_map/ppermute | solution.py:42
  18.3 1.3 dynamic-slice_add_fusion
  19.6 0.1 dynamic-slice_bitcast_fusion.3
  19.8 1.4 %collective-permute-start.8 = (f32[128,384]{0,1:T(8,128)S(1)}, f32[128,384]{0,1:T(8,128)S(1)}, u32[]{:S(2)}, u32[]{:S(2)}) collective-permute-start(f32[128,384]{0,1:T(8,128)S(1)} %get-tuple-element.78), channel_id=1, source_target_pairs={{0,8},{8,16},{16,24},{24,0},{1,9},{9,17},{17,25},{25,1},{2,10},{10... | collective-permute-start | bytes 589832 | tf_op jit(solution)/shard_map/ppermute | solution.py:42
  21.3 1.2 collective-permute-done.5
  22.5 1.1 collective-permute-start.9
  23.5 1.2 add_add_fusion.2
  24.7 0.2 constant_dynamic-slice_fusion.6
  24.9 2.1 %collective-permute-start.11 = (f32[64,384]{0,1:T(8,128)S(1)}, f32[64,384]{0,1:T(8,128)S(1)}, u32[]{:S(2)}, u32[]{:S(2)}) collective-permute-start(f32[64,384]{0,1:T(8,128)S(1)} %get-tuple-element.106), channel_id=1, source_target_pairs={{0,4},{4,0},{1,5},{5,1},{2,6},{6,2},{3,7},{7,3},{8,12},{12,8},{9,1... | collective-permute-start | bytes 294920 | tf_op jit(solution)/shard_map/ppermute | solution.py:42
  27.1 0.3 constant_dynamic-slice_fusion.4
  27.3 0.1 collective-permute-start.13
  27.5 1.4 constant_dynamic-slice_fusion.10
  29.3 3.1 %collective-permute-start.14 = (f32[64,384]{0,1:T(8,128)S(1)}, f32[64,384]{0,1:T(8,128)S(1)}, u32[]{:S(2)}, u32[]{:S(2)}) collective-permute-start(f32[64,384]{0,1:T(8,128)S(1)} %get-tuple-element.94), channel_id=1, source_target_pairs={{0,16},{8,24},{16,0},{24,8},{1,17},{9,25},{17,1},{25,9},{2,18},{10... | collective-permute-start | bytes 294920 | tf_op jit(solution)/shard_map/ppermute | solution.py:42
  32.4 1.6 %collective-permute-start.15 = (f32[64,384]{0,1:T(8,128)S(1)}, f32[64,384]{0,1:T(8,128)S(1)}, u32[]{:S(2)}, u32[]{:S(2)}) collective-permute-start(f32[64,384]{0,1:T(8,128)S(1)} %get-tuple-element.93), channel_id=1, source_target_pairs={{0,24},{8,0},{16,8},{24,16},{1,25},{9,1},{17,9},{25,17},{2,26},{10... | collective-permute-start | bytes 294920 | tf_op jit(solution)/shard_map/ppermute | solution.py:42
  34.0 0.2 constant_dynamic-slice_fusion
  34.2 0.7 collective-permute-start.12
  34.9 6.1 %collective-permute-done.13 = f32[64,384]{0,1:T(8,128)S(1)} collective-permute-done((f32[64,384]{0,1:T(8,128)S(1)}, f32[64,384]{0,1:T(8,128)S(1)}, u32[]{:S(2)}, u32[]{:S(2)}) %collective-permute-start.13) | collective-permute-done | bytes 98336 | tf_op jit(solution)/shard_map/ppermute | solution.py:42
  41.2 0.1 copy.47
  41.5 0.7 pad_maximum_fusion.3
  42.2 7.1 %all-to-all-start = ((f32[8,24,384]{2,1,0:T(8,128)}), f32[8,24,384]{2,1,0:T(8,128)S(1)}, u32[]{:S(2)}, u32[]{:S(2)}) async-start(f32[8,24,384]{2,1,0:T(8,128)} %pad_maximum_fusion.3), calls=%async_computation | async-start | bytes 589824 | tf_op jit(solution)/shard_map/all_to_all | solution.py:73
  49.4 0.8 collective-permute-start.3
  50.3 2.1 %collective-permute-done.3 = f32[2,24,128]{2,1,0:T(8,128)S(1)} collective-permute-done((f32[2,24,128]{2,1,0:T(8,128)S(1)}, f32[2,24,128]{2,1,0:T(8,128)S(1)}, u32[]{:S(2)}, u32[]{:S(2)}) %collective-permute-start.3) | collective-permute-done | bytes 24608 | tf_op jit(solution)/shard_map/ppermute | solution.py:22
  52.5 6.6 %all-to-all-done = f32[8,24,384]{2,1,0:T(8,128)S(1)} async-done(((f32[8,24,384]{2,1,0:T(8,128)}), f32[8,24,384]{2,1,0:T(8,128)S(1)}, u32[]{:S(2)}, u32[]{:S(2)}) %all-to-all-start) | async-done | bytes 294944 | tf_op jit(solution)/shard_map/all_to_all | solution.py:73
  59.2 0.3 fusion.2
  59.5 0.8 collective-permute-start.16
  60.3 2.2 %collective-permute-done.16 = f32[2,24,128]{2,1,0:T(8,128)S(1)} collective-permute-done((f32[2,24,128]{2,1,0:T(8,128)S(1)}, f32[2,24,128]{2,1,0:T(8,128)S(1)}, u32[]{:S(2)}, u32[]{:S(2)}) %collective-permute-start.16) | collective-permute-done | bytes 24608 | tf_op jit(solution)/shard_map/ppermute | solution.py:22
  62.7 0.5 fusion.7
  63.4 0.8 maximum_maximum_fusion
  64.2 3.5 %all-to-all-start.1 = ((f32[8,40,384]{2,1,0:T(8,128)}), f32[8,40,384]{2,1,0:T(8,128)S(1)}, u32[]{:S(2)}, u32[]{:S(2)}) async-start(f32[8,40,384]{2,1,0:T(8,128)} %maximum_maximum_fusion), calls=%async_computation.1 | async-start | bytes 983040 | tf_op jit(solution)/shard_map/all_to_all | solution.py:73
  67.8 11.7 %all-to-all-done.1 = f32[8,40,384]{2,1,0:T(8,128)S(1)} async-done(((f32[8,40,384]{2,1,0:T(8,128)}), f32[8,40,384]{2,1,0:T(8,128)S(1)}, u32[]{:S(2)}, u32[]{:S(2)}) %all-to-all-start.1) | async-done | bytes 491552 | tf_op jit(solution)/shard_map/all_to_all | solution.py:73
  79.5 2.7 %collective-permute-start.17 = (f32[128,384]{1,0:T(8,128)S(1)}, f32[128,384]{1,0:T(8,128)S(1)}, u32[]{:S(2)}, u32[]{:S(2)}) collective-permute-start(f32[128,384]{1,0:T(8,128)S(1)} %bitcast.118), channel_id=1, source_target_pairs={{0,4},{4,0},{1,5},{5,1},{2,6},{6,2},{3,7},{7,3},{8,12},{12,8},{9,1... | collective-permute-start | bytes 589832 | tf_op jit(solution)/shard_map/ppermute | solution.py:22
  82.2 0.6 collective-permute-start.18
  82.8 4.3 %collective-permute-start.19 = (f32[80,384]{1,0:T(8,128)S(1)}, f32[80,384]{1,0:T(8,128)S(1)}, u32[]{:S(2)}, u32[]{:S(2)}) collective-permute-start(f32[80,384]{1,0:T(8,128)S(1)} %pad_maximum_fusion.6), channel_id=1, source_target_pairs={{0,16},{8,24},{16,0},{24,8},{1,17},{9,25},{17,1},{25,9},{2,18},{10... | collective-permute-start | bytes 368648 | tf_op jit(solution)/shard_map/ppermute | solution.py:61
  87.1 1.2 broadcast_in_dim.35
  88.4 3.6 %all-to-all-start.2 = ((f32[4,256,384]{2,1,0:T(8,128)}), f32[4,256,384]{2,1,0:T(8,128)S(1)}, u32[]{:S(2)}, u32[]{:S(2)}) async-start(f32[4,256,384]{2,1,0:T(8,128)} %broadcast_in_dim.35), calls=%async_computation.2 | async-start | bytes 3145728 | tf_op jit(solution)/shard_map/all_to_all | solution.py:73
  92.1 2.5 %collective-permute-start.24 = (f32[16,384]{1,0:T(8,128)S(1)}, f32[16,384]{1,0:T(8,128)S(1)}, u32[]{:S(2)}, u32[]{:S(2)}) collective-permute-start(f32[16,384]{1,0:T(8,128)S(1)} %slice_reduce_fusion.1), channel_id=1, source_target_pairs={{0,4},{4,0},{1,5},{5,1},{2,6},{6,2},{3,7},{7,3},{8,12},{12,8},{9,1... | collective-permute-start | bytes 73736 | tf_op jit(solution)/shard_map/ppermute | solution.py:22
  94.7 1.8 %collective-permute-done.24 = f32[16,384]{1,0:T(8,128)S(1)} collective-permute-done((f32[16,384]{1,0:T(8,128)S(1)}, f32[16,384]{1,0:T(8,128)S(1)}, u32[]{:S(2)}, u32[]{:S(2)}) %collective-permute-start.24) | collective-permute-done | bytes 24608 | tf_op jit(solution)/shard_map/ppermute | solution.py:22
  96.5 2.6 %collective-permute-start.21 = (f32[256,384]{1,0:T(8,128)S(1)}, f32[256,384]{1,0:T(8,128)S(1)}, u32[]{:S(2)}, u32[]{:S(2)}) collective-permute-start(f32[256,384]{1,0:T(8,128)S(1)} %bitcast.113), channel_id=1, source_target_pairs={{0,4},{4,0},{1,5},{5,1},{2,6},{6,2},{3,7},{7,3},{8,12},{12,8},{9,1... | collective-permute-start | bytes 1179656 | tf_op jit(solution)/shard_map/ppermute | solution.py:22
  99.1 3.9 %collective-permute-done.25 = f32[16,384]{1,0:T(8,128)S(1)} collective-permute-done((f32[16,384]{1,0:T(8,128)S(1)}, f32[16,384]{1,0:T(8,128)S(1)}, u32[]{:S(2)}, u32[]{:S(2)}) %collective-permute-start.25) | collective-permute-done | bytes 24608 | tf_op jit(solution)/shard_map/ppermute | solution.py:22
  103.0 1.1 collective-permute-start.26
  104.2 3.1 %collective-permute-done.26 = f32[32,384]{1,0:T(8,128)S(1)} collective-permute-done((f32[32,384]{1,0:T(8,128)S(1)}, f32[32,384]{1,0:T(8,128)S(1)}, u32[]{:S(2)}, u32[]{:S(2)}) %collective-permute-start.26) | collective-permute-done | bytes 49184 | tf_op jit(solution)/shard_map/ppermute | solution.py:22
  107.3 1.3 all-to-all-done.2
  108.6 10.5 %collective-permute-start.23 = (f32[64,2,8,384]{3,2,1,0:T(8,128)S(1)}, f32[64,2,8,384]{3,2,1,0:T(8,128)}, u32[]{:S(2)}, u32[]{:S(2)}) collective-permute-start(f32[64,2,8,384]{3,2,1,0:T(8,128)S(1)} %bitcast.99), channel_id=1, source_target_pairs={{0,2},{2,0},{1,3},{3,1},{4,6},{6,4},{5,7},{7,5},{8,10},{10,8},{9,1... | collective-permute-start | bytes 4718600 | tf_op jit(solution)/shard_map/ppermute | solution.py:22
  119.3 4.3 %finish.3 = (f32[4,192,1536]{2,1,0:T(8,128)}, f32[4,64,1536]{2,1,0:T(8,128)}, f32[4,64,1536]{2,1,0:T(8,128)}) custom-call(s32[1]{0:T(128)} %bitcast.refs_0_, f32[64,2,8,384]{3,2,1,0:T(8,128)S(1)} %bitcast.100, f32[4,192,128]{2,1,0:T(8,128)S(1)} %copy-done, f32[4,192,1536]{2,1,0:T(8,128)} %refs_4_.5, f32[4,64,1536]{2,1,0:T(8,128)} %refs_5_.5, ...), custom_call_target="tpu_custom_call" | custom-call | flops 603979776 | bytes 5242880 | tf_op jit(solution)/shard_map/finish/pallas_call | solution.py:131
  123.8 0.7 fusion.22
  124.5 0.3 collective-permute-start.28
  124.8 1.4 %collective-permute-start.22 = (f32[64,1,8,384]{3,2,1,0:T(8,128)S(1)}, f32[64,1,8,384]{3,2,1,0:T(8,128)S(1)}, u32[]{:S(2)}, u32[]{:S(2)}) collective-permute-start(f32[64,1,8,384]{3,2,1,0:T(8,128)S(1)} %bitcast.101), channel_id=1, source_target_pairs={{0,2},{2,0},{1,3},{3,1},{4,6},{6,4},{5,7},{7,5},{8,10},{10,8},{9,1... | collective-permute-start | bytes 2359304 | tf_op jit(solution)/shard_map/ppermute | solution.py:22
  126.2 5.2 %finish.4 = (f32[4,192,1536]{2,1,0:T(8,128)}, f32[4,64,1536]{2,1,0:T(8,128)}, f32[4,64,1536]{2,1,0:T(8,128)}) custom-call(s32[1]{0:T(128)} %bitcast.1.refs_0_, f32[64,2,8,384]{3,2,1,0:T(8,128)} %collective-permute-done.23.refs_1_, f32[4,192,128]{2,1,0:T(8,128)S(1)} %copy-done, ...), custom_call_target="tpu_custom_call", output_to_operand_aliasing={{0}: (6, {}), {1}: (7, {}), {2}: (8, {})} | custom-call | flops 603979776 | bytes 5242880 | tf_op jit(solution)/shard_map/finish/pallas_call | solution.py:131
  131.4 0.1 select_reduce_fusion
  131.6 0.4 fusion
  132.0 0.1 collective-permute-start.29
  132.2 4.9 %finish.5 = (f32[4,192,1536]{2,1,0:T(8,128)}, f32[4,64,1536]{2,1,0:T(8,128)}, f32[4,64,1536]{2,1,0:T(8,128)}) custom-call(s32[2]{0:T(128)S(1)} %pad_add_fusion.refs_0_, f32[64,1,8,384]{3,2,1,0:T(8,128)S(1)} %bitcast.102, f32[64,1,8,384]{3,2,1,0:T(8,128)S(1)} %collective-permute-done.22.refs_2_, ...), custom_call_target="tpu_custom_call", output_to_operand_aliasing={{0}: (7, {}), {1}: (8, {}), {2}: (9, {})} | custom-call | flops 603979776 | bytes 5242880 | tf_op jit(solution)/shard_map/finish/pallas_call | solution.py:131
  137.1 0.8 pad_maximum_fusion.2
  (87 shorter events, 2.7 us)
Async XLA Ops:
  1.8 5.2 %collective-permute-start = (f32[2,192,512]{2,1,0:T(8,128)S(1)}, f32[2,192,512]{2,1,0:T(8,128)S(1)}, u32[]{:S(2)}, u32[]{:S(2)}) collective-permute-start(f32[2,192,512]{2,1,0:T(8,128)S(1)} %dynamic-slice_bitcast_fusion), channel_id=1, source_target_pairs={{0,2},{2,0},{1,3},{3,1},{4,6},{6,4},{5,7},{7,5},{8,10},{10,8},{9,1... | collective-permute-start | bytes 2359304 | tf_op jit(solution)/shard_map/ppermute | solution.py:22
  6.3 7.8 %collective-permute-start.1 = (f32[2,192,512]{2,1,0:T(8,128)S(1)}, f32[2,192,512]{2,1,0:T(8,128)S(1)}, u32[]{:S(2)}, u32[]{:S(2)}) collective-permute-start(f32[2,192,512]{2,1,0:T(8,128)S(1)} %constant_dynamic-slice_fusion.15), channel_id=1, source_target_pairs={{0,2},{2,0},{1,3},{3,1},{4,6},{6,4},{5,7},{7,5},{8,10},{10,8},{9,1... | collective-permute-start | bytes 2359304 | tf_op jit(solution)/shard_map/ppermute | solution.py:22
  10.4 7.9 %collective-permute-start.2 = (f32[2,192,512]{2,1,0:T(8,128)S(1)}, f32[2,192,512]{2,1,0:T(8,128)S(1)}, u32[]{:S(2)}, u32[]{:S(2)}) collective-permute-start(f32[2,192,512]{2,1,0:T(8,128)S(1)} %constant_dynamic-slice_fusion.14), channel_id=1, source_target_pairs={{0,2},{2,0},{1,3},{3,1},{4,6},{6,4},{5,7},{7,5},{8,10},{10,8},{9,1... | collective-permute-start | bytes 2359304 | tf_op jit(solution)/shard_map/ppermute | solution.py:22
  10.9 8.9 %collective-permute-start.4 = (f32[128,384]{0,1:T(8,128)}, f32[128,384]{0,1:T(8,128)}, u32[]{:S(2)}, u32[]{:S(2)}) collective-permute-start(f32[128,384]{0,1:T(8,128)} %get-tuple-element.84), channel_id=1, source_target_pairs={{0,8},{8,16},{16,24},{24,0},{1,9},{9,17},{17,25},{25,1},{2,10},{10... | collective-permute-start | bytes 589832 | tf_op jit(solution)/shard_map/ppermute | solution.py:42
  10.9 11.6 %collective-permute-start.5 = (f32[128,384]{0,1:T(8,128)}, f32[128,384]{0,1:T(8,128)}, u32[]{:S(2)}, u32[]{:S(2)}) collective-permute-start(f32[128,384]{0,1:T(8,128)} %get-tuple-element.83), channel_id=1, source_target_pairs={{0,16},{8,24},{16,0},{24,8},{1,17},{9,25},{17,1},{25,9},{2,18},{10... | collective-permute-start | bytes 589832 | tf_op jit(solution)/shard_map/ppermute | solution.py:42
  13.0 10.5 %collective-permute-start.6 = (f32[128,384]{0,1:T(8,128)S(1)}, f32[128,384]{0,1:T(8,128)}, u32[]{:S(2)}, u32[]{:S(2)}) collective-permute-start(f32[128,384]{0,1:T(8,128)S(1)} %get-tuple-element.82), channel_id=1, source_target_pairs={{0,24},{8,0},{16,8},{24,16},{1,25},{9,1},{17,9},{25,17},{2,26},{10... | collective-permute-start | bytes 589832 | tf_op jit(solution)/shard_map/ppermute | solution.py:42
  15.5 11.5 %collective-permute-start.7 = (f32[256,384]{0,1:T(8,128)S(1)}, f32[256,384]{0,1:T(8,128)S(1)}, u32[]{:S(2)}, u32[]{:S(2)}) collective-permute-start(f32[256,384]{0,1:T(8,128)S(1)} %get-tuple-element.80), channel_id=1, source_target_pairs={{0,4},{4,0},{1,5},{5,1},{2,6},{6,2},{3,7},{7,3},{8,12},{12,8},{9,1... | collective-permute-start | bytes 1179656 | tf_op jit(solution)/shard_map/ppermute | solution.py:42
  19.7 9.6 %collective-permute-start.10 = (f32[128,384]{0,1:T(8,128)S(1)}, f32[128,384]{0,1:T(8,128)S(1)}, u32[]{:S(2)}, u32[]{:S(2)}) collective-permute-start(f32[128,384]{0,1:T(8,128)S(1)} %get-tuple-element.76), channel_id=1, source_target_pairs={{0,24},{8,0},{16,8},{24,16},{1,25},{9,1},{17,9},{25,17},{2,26},{10... | collective-permute-start | bytes 589832 | tf_op jit(solution)/shard_map/ppermute | solution.py:42
  19.8 12.6 %collective-permute-start.8 = (f32[128,384]{0,1:T(8,128)S(1)}, f32[128,384]{0,1:T(8,128)S(1)}, u32[]{:S(2)}, u32[]{:S(2)}) collective-permute-start(f32[128,384]{0,1:T(8,128)S(1)} %get-tuple-element.78), channel_id=1, source_target_pairs={{0,8},{8,16},{16,24},{24,0},{1,9},{9,17},{17,25},{25,1},{2,10},{10... | collective-permute-start | bytes 589832 | tf_op jit(solution)/shard_map/ppermute | solution.py:42
  22.5 11.5 %collective-permute-start.9 = (f32[128,384]{0,1:T(8,128)S(1)}, f32[128,384]{0,1:T(8,128)S(1)}, u32[]{:S(2)}, u32[]{:S(2)}) collective-permute-start(f32[128,384]{0,1:T(8,128)S(1)} %get-tuple-element.77), channel_id=1, source_target_pairs={{0,16},{8,24},{16,0},{24,8},{1,17},{9,25},{17,1},{25,9},{2,18},{10... | collective-permute-start | bytes 589832 | tf_op jit(solution)/shard_map/ppermute | solution.py:42
  24.9 16.2 %collective-permute-start.11 = (f32[64,384]{0,1:T(8,128)S(1)}, f32[64,384]{0,1:T(8,128)S(1)}, u32[]{:S(2)}, u32[]{:S(2)}) collective-permute-start(f32[64,384]{0,1:T(8,128)S(1)} %get-tuple-element.106), channel_id=1, source_target_pairs={{0,4},{4,0},{1,5},{5,1},{2,6},{6,2},{3,7},{7,3},{8,12},{12,8},{9,1... | collective-permute-start | bytes 294920 | tf_op jit(solution)/shard_map/ppermute | solution.py:42
  27.3 13.7 %collective-permute-start.13 = (f32[64,384]{0,1:T(8,128)S(1)}, f32[64,384]{0,1:T(8,128)S(1)}, u32[]{:S(2)}, u32[]{:S(2)}) collective-permute-start(f32[64,384]{0,1:T(8,128)S(1)} %get-tuple-element.92), channel_id=1, source_target_pairs={{0,8},{8,16},{16,24},{24,0},{1,9},{9,17},{17,25},{25,1},{2,10},{10... | collective-permute-start | bytes 294920 | tf_op jit(solution)/shard_map/ppermute | solution.py:42
  29.3 11.7 %collective-permute-start.14 = (f32[64,384]{0,1:T(8,128)S(1)}, f32[64,384]{0,1:T(8,128)S(1)}, u32[]{:S(2)}, u32[]{:S(2)}) collective-permute-start(f32[64,384]{0,1:T(8,128)S(1)} %get-tuple-element.94), channel_id=1, source_target_pairs={{0,16},{8,24},{16,0},{24,8},{1,17},{9,25},{17,1},{25,9},{2,18},{10... | collective-permute-start | bytes 294920 | tf_op jit(solution)/shard_map/ppermute | solution.py:42
  32.4 8.6 %collective-permute-start.15 = (f32[64,384]{0,1:T(8,128)S(1)}, f32[64,384]{0,1:T(8,128)S(1)}, u32[]{:S(2)}, u32[]{:S(2)}) collective-permute-start(f32[64,384]{0,1:T(8,128)S(1)} %get-tuple-element.93), channel_id=1, source_target_pairs={{0,24},{8,0},{16,8},{24,16},{1,25},{9,1},{17,9},{25,17},{2,26},{10... | collective-permute-start | bytes 294920 | tf_op jit(solution)/shard_map/ppermute | solution.py:42
  34.2 7.2 %collective-permute-start.12 = (f32[64,384]{0,1:T(8,128)S(1)}, f32[64,384]{0,1:T(8,128)S(1)}, u32[]{:S(2)}, u32[]{:S(2)}) collective-permute-start(f32[64,384]{0,1:T(8,128)S(1)} %get-tuple-element.104), channel_id=1, source_target_pairs={{0,4},{4,0},{1,5},{5,1},{2,6},{6,2},{3,7},{7,3},{8,12},{12,8},{9,1... | collective-permute-start | bytes 294920 | tf_op jit(solution)/shard_map/ppermute | solution.py:42
  41.2 18.0 %copy-start = (f32[4,192,128]{2,1,0:T(8,128)S(1)}, f32[4,192,128]{2,1,0:T(8,128)}, u32[]{:S(2)}) copy-start(f32[4,192,128]{2,1,0:T(8,128)} %refs_3_.5) | copy-start | bytes 1179652
  42.2 16.8 %all-to-all-start = ((f32[8,24,384]{2,1,0:T(8,128)}), f32[8,24,384]{2,1,0:T(8,128)S(1)}, u32[]{:S(2)}, u32[]{:S(2)}) async-start(f32[8,24,384]{2,1,0:T(8,128)} %pad_maximum_fusion.3), calls=%async_computation | async-start | bytes 589824 | tf_op jit(solution)/shard_map/all_to_all | solution.py:73
  49.4 2.9 %collective-permute-start.3 = (f32[2,24,128]{2,1,0:T(8,128)S(1)}, f32[2,24,128]{2,1,0:T(8,128)S(1)}, u32[]{:S(2)}, u32[]{:S(2)}) collective-permute-start(f32[2,24,128]{2,1,0:T(8,128)S(1)} %pad_maximum_fusion.10), channel_id=1, source_target_pairs={{0,1},{1,0},{2,3},{3,2},{4,5},{5,4},{6,7},{7,6},{8,9},{9,8},{10,11... | collective-permute-start | bytes 73736 | tf_op jit(solution)/shard_map/ppermute | solution.py:22
  59.5 3.0 %collective-permute-start.16 = (f32[2,24,128]{2,1,0:T(8,128)S(1)}, f32[2,24,128]{2,1,0:T(8,128)S(1)}, u32[]{:S(2)}, u32[]{:S(2)}) collective-permute-start(f32[2,24,128]{2,1,0:T(8,128)S(1)} %fusion.2), channel_id=1, source_target_pairs={{0,1},{1,0},{2,3},{3,2},{4,5},{5,4},{6,7},{7,6},{8,9},{9,8},{10,11... | collective-permute-start | bytes 73736 | tf_op jit(solution)/shard_map/ppermute | solution.py:22
  64.2 15.3 %all-to-all-start.1 = ((f32[8,40,384]{2,1,0:T(8,128)}), f32[8,40,384]{2,1,0:T(8,128)S(1)}, u32[]{:S(2)}, u32[]{:S(2)}) async-start(f32[8,40,384]{2,1,0:T(8,128)} %maximum_maximum_fusion), calls=%async_computation.1 | async-start | bytes 983040 | tf_op jit(solution)/shard_map/all_to_all | solution.py:73
  79.5 7.6 %collective-permute-start.17 = (f32[128,384]{1,0:T(8,128)S(1)}, f32[128,384]{1,0:T(8,128)S(1)}, u32[]{:S(2)}, u32[]{:S(2)}) collective-permute-start(f32[128,384]{1,0:T(8,128)S(1)} %bitcast.118), channel_id=1, source_target_pairs={{0,4},{4,0},{1,5},{5,1},{2,6},{6,2},{3,7},{7,3},{8,12},{12,8},{9,1... | collective-permute-start | bytes 589832 | tf_op jit(solution)/shard_map/ppermute | solution.py:22
  82.2 9.8 %collective-permute-start.18 = (f32[80,384]{1,0:T(8,128)S(1)}, f32[80,384]{1,0:T(8,128)S(1)}, u32[]{:S(2)}, u32[]{:S(2)}) collective-permute-start(f32[80,384]{1,0:T(8,128)S(1)} %pad_maximum_fusion.6), channel_id=1, source_target_pairs={{0,8},{8,16},{16,24},{24,0},{1,9},{9,17},{17,25},{25,1},{2,10},{10... | collective-permute-start | bytes 368648 | tf_op jit(solution)/shard_map/ppermute | solution.py:61
  82.8 9.3 %collective-permute-start.19 = (f32[80,384]{1,0:T(8,128)S(1)}, f32[80,384]{1,0:T(8,128)S(1)}, u32[]{:S(2)}, u32[]{:S(2)}) collective-permute-start(f32[80,384]{1,0:T(8,128)S(1)} %pad_maximum_fusion.6), channel_id=1, source_target_pairs={{0,16},{8,24},{16,0},{24,8},{1,17},{9,25},{17,1},{25,9},{2,18},{10... | collective-permute-start | bytes 368648 | tf_op jit(solution)/shard_map/ppermute | solution.py:61
  87.1 5.0 %collective-permute-start.20 = (f32[80,384]{1,0:T(8,128)S(1)}, f32[80,384]{1,0:T(8,128)S(1)}, u32[]{:S(2)}, u32[]{:S(2)}) collective-permute-start(f32[80,384]{1,0:T(8,128)S(1)} %pad_maximum_fusion.6), channel_id=1, source_target_pairs={{0,24},{8,0},{16,8},{24,16},{1,25},{9,1},{17,9},{25,17},{2,26},{10... | collective-permute-start | bytes 368648 | tf_op jit(solution)/shard_map/ppermute | solution.py:61
  88.4 20.2 %all-to-all-start.2 = ((f32[4,256,384]{2,1,0:T(8,128)}), f32[4,256,384]{2,1,0:T(8,128)S(1)}, u32[]{:S(2)}, u32[]{:S(2)}) async-start(f32[4,256,384]{2,1,0:T(8,128)} %broadcast_in_dim.35), calls=%async_computation.2 | async-start | bytes 3145728 | tf_op jit(solution)/shard_map/all_to_all | solution.py:73
  92.1 4.3 %collective-permute-start.24 = (f32[16,384]{1,0:T(8,128)S(1)}, f32[16,384]{1,0:T(8,128)S(1)}, u32[]{:S(2)}, u32[]{:S(2)}) collective-permute-start(f32[16,384]{1,0:T(8,128)S(1)} %slice_reduce_fusion.1), channel_id=1, source_target_pairs={{0,4},{4,0},{1,5},{5,1},{2,6},{6,2},{3,7},{7,3},{8,12},{12,8},{9,1... | collective-permute-start | bytes 73736 | tf_op jit(solution)/shard_map/ppermute | solution.py:22
  96.4 6.6 %collective-permute-start.25 = (f32[16,384]{1,0:T(8,128)S(1)}, f32[16,384]{1,0:T(8,128)S(1)}, u32[]{:S(2)}, u32[]{:S(2)}) collective-permute-start(f32[16,384]{1,0:T(8,128)S(1)} %add.303), channel_id=1, source_target_pairs={{0,128},{32,160},{64,192},{96,224},{128,0},{160,32},{192,64},{224,... | collective-permute-start | bytes 73736 | tf_op jit(solution)/shard_map/ppermute | solution.py:22
  96.5 22.6 %collective-permute-start.21 = (f32[256,384]{1,0:T(8,128)S(1)}, f32[256,384]{1,0:T(8,128)S(1)}, u32[]{:S(2)}, u32[]{:S(2)}) collective-permute-start(f32[256,384]{1,0:T(8,128)S(1)} %bitcast.113), channel_id=1, source_target_pairs={{0,4},{4,0},{1,5},{5,1},{2,6},{6,2},{3,7},{7,3},{8,12},{12,8},{9,1... | collective-permute-start | bytes 1179656 | tf_op jit(solution)/shard_map/ppermute | solution.py:22
  103.0 4.2 %collective-permute-start.26 = (f32[32,384]{1,0:T(8,128)S(1)}, f32[32,384]{1,0:T(8,128)S(1)}, u32[]{:S(2)}, u32[]{:S(2)}) collective-permute-start(f32[32,384]{1,0:T(8,128)S(1)} %pad_maximum_fusion.8), channel_id=1, source_target_pairs={{0,64},{32,96},{64,0},{96,32},{128,192},{160,224},{192,128},{224,1... | collective-permute-start | bytes 147464 | tf_op jit(solution)/shard_map/ppermute | solution.py:22
  108.6 17.7 %collective-permute-start.23 = (f32[64,2,8,384]{3,2,1,0:T(8,128)S(1)}, f32[64,2,8,384]{3,2,1,0:T(8,128)}, u32[]{:S(2)}, u32[]{:S(2)}) collective-permute-start(f32[64,2,8,384]{3,2,1,0:T(8,128)S(1)} %bitcast.99), channel_id=1, source_target_pairs={{0,2},{2,0},{1,3},{3,1},{4,6},{6,4},{5,7},{7,5},{8,10},{10,8},{9,1... | collective-permute-start | bytes 4718600 | tf_op jit(solution)/shard_map/ppermute | solution.py:22
  119.2 4.5 %collective-permute-start.27 = (f32[64,384]{1,0:T(8,128)S(1)}, f32[64,384]{1,0:T(8,128)S(1)}, u32[]{:S(2)}, u32[]{:S(2)}) collective-permute-start(f32[64,384]{1,0:T(8,128)S(1)} %pad_maximum_fusion.7), channel_id=1, source_target_pairs={{0,32},{32,0},{64,96},{96,64},{128,160},{160,128},{192,224},{224,1... | collective-permute-start | bytes 294920 | tf_op jit(solution)/shard_map/ppermute | solution.py:22
  124.5 7.0 %collective-permute-start.28 = (f32[2,128,128]{2,1,0:T(8,128)S(1)}, f32[2,128,128]{2,1,0:T(8,128)S(1)}, u32[]{:S(2)}, u32[]{:S(2)}) collective-permute-start(f32[2,128,128]{2,1,0:T(8,128)S(1)} %fusion.22), channel_id=1, source_target_pairs={{0,1},{1,0},{2,3},{3,2},{4,5},{5,4},{6,7},{7,6},{8,9},{9,8},{10,11... | collective-permute-start | bytes 393224 | tf_op jit(solution)/shard_map/ppermute | solution.py:22
  124.8 7.4 %collective-permute-start.22 = (f32[64,1,8,384]{3,2,1,0:T(8,128)S(1)}, f32[64,1,8,384]{3,2,1,0:T(8,128)S(1)}, u32[]{:S(2)}, u32[]{:S(2)}) collective-permute-start(f32[64,1,8,384]{3,2,1,0:T(8,128)S(1)} %bitcast.101), channel_id=1, source_target_pairs={{0,2},{2,0},{1,3},{3,1},{4,6},{6,4},{5,7},{7,5},{8,10},{10,8},{9,1... | collective-permute-start | bytes 2359304 | tf_op jit(solution)/shard_map/ppermute | solution.py:22
  132.0 5.1 %collective-permute-start.29 = (f32[2,192,128]{2,1,0:T(8,128)S(1)}, f32[2,192,128]{2,1,0:T(8,128)S(1)}, u32[]{:S(2)}, u32[]{:S(2)}) collective-permute-start(f32[2,192,128]{2,1,0:T(8,128)S(1)} %fusion), channel_id=1, source_target_pairs={{0,2},{2,0},{1,3},{3,1},{4,6},{6,4},{5,7},{7,5},{8,10},{10,8},{9,1... | collective-permute-start | bytes 589832 | tf_op jit(solution)/shard_map/ppermute | solution.py:22

commit v8 on v7

--- a/solution.py
+++ b/solution.py
@@ -148,7 +148,7 @@
         ],
         compiler_params=pltpu.CompilerParams(vmem_limit_bytes=20 << 20),
         cost_estimate=pl.CostEstimate(
-            flops=12 * steps * depth * rank * some, bytes_accessed=8 * steps * (depth + rank) * some, transcendentals=0
+            flops=0, bytes_accessed=0, transcendentals=0
         ),
         name="finish",
     )(jnp.stack(pairs), *sources, basis, weights, first, second, *kept)
@@ -236,12 +236,11 @@
     little = little[:, : -part.shape[0]].reshape(-1, 3 * rank)
     part = part + flip(part, "xh")
     little = gather(little, "xh").reshape(-1, 1, small, 3 * rank)
-
-    done = finish((0, 2), [core], [across], basis, *nearby, None)
+    done = finish((1,), [core, 1 - core], [little, flip(little, "core")], basis, *nearby, None)
 
     refresh = part
     for bit in (2, 1, 0):
-        mine, moved = refresh, flip(refresh if bit else after(refresh, little), "z", 1 << bit)
+        mine, moved = refresh, flip(after(refresh, little) if bit == 1 else refresh, "z", 1 << bit)
         if bit == 0:
             mine = after(mine, *done)
         refresh = jnp.concatenate(in_order((z >> bit) & 1, mine, moved))
@@ -249,18 +248,19 @@
     refresh = jnp.stack([refresh[:, :, i * rank : (i + 1) * rank] for i in range(3)], axis=1)
     refresh = refresh.reshape(half, depth, rank)
     gram = jnp.einsum("ldr,lds->lrs", refresh, refresh, precision=HIGH)
-
+    across = after(across, *done)
     other = flip(across, "core")
-    done = finish((0, 2), [1 - core], [after(other, gram)], basis, *nearby, done)
+    done = finish((0, 2), [core], [after(across, gram)], basis, *nearby, done)
     gram = after(gram, *done) + flip(gram, "xl")
-    done = finish((1,), [core, 1 - core], [little, flip(little, "core")], basis, *nearby, done)
-    new_weights, new_first, new_second = done
     sumsq = jnp.einsum("lrr->l", gram)
     factor = jnp.sqrt(jnp.float32(rank)) / (2.0 * jnp.sqrt(sumsq + 1e-06))
     scaled = refresh * factor[:, None, None]
     gram_scaled = gram * (factor * factor)[:, None, None]
     basis_new = 1.5 * scaled - 0.5 * jnp.einsum("ldr,lrs->lds", scaled, gram_scaled, precision=HIGH)
-    new_basis = jnp.concatenate(in_order(core, after(basis_new, *done), flip(basis_new, "core")), axis=0)
+    moved = flip(basis_new, "core")
+    done = finish((0, 2), [1 - core], [after(other, basis_new)], basis, *nearby, done)
+    new_weights, new_first, new_second = done
+    new_basis = jnp.concatenate(in_order(core, after(basis_new, *done), moved), axis=0)
     return (new_weights, new_first, new_second, new_basis)
 
 

time: 139 us -> 146 us (1.050)
  starting transfers between devices: 62.2 us -> 68.2 us
  other arithmetic: 8.5 us -> 12.5 us
  waiting for transfers between devices: 40.7 us -> 37.8 us
    ppermute x15, starting transfers between devices: 26.9 us -> 32.9 us  [flip(): return lax.ppermute(x, axis, [(i, i ^ bit) for i in range(n)])]
    ppermute x15, waiting for transfers between devices: 13.7 us -> 8.51 us  [flip(): return lax.ppermute(x, axis, [(i, i ^ bit) for i in range(n)])]
    ppermute x3, waiting for transfers between devices: 0.01 us -> 3.56 us  [around(): lax.ppermute(x, axis, [(i, (i + k) % n) for i in range(n)])]
    select_n x5, other arithmetic: 0.15 us -> 2.9 us  [in_order(): return (jnp.where(first, mine, other), jnp.where(first, other, mine))]
  transfers between devices with their start and end apart: 33 -> 33, of which waited for: 12 -> 13; matrix products, arithmetic and copies ran while one was open for 10% -> 12% of each run, Pallas kernels for 10% -> 9%
where the time goes in v8:
time: 146 us; the launch traced here: 145 us
  starting transfers between devices  68.2 us (47%)
  waiting for transfers between devices  37.8 us (26%)
  Pallas kernels  13.5 us (9%)
  other arithmetic  12.5 us (9%)
  local copies, waits for them, and re-layouts  9.63 us (7%)
  matrix products  2.52 us (2%)
    ppermute x15, starting transfers between devices, flip(): return lax.ppermute(x, axis, [(i, i ^ bit) for i in range(n)])  32.9 us
    all_to_all x3, waiting for transfers between devices, exchange(): return lax.all_to_all(parts, axis, split_axis=0, concat_axis=0)  18.3 us
    ppermute x12, starting transfers between devices, scatter(): lax.ppermute(parts[k], axis, [(i, (i + k) % n) for i in range(n)])  16.3 us
    all_to_all x3, starting transfers between devices, exchange(): return lax.all_to_all(parts, axis, split_axis=0, concat_axis=0)  14.2 us
    pallas_call x3, Pallas kernels, finish(): pl.pallas_call(functools.partial(finish_kernel, chunks, count), in_specs=...  13.5 us
    ppermute x15, waiting for transfers between devices, flip(): return lax.ppermute(x, axis, [(i, i ^ bit) for i in range(n)])  8.51 us
    ppermute x12, waiting for transfers between devices, scatter(): lax.ppermute(parts[k], axis, [(i, (i + k) % n) for i in range(n)])  7.41 us
    ppermute x3, starting transfers between devices, around(): lax.ppermute(x, axis, [(i, (i + k) % n) for i in range(n)])  4.88 us
  transfers between devices with their start and end apart: 33, of which 13 were waited for; matrix products, arithmetic and copies ran while one was open for 12% of the time, Pallas kernels for 9%

profile of v8, /device:TPU:1, one launch (start us, length us, event | category | flops | bytes accessed | tf_op | source)
XLA Modules:
  0.0 145.4 jit_solution(2596429997649946948)
XLA Ops:
  0.6 1.2 dynamic-slice_bitcast_fusion
  1.8 3.3 %collective-permute-start = (f32[2,192,512]{2,1,0:T(8,128)S(1)}, f32[2,192,512]{2,1,0:T(8,128)S(1)}, u32[]{:S(2)}, u32[]{:S(2)}) collective-permute-start(f32[2,192,512]{2,1,0:T(8,128)S(1)} %dynamic-slice_bitcast_fusion), channel_id=1, source_target_pairs={{0,2},{2,0},{1,3},{3,1},{4,6},{6,4},{5,7},{7,5},{8,10},{10,8},{9,1... | collective-permute-start | bytes 2359304 | tf_op jit(solution)/shard_map/ppermute | solution.py:22
  5.2 1.2 constant_dynamic-slice_fusion.15
  6.5 0.6 collective-permute-done
  7.1 1.3 dynamic-slice_add_fusion.2
  8.3 0.9 dynamic-slice_bitcast_fusion.7
  9.2 1.2 constant_dynamic-slice_fusion.14
  10.4 0.5 collective-permute-start.2
  10.9 2.2 %collective-permute-start.5 = (f32[128,384]{0,1:T(8,128)}, f32[128,384]{0,1:T(8,128)}, u32[]{:S(2)}, u32[]{:S(2)}) collective-permute-start(f32[128,384]{0,1:T(8,128)} %get-tuple-element.87), channel_id=1, source_target_pairs={{0,16},{8,24},{16,0},{24,8},{1,17},{9,25},{17,1},{25,9},{2,18},{10... | collective-permute-start | bytes 589832 | tf_op jit(solution)/shard_map/ppermute | solution.py:42
  13.0 1.1 collective-permute-start.6
  14.1 1.3 dynamic-slice_add_fusion.1
  15.5 2.8 %collective-permute-start.7 = (f32[256,384]{0,1:T(8,128)S(1)}, f32[256,384]{0,1:T(8,128)S(1)}, u32[]{:S(2)}, u32[]{:S(2)}) collective-permute-start(f32[256,384]{0,1:T(8,128)S(1)} %get-tuple-element.84), channel_id=1, source_target_pairs={{0,4},{4,0},{1,5},{5,1},{2,6},{6,2},{3,7},{7,3},{8,12},{12,8},{9,1... | collective-permute-start | bytes 1179656 | tf_op jit(solution)/shard_map/ppermute | solution.py:42
  18.3 1.3 dynamic-slice_add_fusion
  19.8 1.4 collective-permute-start.8
  21.3 1.2 collective-permute-done.5
  22.5 1.1 collective-permute-start.9
  23.5 1.2 add_add_fusion.2
  24.9 2.1 %collective-permute-start.11 = (f32[64,384]{0,1:T(8,128)S(1)}, f32[64,384]{0,1:T(8,128)S(1)}, u32[]{:S(2)}, u32[]{:S(2)}) collective-permute-start(f32[64,384]{0,1:T(8,128)S(1)} %get-tuple-element.110), channel_id=1, source_target_pairs={{0,4},{4,0},{1,5},{5,1},{2,6},{6,2},{3,7},{7,3},{8,12},{12,8},{9,1... | collective-permute-start | bytes 294920 | tf_op jit(solution)/shard_map/ppermute | solution.py:42
  27.5 1.4 constant_dynamic-slice_fusion.10
  29.3 3.1 %collective-permute-start.14 = (f32[64,384]{0,1:T(8,128)S(1)}, f32[64,384]{0,1:T(8,128)S(1)}, u32[]{:S(2)}, u32[]{:S(2)}) collective-permute-start(f32[64,384]{0,1:T(8,128)S(1)} %get-tuple-element.98), channel_id=1, source_target_pairs={{0,16},{8,24},{16,0},{24,8},{1,17},{9,25},{17,1},{25,9},{2,18},{10... | collective-permute-start | bytes 294920 | tf_op jit(solution)/shard_map/ppermute | solution.py:42
  32.4 1.6 %collective-permute-start.15 = (f32[64,384]{0,1:T(8,128)S(1)}, f32[64,384]{0,1:T(8,128)S(1)}, u32[]{:S(2)}, u32[]{:S(2)}) collective-permute-start(f32[64,384]{0,1:T(8,128)S(1)} %get-tuple-element.97), channel_id=1, source_target_pairs={{0,24},{8,0},{16,8},{24,16},{1,25},{9,1},{17,9},{25,17},{2,26},{10... | collective-permute-start | bytes 294920 | tf_op jit(solution)/shard_map/ppermute | solution.py:42
  34.2 0.7 collective-permute-start.12
  34.9 6.1 %collective-permute-done.13 = f32[64,384]{0,1:T(8,128)S(1)} collective-permute-done((f32[64,384]{0,1:T(8,128)S(1)}, f32[64,384]{0,1:T(8,128)S(1)}, u32[]{:S(2)}, u32[]{:S(2)}) %collective-permute-start.13) | collective-permute-done | bytes 98336 | tf_op jit(solution)/shard_map/ppermute | solution.py:42
  41.5 0.7 pad_maximum_fusion.3
  42.2 7.1 %all-to-all-start = ((f32[8,24,384]{2,1,0:T(8,128)}), f32[8,24,384]{2,1,0:T(8,128)S(1)}, u32[]{:S(2)}, u32[]{:S(2)}) async-start(f32[8,24,384]{2,1,0:T(8,128)} %pad_maximum_fusion.3), calls=%async_computation | async-start | bytes 589824 | tf_op jit(solution)/shard_map/all_to_all | solution.py:73
  49.4 0.8 collective-permute-start.3
  50.3 2.1 %collective-permute-done.3 = f32[2,24,128]{2,1,0:T(8,128)S(1)} collective-permute-done((f32[2,24,128]{2,1,0:T(8,128)S(1)}, f32[2,24,128]{2,1,0:T(8,128)S(1)}, u32[]{:S(2)}, u32[]{:S(2)}) %collective-permute-start.3) | collective-permute-done | bytes 24608 | tf_op jit(solution)/shard_map/ppermute | solution.py:22
  52.5 6.6 %all-to-all-done = f32[8,24,384]{2,1,0:T(8,128)S(1)} async-done(((f32[8,24,384]{2,1,0:T(8,128)}), f32[8,24,384]{2,1,0:T(8,128)S(1)}, u32[]{:S(2)}, u32[]{:S(2)}) %all-to-all-start) | async-done | bytes 294944 | tf_op jit(solution)/shard_map/all_to_all | solution.py:73
  59.2 0.3 fusion.2
  59.5 0.8 collective-permute-start.16
  60.3 2.2 %collective-permute-done.16 = f32[2,24,128]{2,1,0:T(8,128)S(1)} collective-permute-done((f32[2,24,128]{2,1,0:T(8,128)S(1)}, f32[2,24,128]{2,1,0:T(8,128)S(1)}, u32[]{:S(2)}, u32[]{:S(2)}) %collective-permute-start.16) | collective-permute-done | bytes 24608 | tf_op jit(solution)/shard_map/ppermute | solution.py:22
  62.7 0.5 fusion.7
  63.4 0.8 maximum_maximum_fusion
  64.2 3.5 %all-to-all-start.1 = ((f32[8,40,384]{2,1,0:T(8,128)}), f32[8,40,384]{2,1,0:T(8,128)S(1)}, u32[]{:S(2)}, u32[]{:S(2)}) async-start(f32[8,40,384]{2,1,0:T(8,128)} %maximum_maximum_fusion), calls=%async_computation.1 | async-start | bytes 983040 | tf_op jit(solution)/shard_map/all_to_all | solution.py:73
  67.8 11.7 %all-to-all-done.1 = f32[8,40,384]{2,1,0:T(8,128)S(1)} async-done(((f32[8,40,384]{2,1,0:T(8,128)}), f32[8,40,384]{2,1,0:T(8,128)S(1)}, u32[]{:S(2)}, u32[]{:S(2)}) %all-to-all-start.1) | async-done | bytes 491552 | tf_op jit(solution)/shard_map/all_to_all | solution.py:73
  79.5 2.7 %collective-permute-start.17 = (f32[128,384]{1,0:T(8,128)S(1)}, f32[128,384]{1,0:T(8,128)S(1)}, u32[]{:S(2)}, u32[]{:S(2)}) collective-permute-start(f32[128,384]{1,0:T(8,128)S(1)} %bitcast.118), channel_id=1, source_target_pairs={{0,4},{4,0},{1,5},{5,1},{2,6},{6,2},{3,7},{7,3},{8,12},{12,8},{9,1... | collective-permute-start | bytes 589832 | tf_op jit(solution)/shard_map/ppermute | solution.py:22
  82.2 0.6 collective-permute-start.18
  82.8 4.3 %collective-permute-start.19 = (f32[80,384]{1,0:T(8,128)S(1)}, f32[80,384]{1,0:T(8,128)S(1)}, u32[]{:S(2)}, u32[]{:S(2)}) collective-permute-start(f32[80,384]{1,0:T(8,128)S(1)} %pad_maximum_fusion.6), channel_id=1, source_target_pairs={{0,16},{8,24},{16,0},{24,8},{1,17},{9,25},{17,1},{25,9},{2,18},{10... | collective-permute-start | bytes 368648 | tf_op jit(solution)/shard_map/ppermute | solution.py:61
  87.2 0.9 collective-permute-done.18
  88.2 2.5 %collective-permute-done.19 = f32[80,384]{1,0:T(8,128)S(1)} collective-permute-done((f32[80,384]{1,0:T(8,128)S(1)}, f32[80,384]{1,0:T(8,128)S(1)}, u32[]{:S(2)}, u32[]{:S(2)}) %collective-permute-start.19) | collective-permute-done | bytes 122912 | tf_op jit(solution)/shard_map/ppermute | solution.py:61
  91.1 2.9 %collective-permute-start.24 = (f32[16,384]{1,0:T(8,128)S(1)}, f32[16,384]{1,0:T(8,128)S(1)}, u32[]{:S(2)}, u32[]{:S(2)}) collective-permute-start(f32[16,384]{1,0:T(8,128)S(1)} %slice_reduce_fusion.1), channel_id=1, source_target_pairs={{0,4},{4,0},{1,5},{5,1},{2,6},{6,2},{3,7},{7,3},{8,12},{12,8},{9,1... | collective-permute-start | bytes 73736 | tf_op jit(solution)/shard_map/ppermute | solution.py:22
  94.0 1.3 broadcast_in_dim.30
  95.3 3.6 %all-to-all-start.2 = ((f32[4,256,384]{2,1,0:T(8,128)}), f32[4,256,384]{2,1,0:T(8,128)S(1)}, u32[]{:S(2)}, u32[]{:S(2)}) async-start(f32[4,256,384]{2,1,0:T(8,128)} %broadcast_in_dim.30), calls=%async_computation.2 | async-start | bytes 3145728 | tf_op jit(solution)/shard_map/all_to_all | solution.py:73
  98.8 0.5 collective-permute-done.24
  99.5 10.1 %collective-permute-start.22 = (f32[64,1,8,384]{3,2,1,0:T(8,128)S(1)}, f32[64,1,8,384]{3,2,1,0:T(8,128)S(1)}, u32[]{:S(2)}, u32[]{:S(2)}) collective-permute-start(f32[64,1,8,384]{3,2,1,0:T(8,128)S(1)} %bitcast.101), channel_id=1, source_target_pairs={{0,2},{2,0},{1,3},{3,1},{4,6},{6,4},{5,7},{7,5},{8,10},{10,8},{9,1... | collective-permute-start | bytes 2359304 | tf_op jit(solution)/shard_map/ppermute | solution.py:22
  109.6 0.6 copy-done.1
  110.2 0.6 pad_maximum_fusion.8
  110.9 1.9 %collective-permute-start.26 = (f32[32,384]{1,0:T(8,128)}, f32[32,384]{1,0:T(8,128)}, u32[]{:S(2)}, u32[]{:S(2)}) collective-permute-start(f32[32,384]{1,0:T(8,128)} %pad_maximum_fusion.8), channel_id=1, source_target_pairs={{0,64},{32,96},{64,0},{96,32},{128,192},{160,224},{192,128},{224,1... | collective-permute-start | bytes 147464 | tf_op jit(solution)/shard_map/ppermute | solution.py:22
  112.8 2.4 %collective-permute-done.26 = f32[32,384]{1,0:T(8,128)} collective-permute-done((f32[32,384]{1,0:T(8,128)}, f32[32,384]{1,0:T(8,128)}, u32[]{:S(2)}, u32[]{:S(2)}) %collective-permute-start.26) | collective-permute-done | bytes 49184 | tf_op jit(solution)/shard_map/ppermute | solution.py:22
  115.2 0.8 broadcast_select_fusion.5
  116.0 0.6 pad_maximum_fusion.7
  116.7 1.1 collective-permute-start.27
  117.9 4.9 %finish.3 = (f32[4,192,1536]{2,1,0:T(8,128)}, f32[4,64,1536]{2,1,0:T(8,128)}, f32[4,64,1536]{2,1,0:T(8,128)}) custom-call(s32[2]{0:T(128)S(1)} %pad_add_fusion.refs_0_, f32[64,1,8,384]{3,2,1,0:T(8,128)S(1)} %bitcast.102, f32[64,1,8,384]{3,2,1,0:T(8,128)S(1)} %collective-permute-done.22.refs_2_, f32[4,192,128]{2,1,0:T(8,128)S(1)} %copy-done, ...), custom_call_target="tpu_custom_call" | custom-call | tf_op jit(solution)/shard_map/finish/pallas_call | solution.py:131
  122.8 7.3 %collective-permute-start.23 = (f32[64,2,8,384]{3,2,1,0:T(8,128)S(1)}, f32[64,2,8,384]{3,2,1,0:T(8,128)S(1)}, u32[]{:S(2)}, u32[]{:S(2)}) collective-permute-start(f32[64,2,8,384]{3,2,1,0:T(8,128)S(1)} %bitcast.99), channel_id=1, source_target_pairs={{0,2},{2,0},{1,3},{3,1},{4,6},{6,4},{5,7},{7,5},{8,10},{10,8},{9,1... | collective-permute-start | bytes 4718600 | tf_op jit(solution)/shard_map/ppermute | solution.py:22
  130.1 1.0 broadcast_select_fusion.3
  131.1 0.7 fusion.21
  131.8 0.3 collective-permute-start.28
  132.1 4.3 %finish.4 = (f32[4,192,1536]{2,1,0:T(8,128)}, f32[4,64,1536]{2,1,0:T(8,128)}, f32[4,64,1536]{2,1,0:T(8,128)}) custom-call(s32[1]{0:T(128)} %bitcast.37.refs_0_, f32[64,2,8,384]{3,2,1,0:T(8,128)S(1)} %bitcast.100, f32[4,192,128]{2,1,0:T(8,128)S(1)} %copy-done, f32[4,192,1536]{2,1,0:T(8,128)} %refs_3_.5, ...), custom_call_target="tpu_custom_call", output_to_operand_aliasing={{0}: (6, {}), {1}: (7, {}), {2}: (8, {})} | custom-call | tf_op jit(solution)/shard_map/finish/pallas_call | solution.py:131
  136.5 0.7 collective-permute-done.28
  137.3 1.1 fusion
  138.4 0.8 collective-permute-start.29
  139.2 4.3 %finish.5 = (f32[4,192,1536]{2,1,0:T(8,128)}, f32[4,64,1536]{2,1,0:T(8,128)}, f32[4,64,1536]{2,1,0:T(8,128)}) custom-call(s32[1]{0:T(128)} %bitcast.refs_0_, f32[64,2,8,384]{3,2,1,0:T(8,128)S(1)} %collective-permute-done.23.refs_1_, f32[4,192,128]{2,1,0:T(8,128)S(1)} %copy-done, ...), custom_call_target="tpu_custom_call", output_to_operand_aliasing={{0}: (6, {}), {1}: (7, {}), {2}: (8, {})} | custom-call | tf_op jit(solution)/shard_map/finish/pallas_call | solution.py:131
  143.6 1.1 broadcast_select_fusion.1
  144.6 0.8 pad_maximum_fusion.2
  (91 shorter events, 3.9 us)
Async XLA Ops:
  1.8 5.2 %collective-permute-start = (f32[2,192,512]{2,1,0:T(8,128)S(1)}, f32[2,192,512]{2,1,0:T(8,128)S(1)}, u32[]{:S(2)}, u32[]{:S(2)}) collective-permute-start(f32[2,192,512]{2,1,0:T(8,128)S(1)} %dynamic-slice_bitcast_fusion), channel_id=1, source_target_pairs={{0,2},{2,0},{1,3},{3,1},{4,6},{6,4},{5,7},{7,5},{8,10},{10,8},{9,1... | collective-permute-start | bytes 2359304 | tf_op jit(solution)/shard_map/ppermute | solution.py:22
  6.3 7.8 %collective-permute-start.1 = (f32[2,192,512]{2,1,0:T(8,128)S(1)}, f32[2,192,512]{2,1,0:T(8,128)S(1)}, u32[]{:S(2)}, u32[]{:S(2)}) collective-permute-start(f32[2,192,512]{2,1,0:T(8,128)S(1)} %constant_dynamic-slice_fusion.15), channel_id=1, source_target_pairs={{0,2},{2,0},{1,3},{3,1},{4,6},{6,4},{5,7},{7,5},{8,10},{10,8},{9,1... | collective-permute-start | bytes 2359304 | tf_op jit(solution)/shard_map/ppermute | solution.py:22
  10.4 7.9 %collective-permute-start.2 = (f32[2,192,512]{2,1,0:T(8,128)S(1)}, f32[2,192,512]{2,1,0:T(8,128)S(1)}, u32[]{:S(2)}, u32[]{:S(2)}) collective-permute-start(f32[2,192,512]{2,1,0:T(8,128)S(1)} %constant_dynamic-slice_fusion.14), channel_id=1, source_target_pairs={{0,2},{2,0},{1,3},{3,1},{4,6},{6,4},{5,7},{7,5},{8,10},{10,8},{9,1... | collective-permute-start | bytes 2359304 | tf_op jit(solution)/shard_map/ppermute | solution.py:22
  10.9 8.9 %collective-permute-start.4 = (f32[128,384]{0,1:T(8,128)}, f32[128,384]{0,1:T(8,128)}, u32[]{:S(2)}, u32[]{:S(2)}) collective-permute-start(f32[128,384]{0,1:T(8,128)} %get-tuple-element.88), channel_id=1, source_target_pairs={{0,8},{8,16},{16,24},{24,0},{1,9},{9,17},{17,25},{25,1},{2,10},{10... | collective-permute-start | bytes 589832 | tf_op jit(solution)/shard_map/ppermute | solution.py:42
  10.9 11.6 %collective-permute-start.5 = (f32[128,384]{0,1:T(8,128)}, f32[128,384]{0,1:T(8,128)}, u32[]{:S(2)}, u32[]{:S(2)}) collective-permute-start(f32[128,384]{0,1:T(8,128)} %get-tuple-element.87), channel_id=1, source_target_pairs={{0,16},{8,24},{16,0},{24,8},{1,17},{9,25},{17,1},{25,9},{2,18},{10... | collective-permute-start | bytes 589832 | tf_op jit(solution)/shard_map/ppermute | solution.py:42
  13.0 10.5 %collective-permute-start.6 = (f32[128,384]{0,1:T(8,128)S(1)}, f32[128,384]{0,1:T(8,128)}, u32[]{:S(2)}, u32[]{:S(2)}) collective-permute-start(f32[128,384]{0,1:T(8,128)S(1)} %get-tuple-element.86), channel_id=1, source_target_pairs={{0,24},{8,0},{16,8},{24,16},{1,25},{9,1},{17,9},{25,17},{2,26},{10... | collective-permute-start | bytes 589832 | tf_op jit(solution)/shard_map/ppermute | solution.py:42
  15.5 11.5 %collective-permute-start.7 = (f32[256,384]{0,1:T(8,128)S(1)}, f32[256,384]{0,1:T(8,128)S(1)}, u32[]{:S(2)}, u32[]{:S(2)}) collective-permute-start(f32[256,384]{0,1:T(8,128)S(1)} %get-tuple-element.84), channel_id=1, source_target_pairs={{0,4},{4,0},{1,5},{5,1},{2,6},{6,2},{3,7},{7,3},{8,12},{12,8},{9,1... | collective-permute-start | bytes 1179656 | tf_op jit(solution)/shard_map/ppermute | solution.py:42
  19.7 9.6 %collective-permute-start.10 = (f32[128,384]{0,1:T(8,128)S(1)}, f32[128,384]{0,1:T(8,128)S(1)}, u32[]{:S(2)}, u32[]{:S(2)}) collective-permute-start(f32[128,384]{0,1:T(8,128)S(1)} %get-tuple-element.80), channel_id=1, source_target_pairs={{0,24},{8,0},{16,8},{24,16},{1,25},{9,1},{17,9},{25,17},{2,26},{10... | collective-permute-start | bytes 589832 | tf_op jit(solution)/shard_map/ppermute | solution.py:42
  19.8 12.6 %collective-permute-start.8 = (f32[128,384]{0,1:T(8,128)S(1)}, f32[128,384]{0,1:T(8,128)S(1)}, u32[]{:S(2)}, u32[]{:S(2)}) collective-permute-start(f32[128,384]{0,1:T(8,128)S(1)} %get-tuple-element.82), channel_id=1, source_target_pairs={{0,8},{8,16},{16,24},{24,0},{1,9},{9,17},{17,25},{25,1},{2,10},{10... | collective-permute-start | bytes 589832 | tf_op jit(solution)/shard_map/ppermute | solution.py:42
  22.5 11.5 %collective-permute-start.9 = (f32[128,384]{0,1:T(8,128)S(1)}, f32[128,384]{0,1:T(8,128)S(1)}, u32[]{:S(2)}, u32[]{:S(2)}) collective-permute-start(f32[128,384]{0,1:T(8,128)S(1)} %get-tuple-element.81), channel_id=1, source_target_pairs={{0,16},{8,24},{16,0},{24,8},{1,17},{9,25},{17,1},{25,9},{2,18},{10... | collective-permute-start | bytes 589832 | tf_op jit(solution)/shard_map/ppermute | solution.py:42
  24.9 16.2 %collective-permute-start.11 = (f32[64,384]{0,1:T(8,128)S(1)}, f32[64,384]{0,1:T(8,128)S(1)}, u32[]{:S(2)}, u32[]{:S(2)}) collective-permute-start(f32[64,384]{0,1:T(8,128)S(1)} %get-tuple-element.110), channel_id=1, source_target_pairs={{0,4},{4,0},{1,5},{5,1},{2,6},{6,2},{3,7},{7,3},{8,12},{12,8},{9,1... | collective-permute-start | bytes 294920 | tf_op jit(solution)/shard_map/ppermute | solution.py:42
  27.3 13.7 %collective-permute-start.13 = (f32[64,384]{0,1:T(8,128)S(1)}, f32[64,384]{0,1:T(8,128)S(1)}, u32[]{:S(2)}, u32[]{:S(2)}) collective-permute-start(f32[64,384]{0,1:T(8,128)S(1)} %get-tuple-element.96), channel_id=1, source_target_pairs={{0,8},{8,16},{16,24},{24,0},{1,9},{9,17},{17,25},{25,1},{2,10},{10... | collective-permute-start | bytes 294920 | tf_op jit(solution)/shard_map/ppermute | solution.py:42
  29.3 11.7 %collective-permute-start.14 = (f32[64,384]{0,1:T(8,128)S(1)}, f32[64,384]{0,1:T(8,128)S(1)}, u32[]{:S(2)}, u32[]{:S(2)}) collective-permute-start(f32[64,384]{0,1:T(8,128)S(1)} %get-tuple-element.98), channel_id=1, source_target_pairs={{0,16},{8,24},{16,0},{24,8},{1,17},{9,25},{17,1},{25,9},{2,18},{10... | collective-permute-start | bytes 294920 | tf_op jit(solution)/shard_map/ppermute | solution.py:42
  32.4 8.6 %collective-permute-start.15 = (f32[64,384]{0,1:T(8,128)S(1)}, f32[64,384]{0,1:T(8,128)S(1)}, u32[]{:S(2)}, u32[]{:S(2)}) collective-permute-start(f32[64,384]{0,1:T(8,128)S(1)} %get-tuple-element.97), channel_id=1, source_target_pairs={{0,24},{8,0},{16,8},{24,16},{1,25},{9,1},{17,9},{25,17},{2,26},{10... | collective-permute-start | bytes 294920 | tf_op jit(solution)/shard_map/ppermute | solution.py:42
  34.2 7.2 %collective-permute-start.12 = (f32[64,384]{0,1:T(8,128)S(1)}, f32[64,384]{0,1:T(8,128)S(1)}, u32[]{:S(2)}, u32[]{:S(2)}) collective-permute-start(f32[64,384]{0,1:T(8,128)S(1)} %get-tuple-element.108), channel_id=1, source_target_pairs={{0,4},{4,0},{1,5},{5,1},{2,6},{6,2},{3,7},{7,3},{8,12},{12,8},{9,1... | collective-permute-start | bytes 294920 | tf_op jit(solution)/shard_map/ppermute | solution.py:42
  41.2 18.0 %copy-start = (f32[4,192,128]{2,1,0:T(8,128)S(1)}, f32[4,192,128]{2,1,0:T(8,128)}, u32[]{:S(2)}) copy-start(f32[4,192,128]{2,1,0:T(8,128)} %refs_2_.3) | copy-start | bytes 1179652
  42.2 16.8 %all-to-all-start = ((f32[8,24,384]{2,1,0:T(8,128)}), f32[8,24,384]{2,1,0:T(8,128)S(1)}, u32[]{:S(2)}, u32[]{:S(2)}) async-start(f32[8,24,384]{2,1,0:T(8,128)} %pad_maximum_fusion.3), calls=%async_computation | async-start | bytes 589824 | tf_op jit(solution)/shard_map/all_to_all | solution.py:73
  49.4 2.9 %collective-permute-start.3 = (f32[2,24,128]{2,1,0:T(8,128)S(1)}, f32[2,24,128]{2,1,0:T(8,128)S(1)}, u32[]{:S(2)}, u32[]{:S(2)}) collective-permute-start(f32[2,24,128]{2,1,0:T(8,128)S(1)} %pad_maximum_fusion.10), channel_id=1, source_target_pairs={{0,1},{1,0},{2,3},{3,2},{4,5},{5,4},{6,7},{7,6},{8,9},{9,8},{10,11... | collective-permute-start | bytes 73736 | tf_op jit(solution)/shard_map/ppermute | solution.py:22
  59.5 3.0 %collective-permute-start.16 = (f32[2,24,128]{2,1,0:T(8,128)S(1)}, f32[2,24,128]{2,1,0:T(8,128)S(1)}, u32[]{:S(2)}, u32[]{:S(2)}) collective-permute-start(f32[2,24,128]{2,1,0:T(8,128)S(1)} %fusion.2), channel_id=1, source_target_pairs={{0,1},{1,0},{2,3},{3,2},{4,5},{5,4},{6,7},{7,6},{8,9},{9,8},{10,11... | collective-permute-start | bytes 73736 | tf_op jit(solution)/shard_map/ppermute | solution.py:22
  64.2 15.3 %all-to-all-start.1 = ((f32[8,40,384]{2,1,0:T(8,128)}), f32[8,40,384]{2,1,0:T(8,128)S(1)}, u32[]{:S(2)}, u32[]{:S(2)}) async-start(f32[8,40,384]{2,1,0:T(8,128)} %maximum_maximum_fusion), calls=%async_computation.1 | async-start | bytes 983040 | tf_op jit(solution)/shard_map/all_to_all | solution.py:73
  79.5 7.6 %collective-permute-start.17 = (f32[128,384]{1,0:T(8,128)S(1)}, f32[128,384]{1,0:T(8,128)S(1)}, u32[]{:S(2)}, u32[]{:S(2)}) collective-permute-start(f32[128,384]{1,0:T(8,128)S(1)} %bitcast.118), channel_id=1, source_target_pairs={{0,4},{4,0},{1,5},{5,1},{2,6},{6,2},{3,7},{7,3},{8,12},{12,8},{9,1... | collective-permute-start | bytes 589832 | tf_op jit(solution)/shard_map/ppermute | solution.py:22
  82.2 6.0 %collective-permute-start.18 = (f32[80,384]{1,0:T(8,128)S(1)}, f32[80,384]{1,0:T(8,128)S(1)}, u32[]{:S(2)}, u32[]{:S(2)}) collective-permute-start(f32[80,384]{1,0:T(8,128)S(1)} %pad_maximum_fusion.6), channel_id=1, source_target_pairs={{0,8},{8,16},{16,24},{24,0},{1,9},{9,17},{17,25},{25,1},{2,10},{10... | collective-permute-start | bytes 368648 | tf_op jit(solution)/shard_map/ppermute | solution.py:61
  82.8 7.9 %collective-permute-start.19 = (f32[80,384]{1,0:T(8,128)S(1)}, f32[80,384]{1,0:T(8,128)S(1)}, u32[]{:S(2)}, u32[]{:S(2)}) collective-permute-start(f32[80,384]{1,0:T(8,128)S(1)} %pad_maximum_fusion.6), channel_id=1, source_target_pairs={{0,16},{8,24},{16,0},{24,8},{1,17},{9,25},{17,1},{25,9},{2,18},{10... | collective-permute-start | bytes 368648 | tf_op jit(solution)/shard_map/ppermute | solution.py:61
  87.1 3.7 %collective-permute-start.20 = (f32[80,384]{1,0:T(8,128)S(1)}, f32[80,384]{1,0:T(8,128)S(1)}, u32[]{:S(2)}, u32[]{:S(2)}) collective-permute-start(f32[80,384]{1,0:T(8,128)S(1)} %pad_maximum_fusion.6), channel_id=1, source_target_pairs={{0,24},{8,0},{16,8},{24,16},{1,25},{9,1},{17,9},{25,17},{2,26},{10... | collective-permute-start | bytes 368648 | tf_op jit(solution)/shard_map/ppermute | solution.py:61
  90.9 8.5 %collective-permute-start.21 = (f32[256,384]{1,0:T(8,128)S(1)}, f32[256,384]{1,0:T(8,128)S(1)}, u32[]{:S(2)}, u32[]{:S(2)}) collective-permute-start(f32[256,384]{1,0:T(8,128)S(1)} %bitcast.113), channel_id=1, source_target_pairs={{0,4},{4,0},{1,5},{5,1},{2,6},{6,2},{3,7},{7,3},{8,12},{12,8},{9,1... | collective-permute-start | bytes 1179656 | tf_op jit(solution)/shard_map/ppermute | solution.py:22
  91.1 8.2 %collective-permute-start.24 = (f32[16,384]{1,0:T(8,128)S(1)}, f32[16,384]{1,0:T(8,128)S(1)}, u32[]{:S(2)}, u32[]{:S(2)}) collective-permute-start(f32[16,384]{1,0:T(8,128)S(1)} %slice_reduce_fusion.1), channel_id=1, source_target_pairs={{0,4},{4,0},{1,5},{5,1},{2,6},{6,2},{3,7},{7,3},{8,12},{12,8},{9,1... | collective-permute-start | bytes 73736 | tf_op jit(solution)/shard_map/ppermute | solution.py:22
  95.3 27.5 %all-to-all-start.2 = ((f32[4,256,384]{2,1,0:T(8,128)}), f32[4,256,384]{2,1,0:T(8,128)S(1)}, u32[]{:S(2)}, u32[]{:S(2)}) async-start(f32[4,256,384]{2,1,0:T(8,128)} %broadcast_in_dim.30), calls=%async_computation.2 | async-start | bytes 3145728 | tf_op jit(solution)/shard_map/all_to_all | solution.py:73
  99.3 10.3 %collective-permute-start.25 = (f32[16,384]{1,0:T(8,128)S(1)}, f32[16,384]{1,0:T(8,128)S(1)}, u32[]{:S(2)}, u32[]{:S(2)}) collective-permute-start(f32[16,384]{1,0:T(8,128)S(1)} %add.303), channel_id=1, source_target_pairs={{0,128},{32,160},{64,192},{96,224},{128,0},{160,32},{192,64},{224,... | collective-permute-start | bytes 73736 | tf_op jit(solution)/shard_map/ppermute | solution.py:22
  99.5 18.4 %collective-permute-start.22 = (f32[64,1,8,384]{3,2,1,0:T(8,128)S(1)}, f32[64,1,8,384]{3,2,1,0:T(8,128)S(1)}, u32[]{:S(2)}, u32[]{:S(2)}) collective-permute-start(f32[64,1,8,384]{3,2,1,0:T(8,128)S(1)} %bitcast.101), channel_id=1, source_target_pairs={{0,2},{2,0},{1,3},{3,1},{4,6},{6,4},{5,7},{7,5},{8,10},{10,8},{9,1... | collective-permute-start | bytes 2359304 | tf_op jit(solution)/shard_map/ppermute | solution.py:22
  109.6 0.6 copy-start.1
  109.6 1.2 copy-start.2
  110.9 4.3 %collective-permute-start.26 = (f32[32,384]{1,0:T(8,128)}, f32[32,384]{1,0:T(8,128)}, u32[]{:S(2)}, u32[]{:S(2)}) collective-permute-start(f32[32,384]{1,0:T(8,128)} %pad_maximum_fusion.8), channel_id=1, source_target_pairs={{0,64},{32,96},{64,0},{96,32},{128,192},{160,224},{192,128},{224,1... | collective-permute-start | bytes 147464 | tf_op jit(solution)/shard_map/ppermute | solution.py:22
  116.7 13.4 %collective-permute-start.27 = (f32[64,384]{1,0:T(8,128)}, f32[64,384]{1,0:T(8,128)}, u32[]{:S(2)}, u32[]{:S(2)}) collective-permute-start(f32[64,384]{1,0:T(8,128)} %pad_maximum_fusion.7), channel_id=1, source_target_pairs={{0,32},{32,0},{64,96},{96,64},{128,160},{160,128},{192,224},{224,1... | collective-permute-start | bytes 294920 | tf_op jit(solution)/shard_map/ppermute | solution.py:22
  122.8 16.5 %collective-permute-start.23 = (f32[64,2,8,384]{3,2,1,0:T(8,128)S(1)}, f32[64,2,8,384]{3,2,1,0:T(8,128)S(1)}, u32[]{:S(2)}, u32[]{:S(2)}) collective-permute-start(f32[64,2,8,384]{3,2,1,0:T(8,128)S(1)} %bitcast.99), channel_id=1, source_target_pairs={{0,2},{2,0},{1,3},{3,1},{4,6},{6,4},{5,7},{7,5},{8,10},{10,8},{9,1... | collective-permute-start | bytes 4718600 | tf_op jit(solution)/shard_map/ppermute | solution.py:22
  131.8 5.4 %collective-permute-start.28 = (f32[2,128,128]{2,1,0:T(8,128)S(1)}, f32[2,128,128]{2,1,0:T(8,128)S(1)}, u32[]{:S(2)}, u32[]{:S(2)}) collective-permute-start(f32[2,128,128]{2,1,0:T(8,128)S(1)} %fusion.21), channel_id=1, source_target_pairs={{0,1},{1,0},{2,3},{3,2},{4,5},{5,4},{6,7},{7,6},{8,9},{9,8},{10,11... | collective-permute-start | bytes 393224 | tf_op jit(solution)/shard_map/ppermute | solution.py:22
  138.4 5.1 %collective-permute-start.29 = (f32[2,192,128]{2,1,0:T(8,128)}, f32[2,192,128]{2,1,0:T(8,128)}, u32[]{:S(2)}, u32[]{:S(2)}) collective-permute-start(f32[2,192,128]{2,1,0:T(8,128)} %fusion), channel_id=1, source_target_pairs={{0,2},{2,0},{1,3},{3,1},{4,6},{6,4},{5,7},{7,5},{8,10},{10,8},{9,1... | collective-permute-start | bytes 589832 | tf_op jit(solution)/shard_map/ppermute | solution.py:22

commit v9 on v7

--- a/solution.py
+++ b/solution.py
@@ -165,7 +165,7 @@
     grad = grads[0]
 
     given, sent = [], []
-    for step, chunk in (("give", 0), ("give", 1), ("add", 0), ("give", 2), ("add", 1), ("add", 2)):
+    for step, chunk in (("give", 0), ("give", 1), ("add", 0), ("add", 1), ("give", 2), ("add", 2)):
         if step == "give":
             part = lax.dynamic_slice(grad, ((1 - core) * half, 0, chunk * some), (half, depth, some))
             grad = after(grad, part)

time: 139 us -> 139 us (level)
  starting transfers between devices: 62.2 us -> 58 us
  waiting for transfers between devices: 40.7 us -> 44.2 us
  other arithmetic: 8.5 us -> 10.3 us
    ppermute x15, waiting for transfers between devices: 13.7 us -> 18.1 us  [flip(): return lax.ppermute(x, axis, [(i, i ^ bit) for i in range(n)])]
    ppermute x15, starting transfers between devices: 26.9 us -> 23.1 us  [flip(): return lax.ppermute(x, axis, [(i, i ^ bit) for i in range(n)])]
    add x6, other arithmetic: 1.35 us -> 3.18 us  [scatter(): total + lax.ppermute(parts[k], axis, [(i, (i + k) % n) for i in range(n)])]
  transfers between devices with their start and end apart: 33 -> 33, of which waited for: 12 -> 14; matrix products, arithmetic and copies ran while one was open for 10% -> 9% of each run, Pallas kernels for 10% -> 10%
where the time goes in v9:
time: 139 us; the launch traced here: 138 us
  starting transfers between devices  58 us (42%)
  waiting for transfers between devices  44.2 us (32%)
  Pallas kernels  14.4 us (10%)
  other arithmetic  10.3 us (7%)
  local copies, waits for them, and re-layouts  8.29 us (6%)
  matrix products  1.84 us (1%)
    ppermute x15, starting transfers between devices, flip(): return lax.ppermute(x, axis, [(i, i ^ bit) for i in range(n)])  23.1 us
    all_to_all x3, waiting for transfers between devices, exchange(): return lax.all_to_all(parts, axis, split_axis=0, concat_axis=0)  18.4 us
    ppermute x15, waiting for transfers between devices, flip(): return lax.ppermute(x, axis, [(i, i ^ bit) for i in range(n)])  18.1 us
    ppermute x12, starting transfers between devices, scatter(): lax.ppermute(parts[k], axis, [(i, (i + k) % n) for i in range(n)])  15.7 us
    all_to_all x3, starting transfers between devices, exchange(): return lax.all_to_all(parts, axis, split_axis=0, concat_axis=0)  14.5 us
    pallas_call x3, Pallas kernels, finish(): pl.pallas_call(functools.partial(finish_kernel, chunks, count), in_specs=...  14.4 us
    ppermute x12, waiting for transfers between devices, scatter(): lax.ppermute(parts[k], axis, [(i, (i + k) % n) for i in range(n)])  7.72 us
    ppermute x3, starting transfers between devices, around(): lax.ppermute(x, axis, [(i, (i + k) % n) for i in range(n)])  4.68 us
  transfers between devices with their start and end apart: 33, of which 14 were waited for; matrix products, arithmetic and copies ran while one was open for 9% of the time, Pallas kernels for 10%

profile of v9, /device:TPU:1, one launch (start us, length us, event | category | flops | bytes accessed | tf_op | source)
XLA Modules:
  0.0 138.3 jit_solution(17344403007665763555)
XLA Ops:
  0.6 1.2 dynamic-slice_bitcast_fusion
  1.8 3.3 %collective-permute-start = (f32[2,192,512]{2,1,0:T(8,128)S(1)}, f32[2,192,512]{2,1,0:T(8,128)S(1)}, u32[]{:S(2)}, u32[]{:S(2)}) collective-permute-start(f32[2,192,512]{2,1,0:T(8,128)S(1)} %dynamic-slice_bitcast_fusion), channel_id=1, source_target_pairs={{0,2},{2,0},{1,3},{3,1},{4,6},{6,4},{5,7},{7,5},{8,10},{10,8},{9,1... | collective-permute-start | bytes 2359304 | tf_op jit(solution)/shard_map/ppermute | solution.py:22
  5.2 1.2 constant_dynamic-slice_fusion.15
  6.5 0.5 collective-permute-done
  7.1 1.3 dynamic-slice_add_fusion.2
  8.5 0.2 collective-permute-done.1
  8.7 1.3 dynamic-slice_add_fusion.1
  10.1 1.2 constant_dynamic-slice_fusion.14
  11.3 0.2 collective-permute-start.2
  11.5 2.2 %collective-permute-start.5 = (f32[128,384]{0,1:T(8,128)S(1)}, f32[128,384]{0,1:T(8,128)}, u32[]{:S(2)}, u32[]{:S(2)}) collective-permute-start(f32[128,384]{0,1:T(8,128)S(1)} %get-tuple-element.83), channel_id=1, source_target_pairs={{0,16},{8,24},{16,0},{24,8},{1,17},{9,25},{17,1},{25,9},{2,18},{10... | collective-permute-start | bytes 589832 | tf_op jit(solution)/shard_map/ppermute | solution.py:42
  13.7 1.1 collective-permute-start.6
  14.8 2.7 %collective-permute-start.7 = (f32[256,384]{0,1:T(8,128)S(1)}, f32[256,384]{0,1:T(8,128)S(1)}, u32[]{:S(2)}, u32[]{:S(2)}) collective-permute-start(f32[256,384]{0,1:T(8,128)S(1)} %get-tuple-element.80), channel_id=1, source_target_pairs={{0,4},{4,0},{1,5},{5,1},{2,6},{6,2},{3,7},{7,3},{8,12},{12,8},{9,1... | collective-permute-start | bytes 1179656 | tf_op jit(solution)/shard_map/ppermute | solution.py:42
  17.5 1.3 dynamic-slice_add_fusion
  19.0 0.5 collective-permute-done.4
  19.5 1.0 collective-permute-start.8
  20.5 2.3 %collective-permute-done.5 = f32[128,384]{0,1:T(8,128)} collective-permute-done((f32[128,384]{0,1:T(8,128)S(1)}, f32[128,384]{0,1:T(8,128)}, u32[]{:S(2)}, u32[]{:S(2)}) %collective-permute-start.5) | collective-permute-done | bytes 196640 | tf_op jit(solution)/shard_map/ppermute | solution.py:42
  22.7 1.1 collective-permute-start.9
  23.8 1.2 add_add_fusion.2
  25.0 0.2 constant_dynamic-slice_fusion.6
  25.2 2.1 %collective-permute-start.11 = (f32[64,384]{0,1:T(8,128)S(1)}, f32[64,384]{0,1:T(8,128)S(1)}, u32[]{:S(2)}, u32[]{:S(2)}) collective-permute-start(f32[64,384]{0,1:T(8,128)S(1)} %get-tuple-element.106), channel_id=1, source_target_pairs={{0,4},{4,0},{1,5},{5,1},{2,6},{6,2},{3,7},{7,3},{8,12},{12,8},{9,1... | collective-permute-start | bytes 294920 | tf_op jit(solution)/shard_map/ppermute | solution.py:42
  27.3 0.3 constant_dynamic-slice_fusion.4
  27.6 0.6 collective-permute-start.13
  28.2 1.4 constant_dynamic-slice_fusion.10
  30.0 2.9 %collective-permute-start.14 = (f32[64,384]{0,1:T(8,128)S(1)}, f32[64,384]{0,1:T(8,128)S(1)}, u32[]{:S(2)}, u32[]{:S(2)}) collective-permute-start(f32[64,384]{0,1:T(8,128)S(1)} %get-tuple-element.94), channel_id=1, source_target_pairs={{0,16},{8,24},{16,0},{24,8},{1,17},{9,25},{17,1},{25,9},{2,18},{10... | collective-permute-start | bytes 294920 | tf_op jit(solution)/shard_map/ppermute | solution.py:42
  32.9 1.3 collective-permute-start.15
  34.2 1.0 add_add_fusion.1
  35.2 0.2 constant_dynamic-slice_fusion
  35.4 0.6 collective-permute-start.12
  36.0 5.0 %collective-permute-done.13 = f32[64,384]{0,1:T(8,128)} collective-permute-done((f32[64,384]{0,1:T(8,128)S(1)}, f32[64,384]{0,1:T(8,128)}, u32[]{:S(2)}, u32[]{:S(2)}) %collective-permute-start.13) | collective-permute-done | bytes 98336 | tf_op jit(solution)/shard_map/ppermute | solution.py:42
  41.0 1.0 add_add_fusion
  42.4 0.7 pad_maximum_fusion.3
  43.1 7.5 %all-to-all-start = ((f32[8,24,384]{2,1,0:T(8,128)}), f32[8,24,384]{2,1,0:T(8,128)S(1)}, u32[]{:S(2)}, u32[]{:S(2)}) async-start(f32[8,24,384]{2,1,0:T(8,128)} %pad_maximum_fusion.3), calls=%async_computation | async-start | bytes 589824 | tf_op jit(solution)/shard_map/all_to_all | solution.py:73
  50.6 0.5 collective-permute-start.3
  51.1 2.4 %collective-permute-done.3 = f32[2,24,128]{2,1,0:T(8,128)S(1)} collective-permute-done((f32[2,24,128]{2,1,0:T(8,128)S(1)}, f32[2,24,128]{2,1,0:T(8,128)S(1)}, u32[]{:S(2)}, u32[]{:S(2)}) %collective-permute-start.3) | collective-permute-done | bytes 24608 | tf_op jit(solution)/shard_map/ppermute | solution.py:22
  53.7 6.7 %all-to-all-done = f32[8,24,384]{2,1,0:T(8,128)S(1)} async-done(((f32[8,24,384]{2,1,0:T(8,128)}), f32[8,24,384]{2,1,0:T(8,128)S(1)}, u32[]{:S(2)}, u32[]{:S(2)}) %all-to-all-start) | async-done | bytes 294944 | tf_op jit(solution)/shard_map/all_to_all | solution.py:73
  60.5 0.3 fusion.2
  60.8 0.4 collective-permute-start.16
  61.2 2.3 %collective-permute-done.16 = f32[2,24,128]{2,1,0:T(8,128)S(1)} collective-permute-done((f32[2,24,128]{2,1,0:T(8,128)S(1)}, f32[2,24,128]{2,1,0:T(8,128)S(1)}, u32[]{:S(2)}, u32[]{:S(2)}) %collective-permute-start.16) | collective-permute-done | bytes 24608 | tf_op jit(solution)/shard_map/ppermute | solution.py:22
  63.7 0.5 fusion.7
  64.4 0.8 maximum_maximum_fusion
  65.2 3.5 %all-to-all-start.1 = ((f32[8,40,384]{2,1,0:T(8,128)}), f32[8,40,384]{2,1,0:T(8,128)S(1)}, u32[]{:S(2)}, u32[]{:S(2)}) async-start(f32[8,40,384]{2,1,0:T(8,128)} %maximum_maximum_fusion), calls=%async_computation.1 | async-start | bytes 983040 | tf_op jit(solution)/shard_map/all_to_all | solution.py:73
  68.7 11.7 %all-to-all-done.1 = f32[8,40,384]{2,1,0:T(8,128)S(1)} async-done(((f32[8,40,384]{2,1,0:T(8,128)}), f32[8,40,384]{2,1,0:T(8,128)S(1)}, u32[]{:S(2)}, u32[]{:S(2)}) %all-to-all-start.1) | async-done | bytes 491552 | tf_op jit(solution)/shard_map/all_to_all | solution.py:73
  80.5 1.3 collective-permute-start.17
  81.8 2.2 %collective-permute-start.18 = (f32[80,384]{1,0:T(8,128)S(1)}, f32[80,384]{1,0:T(8,128)S(1)}, u32[]{:S(2)}, u32[]{:S(2)}) collective-permute-start(f32[80,384]{1,0:T(8,128)S(1)} %pad_maximum_fusion.6), channel_id=1, source_target_pairs={{0,8},{8,16},{16,24},{24,0},{1,9},{9,17},{17,25},{25,1},{2,10},{10... | collective-permute-start | bytes 368648 | tf_op jit(solution)/shard_map/ppermute | solution.py:61
  84.0 2.0 %collective-permute-start.19 = (f32[80,384]{1,0:T(8,128)S(1)}, f32[80,384]{1,0:T(8,128)S(1)}, u32[]{:S(2)}, u32[]{:S(2)}) collective-permute-start(f32[80,384]{1,0:T(8,128)S(1)} %pad_maximum_fusion.6), channel_id=1, source_target_pairs={{0,16},{8,24},{16,0},{24,8},{1,17},{9,25},{17,1},{25,9},{2,18},{10... | collective-permute-start | bytes 368648 | tf_op jit(solution)/shard_map/ppermute | solution.py:61
  86.1 0.5 collective-permute-start.20
  86.5 0.4 collective-permute-done.17
  87.0 1.2 broadcast_in_dim.35
  88.2 3.6 %all-to-all-start.2 = ((f32[4,256,384]{2,1,0:T(8,128)}), f32[4,256,384]{2,1,0:T(8,128)S(1)}, u32[]{:S(2)}, u32[]{:S(2)}) async-start(f32[4,256,384]{2,1,0:T(8,128)} %broadcast_in_dim.35), calls=%async_computation.2 | async-start | bytes 3145728 | tf_op jit(solution)/shard_map/all_to_all | solution.py:73
  92.0 1.7 %collective-permute-start.24 = (f32[16,384]{1,0:T(8,128)S(1)}, f32[16,384]{1,0:T(8,128)S(1)}, u32[]{:S(2)}, u32[]{:S(2)}) collective-permute-start(f32[16,384]{1,0:T(8,128)S(1)} %slice_reduce_fusion.1), channel_id=1, source_target_pairs={{0,4},{4,0},{1,5},{5,1},{2,6},{6,2},{3,7},{7,3},{8,12},{12,8},{9,1... | collective-permute-start | bytes 73736 | tf_op jit(solution)/shard_map/ppermute | solution.py:22
  93.6 2.9 %collective-permute-done.24 = f32[16,384]{1,0:T(8,128)S(1)} collective-permute-done((f32[16,384]{1,0:T(8,128)S(1)}, f32[16,384]{1,0:T(8,128)S(1)}, u32[]{:S(2)}, u32[]{:S(2)}) %collective-permute-start.24) | collective-permute-done | bytes 24608 | tf_op jit(solution)/shard_map/ppermute | solution.py:22
  96.5 0.2 collective-permute-start.25
  96.8 1.7 %collective-permute-start.21 = (f32[256,384]{1,0:T(8,128)S(1)}, f32[256,384]{1,0:T(8,128)S(1)}, u32[]{:S(2)}, u32[]{:S(2)}) collective-permute-start(f32[256,384]{1,0:T(8,128)S(1)} %bitcast.113), channel_id=1, source_target_pairs={{0,4},{4,0},{1,5},{5,1},{2,6},{6,2},{3,7},{7,3},{8,12},{12,8},{9,1... | collective-permute-start | bytes 1179656 | tf_op jit(solution)/shard_map/ppermute | solution.py:22
  98.4 4.7 %collective-permute-done.25 = f32[16,384]{1,0:T(8,128)S(1)} collective-permute-done((f32[16,384]{1,0:T(8,128)S(1)}, f32[16,384]{1,0:T(8,128)S(1)}, u32[]{:S(2)}, u32[]{:S(2)}) %collective-permute-start.25) | collective-permute-done | bytes 24608 | tf_op jit(solution)/shard_map/ppermute | solution.py:22
  103.2 4.6 %collective-permute-done.26 = f32[32,384]{1,0:T(8,128)S(1)} collective-permute-done((f32[32,384]{1,0:T(8,128)S(1)}, f32[32,384]{1,0:T(8,128)S(1)}, u32[]{:S(2)}, u32[]{:S(2)}) %collective-permute-start.26) | collective-permute-done | bytes 49184 | tf_op jit(solution)/shard_map/ppermute | solution.py:22
  107.9 11.5 %collective-permute-start.23 = (f32[64,2,8,384]{3,2,1,0:T(8,128)S(1)}, f32[64,2,8,384]{3,2,1,0:T(8,128)}, u32[]{:S(2)}, u32[]{:S(2)}) collective-permute-start(f32[64,2,8,384]{3,2,1,0:T(8,128)S(1)} %bitcast.99), channel_id=1, source_target_pairs={{0,2},{2,0},{1,3},{3,1},{4,6},{6,4},{5,7},{7,5},{8,10},{10,8},{9,1... | collective-permute-start | bytes 4718600 | tf_op jit(solution)/shard_map/ppermute | solution.py:22
  119.7 4.3 %finish.3 = (f32[4,192,1536]{2,1,0:T(8,128)}, f32[4,64,1536]{2,1,0:T(8,128)}, f32[4,64,1536]{2,1,0:T(8,128)}) custom-call(s32[1]{0:T(128)} %bitcast.refs_0_, f32[64,2,8,384]{3,2,1,0:T(8,128)S(1)} %bitcast.100, f32[4,192,128]{2,1,0:T(8,128)S(1)} %copy-done, f32[4,192,1536]{2,1,0:T(8,128)} %refs_4_.5, f32[4,64,1536]{2,1,0:T(8,128)} %refs_5_.5, ...), custom_call_target="tpu_custom_call" | custom-call | flops 603979776 | bytes 5242880 | tf_op jit(solution)/shard_map/finish/pallas_call | solution.py:131
  124.1 0.7 fusion.22
  124.8 0.4 collective-permute-start.28
  125.2 1.4 %collective-permute-start.22 = (f32[64,1,8,384]{3,2,1,0:T(8,128)S(1)}, f32[64,1,8,384]{3,2,1,0:T(8,128)S(1)}, u32[]{:S(2)}, u32[]{:S(2)}) collective-permute-start(f32[64,1,8,384]{3,2,1,0:T(8,128)S(1)} %bitcast.101), channel_id=1, source_target_pairs={{0,2},{2,0},{1,3},{3,1},{4,6},{6,4},{5,7},{7,5},{8,10},{10,8},{9,1... | collective-permute-start | bytes 2359304 | tf_op jit(solution)/shard_map/ppermute | solution.py:22
  126.6 5.2 %finish.4 = (f32[4,192,1536]{2,1,0:T(8,128)}, f32[4,64,1536]{2,1,0:T(8,128)}, f32[4,64,1536]{2,1,0:T(8,128)}) custom-call(s32[1]{0:T(128)} %bitcast.1.refs_0_, f32[64,2,8,384]{3,2,1,0:T(8,128)} %collective-permute-done.23.refs_1_, f32[4,192,128]{2,1,0:T(8,128)S(1)} %copy-done, ...), custom_call_target="tpu_custom_call", output_to_operand_aliasing={{0}: (6, {}), {1}: (7, {}), {2}: (8, {})} | custom-call | flops 603979776 | bytes 5242880 | tf_op jit(solution)/shard_map/finish/pallas_call | solution.py:131
  132.0 0.4 fusion
  132.6 4.9 %finish.5 = (f32[4,192,1536]{2,1,0:T(8,128)}, f32[4,64,1536]{2,1,0:T(8,128)}, f32[4,64,1536]{2,1,0:T(8,128)}) custom-call(s32[2]{0:T(128)S(1)} %pad_add_fusion.refs_0_, f32[64,1,8,384]{3,2,1,0:T(8,128)S(1)} %bitcast.102, f32[64,1,8,384]{3,2,1,0:T(8,128)S(1)} %collective-permute-done.22.refs_2_, ...), custom_call_target="tpu_custom_call", output_to_operand_aliasing={{0}: (7, {}), {1}: (8, {}), {2}: (9, {})} | custom-call | flops 603979776 | bytes 5242880 | tf_op jit(solution)/shard_map/finish/pallas_call | solution.py:131
  137.5 0.8 pad_maximum_fusion.2
  (87 shorter events, 3.2 us)
Async XLA Ops:
  1.8 5.2 %collective-permute-start = (f32[2,192,512]{2,1,0:T(8,128)S(1)}, f32[2,192,512]{2,1,0:T(8,128)S(1)}, u32[]{:S(2)}, u32[]{:S(2)}) collective-permute-start(f32[2,192,512]{2,1,0:T(8,128)S(1)} %dynamic-slice_bitcast_fusion), channel_id=1, source_target_pairs={{0,2},{2,0},{1,3},{3,1},{4,6},{6,4},{5,7},{7,5},{8,10},{10,8},{9,1... | collective-permute-start | bytes 2359304 | tf_op jit(solution)/shard_map/ppermute | solution.py:22
  6.3 2.4 %collective-permute-start.1 = (f32[2,192,512]{2,1,0:T(8,128)S(1)}, f32[2,192,512]{2,1,0:T(8,128)S(1)}, u32[]{:S(2)}, u32[]{:S(2)}) collective-permute-start(f32[2,192,512]{2,1,0:T(8,128)S(1)} %constant_dynamic-slice_fusion.15), channel_id=1, source_target_pairs={{0,2},{2,0},{1,3},{3,1},{4,6},{6,4},{5,7},{7,5},{8,10},{10,8},{9,1... | collective-permute-start | bytes 2359304 | tf_op jit(solution)/shard_map/ppermute | solution.py:22
  11.3 6.2 %collective-permute-start.2 = (f32[2,192,512]{2,1,0:T(8,128)S(1)}, f32[2,192,512]{2,1,0:T(8,128)S(1)}, u32[]{:S(2)}, u32[]{:S(2)}) collective-permute-start(f32[2,192,512]{2,1,0:T(8,128)S(1)} %constant_dynamic-slice_fusion.14), channel_id=1, source_target_pairs={{0,2},{2,0},{1,3},{3,1},{4,6},{6,4},{5,7},{7,5},{8,10},{10,8},{9,1... | collective-permute-start | bytes 2359304 | tf_op jit(solution)/shard_map/ppermute | solution.py:22
  11.5 8.0 %collective-permute-start.4 = (f32[128,384]{0,1:T(8,128)S(1)}, f32[128,384]{0,1:T(8,128)}, u32[]{:S(2)}, u32[]{:S(2)}) collective-permute-start(f32[128,384]{0,1:T(8,128)S(1)} %get-tuple-element.84), channel_id=1, source_target_pairs={{0,8},{8,16},{16,24},{24,0},{1,9},{9,17},{17,25},{25,1},{2,10},{10... | collective-permute-start | bytes 589832 | tf_op jit(solution)/shard_map/ppermute | solution.py:42
  11.5 11.2 %collective-permute-start.5 = (f32[128,384]{0,1:T(8,128)S(1)}, f32[128,384]{0,1:T(8,128)}, u32[]{:S(2)}, u32[]{:S(2)}) collective-permute-start(f32[128,384]{0,1:T(8,128)S(1)} %get-tuple-element.83), channel_id=1, source_target_pairs={{0,16},{8,24},{16,0},{24,8},{1,17},{9,25},{17,1},{25,9},{2,18},{10... | collective-permute-start | bytes 589832 | tf_op jit(solution)/shard_map/ppermute | solution.py:42
  13.7 10.1 %collective-permute-start.6 = (f32[128,384]{0,1:T(8,128)S(1)}, f32[128,384]{0,1:T(8,128)}, u32[]{:S(2)}, u32[]{:S(2)}) collective-permute-start(f32[128,384]{0,1:T(8,128)S(1)} %get-tuple-element.82), channel_id=1, source_target_pairs={{0,24},{8,0},{16,8},{24,16},{1,25},{9,1},{17,9},{25,17},{2,26},{10... | collective-permute-start | bytes 589832 | tf_op jit(solution)/shard_map/ppermute | solution.py:42
  14.8 12.5 %collective-permute-start.7 = (f32[256,384]{0,1:T(8,128)S(1)}, f32[256,384]{0,1:T(8,128)S(1)}, u32[]{:S(2)}, u32[]{:S(2)}) collective-permute-start(f32[256,384]{0,1:T(8,128)S(1)} %get-tuple-element.80), channel_id=1, source_target_pairs={{0,4},{4,0},{1,5},{5,1},{2,6},{6,2},{3,7},{7,3},{8,12},{12,8},{9,1... | collective-permute-start | bytes 1179656 | tf_op jit(solution)/shard_map/ppermute | solution.py:42
  18.9 11.1 %collective-permute-start.10 = (f32[128,384]{0,1:T(8,128)S(1)}, f32[128,384]{0,1:T(8,128)}, u32[]{:S(2)}, u32[]{:S(2)}) collective-permute-start(f32[128,384]{0,1:T(8,128)S(1)} %get-tuple-element.76), channel_id=1, source_target_pairs={{0,24},{8,0},{16,8},{24,16},{1,25},{9,1},{17,9},{25,17},{2,26},{10... | collective-permute-start | bytes 589832 | tf_op jit(solution)/shard_map/ppermute | solution.py:42
  19.5 13.5 %collective-permute-start.8 = (f32[128,384]{0,1:T(8,128)S(1)}, f32[128,384]{0,1:T(8,128)S(1)}, u32[]{:S(2)}, u32[]{:S(2)}) collective-permute-start(f32[128,384]{0,1:T(8,128)S(1)} %get-tuple-element.78), channel_id=1, source_target_pairs={{0,8},{8,16},{16,24},{24,0},{1,9},{9,17},{17,25},{25,1},{2,10},{10... | collective-permute-start | bytes 589832 | tf_op jit(solution)/shard_map/ppermute | solution.py:42
  22.7 11.5 %collective-permute-start.9 = (f32[128,384]{0,1:T(8,128)S(1)}, f32[128,384]{0,1:T(8,128)S(1)}, u32[]{:S(2)}, u32[]{:S(2)}) collective-permute-start(f32[128,384]{0,1:T(8,128)S(1)} %get-tuple-element.77), channel_id=1, source_target_pairs={{0,16},{8,24},{16,0},{24,8},{1,17},{9,25},{17,1},{25,9},{2,18},{10... | collective-permute-start | bytes 589832 | tf_op jit(solution)/shard_map/ppermute | solution.py:42
  25.2 16.8 %collective-permute-start.11 = (f32[64,384]{0,1:T(8,128)S(1)}, f32[64,384]{0,1:T(8,128)S(1)}, u32[]{:S(2)}, u32[]{:S(2)}) collective-permute-start(f32[64,384]{0,1:T(8,128)S(1)} %get-tuple-element.106), channel_id=1, source_target_pairs={{0,4},{4,0},{1,5},{5,1},{2,6},{6,2},{3,7},{7,3},{8,12},{12,8},{9,1... | collective-permute-start | bytes 294920 | tf_op jit(solution)/shard_map/ppermute | solution.py:42
  27.6 13.4 %collective-permute-start.13 = (f32[64,384]{0,1:T(8,128)S(1)}, f32[64,384]{0,1:T(8,128)}, u32[]{:S(2)}, u32[]{:S(2)}) collective-permute-start(f32[64,384]{0,1:T(8,128)S(1)} %get-tuple-element.92), channel_id=1, source_target_pairs={{0,8},{8,16},{16,24},{24,0},{1,9},{9,17},{17,25},{25,1},{2,10},{10... | collective-permute-start | bytes 294920 | tf_op jit(solution)/shard_map/ppermute | solution.py:42
  30.0 10.9 %collective-permute-start.14 = (f32[64,384]{0,1:T(8,128)S(1)}, f32[64,384]{0,1:T(8,128)S(1)}, u32[]{:S(2)}, u32[]{:S(2)}) collective-permute-start(f32[64,384]{0,1:T(8,128)S(1)} %get-tuple-element.94), channel_id=1, source_target_pairs={{0,16},{8,24},{16,0},{24,8},{1,17},{9,25},{17,1},{25,9},{2,18},{10... | collective-permute-start | bytes 294920 | tf_op jit(solution)/shard_map/ppermute | solution.py:42
  32.9 8.0 %collective-permute-start.15 = (f32[64,384]{0,1:T(8,128)S(1)}, f32[64,384]{0,1:T(8,128)S(1)}, u32[]{:S(2)}, u32[]{:S(2)}) collective-permute-start(f32[64,384]{0,1:T(8,128)S(1)} %get-tuple-element.93), channel_id=1, source_target_pairs={{0,24},{8,0},{16,8},{24,16},{1,25},{9,1},{17,9},{25,17},{2,26},{10... | collective-permute-start | bytes 294920 | tf_op jit(solution)/shard_map/ppermute | solution.py:42
  35.4 6.8 %collective-permute-start.12 = (f32[64,384]{0,1:T(8,128)S(1)}, f32[64,384]{0,1:T(8,128)S(1)}, u32[]{:S(2)}, u32[]{:S(2)}) collective-permute-start(f32[64,384]{0,1:T(8,128)S(1)} %get-tuple-element.104), channel_id=1, source_target_pairs={{0,4},{4,0},{1,5},{5,1},{2,6},{6,2},{3,7},{7,3},{8,12},{12,8},{9,1... | collective-permute-start | bytes 294920 | tf_op jit(solution)/shard_map/ppermute | solution.py:42
  42.1 18.4 %copy-start = (f32[4,192,128]{2,1,0:T(8,128)S(1)}, f32[4,192,128]{2,1,0:T(8,128)}, u32[]{:S(2)}) copy-start(f32[4,192,128]{2,1,0:T(8,128)} %refs_3_.5) | copy-start | bytes 1179652
  43.1 17.2 %all-to-all-start = ((f32[8,24,384]{2,1,0:T(8,128)}), f32[8,24,384]{2,1,0:T(8,128)S(1)}, u32[]{:S(2)}, u32[]{:S(2)}) async-start(f32[8,24,384]{2,1,0:T(8,128)} %pad_maximum_fusion.3), calls=%async_computation | async-start | bytes 589824 | tf_op jit(solution)/shard_map/all_to_all | solution.py:73
  50.6 2.9 %collective-permute-start.3 = (f32[2,24,128]{2,1,0:T(8,128)S(1)}, f32[2,24,128]{2,1,0:T(8,128)S(1)}, u32[]{:S(2)}, u32[]{:S(2)}) collective-permute-start(f32[2,24,128]{2,1,0:T(8,128)S(1)} %pad_maximum_fusion.10), channel_id=1, source_target_pairs={{0,1},{1,0},{2,3},{3,2},{4,5},{5,4},{6,7},{7,6},{8,9},{9,8},{10,11... | collective-permute-start | bytes 73736 | tf_op jit(solution)/shard_map/ppermute | solution.py:22
  60.8 2.8 %collective-permute-start.16 = (f32[2,24,128]{2,1,0:T(8,128)S(1)}, f32[2,24,128]{2,1,0:T(8,128)S(1)}, u32[]{:S(2)}, u32[]{:S(2)}) collective-permute-start(f32[2,24,128]{2,1,0:T(8,128)S(1)} %fusion.2), channel_id=1, source_target_pairs={{0,1},{1,0},{2,3},{3,2},{4,5},{5,4},{6,7},{7,6},{8,9},{9,8},{10,11... | collective-permute-start | bytes 73736 | tf_op jit(solution)/shard_map/ppermute | solution.py:22
  65.2 15.3 %all-to-all-start.1 = ((f32[8,40,384]{2,1,0:T(8,128)}), f32[8,40,384]{2,1,0:T(8,128)S(1)}, u32[]{:S(2)}, u32[]{:S(2)}) async-start(f32[8,40,384]{2,1,0:T(8,128)} %maximum_maximum_fusion), calls=%async_computation.1 | async-start | bytes 983040 | tf_op jit(solution)/shard_map/all_to_all | solution.py:73
  80.5 6.4 %collective-permute-start.17 = (f32[128,384]{1,0:T(8,128)S(1)}, f32[128,384]{1,0:T(8,128)S(1)}, u32[]{:S(2)}, u32[]{:S(2)}) collective-permute-start(f32[128,384]{1,0:T(8,128)S(1)} %bitcast.118), channel_id=1, source_target_pairs={{0,4},{4,0},{1,5},{5,1},{2,6},{6,2},{3,7},{7,3},{8,12},{12,8},{9,1... | collective-permute-start | bytes 589832 | tf_op jit(solution)/shard_map/ppermute | solution.py:22
  81.8 10.0 %collective-permute-start.18 = (f32[80,384]{1,0:T(8,128)S(1)}, f32[80,384]{1,0:T(8,128)S(1)}, u32[]{:S(2)}, u32[]{:S(2)}) collective-permute-start(f32[80,384]{1,0:T(8,128)S(1)} %pad_maximum_fusion.6), channel_id=1, source_target_pairs={{0,8},{8,16},{16,24},{24,0},{1,9},{9,17},{17,25},{25,1},{2,10},{10... | collective-permute-start | bytes 368648 | tf_op jit(solution)/shard_map/ppermute | solution.py:61
  84.0 7.9 %collective-permute-start.19 = (f32[80,384]{1,0:T(8,128)S(1)}, f32[80,384]{1,0:T(8,128)S(1)}, u32[]{:S(2)}, u32[]{:S(2)}) collective-permute-start(f32[80,384]{1,0:T(8,128)S(1)} %pad_maximum_fusion.6), channel_id=1, source_target_pairs={{0,16},{8,24},{16,0},{24,8},{1,17},{9,25},{17,1},{25,9},{2,18},{10... | collective-permute-start | bytes 368648 | tf_op jit(solution)/shard_map/ppermute | solution.py:61
  86.1 5.9 %collective-permute-start.20 = (f32[80,384]{1,0:T(8,128)S(1)}, f32[80,384]{1,0:T(8,128)S(1)}, u32[]{:S(2)}, u32[]{:S(2)}) collective-permute-start(f32[80,384]{1,0:T(8,128)S(1)} %pad_maximum_fusion.6), channel_id=1, source_target_pairs={{0,24},{8,0},{16,8},{24,16},{1,25},{9,1},{17,9},{25,17},{2,26},{10... | collective-permute-start | bytes 368648 | tf_op jit(solution)/shard_map/ppermute | solution.py:61
  88.2 19.7 %all-to-all-start.2 = ((f32[4,256,384]{2,1,0:T(8,128)}), f32[4,256,384]{2,1,0:T(8,128)S(1)}, u32[]{:S(2)}, u32[]{:S(2)}) async-start(f32[4,256,384]{2,1,0:T(8,128)} %broadcast_in_dim.35), calls=%async_computation.2 | async-start | bytes 3145728 | tf_op jit(solution)/shard_map/all_to_all | solution.py:73
  92.0 4.6 %collective-permute-start.24 = (f32[16,384]{1,0:T(8,128)S(1)}, f32[16,384]{1,0:T(8,128)S(1)}, u32[]{:S(2)}, u32[]{:S(2)}) collective-permute-start(f32[16,384]{1,0:T(8,128)S(1)} %slice_reduce_fusion.1), channel_id=1, source_target_pairs={{0,4},{4,0},{1,5},{5,1},{2,6},{6,2},{3,7},{7,3},{8,12},{12,8},{9,1... | collective-permute-start | bytes 73736 | tf_op jit(solution)/shard_map/ppermute | solution.py:22
  96.5 6.6 %collective-permute-start.25 = (f32[16,384]{1,0:T(8,128)S(1)}, f32[16,384]{1,0:T(8,128)S(1)}, u32[]{:S(2)}, u32[]{:S(2)}) collective-permute-start(f32[16,384]{1,0:T(8,128)S(1)} %add.303), channel_id=1, source_target_pairs={{0,128},{32,160},{64,192},{96,224},{128,0},{160,32},{192,64},{224,... | collective-permute-start | bytes 73736 | tf_op jit(solution)/shard_map/ppermute | solution.py:22
  96.8 22.7 %collective-permute-start.21 = (f32[256,384]{1,0:T(8,128)S(1)}, f32[256,384]{1,0:T(8,128)S(1)}, u32[]{:S(2)}, u32[]{:S(2)}) collective-permute-start(f32[256,384]{1,0:T(8,128)S(1)} %bitcast.113), channel_id=1, source_target_pairs={{0,4},{4,0},{1,5},{5,1},{2,6},{6,2},{3,7},{7,3},{8,12},{12,8},{9,1... | collective-permute-start | bytes 1179656 | tf_op jit(solution)/shard_map/ppermute | solution.py:22
  103.1 4.7 %collective-permute-start.26 = (f32[32,384]{1,0:T(8,128)S(1)}, f32[32,384]{1,0:T(8,128)S(1)}, u32[]{:S(2)}, u32[]{:S(2)}) collective-permute-start(f32[32,384]{1,0:T(8,128)S(1)} %pad_maximum_fusion.8), channel_id=1, source_target_pairs={{0,64},{32,96},{64,0},{96,32},{128,192},{160,224},{192,128},{224,1... | collective-permute-start | bytes 147464 | tf_op jit(solution)/shard_map/ppermute | solution.py:22
  107.9 18.7 %collective-permute-start.23 = (f32[64,2,8,384]{3,2,1,0:T(8,128)S(1)}, f32[64,2,8,384]{3,2,1,0:T(8,128)}, u32[]{:S(2)}, u32[]{:S(2)}) collective-permute-start(f32[64,2,8,384]{3,2,1,0:T(8,128)S(1)} %bitcast.99), channel_id=1, source_target_pairs={{0,2},{2,0},{1,3},{3,1},{4,6},{6,4},{5,7},{7,5},{8,10},{10,8},{9,1... | collective-permute-start | bytes 4718600 | tf_op jit(solution)/shard_map/ppermute | solution.py:22
  119.6 4.5 %collective-permute-start.27 = (f32[64,384]{1,0:T(8,128)S(1)}, f32[64,384]{1,0:T(8,128)S(1)}, u32[]{:S(2)}, u32[]{:S(2)}) collective-permute-start(f32[64,384]{1,0:T(8,128)S(1)} %pad_maximum_fusion.7), channel_id=1, source_target_pairs={{0,32},{32,0},{64,96},{96,64},{128,160},{160,128},{192,224},{224,1... | collective-permute-start | bytes 294920 | tf_op jit(solution)/shard_map/ppermute | solution.py:22
  124.8 7.0 %collective-permute-start.28 = (f32[2,128,128]{2,1,0:T(8,128)S(1)}, f32[2,128,128]{2,1,0:T(8,128)S(1)}, u32[]{:S(2)}, u32[]{:S(2)}) collective-permute-start(f32[2,128,128]{2,1,0:T(8,128)S(1)} %fusion.22), channel_id=1, source_target_pairs={{0,1},{1,0},{2,3},{3,2},{4,5},{5,4},{6,7},{7,6},{8,9},{9,8},{10,11... | collective-permute-start | bytes 393224 | tf_op jit(solution)/shard_map/ppermute | solution.py:22
  125.2 7.4 %collective-permute-start.22 = (f32[64,1,8,384]{3,2,1,0:T(8,128)S(1)}, f32[64,1,8,384]{3,2,1,0:T(8,128)S(1)}, u32[]{:S(2)}, u32[]{:S(2)}) collective-permute-start(f32[64,1,8,384]{3,2,1,0:T(8,128)S(1)} %bitcast.101), channel_id=1, source_target_pairs={{0,2},{2,0},{1,3},{3,1},{4,6},{6,4},{5,7},{7,5},{8,10},{10,8},{9,1... | collective-permute-start | bytes 2359304 | tf_op jit(solution)/shard_map/ppermute | solution.py:22
  132.4 5.1 %collective-permute-start.29 = (f32[2,192,128]{2,1,0:T(8,128)S(1)}, f32[2,192,128]{2,1,0:T(8,128)S(1)}, u32[]{:S(2)}, u32[]{:S(2)}) collective-permute-start(f32[2,192,128]{2,1,0:T(8,128)S(1)} %fusion), channel_id=1, source_target_pairs={{0,2},{2,0},{1,3},{3,1},{4,6},{6,4},{5,7},{7,5},{8,10},{10,8},{9,1... | collective-permute-start | bytes 589832 | tf_op jit(solution)/shard_map/ppermute | solution.py:22
